TPU v7x, 128 devices: a whole 4x4x4 slice. The times are simulated.
128 devices in a mesh: dp: 16 (over z, x), tensor: 8 (over y, core).
Axes of the slice: x: 4, y: 4, z: 4, core: 2. Of those that a mesh axis runs over, the one named last changes fastest.
Arguments:
- activations: bfloat16 [8192, 5120], P('dp', 'tensor'), may hold values from -6 to 6
- out_grad: bfloat16 [8192, 5120], P('dp', 'tensor'), may hold values from -6 to 6
- gate_pre: bfloat16 [8192, 14336], P('dp', 'tensor'), may hold values from -6 to 6
- up_pre: bfloat16 [8192, 14336], P('dp', 'tensor'), may hold values from -6 to 6
- down_weight: bfloat16 [14336, 5120], P(('tensor', 'dp')), may hold values from -0.046875 to 0.046875
- proj_model: bfloat16 [5120, 64], replicated, may hold values from -0.078125 to 0.078125
- proj_hidden: bfloat16 [14336, 64], P('tensor'), may hold values from -0.046875 to 0.046875
- lengths: int32 [64], P('dp'), may hold values from 1 to 128, as said below
Outputs:
- grad_gate: bfloat16 [8192, 14336], P('dp', 'tensor')
- grad_up: bfloat16 [8192, 14336], P('dp', 'tensor')
- features: float32 [64, 3, 4096], P('dp')
Inputs may be any that keep to these rules, and one draw needn't show every extreme that they name: In every block of 4 slots of one index of dp the lengths sum to at most 512. In every draw one slot among all 64 has exactly 128 tokens and another exactly 1.
All inputs are finite; a program needn't handle non-finite values.
Results may differ from a plain program's by a relative error of at most 0.003.
Values may be sent and summed in bfloat16 or wider, within the bound.
No kernel may reach another device: no remote copies, remote signals or barrier semaphores. Data moves between devices by JAX's collectives and lax.ppermute only.
A program may use at most 128 MiB of HBM per device.

v0:
```python
import jax
import jax.numpy as jnp
from jax import lax
from jax.sharding import PartitionSpec as P


def pair_features(weight, left, right):
    rows, slots = weight.shape
    width = left.shape[1]
    spread = (weight[:, :, None] * left[:, None, :]).reshape(rows, slots * width)
    mats = lax.dot_general(
        spread,
        right,
        (((0,), (0,)), ((), ())),
        precision=lax.Precision.HIGHEST,
        preferred_element_type=jnp.float32,
    )
    return mats.reshape(slots, width * width)


def on_device(
    activations, out_grad, gate_pre, up_pre, down_weight, proj_model, proj_hidden, lengths
):
    rows_here = activations.shape[0]
    offsets = jnp.cumsum(lengths) - lengths
    rows = jnp.arange(rows_here, dtype=jnp.int32)[:, None]
    member = jnp.logical_and(rows >= offsets[None, :], rows < (offsets + lengths)[None, :]).astype(
        jnp.float32
    )
    live = jnp.sum(member, axis=1)
    masked_part = out_grad * live[:, None].astype(jnp.bfloat16)
    masked = lax.all_gather(masked_part, "tensor", axis=1, tiled=True)
    full_rows = lax.all_gather(down_weight, "dp", axis=0, tiled=True)
    hidden_grad = lax.dot_general(
        masked, full_rows, (((1,), (1,)), ((), ())), preferred_element_type=jnp.float32
    )
    gate32 = gate_pre.astype(jnp.float32)
    up32 = up_pre.astype(jnp.float32)
    sig = jax.nn.sigmoid(gate32)
    silu = gate32 * sig
    grad_up = (hidden_grad * silu).astype(jnp.bfloat16)
    grad_gate = (hidden_grad * up32 * sig * (1.0 + gate32 * (1.0 - sig))).astype(jnp.bfloat16)
    hidden = (silu * up32).astype(jnp.bfloat16)
    hidden_part = jnp.dot(hidden, proj_hidden, preferred_element_type=jnp.float32)
    gate_part = jnp.dot(grad_gate, proj_hidden, preferred_element_type=jnp.float32)
    up_part = jnp.dot(grad_up, proj_hidden, preferred_element_type=jnp.float32)
    width = proj_hidden.shape[1]
    whole_inputs = lax.all_gather(activations, "tensor", axis=1, tiled=True)
    in_proj = jnp.dot(whole_inputs, proj_model, preferred_element_type=jnp.float32)
    summed = lax.psum(jnp.concatenate([hidden_part, gate_part, up_part], axis=1), "tensor")
    hidden_proj = summed[:, :width]
    gate_proj = summed[:, width : 2 * width]
    up_proj = summed[:, 2 * width :]
    out_proj = jnp.dot(masked, proj_model, preferred_element_type=jnp.float32)
    weight = member / jnp.sqrt(lengths.astype(jnp.float32))[None, :]
    features = jnp.stack(
        [
            pair_features(weight, in_proj, gate_proj),
            pair_features(weight, in_proj, up_proj),
            pair_features(weight, hidden_proj, out_proj),
        ],
        axis=1,
    )
    return (grad_gate, grad_up, features)


def solution(mesh):
    return jax.shard_map(
        on_device,
        mesh=mesh,
        in_specs=(
            P("dp", "tensor"),
            P("dp", "tensor"),
            P("dp", "tensor"),
            P("dp", "tensor"),
            P(("tensor", "dp"), None),
            P(),
            P("tensor", None),
            P("dp"),
        ),
        out_specs=(P("dp", "tensor"), P("dp", "tensor"), P("dp", None, None)),
        check_vma=False,
    )
```

profile of v0, /device:TPU:1, one launch (start us, length us, event | category | flops | bytes accessed | tf_op | source)
XLA Modules:
  0.0 283.8 jit_solution(15408122070368239808)
XLA Ops:
  7.2 0.0 all-gather.4.cloned.1.call-start
  7.2 0.8 convert_sqrt_fusion
  8.1 0.8 reduce-window.8
  8.9 0.7 bitcast_subtract_fusion
  9.5 0.1 convert_divide_fusion
  9.6 2.1 broadcast_multiply_fusion
  11.7 0.0 all-gather.4.cloned.1.call-update
  11.7 0.0 all-gather.6.cloned.1.call-start
  11.8 0.7 all-gather.6.cloned.1.call-update
  12.5 0.0 all-gather.8.cloned.1.call-start
  12.5 0.7 all-gather.8.cloned.1.call-update
  13.2 0.0 all-reduce.2.cloned.1.call-start
  13.3 2.7 fusion.8
  16.0 36.0 %all-gather.4.cloned.1.call-done = bf16[512,5120]{1,0:T(8,128)(2,1)} async-done(((bf16[512,640]{1,0:T(8,128)(2,1)}), bf16[512,5120]{1,0:T(8,128)(2,1)}) %all-gather.4.cloned.1.call-update) | async-done | bytes 5242896 | tf_op jit(solution)/shard_map/all_gather | solution.py:32
  52.0 4.0 %fusion.19 = f32[512,64]{1,0:T(8,128)S(1)} fusion(bf16[512,5120]{1,0:T(8,128)(2,1)} %all-gather.4.cloned.1.call-done, bf16[5120,64]{0,1:T(8,128)(2,1)S(1)} %copy-done), kind=kOutput, calls=%fused_computation.35 | convolution fusion | flops 335544320 | bytes 6029312 | tf_op jit(solution)/shard_map/dot_general | solution.py:54
  56.0 117.3 %all-gather.6.cloned.1.call-done = bf16[1792,5120]{1,0:T(8,128)(2,1)} async-done(((bf16[112,5120]{1,0:T(8,128)(2,1)}), bf16[1792,5120]{1,0:T(8,128)(2,1)}) %all-gather.6.cloned.1.call-update) | async-done | bytes 18350096 | tf_op jit(solution)/shard_map/all_gather | solution.py:33
  173.2 19.1 %multiply_convert_fusion = (bf16[512,1792]{1,0:T(8,128)(2,1)S(1)}, bf16[512,1792]{1,0:T(8,128)(2,1)}) fusion(bf16[512,1792]{1,0:T(8,128)(2,1)} %param.10, bf16[512,1792]{1,0:T(8,128)(2,1)} %param.11, bf16[512,5120]{1,0:T(8,128)(2,1)} %all-gather.4.cloned.1.call-done, bf16[1792,5120]{1,0:T(8,128)(2,1)} %all-gather.6.cloned.1.call-done), kind=kOutput, calls=%fused_computation.13 | convolution fusion | flops 9409003520 | bytes 30932992 | tf_op jit(solution)/shard_map/dot_general | solution.py:34
  192.4 2.8 %fusion.17 = f32[512,64]{0,1:T(8,128)S(1)} fusion(bf16[512,1792]{1,0:T(8,128)(2,1)} %get-tuple-element.4, bf16[1792,64]{0,1:T(8,128)(2,1)S(1)} %copy-done.2), kind=kOutput, calls=%fused_computation.33 | convolution fusion | flops 117440512 | bytes 2195456 | tf_op jit(solution)/shard_map/dot_general | solution.py:45
  195.2 0.7 fusion.18
  195.9 0.8 pad_maximum_fusion
  196.7 14.8 %all-gather.8.cloned.1.call-done = bf16[512,5120]{1,0:T(8,128)(2,1)} async-done(((bf16[512,640]{1,0:T(8,128)(2,1)}), bf16[512,5120]{1,0:T(8,128)(2,1)}) %all-gather.8.cloned.1.call-update) | async-done | bytes 5242896 | tf_op jit(solution)/shard_map/all_gather | solution.py:48
  211.5 4.2 %fusion.16 = f32[512,64]{0,1:T(8,128)S(1)} fusion(bf16[512,5120]{1,0:T(8,128)(2,1)} %all-gather.8.cloned.1.call-done, bf16[5120,64]{0,1:T(8,128)(2,1)S(1)} %copy-done), kind=kOutput, calls=%fused_computation.32 | convolution fusion | flops 335544320 | bytes 6029312 | tf_op jit(solution)/shard_map/dot_general | solution.py:49
  215.7 55.9 %all-reduce.2.cloned.1.call-done = f32[512,192]{0,1:T(8,128)} async-done(((f32[512,192]{0,1:T(8,128)}), f32[512,192]{0,1:T(8,128)}) %all-reduce.2.cloned.1.call-update) | async-done | bytes 393232 | tf_op jit(solution)/shard_map/psum | solution.py:50
  271.6 0.9 slice.14
  272.6 0.1 broadcast_multiply_fusion.2
  272.7 1.5 fusion.12
  274.2 0.1 stack_reshape.9
  274.3 1.5 fusion.10
  275.8 0.1 stack_reshape.10
  275.9 0.6 fusion.20
  276.5 0.1 stack_reshape.11
  276.6 0.7 pad_maximum_fusion.1
  (9 shorter events, 0.0 us)
Async XLA Ops:
  7.2 44.8 %copy-start = (bf16[5120,64]{0,1:T(8,128)(2,1)S(1)}, bf16[5120,64]{0,1:T(8,128)(2,1)}, u32[]{:S(2)}) copy-start(bf16[5120,64]{0,1:T(8,128)(2,1)} %param.13) | copy-start | bytes 1966084
  7.2 6.1 %copy-start.3 = (bf16[512,1792]{1,0:T(8,128)(2,1)S(1)}, bf16[512,1792]{1,0:T(8,128)(2,1)}, u32[]{:S(2)}) copy-start(bf16[512,1792]{1,0:T(8,128)(2,1)} %param.10) | copy-start | bytes 5505028
  7.2 6.1 %copy-start.2 = (bf16[1792,64]{0,1:T(8,128)(2,1)S(1)}, bf16[1792,64]{0,1:T(8,128)(2,1)}, u32[]{:S(2)}) copy-start(bf16[1792,64]{0,1:T(8,128)(2,1)} %param.14) | copy-start | bytes 688132
  7.2 44.8 %all-gather.4.cloned.1.call-start = ((), (), s32[]{:S(2)}) async-start(), calls=%async_computation | async-start | bytes 5898240 | tf_op jit(solution)/shard_map/all_gather | solution.py:32
  11.7 161.5 %all-gather.6.cloned.1.call-start = ((), (), s32[]{:S(2)}) async-start(), calls=%async_computation.1 | async-start | bytes 19496960 | tf_op jit(solution)/shard_map/all_gather | solution.py:33
  12.5 199.0 %all-gather.8.cloned.1.call-start = ((), (), s32[]{:S(2)}) async-start(), calls=%async_computation.2 | async-start | bytes 5898240 | tf_op jit(solution)/shard_map/all_gather | solution.py:48
  13.2 258.4 %all-reduce.2.cloned.1.call-start = ((), (), s32[]{:S(2)}) async-start(), calls=%async_computation.3 | async-start | bytes 786432 | tf_op jit(solution)/shard_map/psum | solution.py:50
  192.4 23.3 %copy-start.1 = (bf16[512,1792]{1,0:T(8,128)(2,1)}, bf16[512,1792]{1,0:T(8,128)(2,1)S(1)}, u32[]{:S(2)}) copy-start(bf16[512,1792]{1,0:T(8,128)(2,1)S(1)} %get-tuple-element.3) | copy-start | bytes 5505028
Sparse Core Ops, SparseCore 0:
  11.9 40.1 all-gather.3
  54.1 119.0 all-gather.5
  174.9 36.5 all-gather.7
  213.7 57.9 all-reduce.1
where the time goes:
time: 286 us; the launch traced here: 284 us
  waiting for transfers between devices  225 us (79%)
  matrix products  37.1 us (13%)
  between operations  13.9 us (5%)
  other arithmetic  6.07 us (2%)
    all_gather x1, waiting for transfers between devices, on_device(): full_rows = lax.all_gather(down_weight, 'dp', axis=0, tiled=True)  117 us
    psum x1, waiting for transfers between devices, on_device(): lax.psum(jnp.concatenate([hidden_part, gate_part, up_part], axis=1), 'ten...  55.9 us
    all_gather x1, waiting for transfers between devices, on_device(): masked = lax.all_gather(masked_part, 'tensor', axis=1, tiled=True)  36 us
    dot_general x1, matrix products, on_device(): lax.dot_general(masked, full_rows, (((1,), (1,)), ((), ())), preferred_el...  19.1 us
    all_gather x1, waiting for transfers between devices, on_device(): whole_inputs = lax.all_gather(activations, 'tensor', axis=1, tiled=True)  14.8 us
  transfers between devices with their start and end apart: 4, of which 4 were waited for; matrix products, arithmetic and copies ran while one was open for 12% of the time, Pallas kernels for 0%

commit v1 on v0

v1 whole, which is shorter than its diff:
```python
import functools

import jax
import jax.numpy as jnp
from jax import lax
from jax.experimental import pallas as pl
from jax.experimental.pallas import tpu as pltpu
from jax.sharding import Mesh
from jax.sharding import PartitionSpec as P

AXES = ("z", "x", "y", "c")
F32, BF16 = jnp.float32, jnp.bfloat16
ROWS, FEAT, HID, HALF, RANK, DEPTH = 512, 640, 1792, 896, 64, 5120
SHARD, TOP = 112, 64
STEP = 2 * FEAT
NT = (((1,), (1,)), ((), ()))
ANY = pl.BlockSpec(memory_space=pl.ANY)


def send(value, target):
    def line(z, x, y, c):
        return ((z % 4 * 4 + x % 4) * 4 + y % 4) * 2 + c

    pairs = [
        (line(z, x, y, c), line(*target(z, x, y, c)))
        for z in range(4)
        for x in range(4)
        for y in range(4)
        for c in range(2)
    ]
    return lax.ppermute(value, AXES, pairs)


def up_y(v):
    return send(v, lambda z, x, y, c: (z, x, y + 1, c))


def down_y(v):
    return send(v, lambda z, x, y, c: (z, x, y - 1, c))


def swap(v):
    return send(v, lambda z, x, y, c: (z, x, y, 1 - c))


def mate(v):
    return send(v, lambda z, x, y, c: (3 - z, x, y, c))


def gather_weights(own, c):
    def route(v, zero, one):
        hop = {
            "p": lambda z, x, y, c: (z ^ 1, x, y, c),
            "+": lambda z, x, y, c: (z, x + 1, y, c),
            "-": lambda z, x, y, c: (z, x - 1, y, c),
        }
        return send(v, lambda z, x, y, c: hop[zero if c == 0 else one](z, x, y, c))

    def pick(a, b):
        return jnp.where(c == 0, a, b)

    r1 = route(own, "p", "+")
    r2 = route(own, "+", "-")
    r3 = route(own, "-", "p")
    r4 = route(r1, "+", "p")
    r5 = route(pick(r1, r2), "-", "p")
    r6 = route(pick(r2[:TOP], r1[:TOP]), "+", "+")
    r7 = route(pick(r3[TOP:], r2[TOP:]), "-", "-")
    r8 = route(pick(r4[:TOP], r6), "+", "p")
    r9 = route(pick(r5[TOP:], r7), "-", "p")
    return [own, r1, r2, r3, r4, r5, r6, r7, r8, r9]


def weight_rows(z, x, c):
    zl, first = z % 2, c == 0

    def at(dz, dx):
        return ((zl + dz) % 2 * 4 + (x + dx) % 4) * SHARD

    return jnp.stack(
        [
            at(0, 0),
            jnp.where(first, at(1, 0), at(0, 3)),
            jnp.where(first, at(0, 3), at(0, 1)),
            jnp.where(first, at(0, 1), at(1, 0)),
            at(1, 3),
            at(1, 1),
            at(0, 2),
            at(0, 2) + TOP,
            at(1, 2),
            at(1, 2) + TOP,
        ]
    )


def gather_features(own):
    left, right = up_y(own), down_y(own)
    return [own, left, right, up_y(left[:256]), down_y(right[256:])]


WIDTHS = (SHARD,) * 6 + (TOP, SHARD - TOP, TOP, SHARD - TOP)


def product_kernel(first, rows, where_ref, *refs):
    mine, other, weights = refs[:5], refs[5:10], refs[10:20]
    out_ref, a_buf, w_buf, acc, a_sem, w_sem = refs[20:]
    y, c = where_ref[10], where_ref[11]
    a_copies = []
    for group, (pieces, core) in enumerate(((mine, c), (other, 1 - c))):
        lane = pl.multiple_of(core * FEAT, 128)
        for k, piece in enumerate(pieces):
            slot, lo, hi = (k, 0, 512) if k < 3 else (3, (k - 3) * 256, (k - 2) * 256)
            start, stop = max(lo, first), min(hi, first + rows)
            if start >= stop:
                continue
            a_copies.append(
                pltpu.make_async_copy(
                    piece.at[pl.ds(start - lo, stop - start), :],
                    a_buf.at[slot, pl.ds(start - first, stop - start), pl.ds(lane, FEAT)],
                    a_sem.at[group, k],
                )
            )

    def w_copies(step):
        shift = (0, 3, 1, 2)[step]
        lane = pl.multiple_of(lax.rem(y + shift, 4) * STEP, 128)
        return [
            pltpu.make_async_copy(
                w.at[:, pl.ds(lane, STEP)],
                w_buf.at[step % 2, pl.ds(pl.multiple_of(where_ref[k], 16), WIDTHS[k]), :],
                w_sem.at[step % 2, k],
            )
            for k, w in enumerate(weights)
        ]

    for copy in w_copies(0):
        copy.start()
    for copy in a_copies:
        copy.start()
    for copy in a_copies:
        copy.wait()
    for step in range(4):
        if step < 3:
            for copy in w_copies(step + 1):
                copy.start()
        for copy in w_copies(step):
            copy.wait()
        part = lax.dot_general(a_buf[step], w_buf[step % 2], NT, preferred_element_type=F32)
        if step == 0:
            acc[...] = part
        elif step < 3:
            acc[...] += part
        else:
            out_ref[...] = (acc[...] + part).astype(out_ref.dtype)


def product(first, rows, dtype, where, mine, other, weights):
    return pl.pallas_call(
        functools.partial(product_kernel, first, rows),
        out_shape=jax.ShapeDtypeStruct((rows, HALF), dtype),
        grid_spec=pltpu.PrefetchScalarGridSpec(
            num_scalar_prefetch=1,
            grid=(1,),
            in_specs=[ANY] * 20,
            out_specs=pl.BlockSpec((rows, HALF), lambda i, w: (0, 0)),
            scratch_shapes=[
                pltpu.VMEM((4, rows, STEP), BF16),
                pltpu.VMEM((2, HALF, STEP), BF16),
                pltpu.VMEM((rows, HALF), F32),
                pltpu.SemaphoreType.DMA((2, 5)),
                pltpu.SemaphoreType.DMA((2, 10)),
            ],
        ),
        compiler_params=pltpu.CompilerParams(vmem_limit_bytes=32 << 20),
        cost_estimate=pl.CostEstimate(
            flops=2 * rows * HALF * DEPTH,
            bytes_accessed=2 * DEPTH * (rows + HALF) + 4 * rows * HALF,
            transcendentals=0,
        ),
        name="product",
    )(where, *mine, *other, *weights)


def mask_kernel(live_ref, grad_ref, out_ref):
    rows = lax.broadcasted_iota(jnp.int32, (ROWS, FEAT), 0)
    total = live_ref[0] + live_ref[1] + live_ref[2] + live_ref[3]
    grad = grad_ref[...]
    out_ref[...] = jnp.where(rows < total, grad.astype(F32), 0.0).astype(BF16)


def mask_rows(lengths, out_grad):
    return pl.pallas_call(
        mask_kernel,
        out_shape=jax.ShapeDtypeStruct((ROWS, FEAT), BF16),
        grid_spec=pltpu.PrefetchScalarGridSpec(
            num_scalar_prefetch=1,
            grid=(1,),
            in_specs=[pl.BlockSpec((ROWS, FEAT), lambda i, n: (0, 0))],
            out_specs=pl.BlockSpec((ROWS, FEAT), lambda i, n: (0, 0)),
        ),
        name="mask",
    )(lengths, out_grad)


def early_kernel(where_ref, act_ref, masked_ref, pm_ref, gate_ref, up_ref, ph_ref, out_ref):
    j = pl.program_id(0)
    gate, up = gate_ref[...].astype(F32), up_ref[...].astype(F32)
    hidden = (gate * jax.nn.sigmoid(gate) * up).astype(BF16)
    part = lax.dot_general(hidden, ph_ref[...], NT, preferred_element_type=F32)

    @pl.when(j == 0)
    def _():
        pm = pm_ref[...]
        out_ref[:, 0:64] = lax.dot_general(act_ref[...], pm, NT, preferred_element_type=F32)
        out_ref[:, 64:128] = part
        out_ref[:, 128:192] = lax.dot_general(masked_ref[...], pm, NT, preferred_element_type=F32)

    @pl.when(j > 0)
    def _():
        out_ref[:, 64:128] += part


def early(where, activations, masked, pm_t, gate, up, ph_t):
    whole = pl.BlockSpec((ROWS, FEAT), lambda j, w: (0, 0))
    tile = pl.BlockSpec((ROWS, 256), lambda j, w: (0, j))
    return pl.pallas_call(
        early_kernel,
        out_shape=jax.ShapeDtypeStruct((ROWS, 3 * RANK), F32),
        grid_spec=pltpu.PrefetchScalarGridSpec(
            num_scalar_prefetch=1,
            grid=(7,),
            in_specs=[
                whole,
                whole,
                pl.BlockSpec((RANK, FEAT), lambda j, w: (0, 2 * w[10] + w[11])),
                tile,
                tile,
                pl.BlockSpec((RANK, 256), lambda j, w: (0, j)),
            ],
            out_specs=pl.BlockSpec((ROWS, 3 * RANK), lambda j, w: (0, 0)),
        ),
        cost_estimate=pl.CostEstimate(
            flops=ROWS * HID * 160, bytes_accessed=5 << 20, transcendentals=ROWS * HID
        ),
        name="early",
    )(where, activations, masked, pm_t, gate, up, ph_t)


def grads(gate_ref, up_ref, hidden_grad):
    gate, up = gate_ref[...].astype(F32), up_ref[...].astype(F32)
    sig = jax.nn.sigmoid(gate)
    grad_up = (hidden_grad * (gate * sig)).astype(BF16)
    grad_gate = (hidden_grad * up * sig * (1.0 + gate * (1.0 - sig))).astype(BF16)
    return grad_gate, grad_up


def own_kernel(where_ref, gate_ref, up_ref, h_ref, ph_ref, gg_ref, gu_ref, part_ref):
    grad_gate, grad_up = grads(gate_ref, up_ref, h_ref[...])
    gg_ref[...] = grad_gate
    gu_ref[...] = grad_up
    ph = ph_ref[...]
    part = jnp.concatenate(
        [
            lax.dot_general(g, ph, NT, preferred_element_type=F32)
            for g in (grad_gate, grad_up)
        ],
        axis=1,
    )
    j = pl.program_id(0)

    @pl.when(j == 0)
    def _():
        part_ref[...] = part

    @pl.when(j > 0)
    def _():
        part_ref[...] += part


def own_half(where, gate, up, h, ph_t):
    tile = pl.BlockSpec((ROWS, 128), lambda j, w: (0, 7 * w[12] + j))
    big = jax.ShapeDtypeStruct((ROWS, HID), BF16)
    return pl.pallas_call(
        own_kernel,
        out_shape=(big, big, jax.ShapeDtypeStruct((ROWS, 2 * RANK), F32)),
        grid_spec=pltpu.PrefetchScalarGridSpec(
            num_scalar_prefetch=1,
            grid=(7,),
            in_specs=[
                tile,
                tile,
                pl.BlockSpec((ROWS, 128), lambda j, w: (0, j)),
                pl.BlockSpec((RANK, 128), lambda j, w: (0, 7 * w[12] + j)),
            ],
            out_specs=(tile, tile, pl.BlockSpec((ROWS, 2 * RANK), lambda j, w: (0, 0))),
        ),
        cost_estimate=pl.CostEstimate(
            flops=ROWS * HALF * 280, bytes_accessed=6 << 20, transcendentals=ROWS * HALF
        ),
        name="own_half",
    )(where, gate, up, h, ph_t)


def other_kernel(where_ref, gate_ref, up_ref, h_ref, ph_ref, part_ref, w_ref, in_ref,
                 gg_in, gu_in, before_ref, gg_ref, gu_ref, feat_ref, acc):
    grad_gate, grad_up = grads(gate_ref, up_ref, h_ref[...].astype(F32))
    gg_ref[...] = grad_gate
    gu_ref[...] = grad_up
    ph = ph_ref[...]
    part = jnp.concatenate(
        [
            lax.dot_general(g, ph, NT, preferred_element_type=F32)
            for g in (grad_gate, grad_up)
        ],
        axis=1,
    )
    j = pl.program_id(0)

    @pl.when(j == 0)
    def _():
        acc[...] = part_ref[...] + part

    @pl.when(j > 0)
    def _():
        acc[...] += part

    @pl.when(j == 6)
    def _():
        weight = w_ref[...]
        left = in_ref[...]
        spread = jnp.concatenate([left * weight[:, s : s + 1] for s in range(4)], axis=1)
        feat_ref[...] = before_ref[...] + lax.dot_general(
            spread,
            acc[...],
            (((0,), (0,)), ((), ())),
            precision=lax.Precision.HIGHEST,
            preferred_element_type=F32,
        )


def other_half(k, rows, where, gate, up, h, ph_t, part, weight, in_proj, gg, gu, before):
    tile = pl.BlockSpec((rows, 128), lambda j, w: (k, 7 * (1 - w[12]) + j))
    big = jax.ShapeDtypeStruct((ROWS, HID), BF16)
    feat = pl.BlockSpec((4 * RANK, 2 * RANK), lambda j, w: (0, 0))
    return pl.pallas_call(
        other_kernel,
        out_shape=(big, big, jax.ShapeDtypeStruct((4 * RANK, 2 * RANK), F32)),
        grid_spec=pltpu.PrefetchScalarGridSpec(
            num_scalar_prefetch=1,
            grid=(7,),
            in_specs=[
                tile,
                tile,
                pl.BlockSpec((rows, 128), lambda j, w: (0, j)),
                pl.BlockSpec((RANK, 128), lambda j, w: (0, 7 * (1 - w[12]) + j)),
                pl.BlockSpec((rows, 2 * RANK), lambda j, w: (k, 0)),
                pl.BlockSpec((rows, 4), lambda j, w: (k, 0)),
                pl.BlockSpec((rows, RANK), lambda j, w: (k, 0)),
                ANY,
                ANY,
                feat,
            ],
            out_specs=(tile, tile, feat),
            scratch_shapes=[pltpu.VMEM((rows, 2 * RANK), F32)],
        ),
        input_output_aliases={8: 0, 9: 1},
        cost_estimate=pl.CostEstimate(
            flops=rows * HALF * 280, bytes_accessed=3 << 20, transcendentals=rows * HALF
        ),
        name="other_half",
    )(where, gate, up, h, ph_t, part, weight, in_proj, gg, gu, before)


def sum_tensor(value, c):
    half = value.shape[0] // 2
    top, low = value[:half], value[half:]
    mine = jnp.where(c == 0, top, low) + swap(jnp.where(c == 0, low, top))
    across = send(mine, lambda z, x, y, c: (z, x, y + 2, c))
    mine = (mine + across) + (up_y(mine) + down_y(mine))
    theirs = swap(mine)
    return jnp.concatenate(
        [jnp.where(c == 0, mine, theirs), jnp.where(c == 0, theirs, mine)], axis=0
    )


def on_device(
    activations, out_grad, gate_pre, up_pre, down_weight, proj_model, proj_hidden, lengths
):
    z, x, y, c = (lax.axis_index(a) for a in AXES)
    where = jnp.concatenate(
        [weight_rows(z, x, c), jnp.stack([y, c, z // 2])]
    ).astype(jnp.int32)
    weights = gather_weights(down_weight, c)
    masked = mask_rows(lengths, out_grad)
    theirs = mate(masked)
    a_mine = gather_features(masked)
    b_mine = gather_features(theirs)
    a_other = [swap(v) for v in a_mine]
    b_other = [swap(v) for v in b_mine]

    pm_t, ph_t = proj_model.T, proj_hidden.T
    parts = early(where, activations, masked, pm_t, gate_pre, up_pre, ph_t)
    mixed = lax.all_to_all(parts.reshape(8, 64, 3 * RANK), ("y", "c"), 0, 0)
    slice_proj = jnp.sum(mixed, axis=0)
    in_proj = lax.all_gather(slice_proj[:, :RANK], ("y", "c"), axis=0, tiled=True)

    offsets = jnp.cumsum(lengths) - lengths
    rows = jnp.arange(ROWS, dtype=jnp.int32)[:, None]
    member = jnp.logical_and(rows >= offsets[None, :], rows < (offsets + lengths)[None, :])
    weight = member.astype(F32) / jnp.sqrt(lengths.astype(F32))[None, :]
    slice_weight = lax.dynamic_slice(weight, ((2 * y + c) * 64, 0), (64, 4))
    spread = slice_weight[:, :, None] * slice_proj[:, None, RANK : 2 * RANK]
    down_feat = lax.dot_general(
        spread.reshape(64, 4 * RANK),
        slice_proj[:, 2 * RANK :],
        (((0,), (0,)), ((), ())),
        precision=lax.Precision.HIGHEST,
        preferred_element_type=F32,
    )

    h_out = [product(k * 256, 256, BF16, where, b_mine, b_other, weights) for k in range(2)]
    h_in = [mate(h) for h in h_out]
    h_own = product(0, 512, F32, where, a_mine, a_other, weights)
    grad_gate, grad_up, part = own_half(where, gate_pre, up_pre, h_own, ph_t)
    feat = jnp.zeros((4 * RANK, 2 * RANK), F32)
    for k in range(2):
        grad_gate, grad_up, feat = other_half(
            k, 256, where, gate_pre, up_pre, h_in[k], ph_t, part, weight, in_proj,
            grad_gate, grad_up, feat,
        )
    total = sum_tensor(jnp.concatenate([feat, down_feat], axis=1), c)
    features = total.reshape(4, RANK, 3, RANK).transpose(0, 2, 1, 3).reshape(4, 3, RANK * RANK)
    return grad_gate, grad_up, features


def solution(mesh):
    split = Mesh(mesh.devices.reshape(4, 4, 4, 2), AXES)
    dp, tensor = ("z", "x"), ("y", "c")
    return jax.shard_map(
        on_device,
        mesh=split,
        in_specs=(
            P(dp, tensor),
            P(dp, tensor),
            P(dp, tensor),
            P(dp, tensor),
            P((*tensor, *dp), None),
            P(),
            P(tensor, None),
            P(dp),
        ),
        out_specs=(P(dp, tensor), P(dp, tensor), P(dp, None, None)),
        check_vma=False,
    )
```

time: 286 us -> 205 us (0.72)
  waiting for transfers between devices: 225 us -> 36.3 us
  Pallas kernels: 0 us -> 58.4 us
  starting transfers between devices: 0.16 us -> 58 us
  matrix products: 37.1 us -> 1.88 us
  local copies, waits for them, and re-layouts: 1.26 us -> 25.1 us
  blocking collectives: 0 us -> 16 us
  between operations: 13.9 us -> 1.04 us
    all_gather x3 -> x0, waiting for transfers between devices: 168 us -> none  [the longest x1 117 us: on_device(): full_rows = lax.all_gather(down_weight, 'dp', axis=0, tiled=True)]
    pallas_call x0 -> x8, Pallas kernels: none -> 58.4 us  [the longest x3 25.4 us: product(): pl.pallas_call(functools.partial(product_kernel, first, rows), out_shape=...]
    psum x1 -> x0, waiting for transfers between devices: 55.9 us -> none  [on_device(): lax.psum(jnp.concatenate([hidden_part, gate_part, up_part], axis=1), 'ten...]
    ppermute x0 -> x35, starting transfers between devices: none -> 53.2 us  [send(): return lax.ppermute(value, AXES, pairs)]
    dot_general x9 -> x1, matrix products: 37.1 us -> 1.88 us  [on_device(): lax.dot_general(spread.reshape(64, 4 * RANK), slice_proj[:, 2 * RANK:], (...]
    ppermute x0 -> x35, waiting for transfers between devices: none -> 28.3 us  [send(): return lax.ppermute(value, AXES, pairs)]
    unnamed x8 -> x68, local copies, waits for them, and re-layouts: 0.02 us -> 16.1 us
    all_gather x0 -> x1, blocking collectives: none -> 16 us  [on_device(): lax.all_gather(slice_proj[:, :RANK], ('y', 'c'), axis=0, tiled=True)]
  transfers between devices with their start and end apart: 4 -> 36, of which waited for: 4 -> 9; matrix products, arithmetic and copies ran while one was open for 12% -> 7% of each run, Pallas kernels for 0% -> 25%
where the time goes in v1:
time: 205 us; the launch traced here: 203 us
  Pallas kernels  58.4 us (28%)
  starting transfers between devices  58 us (28%)
  waiting for transfers between devices  36.3 us (18%)
  local copies, waits for them, and re-layouts  25.1 us (12%)
  blocking collectives  16 us (8%)
  other arithmetic  6.08 us (3%)
    ppermute x35, starting transfers between devices, send(): return lax.ppermute(value, AXES, pairs)  53.2 us
    ppermute x35, waiting for transfers between devices, send(): return lax.ppermute(value, AXES, pairs)  28.3 us
    pallas_call x3, Pallas kernels, product(): pl.pallas_call(functools.partial(product_kernel, first, rows), out_shape=...  25.4 us
    unnamed x68, local copies, waits for them, and re-layouts  16.1 us
    all_gather x1, blocking collectives, on_device(): lax.all_gather(slice_proj[:, :RANK], ('y', 'c'), axis=0, tiled=True)  16 us
    pallas_call x2, Pallas kernels, other_half(): pl.pallas_call(other_kernel, out_shape=(big, big, jax.ShapeDtypeStruct((4...  14.7 us
    pallas_call x1, Pallas kernels, early(): pl.pallas_call(early_kernel, out_shape=jax.ShapeDtypeStruct((ROWS, 3 * RA...  8.25 us
    all_to_all x1, waiting for transfers between devices, on_device(): mixed = lax.all_to_all(parts.reshape(8, 64, 3 * RANK), ('y', 'c'), 0, 0)  8 us
  transfers between devices with their start and end apart: 36, of which 9 were waited for; matrix products, arithmetic and copies ran while one was open for 7% of the time, Pallas kernels for 25%

profile of v1, /device:TPU:1, one launch (start us, length us, event | category | flops | bytes accessed | tf_op | source)
XLA Modules:
  0.0 202.9 jit_solution(4074554254227797655)
XLA Ops:
  0.6 2.1 %collective-permute-start.10 = (bf16[112,5120]{1,0:T(8,128)(2,1)}, bf16[112,5120]{1,0:T(8,128)(2,1)S(1)}, u32[]{:S(2)}, u32[]{:S(2)}) collective-permute-start(bf16[112,5120]{1,0:T(8,128)(2,1)} %refs_10_.5), channel_id=1, source_target_pairs={{0,32},{1,9},{2,34},{3,11},{4,36},{5,13},{6,38},{7,15},{8,40},{9,1... | collective-permute-start | bytes 3440648 | tf_op jit(solution)/shard_map/ppermute | solution.py:31
  2.7 1.4 collective-permute-start.11
  4.1 2.8 %mask.1.refs_0_.masked_ref = bf16[512,640]{1,0:T(8,128)(2,1)} custom-call(s32[4]{0:T(128)} %live_ref.1, bf16[512,640]{1,0:T(8,128)(2,1)} %grad_ref.1), custom_call_target="tpu_custom_call" | custom-call | tf_op jit(solution)/shard_map/mask/pallas_call | solution.py:192
  6.9 3.9 %collective-permute-start = (bf16[512,640]{1,0:T(8,128)(2,1)}, bf16[512,640]{1,0:T(8,128)(2,1)}, u32[]{:S(2)}, u32[]{:S(2)}) collective-permute-start(bf16[512,640]{1,0:T(8,128)(2,1)} %mask.1.refs_0_.masked_ref), channel_id=1, source_target_pairs={{0,96},{1,97},{2,98},{3,99},{4,100},{5,101},{6,102},{7,103},{8,104... | collective-permute-start | bytes 1966088 | tf_op jit(solution)/shard_map/ppermute | solution.py:31
  12.0 1.4 collective-permute-start.21
  14.2 8.2 %early.1 = f32[512,192]{1,0:T(8,128)} custom-call(s32[13]{0:T(128)} %concatenate.9.where_ref, bf16[512,640]{1,0:T(8,128)(2,1)} %act_ref.1, bf16[512,640]{1,0:T(8,128)(2,1)} %mask.1.refs_0_.masked_ref, bf16[64,5120]{1,0:T(8,128)(2,1)} %bitcast.33, bf16[512,1792]{1,0:T(8,128)(2,1)} %gate_ref.7, bf16[512,1792]{1,0:T(8,128)(2,1)} %up_ref.7, ...), custom_call_target="tpu_custom_call" | custom-call | flops 146800640 | bytes 5242880 | tf_op jit(solution)/shard_map/early/pallas_call | solution.py:226
  22.4 4.8 %all-to-all-start = ((f32[8,64,192]{2,1,0:T(8,128)}), f32[8,64,192]{2,1,0:T(8,128)}, u32[]{:S(2)}, u32[]{:S(2)}) async-start(f32[8,64,192]{2,1,0:T(8,128)} %bitcast.31), calls=%async_computation | async-start | bytes 1048576 | tf_op jit(solution)/shard_map/all_to_all | solution.py:403
  28.8 8.0 %all-to-all-done = f32[8,64,192]{2,1,0:T(8,128)} async-done(((f32[8,64,192]{2,1,0:T(8,128)}), f32[8,64,192]{2,1,0:T(8,128)}, u32[]{:S(2)}, u32[]{:S(2)}) %all-to-all-start) | async-done | bytes 393248 | tf_op jit(solution)/shard_map/all_to_all | solution.py:403
  41.2 2.4 %collective-permute-start.23 = (bf16[256,640]{1,0:T(8,128)(2,1)S(1)}, bf16[256,640]{1,0:T(8,128)(2,1)S(1)}, u32[]{:S(2)}, u32[]{:S(2)}) collective-permute-start(bf16[256,640]{1,0:T(8,128)(2,1)S(1)} %slice.69), channel_id=1, source_target_pairs={{0,6},{1,7},{2,0},{3,1},{4,2},{5,3},{6,4},{7,5},{8,14},{9,15},{10,... | collective-permute-start | bytes 983048 | tf_op jit(solution)/shard_map/ppermute | solution.py:31
  43.7 2.7 %collective-permute-start.2 = (bf16[512,640]{1,0:T(8,128)(2,1)}, bf16[512,640]{1,0:T(8,128)(2,1)}, u32[]{:S(2)}, u32[]{:S(2)}) collective-permute-start(bf16[512,640]{1,0:T(8,128)(2,1)} %collective-permute-done.refs_0_), channel_id=1, source_target_pairs={{0,6},{1,7},{2,0},{3,1},{4,2},{5,3},{6,4},{7,5},{8,14},{9,15},{10,... | collective-permute-start | bytes 1966088 | tf_op jit(solution)/shard_map/ppermute | solution.py:31
  46.6 6.5 %collective-permute-done.12.refs_13_ = bf16[112,5120]{1,0:T(8,128)(2,1)S(1)} collective-permute-done((bf16[112,5120]{1,0:T(8,128)(2,1)S(1)}, bf16[112,5120]{1,0:T(8,128)(2,1)S(1)}, u32[]{:S(2)}, u32[]{:S(2)}) %collective-permute-start.12) | collective-permute-done | bytes 1146912 | tf_op jit(solution)/shard_map/ppermute | solution.py:31
  54.4 8.2 %collective-permute-done.1.refs_1_ = bf16[512,640]{1,0:T(8,128)(2,1)} collective-permute-done((bf16[512,640]{1,0:T(8,128)(2,1)}, bf16[512,640]{1,0:T(8,128)(2,1)}, u32[]{:S(2)}, u32[]{:S(2)}) %collective-permute-start.1) | collective-permute-done | bytes 655392 | tf_op jit(solution)/shard_map/ppermute | solution.py:31
  64.4 3.7 %collective-permute-start.5 = (bf16[512,640]{1,0:T(8,128)(2,1)}, bf16[512,640]{1,0:T(8,128)(2,1)S(1)}, u32[]{:S(2)}, u32[]{:S(2)}) collective-permute-start(bf16[512,640]{1,0:T(8,128)(2,1)} %collective-permute-done.refs_0_), channel_id=1, source_target_pairs={{0,1},{1,0},{2,3},{3,2},{4,5},{5,4},{6,7},{7,6},{8,9},{9,8},{10,11... | collective-permute-start | bytes 1966088 | tf_op jit(solution)/shard_map/ppermute | solution.py:31
  69.9 1.5 collective-permute-start.16
  71.4 6.2 %collective-permute-done.13.refs_14_ = bf16[112,5120]{1,0:T(8,128)(2,1)S(1)} collective-permute-done((bf16[112,5120]{1,0:T(8,128)(2,1)S(1)}, bf16[112,5120]{1,0:T(8,128)(2,1)S(1)}, u32[]{:S(2)}, u32[]{:S(2)}) %collective-permute-start.13) | collective-permute-done | bytes 1146912 | tf_op jit(solution)/shard_map/ppermute | solution.py:31
  78.6 7.5 %collective-permute-start.6 = (bf16[512,640]{1,0:T(8,128)(2,1)}, bf16[512,640]{1,0:T(8,128)(2,1)}, u32[]{:S(2)}, u32[]{:S(2)}) collective-permute-start(bf16[512,640]{1,0:T(8,128)(2,1)} %collective-permute-done.1.refs_1_), channel_id=1, source_target_pairs={{0,1},{1,0},{2,3},{3,2},{4,5},{5,4},{6,7},{7,6},{8,9},{9,8},{10,11... | collective-permute-start | bytes 1966088 | tf_op jit(solution)/shard_map/ppermute | solution.py:31
  86.2 4.6 %collective-permute-start.8 = (bf16[256,640]{1,0:T(8,128)(2,1)S(1)}, bf16[256,640]{1,0:T(8,128)(2,1)S(1)}, u32[]{:S(2)}, u32[]{:S(2)}) collective-permute-start(bf16[256,640]{1,0:T(8,128)(2,1)S(1)} %collective-permute-done.3.refs_3_), channel_id=1, source_target_pairs={{0,1},{1,0},{2,3},{3,2},{4,5},{5,4},{6,7},{7,6},{8,9},{9,8},{10,11... | collective-permute-start | bytes 983048 | tf_op jit(solution)/shard_map/ppermute | solution.py:31
  90.8 4.7 %collective-permute-start.9 = (bf16[256,640]{1,0:T(8,128)(2,1)S(1)}, bf16[256,640]{1,0:T(8,128)(2,1)S(1)}, u32[]{:S(2)}, u32[]{:S(2)}) collective-permute-start(bf16[256,640]{1,0:T(8,128)(2,1)S(1)} %collective-permute-done.4.refs_4_), channel_id=1, source_target_pairs={{0,1},{1,0},{2,3},{3,2},{4,5},{5,4},{6,7},{7,6},{8,9},{9,8},{10,11... | collective-permute-start | bytes 983048 | tf_op jit(solution)/shard_map/ppermute | solution.py:31
  102.4 1.7 mul.84
  104.1 16.0 %all_gather.3.in_ref = f32[512,64]{1,0:T(8,128)} all-gather(f32[64,64]{1,0:T(8,128)S(1)} %get-tuple-element.24), channel_id=1, replica_groups=mesh['z'=4,'x'=4,'y'=4,'c'=2] {'y','c'}, dimensions={0}, use_global_device_ids=true | all-gather | bytes 147456 | tf_op jit(solution)/shard_map/all_gather | solution.py:405
  120.6 1.9 fusion.2
  133.9 7.8 %product.5 = bf16[256,896]{1,0:T(8,128)(2,1)} custom-call(s32[13]{0:T(128)S(1)} %copy-done.25, bf16[512,640]{1,0:T(8,128)(2,1)} %collective-permute-done.refs_0_, bf16[512,640]{1,0:T(8,128)(2,1)} %collective-permute-done.1.refs_1_, bf16[512,640]{1,0:T(8,128)(2,1)} %collective-permute-done.2.refs_2_, bf16[256,640]{1,0:T(8,128)(2,1)S(1)} %copy-done.18, ...), custom_call_target="tpu_custom_call" | custom-call | flops 2348810240 | bytes 12713984 | tf_op jit(solution)/shard_map/product/pallas_call | solution.py:158
  142.3 7.8 %product.3 = bf16[256,896]{1,0:T(8,128)(2,1)} custom-call(s32[13]{0:T(128)S(1)} %copy-done.25, bf16[512,640]{1,0:T(8,128)(2,1)} %collective-permute-done.refs_0_, bf16[512,640]{1,0:T(8,128)(2,1)} %collective-permute-done.1.refs_1_, bf16[512,640]{1,0:T(8,128)(2,1)} %collective-permute-done.2.refs_2_, bf16[256,640]{1,0:T(8,128)(2,1)S(1)} %copy-done.18, ...), custom_call_target="tpu_custom_call" | custom-call | flops 2348810240 | bytes 12713984 | tf_op jit(solution)/shard_map/product/pallas_call | solution.py:158
  150.1 2.5 %collective-permute-start.19 = (bf16[256,896]{1,0:T(8,128)(2,1)}, bf16[256,896]{1,0:T(8,128)(2,1)}, u32[]{:S(2)}, u32[]{:S(2)}) collective-permute-start(bf16[256,896]{1,0:T(8,128)(2,1)} %product.3), channel_id=1, source_target_pairs={{0,96},{1,97},{2,98},{3,99},{4,100},{5,101},{6,102},{7,103},{8,104... | collective-permute-start | bytes 1376264 | tf_op jit(solution)/shard_map/ppermute | solution.py:31
  152.7 9.8 %product.4.h_ref = f32[512,896]{1,0:T(8,128)S(1)} custom-call(s32[13]{0:T(128)S(1)} %copy-done.25, bf16[512,640]{1,0:T(8,128)(2,1)} %mask.1.refs_0_.masked_ref, bf16[512,640]{1,0:T(8,128)(2,1)} %collective-permute-done.20.refs_1_, bf16[512,640]{1,0:T(8,128)(2,1)} %collective-permute-done.21.refs_2_, bf16[256,640]{1,0:T(8,128)(2,1)S(1)} %copy-done.27, ...), custom_call_target="tpu_custom_call" | custom-call | flops 4697620480 | bytes 16252928 | tf_op jit(solution)/shard_map/product/pallas_call | solution.py:158
  163.7 7.3 %own_half.1 = (bf16[512,1792]{1,0:T(8,128)(2,1)}, bf16[512,1792]{1,0:T(8,128)(2,1)}, f32[512,128]{1,0:T(8,128)}) custom-call(s32[13]{0:T(128)} %concatenate.9.where_ref, bf16[512,1792]{1,0:T(8,128)(2,1)} %gate_ref.7, bf16[512,1792]{1,0:T(8,128)(2,1)} %up_ref.7, f32[512,896]{1,0:T(8,128)} %copy-done.16, bf16[64,1792]{1,0:T(8,128)(2,1)} %bitcast.28), custom_call_target="tpu_custom_call" | custom-call | flops 128450560 | bytes 6291456 | tf_op jit(solution)/shard_map/own_half/pallas_call | solution.py:283
  171.8 7.3 %other_half.2 = (bf16[512,1792]{1,0:T(8,128)(2,1)}, bf16[512,1792]{1,0:T(8,128)(2,1)}, f32[256,128]{1,0:T(8,128)}) custom-call(s32[13]{0:T(128)} %concatenate.9.where_ref, bf16[512,1792]{1,0:T(8,128)(2,1)} %gate_ref.7, bf16[512,1792]{1,0:T(8,128)(2,1)} %up_ref.7, ...), custom_call_target="tpu_custom_call", output_to_operand_aliasing={{0}: (8, {}), {1}: (9, {})} | custom-call | flops 64225280 | bytes 3145728 | tf_op jit(solution)/shard_map/other_half/pallas_call | solution.py:345
  179.1 7.4 %other_half.3 = (bf16[512,1792]{1,0:T(8,128)(2,1)}, bf16[512,1792]{1,0:T(8,128)(2,1)}, f32[256,128]{1,0:T(8,128)}) custom-call(s32[13]{0:T(128)} %concatenate.9.where_ref, bf16[512,1792]{1,0:T(8,128)(2,1)} %gate_ref.7, bf16[512,1792]{1,0:T(8,128)(2,1)} %up_ref.7, ...), custom_call_target="tpu_custom_call", output_to_operand_aliasing={{0}: (8, {}), {1}: (9, {})} | custom-call | flops 64225280 | bytes 3145728 | tf_op jit(solution)/shard_map/other_half/pallas_call | solution.py:345
  190.3 2.7 %collective-permute-start.33 = (f32[128,192]{1,0:T(8,128)S(1)}, f32[128,192]{1,0:T(8,128)S(1)}, u32[]{:S(2)}, u32[]{:S(2)}) collective-permute-start(f32[128,192]{1,0:T(8,128)S(1)} %select_add_fusion), channel_id=1, source_target_pairs={{0,6},{1,7},{2,0},{3,1},{4,2},{5,3},{6,4},{7,5},{8,14},{9,15},{10,... | collective-permute-start | bytes 294920 | tf_op jit(solution)/shard_map/ppermute | solution.py:31
  193.0 3.3 %collective-permute-done.32 = f32[128,192]{1,0:T(8,128)S(1)} collective-permute-done((f32[128,192]{1,0:T(8,128)S(1)}, f32[128,192]{1,0:T(8,128)S(1)}, u32[]{:S(2)}, u32[]{:S(2)}) %collective-permute-start.32) | collective-permute-done | bytes 98336 | tf_op jit(solution)/shard_map/ppermute | solution.py:31
  196.2 1.9 collective-permute-done.33
  198.3 2.2 %collective-permute-start.34 = (f32[128,192]{1,0:T(8,128)S(1)}, f32[128,192]{1,0:T(8,128)S(1)}, u32[]{:S(2)}, u32[]{:S(2)}) collective-permute-start(f32[128,192]{1,0:T(8,128)S(1)} %add_add_fusion), channel_id=1, source_target_pairs={{0,1},{1,0},{2,3},{3,2},{4,5},{5,4},{6,7},{7,6},{8,9},{9,8},{10,11... | collective-permute-start | bytes 294920 | tf_op jit(solution)/shard_map/ppermute | solution.py:31
  (147 shorter events, 41.7 us)
Async XLA Ops:
  0.6 43.1 %collective-permute-start.10 = (bf16[112,5120]{1,0:T(8,128)(2,1)}, bf16[112,5120]{1,0:T(8,128)(2,1)S(1)}, u32[]{:S(2)}, u32[]{:S(2)}) collective-permute-start(bf16[112,5120]{1,0:T(8,128)(2,1)} %refs_10_.5), channel_id=1, source_target_pairs={{0,32},{1,9},{2,34},{3,11},{4,36},{5,13},{6,38},{7,15},{8,40},{9,1... | collective-permute-start | bytes 3440648 | tf_op jit(solution)/shard_map/ppermute | solution.py:31
  2.7 41.0 %collective-permute-start.11 = (bf16[112,5120]{1,0:T(8,128)(2,1)}, bf16[112,5120]{1,0:T(8,128)(2,1)S(1)}, u32[]{:S(2)}, u32[]{:S(2)}) collective-permute-start(bf16[112,5120]{1,0:T(8,128)(2,1)} %refs_10_.5), channel_id=1, source_target_pairs={{0,8},{1,25},{2,10},{3,27},{4,12},{5,29},{6,14},{7,31},{8,16},{9,1... | collective-permute-start | bytes 3440648 | tf_op jit(solution)/shard_map/ppermute | solution.py:31
  6.9 34.4 %collective-permute-start = (bf16[512,640]{1,0:T(8,128)(2,1)}, bf16[512,640]{1,0:T(8,128)(2,1)}, u32[]{:S(2)}, u32[]{:S(2)}) collective-permute-start(bf16[512,640]{1,0:T(8,128)(2,1)} %mask.1.refs_0_.masked_ref), channel_id=1, source_target_pairs={{0,96},{1,97},{2,98},{3,99},{4,100},{5,101},{6,102},{7,103},{8,104... | collective-permute-start | bytes 1966088 | tf_op jit(solution)/shard_map/ppermute | solution.py:31
  10.7 27.3 %collective-permute-start.20 = (bf16[512,640]{1,0:T(8,128)(2,1)}, bf16[512,640]{1,0:T(8,128)(2,1)}, u32[]{:S(2)}, u32[]{:S(2)}) collective-permute-start(bf16[512,640]{1,0:T(8,128)(2,1)} %mask.1.refs_0_.masked_ref), channel_id=1, source_target_pairs={{0,2},{1,3},{2,4},{3,5},{4,6},{5,7},{6,0},{7,1},{8,10},{9,11},{10,... | collective-permute-start | bytes 1966088 | tf_op jit(solution)/shard_map/ppermute | solution.py:31
  12.0 27.8 %collective-permute-start.21 = (bf16[512,640]{1,0:T(8,128)(2,1)}, bf16[512,640]{1,0:T(8,128)(2,1)}, u32[]{:S(2)}, u32[]{:S(2)}) collective-permute-start(bf16[512,640]{1,0:T(8,128)(2,1)} %mask.1.refs_0_.masked_ref), channel_id=1, source_target_pairs={{0,6},{1,7},{2,0},{3,1},{4,2},{5,3},{6,4},{7,5},{8,14},{9,15},{10,... | collective-permute-start | bytes 1966088 | tf_op jit(solution)/shard_map/ppermute | solution.py:31
  22.4 14.4 %all-to-all-start = ((f32[8,64,192]{2,1,0:T(8,128)}), f32[8,64,192]{2,1,0:T(8,128)}, u32[]{:S(2)}, u32[]{:S(2)}) async-start(f32[8,64,192]{2,1,0:T(8,128)} %bitcast.31), calls=%async_computation | async-start | bytes 1048576 | tf_op jit(solution)/shard_map/all_to_all | solution.py:403
  38.0 15.1 %collective-permute-start.12 = (bf16[112,5120]{1,0:T(8,128)(2,1)S(1)}, bf16[112,5120]{1,0:T(8,128)(2,1)S(1)}, u32[]{:S(2)}, u32[]{:S(2)}) collective-permute-start(bf16[112,5120]{1,0:T(8,128)(2,1)S(1)} %copy-done.9), channel_id=1, source_target_pairs={{0,24},{1,33},{2,26},{3,35},{4,28},{5,37},{6,30},{7,39},{8,0},{9,4... | collective-permute-start | bytes 3440648 | tf_op jit(solution)/shard_map/ppermute | solution.py:31
  39.8 29.2 %collective-permute-start.22 = (bf16[256,640]{1,0:T(8,128)(2,1)S(1)}, bf16[256,640]{1,0:T(8,128)(2,1)S(1)}, u32[]{:S(2)}, u32[]{:S(2)}) collective-permute-start(bf16[256,640]{1,0:T(8,128)(2,1)S(1)} %slice.68), channel_id=1, source_target_pairs={{0,2},{1,3},{2,4},{3,5},{4,6},{5,7},{6,0},{7,1},{8,10},{9,11},{10,... | collective-permute-start | bytes 983048 | tf_op jit(solution)/shard_map/ppermute | solution.py:31
  41.2 28.7 %collective-permute-start.23 = (bf16[256,640]{1,0:T(8,128)(2,1)S(1)}, bf16[256,640]{1,0:T(8,128)(2,1)S(1)}, u32[]{:S(2)}, u32[]{:S(2)}) collective-permute-start(bf16[256,640]{1,0:T(8,128)(2,1)S(1)} %slice.69), channel_id=1, source_target_pairs={{0,6},{1,7},{2,0},{3,1},{4,2},{5,3},{6,4},{7,5},{8,14},{9,15},{10,... | collective-permute-start | bytes 983048 | tf_op jit(solution)/shard_map/ppermute | solution.py:31
  43.7 18.9 %collective-permute-start.1 = (bf16[512,640]{1,0:T(8,128)(2,1)}, bf16[512,640]{1,0:T(8,128)(2,1)}, u32[]{:S(2)}, u32[]{:S(2)}) collective-permute-start(bf16[512,640]{1,0:T(8,128)(2,1)} %collective-permute-done.refs_0_), channel_id=1, source_target_pairs={{0,2},{1,3},{2,4},{3,5},{4,6},{5,7},{6,0},{7,1},{8,10},{9,11},{10,... | collective-permute-start | bytes 1966088 | tf_op jit(solution)/shard_map/ppermute | solution.py:31
  43.7 20.7 %collective-permute-start.2 = (bf16[512,640]{1,0:T(8,128)(2,1)}, bf16[512,640]{1,0:T(8,128)(2,1)}, u32[]{:S(2)}, u32[]{:S(2)}) collective-permute-start(bf16[512,640]{1,0:T(8,128)(2,1)} %collective-permute-done.refs_0_), channel_id=1, source_target_pairs={{0,6},{1,7},{2,0},{3,1},{4,2},{5,3},{6,4},{7,5},{8,14},{9,15},{10,... | collective-permute-start | bytes 1966088 | tf_op jit(solution)/shard_map/ppermute | solution.py:31
  53.1 18.3 %collective-permute-start.15 = (bf16[64,5120]{1,0:T(8,128)(2,1)S(1)}, bf16[64,5120]{1,0:T(8,128)(2,1)S(1)}, u32[]{:S(2)}, u32[]{:S(2)}) collective-permute-start(bf16[64,5120]{1,0:T(8,128)(2,1)S(1)} %slice_select_fusion.1), channel_id=1, source_target_pairs={{0,8},{1,9},{2,10},{3,11},{4,12},{5,13},{6,14},{7,15},{8,16},{9,17... | collective-permute-start | bytes 1966088 | tf_op jit(solution)/shard_map/ppermute | solution.py:31
  62.6 15.0 %collective-permute-start.13 = (bf16[112,5120]{1,0:T(8,128)(2,1)S(1)}, bf16[112,5120]{1,0:T(8,128)(2,1)S(1)}, u32[]{:S(2)}, u32[]{:S(2)}) collective-permute-start(bf16[112,5120]{1,0:T(8,128)(2,1)S(1)} %collective-permute-done.10.refs_11_), channel_id=1, source_target_pairs={{0,8},{1,33},{2,10},{3,35},{4,12},{5,37},{6,14},{7,39},{8,16},{9,4... | collective-permute-start | bytes 3440648 | tf_op jit(solution)/shard_map/ppermute | solution.py:31
  64.4 14.2 %collective-permute-start.5 = (bf16[512,640]{1,0:T(8,128)(2,1)}, bf16[512,640]{1,0:T(8,128)(2,1)S(1)}, u32[]{:S(2)}, u32[]{:S(2)}) collective-permute-start(bf16[512,640]{1,0:T(8,128)(2,1)} %collective-permute-done.refs_0_), channel_id=1, source_target_pairs={{0,1},{1,0},{2,3},{3,2},{4,5},{5,4},{6,7},{7,6},{8,9},{9,8},{10,11... | collective-permute-start | bytes 1966088 | tf_op jit(solution)/shard_map/ppermute | solution.py:31
  69.1 27.2 %collective-permute-start.14 = (bf16[112,5120]{1,0:T(8,128)(2,1)S(1)}, bf16[112,5120]{1,0:T(8,128)(2,1)S(1)}, u32[]{:S(2)}, u32[]{:S(2)}) collective-permute-start(bf16[112,5120]{1,0:T(8,128)(2,1)S(1)} %broadcast_select_fusion), channel_id=1, source_target_pairs={{0,24},{1,33},{2,26},{3,35},{4,28},{5,37},{6,30},{7,39},{8,0},{9,4... | collective-permute-start | bytes 3440648 | tf_op jit(solution)/shard_map/ppermute | solution.py:31
  69.9 20.9 %collective-permute-start.16 = (bf16[48,5120]{1,0:T(8,128)(2,1)S(1)}, bf16[48,5120]{1,0:T(8,128)(2,1)S(1)}, u32[]{:S(2)}, u32[]{:S(2)}) collective-permute-start(bf16[48,5120]{1,0:T(8,128)(2,1)S(1)} %slice_select_fusion.3), channel_id=1, source_target_pairs={{0,24},{1,25},{2,26},{3,27},{4,28},{5,29},{6,30},{7,31},{8,0},{9,1... | collective-permute-start | bytes 1474568 | tf_op jit(solution)/shard_map/ppermute | solution.py:31
  71.4 14.7 %collective-permute-start.3 = (bf16[256,640]{1,0:T(8,128)(2,1)S(1)}, bf16[256,640]{1,0:T(8,128)(2,1)S(1)}, u32[]{:S(2)}, u32[]{:S(2)}) collective-permute-start(bf16[256,640]{1,0:T(8,128)(2,1)S(1)} %slice.60), channel_id=1, source_target_pairs={{0,2},{1,3},{2,4},{3,5},{4,6},{5,7},{6,0},{7,1},{8,10},{9,11},{10,... | collective-permute-start | bytes 983048 | tf_op jit(solution)/shard_map/ppermute | solution.py:31
  77.6 8.6 %collective-permute-start.4 = (bf16[256,640]{1,0:T(8,128)(2,1)S(1)}, bf16[256,640]{1,0:T(8,128)(2,1)S(1)}, u32[]{:S(2)}, u32[]{:S(2)}) collective-permute-start(bf16[256,640]{1,0:T(8,128)(2,1)S(1)} %slice.61), channel_id=1, source_target_pairs={{0,6},{1,7},{2,0},{3,1},{4,2},{5,3},{6,4},{7,5},{8,14},{9,15},{10,... | collective-permute-start | bytes 983048 | tf_op jit(solution)/shard_map/ppermute | solution.py:31
  78.6 41.5 %collective-permute-start.6 = (bf16[512,640]{1,0:T(8,128)(2,1)}, bf16[512,640]{1,0:T(8,128)(2,1)}, u32[]{:S(2)}, u32[]{:S(2)}) collective-permute-start(bf16[512,640]{1,0:T(8,128)(2,1)} %collective-permute-done.1.refs_1_), channel_id=1, source_target_pairs={{0,1},{1,0},{2,3},{3,2},{4,5},{5,4},{6,7},{7,6},{8,9},{9,8},{10,11... | collective-permute-start | bytes 1966088 | tf_op jit(solution)/shard_map/ppermute | solution.py:31
  86.1 34.2 %collective-permute-start.7 = (bf16[512,640]{1,0:T(8,128)(2,1)}, bf16[512,640]{1,0:T(8,128)(2,1)}, u32[]{:S(2)}, u32[]{:S(2)}) collective-permute-start(bf16[512,640]{1,0:T(8,128)(2,1)} %collective-permute-done.2.refs_2_), channel_id=1, source_target_pairs={{0,1},{1,0},{2,3},{3,2},{4,5},{5,4},{6,7},{7,6},{8,9},{9,8},{10,11... | collective-permute-start | bytes 1966088 | tf_op jit(solution)/shard_map/ppermute | solution.py:31
  86.2 12.7 %collective-permute-start.8 = (bf16[256,640]{1,0:T(8,128)(2,1)S(1)}, bf16[256,640]{1,0:T(8,128)(2,1)S(1)}, u32[]{:S(2)}, u32[]{:S(2)}) collective-permute-start(bf16[256,640]{1,0:T(8,128)(2,1)S(1)} %collective-permute-done.3.refs_3_), channel_id=1, source_target_pairs={{0,1},{1,0},{2,3},{3,2},{4,5},{5,4},{6,7},{7,6},{8,9},{9,8},{10,11... | collective-permute-start | bytes 983048 | tf_op jit(solution)/shard_map/ppermute | solution.py:31
  90.8 9.3 %collective-permute-start.9 = (bf16[256,640]{1,0:T(8,128)(2,1)S(1)}, bf16[256,640]{1,0:T(8,128)(2,1)S(1)}, u32[]{:S(2)}, u32[]{:S(2)}) collective-permute-start(bf16[256,640]{1,0:T(8,128)(2,1)S(1)} %collective-permute-done.4.refs_4_), channel_id=1, source_target_pairs={{0,1},{1,0},{2,3},{3,2},{4,5},{5,4},{6,7},{7,6},{8,9},{9,8},{10,11... | collective-permute-start | bytes 983048 | tf_op jit(solution)/shard_map/ppermute | solution.py:31
  96.3 26.5 %collective-permute-start.17 = (bf16[64,5120]{1,0:T(8,128)(2,1)}, bf16[64,5120]{1,0:T(8,128)(2,1)}, u32[]{:S(2)}, u32[]{:S(2)}) collective-permute-start(bf16[64,5120]{1,0:T(8,128)(2,1)} %slice_select_fusion), channel_id=1, source_target_pairs={{0,8},{1,33},{2,10},{3,35},{4,12},{5,37},{6,14},{7,39},{8,16},{9,4... | collective-permute-start | bytes 1966088 | tf_op jit(solution)/shard_map/ppermute | solution.py:31
  99.6 42.1 %collective-permute-start.24 = (bf16[512,640]{1,0:T(8,128)(2,1)}, bf16[512,640]{1,0:T(8,128)(2,1)}, u32[]{:S(2)}, u32[]{:S(2)}) collective-permute-start(bf16[512,640]{1,0:T(8,128)(2,1)} %mask.1.refs_0_.masked_ref), channel_id=1, source_target_pairs={{0,1},{1,0},{2,3},{3,2},{4,5},{5,4},{6,7},{7,6},{8,9},{9,8},{10,11... | collective-permute-start | bytes 1966088 | tf_op jit(solution)/shard_map/ppermute | solution.py:31
  100.9 21.6 %collective-permute-start.18 = (bf16[48,5120]{1,0:T(8,128)(2,1)}, bf16[48,5120]{1,0:T(8,128)(2,1)}, u32[]{:S(2)}, u32[]{:S(2)}) collective-permute-start(bf16[48,5120]{1,0:T(8,128)(2,1)} %slice_select_fusion.2), channel_id=1, source_target_pairs={{0,24},{1,33},{2,26},{3,35},{4,28},{5,37},{6,30},{7,39},{8,0},{9,4... | collective-permute-start | bytes 1474568 | tf_op jit(solution)/shard_map/ppermute | solution.py:31
  120.1 30.0 %collective-permute-start.25 = (bf16[512,640]{1,0:T(8,128)(2,1)}, bf16[512,640]{1,0:T(8,128)(2,1)S(1)}, u32[]{:S(2)}, u32[]{:S(2)}) collective-permute-start(bf16[512,640]{1,0:T(8,128)(2,1)} %collective-permute-done.20.refs_1_), channel_id=1, source_target_pairs={{0,1},{1,0},{2,3},{3,2},{4,5},{5,4},{6,7},{7,6},{8,9},{9,8},{10,11... | collective-permute-start | bytes 1966088 | tf_op jit(solution)/shard_map/ppermute | solution.py:31
  120.2 32.4 %collective-permute-start.26 = (bf16[512,640]{1,0:T(8,128)(2,1)}, bf16[512,640]{1,0:T(8,128)(2,1)S(1)}, u32[]{:S(2)}, u32[]{:S(2)}) collective-permute-start(bf16[512,640]{1,0:T(8,128)(2,1)} %collective-permute-done.21.refs_2_), channel_id=1, source_target_pairs={{0,1},{1,0},{2,3},{3,2},{4,5},{5,4},{6,7},{7,6},{8,9},{9,8},{10,11... | collective-permute-start | bytes 1966088 | tf_op jit(solution)/shard_map/ppermute | solution.py:31
  122.5 30.1 %collective-permute-start.27 = (bf16[256,640]{1,0:T(8,128)(2,1)}, bf16[256,640]{1,0:T(8,128)(2,1)S(1)}, u32[]{:S(2)}, u32[]{:S(2)}) collective-permute-start(bf16[256,640]{1,0:T(8,128)(2,1)} %copy-done.26), channel_id=1, source_target_pairs={{0,1},{1,0},{2,3},{3,2},{4,5},{5,4},{6,7},{7,6},{8,9},{9,8},{10,11... | collective-permute-start | bytes 983048 | tf_op jit(solution)/shard_map/ppermute | solution.py:31
  122.8 29.9 %collective-permute-start.28 = (bf16[256,640]{1,0:T(8,128)(2,1)}, bf16[256,640]{1,0:T(8,128)(2,1)S(1)}, u32[]{:S(2)}, u32[]{:S(2)}) collective-permute-start(bf16[256,640]{1,0:T(8,128)(2,1)} %copy-done.28), channel_id=1, source_target_pairs={{0,1},{1,0},{2,3},{3,2},{4,5},{5,4},{6,7},{7,6},{8,9},{9,8},{10,11... | collective-permute-start | bytes 983048 | tf_op jit(solution)/shard_map/ppermute | solution.py:31
  141.7 29.3 %collective-permute-start.29 = (bf16[256,896]{1,0:T(8,128)(2,1)}, bf16[256,896]{1,0:T(8,128)(2,1)}, u32[]{:S(2)}, u32[]{:S(2)}) collective-permute-start(bf16[256,896]{1,0:T(8,128)(2,1)} %product.5), channel_id=1, source_target_pairs={{0,96},{1,97},{2,98},{3,99},{4,100},{5,101},{6,102},{7,103},{8,104... | collective-permute-start | bytes 1376264 | tf_op jit(solution)/shard_map/ppermute | solution.py:31
  150.1 29.0 %collective-permute-start.19 = (bf16[256,896]{1,0:T(8,128)(2,1)}, bf16[256,896]{1,0:T(8,128)(2,1)}, u32[]{:S(2)}, u32[]{:S(2)}) collective-permute-start(bf16[256,896]{1,0:T(8,128)(2,1)} %product.3), channel_id=1, source_target_pairs={{0,96},{1,97},{2,98},{3,99},{4,100},{5,101},{6,102},{7,103},{8,104... | collective-permute-start | bytes 1376264 | tf_op jit(solution)/shard_map/ppermute | solution.py:31
  190.3 7.8 %collective-permute-start.33 = (f32[128,192]{1,0:T(8,128)S(1)}, f32[128,192]{1,0:T(8,128)S(1)}, u32[]{:S(2)}, u32[]{:S(2)}) collective-permute-start(f32[128,192]{1,0:T(8,128)S(1)} %select_add_fusion), channel_id=1, source_target_pairs={{0,6},{1,7},{2,0},{3,1},{4,2},{5,3},{6,4},{7,5},{8,14},{9,15},{10,... | collective-permute-start | bytes 294920 | tf_op jit(solution)/shard_map/ppermute | solution.py:31
  (38 other events, 344.9 us)

commit v2 on v1

v2 whole, which is shorter than its diff:
```python
import functools

import jax
import jax.numpy as jnp
from jax import lax
from jax.experimental import pallas as pl
from jax.experimental.pallas import tpu as pltpu
from jax.sharding import Mesh
from jax.sharding import PartitionSpec as P

AXES = ("z", "x", "y", "c")
F32, BF16 = jnp.float32, jnp.bfloat16
ROWS, FEAT, HID, HALF, RANK, DEPTH = 512, 640, 1792, 896, 64, 5120
SHARD, TOP = 112, 64
STEP = 2 * FEAT
NT = (((1,), (1,)), ((), ()))
ANY = pl.BlockSpec(memory_space=pl.ANY)


def send(value, target, name="send"):
    def line(z, x, y, c):
        return ((z % 4 * 4 + x % 4) * 4 + y % 4) * 2 + c

    pairs = [
        (line(z, x, y, c), line(*target(z, x, y, c)))
        for z in range(4)
        for x in range(4)
        for y in range(4)
        for c in range(2)
    ]
    with jax.named_scope(name):
        return lax.ppermute(value, AXES, pairs)


def up_y(v, name="up"):
    return send(v, lambda z, x, y, c: (z, x, y + 1, c), name)


def down_y(v, name="down"):
    return send(v, lambda z, x, y, c: (z, x, y - 1, c), name)


def swap(v, name="swap"):
    return send(v, lambda z, x, y, c: (z, x, y, 1 - c), name)


def mate(v, name="mate"):
    return send(v, lambda z, x, y, c: (3 - z, x, y, c), name)


def after(value, *others):
    return lax.optimization_barrier((value, *others))[0]


def pick(c, a, b):
    return jnp.where(c == 0, a, b)


def route(v, zero, one, name):
    hop = {
        "p": lambda z, x, y, c: (z ^ 1, x, y, c),
        "+": lambda z, x, y, c: (z, x + 1, y, c),
        "-": lambda z, x, y, c: (z, x - 1, y, c),
    }
    return send(v, lambda z, x, y, c: hop[zero if c == 0 else one](z, x, y, c), name)


def weight_rows(z, x, c):
    zl, first = z % 2, c == 0

    def at(dz, dx):
        return ((zl + dz) % 2 * 4 + (x + dx) % 4) * SHARD

    return jnp.stack(
        [
            at(0, 0),
            jnp.where(first, at(1, 0), at(0, 3)),
            jnp.where(first, at(0, 3), at(0, 1)),
            jnp.where(first, at(0, 1), at(1, 0)),
            at(1, 3),
            at(1, 1),
            at(0, 2),
            at(0, 2) + TOP,
            at(1, 2),
            at(1, 2) + TOP,
        ]
    )


WIDTHS = (SHARD,) * 6 + (TOP, SHARD - TOP, TOP, SHARD - TOP)


def product_kernel(first, rows, others, where_ref, *refs):
    mine, weights, other = refs[:5], refs[5:15], refs[15 : 15 + others]
    out_ref, a_buf, w_buf, a_sem, w_sem, *acc = refs[15 + others :]
    acc = acc[0] if acc else out_ref
    y, c = where_ref[10], where_ref[11]
    a_copies = []
    lane, swapped = (pl.multiple_of(core * FEAT, 128) for core in (c, 1 - c))
    for k, piece in enumerate(mine):
        slot, lo, hi = (k, 0, 512) if k < 3 else (3, (k - 3) * 256, (k - 2) * 256)
        start, stop = max(lo, first), min(hi, first + rows)
        if start < stop:
            a_copies.append(
                pltpu.make_async_copy(
                    piece.at[pl.ds(start - lo, stop - start), :],
                    a_buf.at[slot, pl.ds(start - first, stop - start), pl.ds(lane, FEAT)],
                    a_sem.at[0, k],
                )
            )
    for slot in range(4):
        ref, at = (other[0], slot * 512) if others == 1 or slot < 3 else (other[1], 0)
        a_copies.append(
            pltpu.make_async_copy(
                ref.at[pl.ds(at + first, rows), :],
                a_buf.at[slot, :, pl.ds(swapped, FEAT)],
                a_sem.at[1, slot],
            )
        )

    def w_copies(step):
        shift = (0, 3, 1, 2)[step]
        lane = pl.multiple_of(lax.rem(y + shift, 4) * STEP, 128)
        return [
            pltpu.make_async_copy(
                w.at[:, pl.ds(lane, STEP)],
                w_buf.at[step % 2, pl.ds(pl.multiple_of(where_ref[k], 16), WIDTHS[k]), :],
                w_sem.at[step % 2, k],
            )
            for k, w in enumerate(weights)
        ]

    for copy in w_copies(0):
        copy.start()
    for copy in a_copies:
        copy.start()
    for copy in a_copies:
        copy.wait()
    for step in range(4):
        if step < 3:
            for copy in w_copies(step + 1):
                copy.start()
        for copy in w_copies(step):
            copy.wait()
        part = lax.dot_general(a_buf[step], w_buf[step % 2], NT, preferred_element_type=F32)
        if step == 0:
            acc[...] = part
        elif step < 3:
            acc[...] += part
        else:
            out_ref[...] = (acc[...] + part).astype(out_ref.dtype)


def product(first, rows, dtype, where, mine, other, weights):
    return pl.pallas_call(
        functools.partial(product_kernel, first, rows, len(other)),
        out_shape=jax.ShapeDtypeStruct((rows, HALF), dtype),
        grid_spec=pltpu.PrefetchScalarGridSpec(
            num_scalar_prefetch=1,
            grid=(1,),
            in_specs=[ANY] * (15 + len(other)),
            out_specs=pl.BlockSpec((rows, HALF), lambda i, w: (0, 0)),
            scratch_shapes=[
                pltpu.VMEM((4, rows, STEP), BF16),
                pltpu.VMEM((2, HALF, STEP), BF16),
                pltpu.SemaphoreType.DMA((2, 5)),
                pltpu.SemaphoreType.DMA((2, 10)),
            ]
            + ([] if dtype == F32 else [pltpu.VMEM((rows, HALF), F32)]),
        ),
        compiler_params=pltpu.CompilerParams(vmem_limit_bytes=(11 if rows == 256 else 18) << 20),
        cost_estimate=pl.CostEstimate(
            flops=2 * rows * HALF * DEPTH,
            bytes_accessed=2 * DEPTH * (rows + HALF) + 4 * rows * HALF,
            transcendentals=0,
        ),
        name="product",
    )(where, *mine, *weights, *other)


def early_kernel(where_ref, act_ref, grad_ref, pm_ref, gate_ref, up_ref, ph_ref, out_ref):
    gate, up = gate_ref[...].astype(F32), up_ref[...].astype(F32)
    hidden = (gate * jax.nn.sigmoid(gate) * up).astype(BF16)
    pm = pm_ref[...]
    out_ref[:, 0:64] = lax.dot_general(act_ref[...], pm, NT, preferred_element_type=F32)
    out_ref[:, 64:128] = lax.dot_general(hidden, ph_ref[...], NT, preferred_element_type=F32)
    out_ref[:, 128:192] = lax.dot_general(grad_ref[...], pm, NT, preferred_element_type=F32)


def early(where, activations, out_grad, pm_t, gate, up, ph_t):
    narrow = pl.BlockSpec((128, FEAT), lambda i, w: (i, 0))
    wide = pl.BlockSpec((128, HID), lambda i, w: (i, 0))
    return pl.pallas_call(
        early_kernel,
        out_shape=jax.ShapeDtypeStruct((ROWS, 3 * RANK), F32),
        grid_spec=pltpu.PrefetchScalarGridSpec(
            num_scalar_prefetch=1,
            grid=(4,),
            in_specs=[
                narrow,
                narrow,
                pl.BlockSpec((RANK, FEAT), lambda i, w: (0, 2 * w[10] + w[11])),
                wide,
                wide,
                pl.BlockSpec((RANK, HID), lambda i, w: (0, 0)),
            ],
            out_specs=pl.BlockSpec((128, 3 * RANK), lambda i, w: (i, 0)),
        ),
        compiler_params=pltpu.CompilerParams(vmem_limit_bytes=12 << 20),
        cost_estimate=pl.CostEstimate(
            flops=ROWS * HID * 160, bytes_accessed=5 << 20, transcendentals=ROWS * HID
        ),
        name="early",
    )(where, activations, out_grad, pm_t, gate, up, ph_t)


def grads(gate_ref, up_ref, hidden_grad, ph_ref, first, total, gg_ref, gu_ref):
    row = first + lax.broadcasted_iota(jnp.int32, hidden_grad.shape, 0)
    hidden_grad = jnp.where(row < total, hidden_grad, 0.0)
    gate, up = gate_ref[...].astype(F32), up_ref[...].astype(F32)
    sig = jax.nn.sigmoid(gate)
    grad_up = (hidden_grad * (gate * sig)).astype(BF16)
    grad_gate = (hidden_grad * up * sig * (1.0 + gate * (1.0 - sig))).astype(BF16)
    gg_ref[...] = grad_gate
    gu_ref[...] = grad_up
    ph = ph_ref[...]
    return jnp.concatenate(
        [
            lax.dot_general(g, ph, NT, preferred_element_type=F32)
            for g in (grad_gate, grad_up)
        ],
        axis=1,
    )


def own_kernel(where_ref, gate_ref, up_ref, h_ref, ph_ref, gg_ref, gu_ref, part_ref):
    part_ref[...] = grads(
        gate_ref, up_ref, h_ref[...], ph_ref, pl.program_id(0) * 64, where_ref[13], gg_ref, gu_ref
    )


def own_half(where, gate, up, h, ph_t):
    tile = pl.BlockSpec((64, HALF), lambda i, w: (i, w[12]))
    big = jax.ShapeDtypeStruct((ROWS, HID), BF16)
    return pl.pallas_call(
        own_kernel,
        out_shape=(big, big, jax.ShapeDtypeStruct((ROWS, 2 * RANK), F32)),
        grid_spec=pltpu.PrefetchScalarGridSpec(
            num_scalar_prefetch=1,
            grid=(8,),
            in_specs=[
                tile,
                tile,
                pl.BlockSpec((64, HALF), lambda i, w: (i, 0)),
                pl.BlockSpec((RANK, HALF), lambda i, w: (0, w[12])),
            ],
            out_specs=(tile, tile, pl.BlockSpec((64, 2 * RANK), lambda i, w: (i, 0))),
        ),
        compiler_params=pltpu.CompilerParams(vmem_limit_bytes=8 << 20),
        cost_estimate=pl.CostEstimate(
            flops=ROWS * HALF * 280, bytes_accessed=6 << 20, transcendentals=ROWS * HALF
        ),
        name="own_half",
    )(where, gate, up, h, ph_t)


def other_kernel(k, where_ref, gate_ref, up_ref, h_ref, ph_ref, part_ref, hi_ref, lo_ref,
                 gg_in, gu_in, *refs):
    gg_ref, gu_ref, feat_ref, acc = refs[-4:]
    i = pl.program_id(0)
    part = grads(
        gate_ref, up_ref, h_ref[...].astype(F32), ph_ref, k * 256 + i * 64, where_ref[13],
        gg_ref, gu_ref,
    )
    acc[pl.ds(pl.multiple_of(i * 64, 64), 64), :] = part_ref[...] + part

    @pl.when(i == 3)
    def _():
        whole = acc[...]
        hi = whole.astype(BF16)
        lo = (whole - hi.astype(F32)).astype(BF16)
        feat = jnp.dot(lo_ref[...], hi, preferred_element_type=F32)
        feat += jnp.dot(hi_ref[...], lo, preferred_element_type=F32)
        feat += jnp.dot(hi_ref[...], hi, preferred_element_type=F32)
        feat_ref[...] = feat if k == 0 else refs[0][...] + feat


def other_half(k, where, gate, up, h, ph_t, part, spread, gg, gu, before):
    tile = pl.BlockSpec((64, HALF), lambda i, w: (4 * k + i, 1 - w[12]))
    big = jax.ShapeDtypeStruct((ROWS, HID), BF16)
    feat = pl.BlockSpec((4 * RANK, 2 * RANK), lambda i, w: (0, 0))
    columns = pl.BlockSpec((4 * RANK, 256), lambda i, w: (0, k))
    return pl.pallas_call(
        functools.partial(other_kernel, k),
        out_shape=(big, big, jax.ShapeDtypeStruct((4 * RANK, 2 * RANK), F32)),
        grid_spec=pltpu.PrefetchScalarGridSpec(
            num_scalar_prefetch=1,
            grid=(4,),
            in_specs=[
                tile,
                tile,
                pl.BlockSpec((64, HALF), lambda i, w: (i, 0)),
                pl.BlockSpec((RANK, HALF), lambda i, w: (0, 1 - w[12])),
                pl.BlockSpec((64, 2 * RANK), lambda i, w: (4 * k + i, 0)),
                columns,
                columns,
                ANY,
                ANY,
            ]
            + [feat] * len(before),
            out_specs=(tile, tile, feat),
            scratch_shapes=[pltpu.VMEM((256, 2 * RANK), F32)],
        ),
        input_output_aliases={8: 0, 9: 1},
        compiler_params=pltpu.CompilerParams(vmem_limit_bytes=8 << 20),
        cost_estimate=pl.CostEstimate(
            flops=256 * HALF * 280, bytes_accessed=3 << 20, transcendentals=256 * HALF
        ),
        name="other_half",
    )(where, gate, up, h, ph_t, part, *spread, gg, gu, *before)


def sum_tensor(value, c):
    half = value.shape[0] // 2
    top, low = value[:half], value[half:]
    mine = jnp.where(c == 0, top, low) + swap(jnp.where(c == 0, low, top))
    across = send(mine, lambda z, x, y, c: (z, x, y + 2, c))
    mine = (mine + across) + (up_y(mine) + down_y(mine))
    theirs = swap(mine)
    return jnp.concatenate(
        [jnp.where(c == 0, mine, theirs), jnp.where(c == 0, theirs, mine)], axis=0
    )


def on_device(
    activations, out_grad, gate_pre, up_pre, down_weight, proj_model, proj_hidden, lengths
):
    z, x, y, c = (lax.axis_index(a) for a in AXES)
    where = jnp.concatenate(
        [weight_rows(z, x, c), jnp.stack([y, c, z // 2, jnp.sum(lengths)])]
    ).astype(jnp.int32)
    own_w = down_weight
    r1 = route(own_w, "p", "+", "r1")
    r2 = route(own_w, "+", "-", "r2")
    theirs = mate(out_grad, "mate_rows")
    a_up, a_down = up_y(out_grad, "a_up"), down_y(out_grad, "a_down")
    r3 = route(after(own_w, theirs, a_up, a_down), "-", "p", "r3")
    a_far1, a_far2 = up_y(a_up[:256], "a_far1"), down_y(a_down[256:], "a_far2")
    r1, r2, r3, theirs, a_far1, a_far2 = lax.optimization_barrier(
        (r1, r2, r3, theirs, a_far1, a_far2)
    )
    r4 = route(r1, "+", "p", "r4")
    r5 = route(pick(c, r1, r2), "-", "p", "r5")
    r6 = route(pick(c, r2[:TOP], r1[:TOP]), "+", "+", "r6")
    b_up, b_down = up_y(theirs, "b_up"), down_y(theirs, "b_down")
    r7 = route(after(pick(c, r3[TOP:], r2[TOP:]), b_up), "-", "-", "r7")
    a_other = [swap(jnp.concatenate([out_grad, a_up, a_down, a_far1, a_far2]), "a_swap")]
    near1, near2, r5, a_other = lax.optimization_barrier(
        (b_up[:256], b_down[256:], r5, a_other)
    )
    b_near = swap(jnp.concatenate([theirs, b_up, b_down]), "b_near_swap")
    b_far1, b_far2 = up_y(near1, "b_far1"), down_y(near2, "b_far2")
    r8 = route(pick(c, r4[:TOP], r6), "+", "p", "r8")
    r9 = route(pick(c, r5[TOP:], r7), "-", "p", "r9")
    weights = [own_w, r1, r2, r3, r4, r5, r6, r7, r8, r9]
    a_mine = [out_grad, a_up, a_down, a_far1, a_far2]
    b_mine = [theirs, b_up, b_down, b_far1, b_far2]
    b_other = [b_near, swap(jnp.concatenate([b_far1, b_far2]), "b_far_swap")]

    pm_t, ph_t = proj_model.T, proj_hidden.T
    parts = early(after(where, b_up), activations, out_grad, pm_t, gate_pre, up_pre, ph_t)
    sums = sum_tensor(after(parts, b_far1, b_far2, r7), c)
    in_proj, hidden_proj, out_proj = (sums[:, i * RANK : (i + 1) * RANK] for i in range(3))

    offsets = jnp.cumsum(lengths) - lengths
    rows = jnp.arange(ROWS, dtype=jnp.int32)[:, None]
    member = jnp.logical_and(rows >= offsets[None, :], rows < (offsets + lengths)[None, :])
    weight = member.astype(F32) / jnp.sqrt(lengths.astype(F32))[None, :]

    def weighted(left):
        return (weight[:, :, None] * left[:, None, :]).reshape(ROWS, 4 * RANK)

    spread = weighted(in_proj).T
    spread_hi = spread.astype(BF16)
    spread_lo = (spread - spread_hi.astype(F32)).astype(BF16)
    down_feat = lax.dot_general(
        weighted(hidden_proj),
        out_proj,
        (((0,), (0,)), ((), ())),
        precision=lax.Precision.HIGHEST,
        preferred_element_type=F32,
    )

    h_out = [product(k * 256, 256, BF16, where, b_mine, b_other, weights) for k in range(2)]
    h_in = [mate(h, "mate_grad") for h in h_out]
    h_own = product(0, 512, F32, after(where, *h_out), a_mine, a_other, weights)
    grad_gate, grad_up, part = own_half(where, gate_pre, up_pre, h_own, ph_t)
    feat = ()
    for k in range(2):
        grad_gate, grad_up, *feat = other_half(
            k, where, gate_pre, up_pre, h_in[k], ph_t, part, (spread_hi, spread_lo),
            grad_gate, grad_up, feat,
        )
    total = jnp.concatenate([sum_tensor(feat[0], c), down_feat], axis=1)
    features = total.reshape(4, RANK, 3, RANK).transpose(0, 2, 1, 3).reshape(4, 3, RANK * RANK)
    return grad_gate, grad_up, features


def solution(mesh):
    split = Mesh(mesh.devices.reshape(4, 4, 4, 2), AXES)
    dp, tensor = ("z", "x"), ("y", "c")
    return jax.shard_map(
        on_device,
        mesh=split,
        in_specs=(
            P(dp, tensor),
            P(dp, tensor),
            P(dp, tensor),
            P(dp, tensor),
            P((*tensor, *dp), None),
            P(),
            P(tensor, None),
            P(dp),
        ),
        out_specs=(P(dp, tensor), P(dp, tensor), P(dp, None, None)),
        check_vma=False,
    )
```

time: 205 us -> 172 us (0.84)
  Pallas kernels: 58.4 us -> 38 us
  waiting for transfers between devices: 36.3 us -> 56.1 us
  blocking collectives: 16 us -> 0 us
  starting transfers between devices: 58 us -> 42.8 us
  other arithmetic: 6.08 us -> 11.4 us
  local copies, waits for them, and re-layouts: 25.1 us -> 21.6 us
    ppermute x35 -> x33, waiting for transfers between devices: 28.3 us -> 56.1 us  [send(): return lax.ppermute(value, AXES, pairs)]
    all_gather x1 -> x0, blocking collectives: 16 us -> none  [on_device(): lax.all_gather(slice_proj[:, :RANK], ('y', 'c'), axis=0, tiled=True)]
    pallas_call x6 -> x5, Pallas kernels: 42.9 us -> 30.9 us  [the longest x3 24.1 us: product(): pl.pallas_call(functools.partial(product_kernel, first, rows, len(other))...]
    ppermute x35 -> x33, starting transfers between devices: 53.2 us -> 42.8 us  [send(): return lax.ppermute(value, AXES, pairs)]
    all_to_all x1 -> x0, waiting for transfers between devices: 8 us -> none  [on_device(): mixed = lax.all_to_all(parts.reshape(8, 64, 3 * RANK), ('y', 'c'), 0, 0)]
    pallas_call x1, Pallas kernels: 8.25 us -> 2.37 us  [early(): pl.pallas_call(early_kernel, out_shape=jax.ShapeDtypeStruct((ROWS, 3 * RA...]
    all_to_all x1 -> x0, starting transfers between devices: 4.84 us -> none  [on_device(): mixed = lax.all_to_all(parts.reshape(8, 64, 3 * RANK), ('y', 'c'), 0, 0)]
    concatenate x0 -> x3, other arithmetic: none -> 3.58 us  [the longest x1 2.63 us: on_device(): b_near = swap(jnp.concatenate([theirs, b_up, b_down]), 'b_near_swap')]
  transfers between devices with their start and end apart: 36 -> 33, of which waited for: 9 -> 15; matrix products, arithmetic and copies ran while one was open for 7% -> 13% of each run, Pallas kernels for 25% -> 16%
where the time goes in v2:
time: 172 us
  waiting for transfers between devices  56.1 us (33%)
  starting transfers between devices  42.8 us (25%)
  Pallas kernels  38 us (22%)
  local copies, waits for them, and re-layouts  21.6 us (13%)
  other arithmetic  11.4 us (7%)
    ppermute x33, waiting for transfers between devices, send(): return lax.ppermute(value, AXES, pairs)  56.1 us
    ppermute x33, starting transfers between devices, send(): return lax.ppermute(value, AXES, pairs)  42.8 us
    pallas_call x3, Pallas kernels, product(): pl.pallas_call(functools.partial(product_kernel, first, rows, len(other))...  24.1 us
    unnamed x86, local copies, waits for them, and re-layouts  14.3 us
    pallas_call x2, Pallas kernels, other_half(): pl.pallas_call(functools.partial(other_kernel, k), out_shape=(big, big, j...  6.76 us
    pallas_call x1, Pallas kernels, own_half(): pl.pallas_call(own_kernel, out_shape=(big, big, jax.ShapeDtypeStruct((ROW...  4.7 us
  transfers between devices with their start and end apart: 33, of which 15 were waited for; matrix products, arithmetic and copies ran while one was open for 13% of the time, Pallas kernels for 16%

profile of v2, /device:TPU:1, one launch (start us, length us, event | category | flops | bytes accessed | tf_op | source)
XLA Modules:
  0.0 171.7 jit_solution(7067168471006513250)
XLA Ops:
  0.6 4.7 %collective-permute-start.2 = (bf16[512,640]{1,0:T(8,128)(2,1)}, bf16[512,640]{1,0:T(8,128)(2,1)}, u32[]{:S(2)}, u32[]{:S(2)}) collective-permute-start(bf16[512,640]{1,0:T(8,128)(2,1)} %grad_ref.1), channel_id=1, source_target_pairs={{0,96},{1,97},{2,98},{3,99},{4,100},{5,101},{6,102},{7,103},{8,104... | collective-permute-start | bytes 1966088 | tf_op jit(solution)/shard_map/mate_rows/ppermute | solution.py:32
  10.7 9.4 %collective-permute-done.2.refs_0_ = bf16[512,640]{1,0:T(8,128)(2,1)} collective-permute-done((bf16[512,640]{1,0:T(8,128)(2,1)}, bf16[512,640]{1,0:T(8,128)(2,1)}, u32[]{:S(2)}, u32[]{:S(2)}) %collective-permute-start.2) | collective-permute-done | bytes 655392 | tf_op jit(solution)/shard_map/mate_rows/ppermute | solution.py:32
  20.1 2.1 %collective-permute-done.3.refs_1_ = bf16[512,640]{1,0:T(8,128)(2,1)S(1)} collective-permute-done((bf16[512,640]{1,0:T(8,128)(2,1)}, bf16[512,640]{1,0:T(8,128)(2,1)S(1)}, u32[]{:S(2)}, u32[]{:S(2)}) %collective-permute-start.3) | collective-permute-done | bytes 655392 | tf_op jit(solution)/shard_map/a_up/ppermute | solution.py:32
  26.4 1.8 %collective-permute-start.7 = (bf16[256,640]{1,0:T(8,128)(2,1)S(1)}, bf16[256,640]{1,0:T(8,128)(2,1)S(1)}, u32[]{:S(2)}, u32[]{:S(2)}) collective-permute-start(bf16[256,640]{1,0:T(8,128)(2,1)S(1)} %slice.69), channel_id=1, source_target_pairs={{0,6},{1,7},{2,0},{3,1},{4,2},{5,3},{6,4},{7,5},{8,14},{9,15},{10,... | collective-permute-start | bytes 983048 | tf_op jit(solution)/shard_map/a_far2/ppermute | solution.py:32
  28.2 2.0 %constant_dynamic-update-slice_fusion.4 = bf16[2048,640]{1,0:T(8,128)(2,1)} fusion(bf16[512,640]{1,0:T(8,128)(2,1)} %grad_ref.1), kind=kLoop, calls=%fused_computation.36 | loop fusion | bytes 1310720
  31.1 2.0 %constant_dynamic-update-slice_fusion.2 = bf16[2048,640]{1,0:T(8,128)(2,1)} fusion(bf16[2048,640]{1,0:T(8,128)(2,1)} %constant_dynamic-update-slice_fusion.3, bf16[512,640]{1,0:T(8,128)(2,1)} %collective-permute-done.4.refs_2_), kind=kLoop, calls=%fused_computation.34 | loop fusion | bytes 1310720
  34.8 2.7 %collective-permute-done.5.refs_8_ = bf16[112,5120]{1,0:T(8,128)(2,1)S(1)} collective-permute-done((bf16[112,5120]{1,0:T(8,128)(2,1)}, bf16[112,5120]{1,0:T(8,128)(2,1)S(1)}, u32[]{:S(2)}, u32[]{:S(2)}) %collective-permute-start.5) | collective-permute-done | bytes 1146912 | tf_op jit(solution)/shard_map/r3/ppermute | solution.py:32
  40.5 3.1 %collective-permute-start.11 = (bf16[2048,640]{1,0:T(8,128)(2,1)}, bf16[2048,640]{1,0:T(8,128)(2,1)}, u32[]{:S(2)}, u32[]{:S(2)}) collective-permute-start(bf16[2048,640]{1,0:T(8,128)(2,1)} %constant_dynamic-update-slice_fusion), channel_id=1, source_target_pairs={{0,1},{1,0},{2,3},{3,2},{4,5},{5,4},{6,7},{7,6},{8,9},{9,8},{10,11... | collective-permute-start | bytes 7864328 | tf_op jit(solution)/shard_map/a_swap/ppermute | solution.py:32
  48.8 13.2 %collective-permute-done.8.refs_1_ = bf16[512,640]{1,0:T(8,128)(2,1)S(1)} collective-permute-done((bf16[512,640]{1,0:T(8,128)(2,1)}, bf16[512,640]{1,0:T(8,128)(2,1)S(1)}, u32[]{:S(2)}, u32[]{:S(2)}) %collective-permute-start.8) | collective-permute-done | bytes 655392 | tf_op jit(solution)/shard_map/b_up/ppermute | solution.py:32
  62.1 3.3 %collective-permute-start.16 = (bf16[48,5120]{1,0:T(8,128)(2,1)S(1)}, bf16[48,5120]{1,0:T(8,128)(2,1)S(1)}, u32[]{:S(2)}, u32[]{:S(2)}) collective-permute-start(bf16[48,5120]{1,0:T(8,128)(2,1)S(1)} %slice_select_fusion.3), channel_id=1, source_target_pairs={{0,24},{1,25},{2,26},{3,27},{4,28},{5,29},{6,30},{7,31},{8,0},{9,1... | collective-permute-start | bytes 1474568 | tf_op jit(solution)/shard_map/r7/ppermute | solution.py:32
  65.5 9.1 %collective-permute-done.10.refs_10_ = bf16[112,5120]{1,0:T(8,128)(2,1)S(1)} collective-permute-done((bf16[112,5120]{1,0:T(8,128)(2,1)S(1)}, bf16[112,5120]{1,0:T(8,128)(2,1)S(1)}, u32[]{:S(2)}, u32[]{:S(2)}) %collective-permute-start.10) | collective-permute-done | bytes 1146912 | tf_op jit(solution)/shard_map/r5/ppermute | solution.py:32
  74.6 2.6 %collective-permute-start.13 = (bf16[256,640]{1,0:T(8,128)(2,1)S(1)}, bf16[256,640]{1,0:T(8,128)(2,1)S(1)}, u32[]{:S(2)}, u32[]{:S(2)}) collective-permute-start(bf16[256,640]{1,0:T(8,128)(2,1)S(1)} %slice.71), channel_id=1, source_target_pairs={{0,6},{1,7},{2,0},{3,1},{4,2},{5,3},{6,4},{7,5},{8,14},{9,15},{10,... | collective-permute-start | bytes 983048 | tf_op jit(solution)/shard_map/b_far2/ppermute | solution.py:32
  79.4 2.4 %early.1 = f32[512,192]{1,0:T(8,128)S(1)} custom-call(s32[14]{0:T(128)S(1)} %concatenate.21.where_ref, bf16[512,640]{1,0:T(8,128)(2,1)S(1)} %copy-done.30, bf16[512,640]{1,0:T(8,128)(2,1)S(1)} %copy-done.26, bf16[64,5120]{1,0:T(8,128)(2,1)S(1)} %bitcast.40, bf16[512,1792]{1,0:T(8,128)(2,1)S(1)} %copy-done, bf16[512,1792]{1,0:T(8,128)(2,1)S(1)} %copy-done.1, ...), custom_call_target="tpu_custom_call" | custom-call | flops 146800640 | bytes 5242880 | tf_op jit(solution)/shard_map/early/pallas_call | solution.py:193
  82.2 2.6 %pad_maximum_fusion = bf16[1536,640]{1,0:T(8,128)(2,1)} fusion(bf16[512,640]{1,0:T(8,128)(2,1)S(1)} %collective-permute-done.9.refs_2_, bf16[512,640]{1,0:T(8,128)(2,1)S(1)} %collective-permute-done.8.refs_1_, bf16[512,640]{1,0:T(8,128)(2,1)} %collective-permute-done.2.refs_0_), kind=kLoop, calls=%fused_computation | loop fusion | flops 5898240 | bytes 3932160 | tf_op jit(solution)/shard_map/concatenate | solution.py:361
  85.3 2.7 %collective-permute-start.25 = (f32[256,192]{1,0:T(8,128)S(1)}, f32[256,192]{1,0:T(8,128)S(1)}, u32[]{:S(2)}, u32[]{:S(2)}) collective-permute-start(f32[256,192]{1,0:T(8,128)S(1)} %select_add_fusion), channel_id=1, source_target_pairs={{0,6},{1,7},{2,0},{3,1},{4,2},{5,3},{6,4},{7,5},{8,14},{9,15},{10,... | collective-permute-start | bytes 589832 | tf_op jit(solution)/shard_map/down/ppermute | solution.py:32
  88.0 2.0 %collective-permute-done.15.refs_11_ = bf16[64,5120]{1,0:T(8,128)(2,1)S(1)} collective-permute-done((bf16[64,5120]{1,0:T(8,128)(2,1)S(1)}, bf16[64,5120]{1,0:T(8,128)(2,1)S(1)}, u32[]{:S(2)}, u32[]{:S(2)}) %collective-permute-start.15) | collective-permute-done | bytes 655392 | tf_op jit(solution)/shard_map/r6/ppermute | solution.py:32
  91.1 3.3 %collective-permute-done.24 = f32[256,192]{1,0:T(8,128)S(1)} collective-permute-done((f32[256,192]{1,0:T(8,128)S(1)}, f32[256,192]{1,0:T(8,128)S(1)}, u32[]{:S(2)}, u32[]{:S(2)}) %collective-permute-start.24) | collective-permute-done | bytes 196640 | tf_op jit(solution)/shard_map/up/ppermute | solution.py:32
  94.4 4.4 %collective-permute-done.25 = f32[256,192]{1,0:T(8,128)S(1)} collective-permute-done((f32[256,192]{1,0:T(8,128)S(1)}, f32[256,192]{1,0:T(8,128)S(1)}, u32[]{:S(2)}, u32[]{:S(2)}) %collective-permute-start.25) | collective-permute-done | bytes 196640 | tf_op jit(solution)/shard_map/down/ppermute | solution.py:32
  98.8 2.1 %collective-permute-done.23 = f32[256,192]{1,0:T(8,128)S(1)} collective-permute-done((f32[256,192]{1,0:T(8,128)S(1)}, f32[256,192]{1,0:T(8,128)S(1)}, u32[]{:S(2)}, u32[]{:S(2)}) %collective-permute-start.23) | collective-permute-done | bytes 196640 | tf_op jit(solution)/shard_map/send/ppermute | solution.py:32
  103.7 3.6 %collective-permute-start.20 = (bf16[512,640]{1,0:T(8,128)(2,1)}, bf16[512,640]{1,0:T(8,128)(2,1)}, u32[]{:S(2)}, u32[]{:S(2)}) collective-permute-start(bf16[512,640]{1,0:T(8,128)(2,1)} %pad_maximum_fusion.1), channel_id=1, source_target_pairs={{0,1},{1,0},{2,3},{3,2},{4,5},{5,4},{6,7},{7,6},{8,9},{9,8},{10,11... | collective-permute-start | bytes 1966088 | tf_op jit(solution)/shard_map/b_far_swap/ppermute | solution.py:32
  109.0 1.7 %copy.24 = f32[512,64]{0,1:T(8,128)} copy(f32[512,64]{1,0:T(8,128)} %get-tuple-element.53) | data formatting | bytes 262144 | tf_op jit(solution)/shard_map/slice | solution.py:373
  110.7 1.7 copy.23
  120.1 6.9 %product.4 = bf16[256,896]{1,0:T(8,128)(2,1)S(1)} custom-call(s32[14]{0:T(128)S(1)} %concatenate.21.where_ref, bf16[512,640]{1,0:T(8,128)(2,1)} %collective-permute-done.2.refs_0_, bf16[512,640]{1,0:T(8,128)(2,1)S(1)} %copy-done.4, bf16[512,640]{1,0:T(8,128)(2,1)S(1)} %copy-done.6, bf16[256,640]{1,0:T(8,128)(2,1)S(1)} %copy-done.23, ...), custom_call_target="tpu_custom_call" | custom-call | flops 2348810240 | bytes 12713984 | tf_op jit(solution)/shard_map/product/pallas_call | solution.py:155
  127.3 7.4 %product.3 = bf16[256,896]{1,0:T(8,128)(2,1)S(1)} custom-call(s32[14]{0:T(128)S(1)} %concatenate.21.where_ref, bf16[512,640]{1,0:T(8,128)(2,1)} %collective-permute-done.2.refs_0_, bf16[512,640]{1,0:T(8,128)(2,1)S(1)} %copy-done.4, bf16[512,640]{1,0:T(8,128)(2,1)S(1)} %copy-done.6, bf16[256,640]{1,0:T(8,128)(2,1)S(1)} %copy-done.23, ...), custom_call_target="tpu_custom_call" | custom-call | flops 2348810240 | bytes 12713984 | tf_op jit(solution)/shard_map/product/pallas_call | solution.py:155
  134.7 2.1 %collective-permute-start.21 = (bf16[256,896]{1,0:T(8,128)(2,1)S(1)}, bf16[256,896]{1,0:T(8,128)(2,1)S(1)}, u32[]{:S(2)}, u32[]{:S(2)}) collective-permute-start(bf16[256,896]{1,0:T(8,128)(2,1)S(1)} %product.3), channel_id=1, source_target_pairs={{0,96},{1,97},{2,98},{3,99},{4,100},{5,101},{6,102},{7,103},{8,104... | collective-permute-start | bytes 1376264 | tf_op jit(solution)/shard_map/mate_grad/ppermute | solution.py:32
  136.9 9.9 %product.5.h_ref = f32[512,896]{1,0:T(8,128)S(1)} custom-call(s32[14]{0:T(128)S(1)} %concatenate.21.where_ref, bf16[512,640]{1,0:T(8,128)(2,1)S(1)} %copy-done.27, bf16[512,640]{1,0:T(8,128)(2,1)S(1)} %copy-done.29, bf16[512,640]{1,0:T(8,128)(2,1)} %collective-permute-done.4.refs_2_, bf16[256,640]{1,0:T(8,128)(2,1)S(1)} %copy-done.33, ...), custom_call_target="tpu_custom_call" | custom-call | flops 4697620480 | bytes 16252928 | tf_op jit(solution)/shard_map/product/pallas_call | solution.py:155
  146.8 4.7 %own_half.1 = (bf16[512,1792]{1,0:T(8,128)(2,1)}, bf16[512,1792]{1,0:T(8,128)(2,1)}, f32[512,128]{1,0:T(8,128)S(1)}) custom-call(s32[14]{0:T(128)S(1)} %concatenate.21.where_ref, bf16[512,1792]{1,0:T(8,128)(2,1)S(1)} %copy-done, bf16[512,1792]{1,0:T(8,128)(2,1)S(1)} %copy-done.2, f32[512,896]{1,0:T(8,128)S(1)} %product.5.h_ref, bf16[64,1792]{1,0:T(8,128)(2,1)S(1)} %bitcast.37), custom_call_target="tpu_custom_call" | custom-call | flops 128450560 | bytes 6291456 | tf_op jit(solution)/shard_map/own_half/pallas_call | solution.py:245
  151.5 3.4 %other_half.2 = (bf16[512,1792]{1,0:T(8,128)(2,1)}, bf16[512,1792]{1,0:T(8,128)(2,1)}, f32[256,128]{1,0:T(8,128)S(1)}) custom-call(s32[14]{0:T(128)S(1)} %concatenate.21.where_ref, bf16[512,1792]{1,0:T(8,128)(2,1)S(1)} %copy-done, bf16[512,1792]{1,0:T(8,128)(2,1)S(1)} %copy-done.2, ...), custom_call_target="tpu_custom_call", output_to_operand_aliasing={{0}: (8, {}), {1}: (9, {})} | custom-call | flops 64225280 | bytes 3145728 | tf_op jit(solution)/shard_map/other_half/pallas_call | solution.py:293
  154.9 3.4 %other_half.3 = (bf16[512,1792]{1,0:T(8,128)(2,1)}, bf16[512,1792]{1,0:T(8,128)(2,1)}, f32[256,128]{1,0:T(8,128)S(1)}) custom-call(s32[14]{0:T(128)S(1)} %concatenate.21.where_ref, bf16[512,1792]{1,0:T(8,128)(2,1)S(1)} %copy-done, bf16[512,1792]{1,0:T(8,128)(2,1)S(1)} %copy-done.2, ...), custom_call_target="tpu_custom_call", output_to_operand_aliasing={{0}: (8, {}), {1}: (9, {})} | custom-call | flops 64225280 | bytes 3145728 | tf_op jit(solution)/shard_map/other_half/pallas_call | solution.py:293
  160.7 1.8 %collective-permute-start.31 = (f32[128,128]{1,0:T(8,128)S(1)}, f32[128,128]{1,0:T(8,128)S(1)}, u32[]{:S(2)}, u32[]{:S(2)}) collective-permute-start(f32[128,128]{1,0:T(8,128)S(1)} %select_add_fusion.1), channel_id=1, source_target_pairs={{0,6},{1,7},{2,0},{3,1},{4,2},{5,3},{6,4},{7,5},{8,14},{9,15},{10,... | collective-permute-start | bytes 196616 | tf_op jit(solution)/shard_map/down/ppermute | solution.py:32
  164.2 3.0 %collective-permute-done.29 = f32[128,128]{1,0:T(8,128)S(1)} collective-permute-done((f32[128,128]{1,0:T(8,128)S(1)}, f32[128,128]{1,0:T(8,128)S(1)}, u32[]{:S(2)}, u32[]{:S(2)}) %collective-permute-start.29) | collective-permute-done | bytes 65568 | tf_op jit(solution)/shard_map/send/ppermute | solution.py:32
  167.2 2.1 %collective-permute-start.32 = (f32[128,128]{1,0:T(8,128)S(1)}, f32[128,128]{1,0:T(8,128)S(1)}, u32[]{:S(2)}, u32[]{:S(2)}) collective-permute-start(f32[128,128]{1,0:T(8,128)S(1)} %add_add_fusion.1), channel_id=1, source_target_pairs={{0,1},{1,0},{2,3},{3,2},{4,5},{5,4},{6,7},{7,6},{8,9},{9,8},{10,11... | collective-permute-start | bytes 196616 | tf_op jit(solution)/shard_map/swap/ppermute | solution.py:32
  (163 shorter events, 43.4 us)
Async XLA Ops:
  0.6 19.4 %collective-permute-start.2 = (bf16[512,640]{1,0:T(8,128)(2,1)}, bf16[512,640]{1,0:T(8,128)(2,1)}, u32[]{:S(2)}, u32[]{:S(2)}) collective-permute-start(bf16[512,640]{1,0:T(8,128)(2,1)} %grad_ref.1), channel_id=1, source_target_pairs={{0,96},{1,97},{2,98},{3,99},{4,100},{5,101},{6,102},{7,103},{8,104... | collective-permute-start | bytes 1966088 | tf_op jit(solution)/shard_map/mate_rows/ppermute | solution.py:32
  5.3 16.9 %collective-permute-start.3 = (bf16[512,640]{1,0:T(8,128)(2,1)}, bf16[512,640]{1,0:T(8,128)(2,1)S(1)}, u32[]{:S(2)}, u32[]{:S(2)}) collective-permute-start(bf16[512,640]{1,0:T(8,128)(2,1)} %grad_ref.1), channel_id=1, source_target_pairs={{0,2},{1,3},{2,4},{3,5},{4,6},{5,7},{6,0},{7,1},{8,10},{9,11},{10,... | collective-permute-start | bytes 1966088 | tf_op jit(solution)/shard_map/a_up/ppermute | solution.py:32
  6.6 15.6 %collective-permute-start.4 = (bf16[512,640]{1,0:T(8,128)(2,1)}, bf16[512,640]{1,0:T(8,128)(2,1)}, u32[]{:S(2)}, u32[]{:S(2)}) collective-permute-start(bf16[512,640]{1,0:T(8,128)(2,1)} %grad_ref.1), channel_id=1, source_target_pairs={{0,6},{1,7},{2,0},{3,1},{4,2},{5,3},{6,4},{7,5},{8,14},{9,15},{10,... | collective-permute-start | bytes 1966088 | tf_op jit(solution)/shard_map/a_down/ppermute | solution.py:32
  8.0 26.7 %collective-permute-start = (bf16[112,5120]{1,0:T(8,128)(2,1)}, bf16[112,5120]{1,0:T(8,128)(2,1)}, u32[]{:S(2)}, u32[]{:S(2)}) collective-permute-start(bf16[112,5120]{1,0:T(8,128)(2,1)} %refs_5_.5), channel_id=1, source_target_pairs={{0,32},{1,9},{2,34},{3,11},{4,36},{5,13},{6,38},{7,15},{8,40},{9,1... | collective-permute-start | bytes 3440648 | tf_op jit(solution)/shard_map/r1/ppermute | solution.py:32
  9.2 25.5 %collective-permute-start.1 = (bf16[112,5120]{1,0:T(8,128)(2,1)}, bf16[112,5120]{1,0:T(8,128)(2,1)S(1)}, u32[]{:S(2)}, u32[]{:S(2)}) collective-permute-start(bf16[112,5120]{1,0:T(8,128)(2,1)} %refs_5_.5), channel_id=1, source_target_pairs={{0,8},{1,25},{2,10},{3,27},{4,12},{5,29},{6,14},{7,31},{8,16},{9,1... | collective-permute-start | bytes 3440648 | tf_op jit(solution)/shard_map/r2/ppermute | solution.py:32
  22.2 15.2 %collective-permute-start.5 = (bf16[112,5120]{1,0:T(8,128)(2,1)}, bf16[112,5120]{1,0:T(8,128)(2,1)S(1)}, u32[]{:S(2)}, u32[]{:S(2)}) collective-permute-start(bf16[112,5120]{1,0:T(8,128)(2,1)} %refs_5_.5), channel_id=1, source_target_pairs={{0,24},{1,33},{2,26},{3,35},{4,28},{5,37},{6,30},{7,39},{8,0},{9,4... | collective-permute-start | bytes 3440648 | tf_op jit(solution)/shard_map/r3/ppermute | solution.py:32
  24.4 8.7 %collective-permute-start.6 = (bf16[256,640]{1,0:T(8,128)(2,1)S(1)}, bf16[256,640]{1,0:T(8,128)(2,1)S(1)}, u32[]{:S(2)}, u32[]{:S(2)}) collective-permute-start(bf16[256,640]{1,0:T(8,128)(2,1)S(1)} %slice.68), channel_id=1, source_target_pairs={{0,2},{1,3},{2,4},{3,5},{4,6},{5,7},{6,0},{7,1},{8,10},{9,11},{10,... | collective-permute-start | bytes 983048 | tf_op jit(solution)/shard_map/a_far1/ppermute | solution.py:32
  26.4 6.7 %collective-permute-start.7 = (bf16[256,640]{1,0:T(8,128)(2,1)S(1)}, bf16[256,640]{1,0:T(8,128)(2,1)S(1)}, u32[]{:S(2)}, u32[]{:S(2)}) collective-permute-start(bf16[256,640]{1,0:T(8,128)(2,1)S(1)} %slice.69), channel_id=1, source_target_pairs={{0,6},{1,7},{2,0},{3,1},{4,2},{5,3},{6,4},{7,5},{8,14},{9,15},{10,... | collective-permute-start | bytes 983048 | tf_op jit(solution)/shard_map/a_far2/ppermute | solution.py:32
  40.5 34.1 %collective-permute-start.11 = (bf16[2048,640]{1,0:T(8,128)(2,1)}, bf16[2048,640]{1,0:T(8,128)(2,1)}, u32[]{:S(2)}, u32[]{:S(2)}) collective-permute-start(bf16[2048,640]{1,0:T(8,128)(2,1)} %constant_dynamic-update-slice_fusion), channel_id=1, source_target_pairs={{0,1},{1,0},{2,3},{3,2},{4,5},{5,4},{6,7},{7,6},{8,9},{9,8},{10,11... | collective-permute-start | bytes 7864328 | tf_op jit(solution)/shard_map/a_swap/ppermute | solution.py:32
  44.3 17.7 %collective-permute-start.8 = (bf16[512,640]{1,0:T(8,128)(2,1)}, bf16[512,640]{1,0:T(8,128)(2,1)S(1)}, u32[]{:S(2)}, u32[]{:S(2)}) collective-permute-start(bf16[512,640]{1,0:T(8,128)(2,1)} %collective-permute-done.2.refs_0_), channel_id=1, source_target_pairs={{0,2},{1,3},{2,4},{3,5},{4,6},{5,7},{6,0},{7,1},{8,10},{9,11},{10,... | collective-permute-start | bytes 1966088 | tf_op jit(solution)/shard_map/b_up/ppermute | solution.py:32
  45.7 19.7 %collective-permute-start.9 = (bf16[512,640]{1,0:T(8,128)(2,1)}, bf16[512,640]{1,0:T(8,128)(2,1)S(1)}, u32[]{:S(2)}, u32[]{:S(2)}) collective-permute-start(bf16[512,640]{1,0:T(8,128)(2,1)} %collective-permute-done.2.refs_0_), channel_id=1, source_target_pairs={{0,6},{1,7},{2,0},{3,1},{4,2},{5,3},{6,4},{7,5},{8,14},{9,15},{10,... | collective-permute-start | bytes 1966088 | tf_op jit(solution)/shard_map/b_down/ppermute | solution.py:32
  47.1 43.0 %collective-permute-start.14 = (bf16[112,5120]{1,0:T(8,128)(2,1)}, bf16[112,5120]{1,0:T(8,128)(2,1)S(1)}, u32[]{:S(2)}, u32[]{:S(2)}) collective-permute-start(bf16[112,5120]{1,0:T(8,128)(2,1)} %collective-permute-done.refs_6_), channel_id=1, source_target_pairs={{0,8},{1,33},{2,10},{3,35},{4,12},{5,37},{6,14},{7,39},{8,16},{9,4... | collective-permute-start | bytes 3440648 | tf_op jit(solution)/shard_map/r4/ppermute | solution.py:32
  47.2 27.4 %collective-permute-start.10 = (bf16[112,5120]{1,0:T(8,128)(2,1)S(1)}, bf16[112,5120]{1,0:T(8,128)(2,1)S(1)}, u32[]{:S(2)}, u32[]{:S(2)}) collective-permute-start(bf16[112,5120]{1,0:T(8,128)(2,1)S(1)} %broadcast_select_fusion), channel_id=1, source_target_pairs={{0,24},{1,33},{2,26},{3,35},{4,28},{5,37},{6,30},{7,39},{8,0},{9,4... | collective-permute-start | bytes 3440648 | tf_op jit(solution)/shard_map/r5/ppermute | solution.py:32
  62.1 19.7 %collective-permute-start.16 = (bf16[48,5120]{1,0:T(8,128)(2,1)S(1)}, bf16[48,5120]{1,0:T(8,128)(2,1)S(1)}, u32[]{:S(2)}, u32[]{:S(2)}) collective-permute-start(bf16[48,5120]{1,0:T(8,128)(2,1)S(1)} %slice_select_fusion.3), channel_id=1, source_target_pairs={{0,24},{1,25},{2,26},{3,27},{4,28},{5,29},{6,30},{7,31},{8,0},{9,1... | collective-permute-start | bytes 1474568 | tf_op jit(solution)/shard_map/r7/ppermute | solution.py:32
  74.6 7.4 %collective-permute-start.12 = (bf16[256,640]{1,0:T(8,128)(2,1)S(1)}, bf16[256,640]{1,0:T(8,128)(2,1)S(1)}, u32[]{:S(2)}, u32[]{:S(2)}) collective-permute-start(bf16[256,640]{1,0:T(8,128)(2,1)S(1)} %slice.70), channel_id=1, source_target_pairs={{0,2},{1,3},{2,4},{3,5},{4,6},{5,7},{6,0},{7,1},{8,10},{9,11},{10,... | collective-permute-start | bytes 983048 | tf_op jit(solution)/shard_map/b_far1/ppermute | solution.py:32
  74.6 7.4 %collective-permute-start.13 = (bf16[256,640]{1,0:T(8,128)(2,1)S(1)}, bf16[256,640]{1,0:T(8,128)(2,1)S(1)}, u32[]{:S(2)}, u32[]{:S(2)}) collective-permute-start(bf16[256,640]{1,0:T(8,128)(2,1)S(1)} %slice.71), channel_id=1, source_target_pairs={{0,6},{1,7},{2,0},{3,1},{4,2},{5,3},{6,4},{7,5},{8,14},{9,15},{10,... | collective-permute-start | bytes 983048 | tf_op jit(solution)/shard_map/b_far2/ppermute | solution.py:32
  78.4 11.6 %collective-permute-start.15 = (bf16[64,5120]{1,0:T(8,128)(2,1)S(1)}, bf16[64,5120]{1,0:T(8,128)(2,1)S(1)}, u32[]{:S(2)}, u32[]{:S(2)}) collective-permute-start(bf16[64,5120]{1,0:T(8,128)(2,1)S(1)} %slice_select_fusion.1), channel_id=1, source_target_pairs={{0,8},{1,9},{2,10},{3,11},{4,12},{5,13},{6,14},{7,15},{8,16},{9,17... | collective-permute-start | bytes 1966088 | tf_op jit(solution)/shard_map/r6/ppermute | solution.py:32
  82.1 3.1 %collective-permute-start.22 = (f32[256,192]{1,0:T(8,128)S(1)}, f32[256,192]{1,0:T(8,128)S(1)}, u32[]{:S(2)}, u32[]{:S(2)}) collective-permute-start(f32[256,192]{1,0:T(8,128)S(1)} %slice_select_fusion.4), channel_id=1, source_target_pairs={{0,1},{1,0},{2,3},{3,2},{4,5},{5,4},{6,7},{7,6},{8,9},{9,8},{10,11... | collective-permute-start | bytes 589832 | tf_op jit(solution)/shard_map/swap/ppermute | solution.py:32
  84.8 28.9 %collective-permute-start.19 = (bf16[1536,640]{1,0:T(8,128)(2,1)}, bf16[1536,640]{1,0:T(8,128)(2,1)}, u32[]{:S(2)}, u32[]{:S(2)}) collective-permute-start(bf16[1536,640]{1,0:T(8,128)(2,1)} %pad_maximum_fusion), channel_id=1, source_target_pairs={{0,1},{1,0},{2,3},{3,2},{4,5},{5,4},{6,7},{7,6},{8,9},{9,8},{10,11... | collective-permute-start | bytes 5898248 | tf_op jit(solution)/shard_map/b_near_swap/ppermute | solution.py:32
  85.3 9.2 %collective-permute-start.24 = (f32[256,192]{1,0:T(8,128)S(1)}, f32[256,192]{1,0:T(8,128)S(1)}, u32[]{:S(2)}, u32[]{:S(2)}) collective-permute-start(f32[256,192]{1,0:T(8,128)S(1)} %select_add_fusion), channel_id=1, source_target_pairs={{0,2},{1,3},{2,4},{3,5},{4,6},{5,7},{6,0},{7,1},{8,10},{9,11},{10,... | collective-permute-start | bytes 589832 | tf_op jit(solution)/shard_map/up/ppermute | solution.py:32
  85.3 13.5 %collective-permute-start.25 = (f32[256,192]{1,0:T(8,128)S(1)}, f32[256,192]{1,0:T(8,128)S(1)}, u32[]{:S(2)}, u32[]{:S(2)}) collective-permute-start(f32[256,192]{1,0:T(8,128)S(1)} %select_add_fusion), channel_id=1, source_target_pairs={{0,6},{1,7},{2,0},{3,1},{4,2},{5,3},{6,4},{7,5},{8,14},{9,15},{10,... | collective-permute-start | bytes 589832 | tf_op jit(solution)/shard_map/down/ppermute | solution.py:32
  90.1 10.9 %collective-permute-start.23 = (f32[256,192]{1,0:T(8,128)S(1)}, f32[256,192]{1,0:T(8,128)S(1)}, u32[]{:S(2)}, u32[]{:S(2)}) collective-permute-start(f32[256,192]{1,0:T(8,128)S(1)} %select_add_fusion), channel_id=1, source_target_pairs={{0,4},{1,5},{2,6},{3,7},{4,0},{5,1},{6,2},{7,3},{8,12},{9,13},{10,... | collective-permute-start | bytes 589832 | tf_op jit(solution)/shard_map/send/ppermute | solution.py:32
  91.1 22.6 %collective-permute-start.17 = (bf16[64,5120]{1,0:T(8,128)(2,1)}, bf16[64,5120]{1,0:T(8,128)(2,1)}, u32[]{:S(2)}, u32[]{:S(2)}) collective-permute-start(bf16[64,5120]{1,0:T(8,128)(2,1)} %slice_select_fusion), channel_id=1, source_target_pairs={{0,8},{1,33},{2,10},{3,35},{4,12},{5,37},{6,14},{7,39},{8,16},{9,4... | collective-permute-start | bytes 1966088 | tf_op jit(solution)/shard_map/r8/ppermute | solution.py:32
  101.0 6.3 %collective-permute-start.26 = (f32[256,192]{1,0:T(8,128)S(1)}, f32[256,192]{1,0:T(8,128)S(1)}, u32[]{:S(2)}, u32[]{:S(2)}) collective-permute-start(f32[256,192]{1,0:T(8,128)S(1)} %add_add_fusion), channel_id=1, source_target_pairs={{0,1},{1,0},{2,3},{3,2},{4,5},{5,4},{6,7},{7,6},{8,9},{9,8},{10,11... | collective-permute-start | bytes 589832 | tf_op jit(solution)/shard_map/swap/ppermute | solution.py:32
  102.8 10.9 %collective-permute-start.18 = (bf16[48,5120]{1,0:T(8,128)(2,1)}, bf16[48,5120]{1,0:T(8,128)(2,1)}, u32[]{:S(2)}, u32[]{:S(2)}) collective-permute-start(bf16[48,5120]{1,0:T(8,128)(2,1)} %slice_select_fusion.2), channel_id=1, source_target_pairs={{0,24},{1,33},{2,26},{3,35},{4,28},{5,37},{6,30},{7,39},{8,0},{9,4... | collective-permute-start | bytes 1474568 | tf_op jit(solution)/shard_map/r9/ppermute | solution.py:32
  103.7 10.0 %collective-permute-start.20 = (bf16[512,640]{1,0:T(8,128)(2,1)}, bf16[512,640]{1,0:T(8,128)(2,1)}, u32[]{:S(2)}, u32[]{:S(2)}) collective-permute-start(bf16[512,640]{1,0:T(8,128)(2,1)} %pad_maximum_fusion.1), channel_id=1, source_target_pairs={{0,1},{1,0},{2,3},{3,2},{4,5},{5,4},{6,7},{7,6},{8,9},{9,8},{10,11... | collective-permute-start | bytes 1966088 | tf_op jit(solution)/shard_map/b_far_swap/ppermute | solution.py:32
  127.1 24.4 %collective-permute-start.27 = (bf16[256,896]{1,0:T(8,128)(2,1)S(1)}, bf16[256,896]{1,0:T(8,128)(2,1)S(1)}, u32[]{:S(2)}, u32[]{:S(2)}) collective-permute-start(bf16[256,896]{1,0:T(8,128)(2,1)S(1)} %product.4), channel_id=1, source_target_pairs={{0,96},{1,97},{2,98},{3,99},{4,100},{5,101},{6,102},{7,103},{8,104... | collective-permute-start | bytes 1376264 | tf_op jit(solution)/shard_map/mate_grad/ppermute | solution.py:32
  134.7 20.1 %collective-permute-start.21 = (bf16[256,896]{1,0:T(8,128)(2,1)S(1)}, bf16[256,896]{1,0:T(8,128)(2,1)S(1)}, u32[]{:S(2)}, u32[]{:S(2)}) collective-permute-start(bf16[256,896]{1,0:T(8,128)(2,1)S(1)} %product.3), channel_id=1, source_target_pairs={{0,96},{1,97},{2,98},{3,99},{4,100},{5,101},{6,102},{7,103},{8,104... | collective-permute-start | bytes 1376264 | tf_op jit(solution)/shard_map/mate_grad/ppermute | solution.py:32
  159.8 4.4 %collective-permute-start.30 = (f32[128,128]{1,0:T(8,128)S(1)}, f32[128,128]{1,0:T(8,128)S(1)}, u32[]{:S(2)}, u32[]{:S(2)}) collective-permute-start(f32[128,128]{1,0:T(8,128)S(1)} %select_add_fusion.1), channel_id=1, source_target_pairs={{0,2},{1,3},{2,4},{3,5},{4,6},{5,7},{6,0},{7,1},{8,10},{9,11},{10,... | collective-permute-start | bytes 196616 | tf_op jit(solution)/shard_map/up/ppermute | solution.py:32
  160.7 3.5 %collective-permute-start.31 = (f32[128,128]{1,0:T(8,128)S(1)}, f32[128,128]{1,0:T(8,128)S(1)}, u32[]{:S(2)}, u32[]{:S(2)}) collective-permute-start(f32[128,128]{1,0:T(8,128)S(1)} %select_add_fusion.1), channel_id=1, source_target_pairs={{0,6},{1,7},{2,0},{3,1},{4,2},{5,3},{6,4},{7,5},{8,14},{9,15},{10,... | collective-permute-start | bytes 196616 | tf_op jit(solution)/shard_map/down/ppermute | solution.py:32
  162.6 4.6 %collective-permute-start.29 = (f32[128,128]{1,0:T(8,128)S(1)}, f32[128,128]{1,0:T(8,128)S(1)}, u32[]{:S(2)}, u32[]{:S(2)}) collective-permute-start(f32[128,128]{1,0:T(8,128)S(1)} %select_add_fusion.1), channel_id=1, source_target_pairs={{0,4},{1,5},{2,6},{3,7},{4,0},{5,1},{6,2},{7,3},{8,12},{9,13},{10,... | collective-permute-start | bytes 196616 | tf_op jit(solution)/shard_map/send/ppermute | solution.py:32
  167.2 3.0 %collective-permute-start.32 = (f32[128,128]{1,0:T(8,128)S(1)}, f32[128,128]{1,0:T(8,128)S(1)}, u32[]{:S(2)}, u32[]{:S(2)}) collective-permute-start(f32[128,128]{1,0:T(8,128)S(1)} %add_add_fusion.1), channel_id=1, source_target_pairs={{0,1},{1,0},{2,3},{3,2},{4,5},{5,4},{6,7},{7,6},{8,9},{9,8},{10,11... | collective-permute-start | bytes 196616 | tf_op jit(solution)/shard_map/swap/ppermute | solution.py:32
  (42 other events, 500.2 us)

commit v3 on v2

v3 whole, which is shorter than its diff:
```python
import functools

import jax
import jax.numpy as jnp
from jax import lax
from jax.experimental import pallas as pl
from jax.experimental.pallas import tpu as pltpu
from jax.sharding import Mesh
from jax.sharding import PartitionSpec as P

AXES = ("z", "x", "y", "c")
F32, BF16 = jnp.float32, jnp.bfloat16
ROWS, FEAT, HID, HALF, RANK, DEPTH = 512, 640, 1792, 896, 64, 5120
SHARD = 112
STEP = 2 * FEAT
NT = (((1,), (1,)), ((), ()))
ANY = pl.BlockSpec(memory_space=pl.ANY)


def send(value, target, name="send"):
    def line(z, x, y, c):
        return ((z % 4 * 4 + x % 4) * 4 + y % 4) * 2 + c

    pairs = [
        (line(z, x, y, c), line(*target(z, x, y, c)))
        for z in range(4)
        for x in range(4)
        for y in range(4)
        for c in range(2)
    ]
    with jax.named_scope(name):
        return lax.ppermute(value, AXES, pairs)


def up_y(v, name="up"):
    return send(v, lambda z, x, y, c: (z, x, y + 1, c), name)


def down_y(v, name="down"):
    return send(v, lambda z, x, y, c: (z, x, y - 1, c), name)


def along_y(v, way, name):
    return send(v, lambda z, x, y, c: (z, x, y + way * (1 - 2 * c), c), name)


def swap(v, name="swap"):
    return send(v, lambda z, x, y, c: (z, x, y, 1 - c), name)


def mate(v, name="mate"):
    return send(v, lambda z, x, y, c: (3 - z, x, y, c), name)


def after(value, *others):
    return lax.optimization_barrier((value, *others))[0]


def pick(c, a, b):
    return jnp.where(c == 0, a, b)


def route(v, zero, one, name):
    hop = {
        "p": lambda z, x, y, c: (z ^ 1, x, y, c),
        "+": lambda z, x, y, c: (z, x + 1, y, c),
        "-": lambda z, x, y, c: (z, x - 1, y, c),
    }
    return send(v, lambda z, x, y, c: hop[zero if c == 0 else one](z, x, y, c), name)


def slots(z, x, c):
    zl, first = z % 2, c == 0

    def at(dz, dx):
        return (zl + dz) % 2 * 4 + (x + dx) % 4

    held = jnp.stack(
        [
            at(0, 0),
            jnp.where(first, at(1, 0), at(0, 3)),
            jnp.where(first, at(0, 3), at(0, 1)),
            jnp.where(first, at(0, 1), at(1, 0)),
            at(1, 3),
            at(1, 1),
            at(0, 2),
            at(1, 2),
        ]
    )
    shard = jnp.arange(8)
    return jnp.sum(jnp.where(held[None, :] == shard[:, None], shard[None, :], 0), axis=1)


def product_kernel(shards, where_ref, *refs):
    mine, other, weights = refs[:4], refs[4:8], refs[8 : 8 + shards]
    out_ref, a_buf, w_buf, a_sem, w_sem, *acc = refs[8 + shards :]
    acc = acc[0] if acc else out_ref
    y, c = where_ref[16], where_ref[17]
    a_copies = []
    for group, (pieces, core) in enumerate(((mine, c), (other, 1 - c))):
        lane = pl.multiple_of(core * FEAT, 128)
        for k in range(4):
            a_copies.append(
                pltpu.make_async_copy(
                    pieces[k], a_buf.at[k, :, pl.ds(lane, FEAT)], a_sem.at[group, k]
                )
            )

    def w_copies(step):
        shift = (0, 3 - 2 * c, 1 + 2 * c, 2)[step]
        lane = pl.multiple_of(lax.rem(y + shift, 4) * STEP, 128)
        return [
            pltpu.make_async_copy(
                w.at[:, pl.ds(lane, STEP)],
                w_buf.at[step % 2, pl.ds(k * 128, SHARD), :],
                w_sem.at[step % 2, k],
            )
            for k, w in enumerate(weights)
        ]

    for copy in w_copies(0):
        copy.start()
    for copy in a_copies:
        copy.start()
    for half in range(2):
        for k in range(shards):
            w_buf[half, k * 128 + SHARD : k * 128 + 128, :] = jnp.zeros((128 - SHARD, STEP), BF16)
    for step in range(4):
        if step < 3:
            for copy in w_copies(step + 1):
                copy.start()
        a_copies[step].wait()
        a_copies[4 + step].wait()
        for copy in w_copies(step):
            copy.wait()
        part = lax.dot_general(a_buf[step], w_buf[step % 2], NT, preferred_element_type=F32)
        if step == 0:
            acc[...] = part
        elif step < 3:
            acc[...] += part
        else:
            out_ref[...] = (acc[...] + part).astype(out_ref.dtype)


def product(dtype, where, mine, other, weights):
    shards = len(weights)
    width = shards * 128
    vmem = pl.BlockSpec(memory_space=pltpu.VMEM)
    return pl.pallas_call(
        functools.partial(product_kernel, shards),
        out_shape=jax.ShapeDtypeStruct((ROWS, width), dtype),
        in_specs=[pl.BlockSpec(memory_space=pltpu.SMEM)] + [vmem] * (8 + shards),
        out_specs=vmem,
        scratch_shapes=[
            pltpu.VMEM((4, ROWS, STEP), BF16),
            pltpu.VMEM((2, width, STEP), BF16),
            pltpu.SemaphoreType.DMA((2, 4)),
            pltpu.SemaphoreType.DMA((2, shards)),
        ]
        + ([] if dtype == F32 else [pltpu.VMEM((ROWS, width), F32)]),
        compiler_params=pltpu.CompilerParams(
            vmem_limit_bytes=(8 << 20) + width * (4 * STEP + 14 * ROWS)
        ),
        cost_estimate=pl.CostEstimate(
            flops=2 * ROWS * width * DEPTH,
            bytes_accessed=2 * DEPTH * (ROWS + width) + 4 * ROWS * width,
            transcendentals=0,
        ),
        name="product",
    )(where, *mine, *other, *weights)


def early_kernel(where_ref, act_ref, grad_ref, pm_ref, gate_ref, up_ref, ph_ref, out_ref):
    gate, up = gate_ref[...].astype(F32), up_ref[...].astype(F32)
    hidden = (gate * jax.nn.sigmoid(gate) * up).astype(BF16)
    pm = pm_ref[...]
    out_ref[:, 0:64] = lax.dot_general(act_ref[...], pm, NT, preferred_element_type=F32)
    out_ref[:, 64:128] = lax.dot_general(hidden, ph_ref[...], NT, preferred_element_type=F32)
    out_ref[:, 128:192] = lax.dot_general(grad_ref[...], pm, NT, preferred_element_type=F32)


def early(where, activations, out_grad, pm_t, gate, up, ph_t):
    narrow = pl.BlockSpec((128, FEAT), lambda i, w: (i, 0))
    wide = pl.BlockSpec((128, HID), lambda i, w: (i, 0))
    return pl.pallas_call(
        early_kernel,
        out_shape=jax.ShapeDtypeStruct((ROWS, 3 * RANK), F32),
        grid_spec=pltpu.PrefetchScalarGridSpec(
            num_scalar_prefetch=1,
            grid=(4,),
            in_specs=[
                narrow,
                narrow,
                pl.BlockSpec((RANK, FEAT), lambda i, w: (0, 2 * w[16] + w[17])),
                wide,
                wide,
                pl.BlockSpec((RANK, HID), lambda i, w: (0, 0)),
            ],
            out_specs=pl.BlockSpec((128, 3 * RANK), lambda i, w: (i, 0)),
        ),
        compiler_params=pltpu.CompilerParams(vmem_limit_bytes=12 << 20),
        cost_estimate=pl.CostEstimate(
            flops=ROWS * HID * 160, bytes_accessed=5 << 20, transcendentals=ROWS * HID
        ),
        name="early",
    )(where, activations, out_grad, pm_t, gate, up, ph_t)


def grads(where_ref, base, h_refs, held, gate_ref, up_ref, ph_ref, gg_ref, gu_ref):
    at = 0
    for h_ref in h_refs:
        width = h_ref.shape[1]
        held[:, at : at + width] = h_ref[...].astype(F32)
        at += width
    hidden_grad = jnp.concatenate(
        [
            held[:, pl.ds(pl.multiple_of(where_ref[base + i] * 128, 128), 128)][:, :SHARD]
            for i in range(8)
        ],
        axis=1,
    )
    row = pl.program_id(0) * 64 + lax.broadcasted_iota(jnp.int32, hidden_grad.shape, 0)
    hidden_grad = jnp.where(row < where_ref[19], hidden_grad, 0.0)
    gate, up = gate_ref[...].astype(F32), up_ref[...].astype(F32)
    sig = jax.nn.sigmoid(gate)
    grad_up = (hidden_grad * (gate * sig)).astype(BF16)
    grad_gate = (hidden_grad * up * sig * (1.0 + gate * (1.0 - sig))).astype(BF16)
    gg_ref[...] = grad_gate
    gu_ref[...] = grad_up
    ph = ph_ref[...]
    return jnp.concatenate(
        [
            lax.dot_general(g, ph, NT, preferred_element_type=F32)
            for g in (grad_gate, grad_up)
        ],
        axis=1,
    )


def own_kernel(n, where_ref, gate_ref, up_ref, ph_ref, *refs):
    gg_ref, gu_ref, part_ref, held = refs[n:]
    part_ref[...] = grads(
        where_ref, 0, refs[:n], held, gate_ref, up_ref, ph_ref, gg_ref, gu_ref
    )


def row_tiles(half):
    tile = pl.BlockSpec((64, HALF), lambda i, w: (i, half(w)))
    return tile, pl.BlockSpec((RANK, HALF), lambda i, w: (0, half(w)))


def pieces_of(h):
    return [pl.BlockSpec((64, p.shape[1]), lambda i, w: (i, 0)) for p in h]


BIG = jax.ShapeDtypeStruct((ROWS, HID), BF16)


def own_half(where, gate, up, h, ph_t):
    tile, ranks = row_tiles(lambda w: w[18])
    return pl.pallas_call(
        functools.partial(own_kernel, len(h)),
        out_shape=(BIG, BIG, jax.ShapeDtypeStruct((ROWS, 2 * RANK), F32)),
        grid_spec=pltpu.PrefetchScalarGridSpec(
            num_scalar_prefetch=1,
            grid=(8,),
            in_specs=[tile, tile, ranks] + pieces_of(h),
            out_specs=(tile, tile, pl.BlockSpec((64, 2 * RANK), lambda i, w: (i, 0))),
            scratch_shapes=[pltpu.VMEM((64, 1024), F32)],
        ),
        compiler_params=pltpu.CompilerParams(vmem_limit_bytes=8 << 20),
        cost_estimate=pl.CostEstimate(
            flops=ROWS * HALF * 280, bytes_accessed=6 << 20, transcendentals=ROWS * HALF
        ),
        name="own_half",
    )(where, gate, up, ph_t, *h)


def other_kernel(n, where_ref, gate_ref, up_ref, ph_ref, part_ref, hi_ref, lo_ref,
                 gg_in, gu_in, *refs):
    gg_ref, gu_ref, feat_ref, held, acc = refs[n:]
    i = pl.program_id(0)
    part = grads(where_ref, 8, refs[:n], held, gate_ref, up_ref, ph_ref, gg_ref, gu_ref)
    acc[pl.ds(pl.multiple_of(i * 64, 64), 64), :] = part_ref[...] + part

    @pl.when(i == 7)
    def _():
        feat_ref[...] = twice(hi_ref[...], lo_ref[...], acc[...])


def parted(value):
    hi = value.astype(BF16)
    return hi, (value - hi.astype(F32)).astype(BF16)


def twice(hi, lo, right):
    right_hi, right_lo = parted(right)
    total = jnp.dot(lo, right_hi, preferred_element_type=F32)
    total += jnp.dot(hi, right_lo, preferred_element_type=F32)
    return total + jnp.dot(hi, right_hi, preferred_element_type=F32)


def other_half(where, gate, up, h, ph_t, part, spread, gg, gu):
    tile, ranks = row_tiles(lambda w: 1 - w[18])
    feat = pl.BlockSpec((4 * RANK, 2 * RANK), lambda i, w: (0, 0))
    spreads = pl.BlockSpec((4 * RANK, ROWS), lambda i, w: (0, 0))
    return pl.pallas_call(
        functools.partial(other_kernel, len(h)),
        out_shape=(BIG, BIG, jax.ShapeDtypeStruct((4 * RANK, 2 * RANK), F32)),
        grid_spec=pltpu.PrefetchScalarGridSpec(
            num_scalar_prefetch=1,
            grid=(8,),
            in_specs=[
                tile,
                tile,
                ranks,
                pl.BlockSpec((64, 2 * RANK), lambda i, w: (i, 0)),
                spreads,
                spreads,
                ANY,
                ANY,
            ]
            + pieces_of(h),
            out_specs=(tile, tile, feat),
            scratch_shapes=[pltpu.VMEM((64, 1024), F32), pltpu.VMEM((ROWS, 2 * RANK), F32)],
        ),
        input_output_aliases={7: 0, 8: 1},
        compiler_params=pltpu.CompilerParams(vmem_limit_bytes=8 << 20),
        cost_estimate=pl.CostEstimate(
            flops=ROWS * HALF * 280, bytes_accessed=6 << 20, transcendentals=ROWS * HALF
        ),
        name="other_half",
    )(where, gate, up, ph_t, part, *spread, gg, gu, *h)


def spread_kernel(where_ref, sums_ref, hi_ref, lo_ref, feat_ref):
    sums = sums_ref[...]
    left = sums[:, : 2 * RANK].T
    right = sums[:, 2 * RANK :]
    row = lax.broadcasted_iota(jnp.int32, (1, ROWS), 1)
    start = jnp.int32(0)
    for s in range(4):
        length = where_ref[20 + s]
        member = jnp.logical_and(row >= start, row < start + length).astype(F32)
        weight = member / jnp.sqrt(jnp.broadcast_to(length, (1, ROWS)).astype(F32))
        hi, lo = parted(left[:RANK] * weight)
        at = pl.ds(s * RANK, RANK)
        hi_ref[at, :] = hi
        lo_ref[at, :] = lo
        feat_ref[at, :] = twice(*parted(left[RANK:] * weight), right)
        start += length


def spread_features(where, sums):
    vmem = pl.BlockSpec(memory_space=pltpu.VMEM)
    side = jax.ShapeDtypeStruct((4 * RANK, ROWS), BF16)
    return pl.pallas_call(
        spread_kernel,
        out_shape=(side, side, jax.ShapeDtypeStruct((4 * RANK, RANK), F32)),
        in_specs=[pl.BlockSpec(memory_space=pltpu.SMEM), vmem],
        out_specs=(vmem, vmem, vmem),
        compiler_params=pltpu.CompilerParams(vmem_limit_bytes=8 << 20),
        name="spread",
    )(where, sums)


def sum_tensor(value, c):
    half = value.shape[0] // 2
    top, low = value[:half], value[half:]
    mine = jnp.where(c == 0, top, low) + swap(jnp.where(c == 0, low, top))
    across = send(mine, lambda z, x, y, c: (z, x, y + 2, c))
    mine = (mine + across) + (up_y(mine) + down_y(mine))
    theirs = swap(mine)
    return jnp.concatenate(
        [jnp.where(c == 0, mine, theirs), jnp.where(c == 0, theirs, mine)], axis=0
    )


def on_device(
    activations, out_grad, gate_pre, up_pre, down_weight, proj_model, proj_hidden, lengths
):
    z, x, y, c = (lax.axis_index(a) for a in AXES)
    where = jnp.concatenate(
        [
            slots(z, x, c),
            slots(3 - z, x, c),
            jnp.stack([y, c, z // 2, jnp.sum(lengths)]),
            lengths,
        ]
    ).astype(jnp.int32)
    own_w = down_weight
    r1 = route(own_w, "p", "+", "r1")
    r2 = route(own_w, "+", "-", "r2")
    r3 = route(own_w, "-", "p", "r3")
    theirs = mate(out_grad, "mate_rows")
    a1 = along_y(out_grad, 1, "a1")
    a2 = along_y(after(out_grad, a1), -1, "a2")
    a_far = along_y(a1, 1, "a_far")
    r1, r2, r3 = lax.optimization_barrier((r1, r2, r3))
    r4 = route(r1, "+", "p", "r4")
    r5 = route(pick(c, r1, r2), "-", "p", "r5")
    r6 = route(r2, "+", "-", "r6")
    theirs, a2, a_far = lax.optimization_barrier((theirs, a2, a_far))
    b1 = along_y(theirs, 1, "b1")
    b2 = along_y(theirs, -1, "b2")
    a_other = [swap(v, "a_swap") for v in (out_grad, a2, a1, a_far)]
    b1, *a_other = lax.optimization_barrier((b1, *a_other))
    b_far = along_y(b1, 1, "b_far")
    r7 = route(after(pick(c, r4, r6), r5), "+", "p", "r7")
    a_mine, b_mine = [out_grad, a1, a2, a_far], [theirs, b1, b2, b_far]
    b_other = [swap(v, "b_swap") for v in (theirs, b2, b1, b_far)]

    pm_t, ph_t = proj_model.T, proj_hidden.T
    parts = early(after(where, b1), activations, out_grad, pm_t, gate_pre, up_pre, ph_t)
    sums = sum_tensor(after(parts, r7), c)
    *spread, down_feat = spread_features(where, sums)

    h1 = product(BF16, where, b_mine, b_other, [own_w, r1, r2, r3])
    h2 = product(BF16, after(where, h1), b_mine, b_other, [r4, r5, r6])
    h3 = product(BF16, after(where, h2), b_mine, b_other, [r7])
    h_in = [mate(h, "mate_grad") for h in (h1, h2, h3)]
    o1 = product(F32, after(where, h2), a_mine, a_other, [own_w, r1, r2, r3, r4, r5, r6])
    o2 = product(F32, after(where, h3), a_mine, a_other, [r7])
    grad_gate, grad_up, part = own_half(where, gate_pre, up_pre, (o1, o2), ph_t)
    grad_gate, grad_up, feat = other_half(
        where, gate_pre, up_pre, h_in, ph_t, part, spread, grad_gate, grad_up
    )
    total = jnp.concatenate([sum_tensor(feat, c), down_feat], axis=1)
    features = total.reshape(4, RANK, 3, RANK).transpose(0, 2, 1, 3).reshape(4, 3, RANK * RANK)
    return grad_gate, grad_up, features


def solution(mesh):
    split = Mesh(mesh.devices.reshape(4, 4, 4, 2), AXES)
    dp, tensor = ("z", "x"), ("y", "c")
    return jax.shard_map(
        on_device,
        mesh=split,
        in_specs=(
            P(dp, tensor),
            P(dp, tensor),
            P(dp, tensor),
            P(dp, tensor),
            P((*tensor, *dp), None),
            P(),
            P(tensor, None),
            P(dp),
        ),
        out_specs=(P(dp, tensor), P(dp, tensor), P(dp, None, None)),
        check_vma=False,
    )
```

time: 172 us -> 167 us (0.971)
  starting transfers between devices: 42.8 us -> 57.8 us
  waiting for transfers between devices: 56.1 us -> 45.1 us
  Pallas kernels: 38 us -> 47.1 us
  other arithmetic: 11.4 us -> 2.39 us
  local copies, waits for them, and re-layouts: 21.6 us -> 13.3 us
    ppermute x33 -> x35, starting transfers between devices: 42.8 us -> 57.8 us  [send(): return lax.ppermute(value, AXES, pairs)]
    ppermute x33 -> x35, waiting for transfers between devices: 56.1 us -> 45.1 us  [send(): return lax.ppermute(value, AXES, pairs)]
    pallas_call x6 -> x8, Pallas kernels: 35.6 us -> 44.7 us  [the longest x5 32.6 us: product(): pl.pallas_call(functools.partial(product_kernel, shards), out_shape=jax.S...]
    slice x6 -> x0, local copies, waits for them, and re-layouts: 4.53 us -> none  [the longest x2 3.44 us: on_device(): sums[:, i * RANK:(i + 1) * RANK]]
    concatenate x3 -> x1, other arithmetic: 3.58 us -> 0.02 us  [on_device(): total = jnp.concatenate([sum_tensor(feat, c), down_feat], axis=1)]
    unnamed x86 -> x62, local copies, waits for them, and re-layouts: 14.3 us -> 11 us
    select_n x5 -> x2, other arithmetic: 3.2 us -> 1.23 us  [pick(): return jnp.where(c == 0, a, b)]
  transfers between devices with their start and end apart: 33 -> 35, of which waited for: 15 -> 11; matrix products, arithmetic and copies ran while one was open for 13% -> 2% of each run, Pallas kernels for 16% -> 25%
where the time goes in v3:
time: 167 us
  starting transfers between devices  57.8 us (35%)
  Pallas kernels  47.1 us (28%)
  waiting for transfers between devices  45.1 us (27%)
  local copies, waits for them, and re-layouts  13.3 us (8%)
  other arithmetic  2.39 us (1%)
    ppermute x35, starting transfers between devices, send(): return lax.ppermute(value, AXES, pairs)  57.8 us
    ppermute x35, waiting for transfers between devices, send(): return lax.ppermute(value, AXES, pairs)  45.1 us
    pallas_call x5, Pallas kernels, product(): pl.pallas_call(functools.partial(product_kernel, shards), out_shape=jax.S...  32.6 us
    unnamed x62, local copies, waits for them, and re-layouts  11 us
    pallas_call x1, Pallas kernels, other_half(): pl.pallas_call(functools.partial(other_kernel, len(h)), out_shape=(BIG, B...  5.94 us
    pallas_call x1, Pallas kernels, own_half(): pl.pallas_call(functools.partial(own_kernel, len(h)), out_shape=(BIG, BIG...  5.11 us
  transfers between devices with their start and end apart: 35, of which 11 were waited for; matrix products, arithmetic and copies ran while one was open for 2% of the time, Pallas kernels for 25%

profile of v3, /device:TPU:1, one launch (start us, length us, event | category | flops | bytes accessed | tf_op | source)
XLA Modules:
  0.0 166.7 jit_solution(5423495490821007470)
XLA Ops:
  0.6 2.1 %collective-permute-start.15 = (bf16[112,5120]{1,0:T(8,128)(2,1)}, bf16[112,5120]{1,0:T(8,128)(2,1)}, u32[]{:S(2)}, u32[]{:S(2)}) collective-permute-start(bf16[112,5120]{1,0:T(8,128)(2,1)} %refs_8_.3), channel_id=1, source_target_pairs={{0,32},{1,9},{2,34},{3,11},{4,36},{5,13},{6,38},{7,15},{8,40},{9,1... | collective-permute-start | bytes 3440648 | tf_op jit(solution)/shard_map/r1/ppermute | solution.py:32
  4.1 1.7 %collective-permute-start.17 = (bf16[112,5120]{1,0:T(8,128)(2,1)}, bf16[112,5120]{1,0:T(8,128)(2,1)}, u32[]{:S(2)}, u32[]{:S(2)}) collective-permute-start(bf16[112,5120]{1,0:T(8,128)(2,1)} %refs_8_.3), channel_id=1, source_target_pairs={{0,24},{1,33},{2,26},{3,35},{4,28},{5,37},{6,30},{7,39},{8,0},{9,4... | collective-permute-start | bytes 3440648 | tf_op jit(solution)/shard_map/r3/ppermute | solution.py:32
  5.8 2.2 %collective-permute-start = (bf16[512,640]{1,0:T(8,128)(2,1)}, bf16[512,640]{1,0:T(8,128)(2,1)S(1)}, u32[]{:S(2)}, u32[]{:S(2)}) collective-permute-start(bf16[512,640]{1,0:T(8,128)(2,1)} %grad_ref.1), channel_id=1, source_target_pairs={{0,96},{1,97},{2,98},{3,99},{4,100},{5,101},{6,102},{7,103},{8,104... | collective-permute-start | bytes 1966088 | tf_op jit(solution)/shard_map/mate_rows/ppermute | solution.py:32
  8.1 2.7 %collective-permute-start.1 = (bf16[512,640]{1,0:T(8,128)(2,1)}, bf16[512,640]{1,0:T(8,128)(2,1)}, u32[]{:S(2)}, u32[]{:S(2)}) collective-permute-start(bf16[512,640]{1,0:T(8,128)(2,1)} %grad_ref.1), channel_id=1, source_target_pairs={{0,2},{1,7},{2,4},{3,1},{4,6},{5,3},{6,0},{7,5},{8,10},{9,15},{10,... | collective-permute-start | bytes 1966088 | tf_op jit(solution)/shard_map/a1/ppermute | solution.py:32
  10.8 15.9 %collective-permute-done.15.refs_9_ = bf16[112,5120]{1,0:T(8,128)(2,1)} collective-permute-done((bf16[112,5120]{1,0:T(8,128)(2,1)}, bf16[112,5120]{1,0:T(8,128)(2,1)}, u32[]{:S(2)}, u32[]{:S(2)}) %collective-permute-start.15) | collective-permute-done | bytes 1146912 | tf_op jit(solution)/shard_map/r1/ppermute | solution.py:32
  26.9 3.2 %collective-permute-done.17.refs_11_ = bf16[112,5120]{1,0:T(8,128)(2,1)} collective-permute-done((bf16[112,5120]{1,0:T(8,128)(2,1)}, bf16[112,5120]{1,0:T(8,128)(2,1)}, u32[]{:S(2)}, u32[]{:S(2)}) %collective-permute-start.17) | collective-permute-done | bytes 1146912 | tf_op jit(solution)/shard_map/r3/ppermute | solution.py:32
  30.2 1.7 %collective-permute-start.18 = (bf16[112,5120]{1,0:T(8,128)(2,1)}, bf16[112,5120]{1,0:T(8,128)(2,1)S(1)}, u32[]{:S(2)}, u32[]{:S(2)}) collective-permute-start(bf16[112,5120]{1,0:T(8,128)(2,1)} %collective-permute-done.15.refs_9_), channel_id=1, source_target_pairs={{0,8},{1,33},{2,10},{3,35},{4,12},{5,37},{6,14},{7,39},{8,16},{9,4... | collective-permute-start | bytes 3440648 | tf_op jit(solution)/shard_map/r4/ppermute | solution.py:32
  32.1 2.5 %collective-permute-start.20 = (bf16[112,5120]{1,0:T(8,128)(2,1)}, bf16[112,5120]{1,0:T(8,128)(2,1)S(1)}, u32[]{:S(2)}, u32[]{:S(2)}) collective-permute-start(bf16[112,5120]{1,0:T(8,128)(2,1)} %copy-done.7), channel_id=1, source_target_pairs={{0,8},{1,25},{2,10},{3,27},{4,12},{5,29},{6,14},{7,31},{8,16},{9,1... | collective-permute-start | bytes 3440648 | tf_op jit(solution)/shard_map/r6/ppermute | solution.py:32
  36.0 1.5 collective-permute-start.3
  37.5 10.4 %collective-permute-done.2.refs_2_ = bf16[512,640]{1,0:T(8,128)(2,1)S(1)} collective-permute-done((bf16[512,640]{1,0:T(8,128)(2,1)S(1)}, bf16[512,640]{1,0:T(8,128)(2,1)S(1)}, u32[]{:S(2)}, u32[]{:S(2)}) %collective-permute-start.2) | collective-permute-done | bytes 655392 | tf_op jit(solution)/shard_map/a2/ppermute | solution.py:32
  48.0 5.4 %collective-permute-start.5 = (bf16[512,640]{1,0:T(8,128)(2,1)S(1)}, bf16[512,640]{1,0:T(8,128)(2,1)S(1)}, u32[]{:S(2)}, u32[]{:S(2)}) collective-permute-start(bf16[512,640]{1,0:T(8,128)(2,1)S(1)} %copy-done.9), channel_id=1, source_target_pairs={{0,1},{1,0},{2,3},{3,2},{4,5},{5,4},{6,7},{7,6},{8,9},{9,8},{10,11... | collective-permute-start | bytes 1966088 | tf_op jit(solution)/shard_map/a_swap/ppermute | solution.py:32
  53.4 2.8 %collective-permute-start.4 = (bf16[512,640]{1,0:T(8,128)(2,1)S(1)}, bf16[512,640]{1,0:T(8,128)(2,1)S(1)}, u32[]{:S(2)}, u32[]{:S(2)}) collective-permute-start(bf16[512,640]{1,0:T(8,128)(2,1)S(1)} %collective-permute-done.refs_0_), channel_id=1, source_target_pairs={{0,2},{1,7},{2,4},{3,1},{4,6},{5,3},{6,0},{7,5},{8,10},{9,15},{10,... | collective-permute-start | bytes 1966088 | tf_op jit(solution)/shard_map/b1/ppermute | solution.py:32
  56.2 1.7 %collective-permute-done.19.refs_9_.refs_13_ = bf16[112,5120]{1,0:T(8,128)(2,1)S(1)} collective-permute-done((bf16[112,5120]{1,0:T(8,128)(2,1)S(1)}, bf16[112,5120]{1,0:T(8,128)(2,1)S(1)}, u32[]{:S(2)}, u32[]{:S(2)}) %collective-permute-start.19) | collective-permute-done | bytes 1146912 | tf_op jit(solution)/shard_map/r5/ppermute | solution.py:32
  58.9 2.5 %collective-permute-start.6 = (bf16[512,640]{1,0:T(8,128)(2,1)S(1)}, bf16[512,640]{1,0:T(8,128)(2,1)S(1)}, u32[]{:S(2)}, u32[]{:S(2)}) collective-permute-start(bf16[512,640]{1,0:T(8,128)(2,1)S(1)} %collective-permute-done.2.refs_2_), channel_id=1, source_target_pairs={{0,1},{1,0},{2,3},{3,2},{4,5},{5,4},{6,7},{7,6},{8,9},{9,8},{10,11... | collective-permute-start | bytes 1966088 | tf_op jit(solution)/shard_map/a_swap/ppermute | solution.py:32
  74.4 5.6 %collective-permute-done.9.refs_2_ = bf16[512,640]{1,0:T(8,128)(2,1)} collective-permute-done((bf16[512,640]{1,0:T(8,128)(2,1)S(1)}, bf16[512,640]{1,0:T(8,128)(2,1)}, u32[]{:S(2)}, u32[]{:S(2)}) %collective-permute-start.9) | collective-permute-done | bytes 655392 | tf_op jit(solution)/shard_map/b2/ppermute | solution.py:32
  79.9 4.9 %collective-permute-start.12 = (bf16[512,640]{1,0:T(8,128)(2,1)}, bf16[512,640]{1,0:T(8,128)(2,1)S(1)}, u32[]{:S(2)}, u32[]{:S(2)}) collective-permute-start(bf16[512,640]{1,0:T(8,128)(2,1)} %collective-permute-done.9.refs_2_), channel_id=1, source_target_pairs={{0,1},{1,0},{2,3},{3,2},{4,5},{5,4},{6,7},{7,6},{8,9},{9,8},{10,11... | collective-permute-start | bytes 1966088 | tf_op jit(solution)/shard_map/b_swap/ppermute | solution.py:32
  84.8 1.5 copy-done.1
  89.6 2.4 %early.1 = f32[512,192]{1,0:T(8,128)S(1)} custom-call(s32[24]{0:T(128)S(1)} %concatenate.12.where_ref, bf16[512,640]{1,0:T(8,128)(2,1)S(1)} %copy-done.16, bf16[512,640]{1,0:T(8,128)(2,1)S(1)} %copy-done.10, bf16[64,5120]{1,0:T(8,128)(2,1)S(1)} %bitcast.32, bf16[512,1792]{1,0:T(8,128)(2,1)S(1)} %copy-done, bf16[512,1792]{1,0:T(8,128)(2,1)S(1)} %copy-done.1, ...), custom_call_target="tpu_custom_call" | custom-call | flops 146800640 | bytes 5242880 | tf_op jit(solution)/shard_map/early/pallas_call | solution.py:185
  92.7 1.8 %collective-permute-done.22 = f32[256,192]{1,0:T(8,128)S(1)} collective-permute-done((f32[256,192]{1,0:T(8,128)S(1)}, f32[256,192]{1,0:T(8,128)S(1)}, u32[]{:S(2)}, u32[]{:S(2)}) %collective-permute-start.22) | collective-permute-done | bytes 196640 | tf_op jit(solution)/shard_map/swap/ppermute | solution.py:32
  94.7 3.6 %collective-permute-start.25 = (f32[256,192]{1,0:T(8,128)S(1)}, f32[256,192]{1,0:T(8,128)S(1)}, u32[]{:S(2)}, u32[]{:S(2)}) collective-permute-start(f32[256,192]{1,0:T(8,128)S(1)} %select_add_fusion), channel_id=1, source_target_pairs={{0,6},{1,7},{2,0},{3,1},{4,2},{5,3},{6,4},{7,5},{8,14},{9,15},{10,... | collective-permute-start | bytes 589832 | tf_op jit(solution)/shard_map/down/ppermute | solution.py:32
  99.7 6.5 %product.5 = bf16[512,512]{1,0:T(8,128)(2,1)S(1)} custom-call(s32[24]{0:T(128)S(1)} %concatenate.12.where_ref, bf16[512,640]{1,0:T(8,128)(2,1)S(1)} %collective-permute-done.refs_0_, bf16[512,640]{1,0:T(8,128)(2,1)S(1)} %collective-permute-done.4.refs_1_, bf16[512,640]{1,0:T(8,128)(2,1)} %collective-permute-done.9.refs_2_, ...), custom_call_target="tpu_custom_call" | custom-call | flops 2684354560 | bytes 11534336 | tf_op jit(solution)/shard_map/product/pallas_call | solution.py:149
  106.2 4.3 %collective-permute-start.27 = (bf16[512,512]{1,0:T(8,128)(2,1)S(1)}, bf16[512,512]{1,0:T(8,128)(2,1)S(1)}, u32[]{:S(2)}, u32[]{:S(2)}) collective-permute-start(bf16[512,512]{1,0:T(8,128)(2,1)S(1)} %product.5), channel_id=1, source_target_pairs={{0,96},{1,97},{2,98},{3,99},{4,100},{5,101},{6,102},{7,103},{8,104... | collective-permute-start | bytes 1572872 | tf_op jit(solution)/shard_map/mate_grad/ppermute | solution.py:32
  110.6 5.7 %product.6 = bf16[512,384]{1,0:T(8,128)(2,1)S(1)} custom-call(s32[24]{0:T(128)S(1)} %concatenate.12.where_ref, bf16[512,640]{1,0:T(8,128)(2,1)S(1)} %collective-permute-done.refs_0_, bf16[512,640]{1,0:T(8,128)(2,1)S(1)} %collective-permute-done.4.refs_1_, bf16[512,640]{1,0:T(8,128)(2,1)} %collective-permute-done.9.refs_2_, ...), custom_call_target="tpu_custom_call" | custom-call | flops 2013265920 | bytes 9961472 | tf_op jit(solution)/shard_map/product/pallas_call | solution.py:149
  117.6 9.6 %product.7.refs_0_ = f32[512,896]{1,0:T(8,128)S(1)} custom-call(s32[24]{0:T(128)S(1)} %concatenate.12.where_ref, bf16[512,640]{1,0:T(8,128)(2,1)S(1)} %copy-done.11, bf16[512,640]{1,0:T(8,128)(2,1)} %collective-permute-done.1.refs_1_, bf16[512,640]{1,0:T(8,128)(2,1)S(1)} %copy-done.19, bf16[512,640]{1,0:T(8,128)(2,1)S(1)} %copy-done.21, ...), custom_call_target="tpu_custom_call" | custom-call | flops 4697620480 | bytes 16252928 | tf_op jit(solution)/shard_map/product/pallas_call | solution.py:149
  127.2 5.5 %product.8 = bf16[512,128]{1,0:T(8,128)(2,1)S(1)} custom-call(s32[24]{0:T(128)S(1)} %concatenate.12.where_ref, bf16[512,640]{1,0:T(8,128)(2,1)S(1)} %collective-permute-done.refs_0_, bf16[512,640]{1,0:T(8,128)(2,1)S(1)} %collective-permute-done.4.refs_1_, bf16[512,640]{1,0:T(8,128)(2,1)} %collective-permute-done.9.refs_2_, ...), custom_call_target="tpu_custom_call" | custom-call | flops 671088640 | bytes 6815744 | tf_op jit(solution)/shard_map/product/pallas_call | solution.py:149
  132.6 3.2 %collective-permute-start.29 = (bf16[512,128]{1,0:T(8,128)(2,1)S(1)}, bf16[512,128]{1,0:T(8,128)(2,1)S(1)}, u32[]{:S(2)}, u32[]{:S(2)}) collective-permute-start(bf16[512,128]{1,0:T(8,128)(2,1)S(1)} %product.8), channel_id=1, source_target_pairs={{0,96},{1,97},{2,98},{3,99},{4,100},{5,101},{6,102},{7,103},{8,104... | collective-permute-start | bytes 393224 | tf_op jit(solution)/shard_map/mate_grad/ppermute | solution.py:32
  135.9 5.4 %product.9.refs_1_ = f32[512,128]{1,0:T(8,128)S(1)} custom-call(s32[24]{0:T(128)S(1)} %concatenate.12.where_ref, bf16[512,640]{1,0:T(8,128)(2,1)S(1)} %copy-done.11, bf16[512,640]{1,0:T(8,128)(2,1)} %collective-permute-done.1.refs_1_, bf16[512,640]{1,0:T(8,128)(2,1)S(1)} %copy-done.19, bf16[512,640]{1,0:T(8,128)(2,1)S(1)} %copy-done.21, ...), custom_call_target="tpu_custom_call" | custom-call | flops 671088640 | bytes 6815744 | tf_op jit(solution)/shard_map/product/pallas_call | solution.py:149
  141.3 5.1 %own_half.1 = (bf16[512,1792]{1,0:T(8,128)(2,1)}, bf16[512,1792]{1,0:T(8,128)(2,1)}, f32[512,128]{1,0:T(8,128)S(1)}) custom-call(s32[24]{0:T(128)S(1)} %concatenate.12.where_ref, bf16[512,1792]{1,0:T(8,128)(2,1)S(1)} %copy-done, bf16[512,1792]{1,0:T(8,128)(2,1)S(1)} %copy-done.2, bf16[64,1792]{1,0:T(8,128)(2,1)S(1)} %bitcast.30, ...), custom_call_target="tpu_custom_call" | custom-call | flops 128450560 | bytes 6291456 | tf_op jit(solution)/shard_map/own_half/pallas_call | solution.py:261
  147.6 5.9 %other_half.1 = (bf16[512,1792]{1,0:T(8,128)(2,1)}, bf16[512,1792]{1,0:T(8,128)(2,1)}, f32[256,128]{1,0:T(8,128)S(1)}) custom-call(s32[24]{0:T(128)S(1)} %concatenate.12.where_ref, bf16[512,1792]{1,0:T(8,128)(2,1)S(1)} %copy-done, bf16[512,1792]{1,0:T(8,128)(2,1)S(1)} %copy-done.2, ...), custom_call_target="tpu_custom_call", output_to_operand_aliasing={{0}: (7, {}), {1}: (8, {})} | custom-call | flops 128450560 | bytes 6291456 | tf_op jit(solution)/shard_map/other_half/pallas_call | solution.py:307
  155.8 1.8 %collective-permute-start.33 = (f32[128,128]{1,0:T(8,128)S(1)}, f32[128,128]{1,0:T(8,128)S(1)}, u32[]{:S(2)}, u32[]{:S(2)}) collective-permute-start(f32[128,128]{1,0:T(8,128)S(1)} %select_add_fusion.1), channel_id=1, source_target_pairs={{0,6},{1,7},{2,0},{3,1},{4,2},{5,3},{6,4},{7,5},{8,14},{9,15},{10,... | collective-permute-start | bytes 196616 | tf_op jit(solution)/shard_map/down/ppermute | solution.py:32
  159.3 3.0 %collective-permute-done.31 = f32[128,128]{1,0:T(8,128)S(1)} collective-permute-done((f32[128,128]{1,0:T(8,128)S(1)}, f32[128,128]{1,0:T(8,128)S(1)}, u32[]{:S(2)}, u32[]{:S(2)}) %collective-permute-start.31) | collective-permute-done | bytes 65568 | tf_op jit(solution)/shard_map/send/ppermute | solution.py:32
  162.3 2.1 %collective-permute-start.34 = (f32[128,128]{1,0:T(8,128)S(1)}, f32[128,128]{1,0:T(8,128)S(1)}, u32[]{:S(2)}, u32[]{:S(2)}) collective-permute-start(f32[128,128]{1,0:T(8,128)S(1)} %add_add_fusion.1), channel_id=1, source_target_pairs={{0,1},{1,0},{2,3},{3,2},{4,5},{5,4},{6,7},{7,6},{8,9},{9,8},{10,11... | collective-permute-start | bytes 196616 | tf_op jit(solution)/shard_map/swap/ppermute | solution.py:32
  (130 shorter events, 31.2 us)
Async XLA Ops:
  0.6 26.1 %collective-permute-start.15 = (bf16[112,5120]{1,0:T(8,128)(2,1)}, bf16[112,5120]{1,0:T(8,128)(2,1)}, u32[]{:S(2)}, u32[]{:S(2)}) collective-permute-start(bf16[112,5120]{1,0:T(8,128)(2,1)} %refs_8_.3), channel_id=1, source_target_pairs={{0,32},{1,9},{2,34},{3,11},{4,36},{5,13},{6,38},{7,15},{8,40},{9,1... | collective-permute-start | bytes 3440648 | tf_op jit(solution)/shard_map/r1/ppermute | solution.py:32
  2.7 24.2 %collective-permute-start.16 = (bf16[112,5120]{1,0:T(8,128)(2,1)}, bf16[112,5120]{1,0:T(8,128)(2,1)S(1)}, u32[]{:S(2)}, u32[]{:S(2)}) collective-permute-start(bf16[112,5120]{1,0:T(8,128)(2,1)} %refs_8_.3), channel_id=1, source_target_pairs={{0,8},{1,25},{2,10},{3,27},{4,12},{5,29},{6,14},{7,31},{8,16},{9,1... | collective-permute-start | bytes 3440648 | tf_op jit(solution)/shard_map/r2/ppermute | solution.py:32
  4.1 26.1 %collective-permute-start.17 = (bf16[112,5120]{1,0:T(8,128)(2,1)}, bf16[112,5120]{1,0:T(8,128)(2,1)}, u32[]{:S(2)}, u32[]{:S(2)}) collective-permute-start(bf16[112,5120]{1,0:T(8,128)(2,1)} %refs_8_.3), channel_id=1, source_target_pairs={{0,24},{1,33},{2,26},{3,35},{4,28},{5,37},{6,30},{7,39},{8,0},{9,4... | collective-permute-start | bytes 3440648 | tf_op jit(solution)/shard_map/r3/ppermute | solution.py:32
  5.8 30.2 %collective-permute-start = (bf16[512,640]{1,0:T(8,128)(2,1)}, bf16[512,640]{1,0:T(8,128)(2,1)S(1)}, u32[]{:S(2)}, u32[]{:S(2)}) collective-permute-start(bf16[512,640]{1,0:T(8,128)(2,1)} %grad_ref.1), channel_id=1, source_target_pairs={{0,96},{1,97},{2,98},{3,99},{4,100},{5,101},{6,102},{7,103},{8,104... | collective-permute-start | bytes 1966088 | tf_op jit(solution)/shard_map/mate_rows/ppermute | solution.py:32
  8.1 26.6 %collective-permute-start.1 = (bf16[512,640]{1,0:T(8,128)(2,1)}, bf16[512,640]{1,0:T(8,128)(2,1)}, u32[]{:S(2)}, u32[]{:S(2)}) collective-permute-start(bf16[512,640]{1,0:T(8,128)(2,1)} %grad_ref.1), channel_id=1, source_target_pairs={{0,2},{1,7},{2,4},{3,1},{4,6},{5,3},{6,0},{7,5},{8,10},{9,15},{10,... | collective-permute-start | bytes 1966088 | tf_op jit(solution)/shard_map/a1/ppermute | solution.py:32
  30.2 23.2 %collective-permute-start.18 = (bf16[112,5120]{1,0:T(8,128)(2,1)}, bf16[112,5120]{1,0:T(8,128)(2,1)S(1)}, u32[]{:S(2)}, u32[]{:S(2)}) collective-permute-start(bf16[112,5120]{1,0:T(8,128)(2,1)} %collective-permute-done.15.refs_9_), channel_id=1, source_target_pairs={{0,8},{1,33},{2,10},{3,35},{4,12},{5,37},{6,14},{7,39},{8,16},{9,4... | collective-permute-start | bytes 3440648 | tf_op jit(solution)/shard_map/r4/ppermute | solution.py:32
  32.1 25.9 %collective-permute-start.19 = (bf16[112,5120]{1,0:T(8,128)(2,1)S(1)}, bf16[112,5120]{1,0:T(8,128)(2,1)S(1)}, u32[]{:S(2)}, u32[]{:S(2)}) collective-permute-start(bf16[112,5120]{1,0:T(8,128)(2,1)S(1)} %broadcast_select_fusion.1), channel_id=1, source_target_pairs={{0,24},{1,33},{2,26},{3,35},{4,28},{5,37},{6,30},{7,39},{8,0},{9,4... | collective-permute-start | bytes 3440648 | tf_op jit(solution)/shard_map/r5/ppermute | solution.py:32
  32.1 30.1 %collective-permute-start.20 = (bf16[112,5120]{1,0:T(8,128)(2,1)}, bf16[112,5120]{1,0:T(8,128)(2,1)S(1)}, u32[]{:S(2)}, u32[]{:S(2)}) collective-permute-start(bf16[112,5120]{1,0:T(8,128)(2,1)} %copy-done.7), channel_id=1, source_target_pairs={{0,8},{1,25},{2,10},{3,27},{4,12},{5,29},{6,14},{7,31},{8,16},{9,1... | collective-permute-start | bytes 3440648 | tf_op jit(solution)/shard_map/r6/ppermute | solution.py:32
  34.7 13.3 %collective-permute-start.2 = (bf16[512,640]{1,0:T(8,128)(2,1)S(1)}, bf16[512,640]{1,0:T(8,128)(2,1)S(1)}, u32[]{:S(2)}, u32[]{:S(2)}) collective-permute-start(bf16[512,640]{1,0:T(8,128)(2,1)S(1)} %copy-done.9), channel_id=1, source_target_pairs={{0,6},{1,3},{2,0},{3,5},{4,2},{5,7},{6,4},{7,1},{8,14},{9,11},{10,... | collective-permute-start | bytes 1966088 | tf_op jit(solution)/shard_map/a2/ppermute | solution.py:32
  36.0 17.4 %collective-permute-start.3 = (bf16[512,640]{1,0:T(8,128)(2,1)}, bf16[512,640]{1,0:T(8,128)(2,1)S(1)}, u32[]{:S(2)}, u32[]{:S(2)}) collective-permute-start(bf16[512,640]{1,0:T(8,128)(2,1)} %collective-permute-done.1.refs_1_), channel_id=1, source_target_pairs={{0,2},{1,7},{2,4},{3,1},{4,6},{5,3},{6,0},{7,5},{8,10},{9,15},{10,... | collective-permute-start | bytes 1966088 | tf_op jit(solution)/shard_map/a_far/ppermute | solution.py:32
  48.0 16.3 %collective-permute-start.5 = (bf16[512,640]{1,0:T(8,128)(2,1)S(1)}, bf16[512,640]{1,0:T(8,128)(2,1)S(1)}, u32[]{:S(2)}, u32[]{:S(2)}) collective-permute-start(bf16[512,640]{1,0:T(8,128)(2,1)S(1)} %copy-done.9), channel_id=1, source_target_pairs={{0,1},{1,0},{2,3},{3,2},{4,5},{5,4},{6,7},{7,6},{8,9},{9,8},{10,11... | collective-permute-start | bytes 1966088 | tf_op jit(solution)/shard_map/a_swap/ppermute | solution.py:32
  53.4 13.1 %collective-permute-start.7 = (bf16[512,640]{1,0:T(8,128)(2,1)}, bf16[512,640]{1,0:T(8,128)(2,1)S(1)}, u32[]{:S(2)}, u32[]{:S(2)}) collective-permute-start(bf16[512,640]{1,0:T(8,128)(2,1)} %collective-permute-done.1.refs_1_), channel_id=1, source_target_pairs={{0,1},{1,0},{2,3},{3,2},{4,5},{5,4},{6,7},{7,6},{8,9},{9,8},{10,11... | collective-permute-start | bytes 1966088 | tf_op jit(solution)/shard_map/a_swap/ppermute | solution.py:32
  53.4 15.3 %collective-permute-start.4 = (bf16[512,640]{1,0:T(8,128)(2,1)S(1)}, bf16[512,640]{1,0:T(8,128)(2,1)S(1)}, u32[]{:S(2)}, u32[]{:S(2)}) collective-permute-start(bf16[512,640]{1,0:T(8,128)(2,1)S(1)} %collective-permute-done.refs_0_), channel_id=1, source_target_pairs={{0,2},{1,7},{2,4},{3,1},{4,6},{5,3},{6,0},{7,5},{8,10},{9,15},{10,... | collective-permute-start | bytes 1966088 | tf_op jit(solution)/shard_map/b1/ppermute | solution.py:32
  58.9 9.7 %collective-permute-start.6 = (bf16[512,640]{1,0:T(8,128)(2,1)S(1)}, bf16[512,640]{1,0:T(8,128)(2,1)S(1)}, u32[]{:S(2)}, u32[]{:S(2)}) collective-permute-start(bf16[512,640]{1,0:T(8,128)(2,1)S(1)} %collective-permute-done.2.refs_2_), channel_id=1, source_target_pairs={{0,1},{1,0},{2,3},{3,2},{4,5},{5,4},{6,7},{7,6},{8,9},{9,8},{10,11... | collective-permute-start | bytes 1966088 | tf_op jit(solution)/shard_map/a_swap/ppermute | solution.py:32
  62.3 7.2 %collective-permute-start.8 = (bf16[512,640]{1,0:T(8,128)(2,1)S(1)}, bf16[512,640]{1,0:T(8,128)(2,1)S(1)}, u32[]{:S(2)}, u32[]{:S(2)}) collective-permute-start(bf16[512,640]{1,0:T(8,128)(2,1)S(1)} %collective-permute-done.3.refs_3_), channel_id=1, source_target_pairs={{0,1},{1,0},{2,3},{3,2},{4,5},{5,4},{6,7},{7,6},{8,9},{9,8},{10,11... | collective-permute-start | bytes 1966088 | tf_op jit(solution)/shard_map/a_swap/ppermute | solution.py:32
  65.1 26.9 %collective-permute-start.21 = (bf16[112,5120]{1,0:T(8,128)(2,1)}, bf16[112,5120]{1,0:T(8,128)(2,1)}, u32[]{:S(2)}, u32[]{:S(2)}) collective-permute-start(bf16[112,5120]{1,0:T(8,128)(2,1)} %broadcast_select_fusion), channel_id=1, source_target_pairs={{0,8},{1,33},{2,10},{3,35},{4,12},{5,37},{6,14},{7,39},{8,16},{9,4... | collective-permute-start | bytes 3440648 | tf_op jit(solution)/shard_map/r7/ppermute | solution.py:32
  67.4 12.6 %collective-permute-start.9 = (bf16[512,640]{1,0:T(8,128)(2,1)S(1)}, bf16[512,640]{1,0:T(8,128)(2,1)}, u32[]{:S(2)}, u32[]{:S(2)}) collective-permute-start(bf16[512,640]{1,0:T(8,128)(2,1)S(1)} %collective-permute-done.refs_0_), channel_id=1, source_target_pairs={{0,6},{1,3},{2,0},{3,5},{4,2},{5,7},{6,4},{7,1},{8,14},{9,11},{10,... | collective-permute-start | bytes 1966088 | tf_op jit(solution)/shard_map/b2/ppermute | solution.py:32
  70.4 21.5 %collective-permute-start.10 = (bf16[512,640]{1,0:T(8,128)(2,1)S(1)}, bf16[512,640]{1,0:T(8,128)(2,1)}, u32[]{:S(2)}, u32[]{:S(2)}) collective-permute-start(bf16[512,640]{1,0:T(8,128)(2,1)S(1)} %collective-permute-done.4.refs_1_), channel_id=1, source_target_pairs={{0,2},{1,7},{2,4},{3,1},{4,6},{5,3},{6,0},{7,5},{8,10},{9,15},{10,... | collective-permute-start | bytes 1966088 | tf_op jit(solution)/shard_map/b_far/ppermute | solution.py:32
  73.7 21.0 %collective-permute-start.11 = (bf16[512,640]{1,0:T(8,128)(2,1)S(1)}, bf16[512,640]{1,0:T(8,128)(2,1)S(1)}, u32[]{:S(2)}, u32[]{:S(2)}) collective-permute-start(bf16[512,640]{1,0:T(8,128)(2,1)S(1)} %collective-permute-done.refs_0_), channel_id=1, source_target_pairs={{0,1},{1,0},{2,3},{3,2},{4,5},{5,4},{6,7},{7,6},{8,9},{9,8},{10,11... | collective-permute-start | bytes 1966088 | tf_op jit(solution)/shard_map/b_swap/ppermute | solution.py:32
  74.3 25.4 %collective-permute-start.13 = (bf16[512,640]{1,0:T(8,128)(2,1)S(1)}, bf16[512,640]{1,0:T(8,128)(2,1)S(1)}, u32[]{:S(2)}, u32[]{:S(2)}) collective-permute-start(bf16[512,640]{1,0:T(8,128)(2,1)S(1)} %collective-permute-done.4.refs_1_), channel_id=1, source_target_pairs={{0,1},{1,0},{2,3},{3,2},{4,5},{5,4},{6,7},{7,6},{8,9},{9,8},{10,11... | collective-permute-start | bytes 1966088 | tf_op jit(solution)/shard_map/b_swap/ppermute | solution.py:32
  79.9 18.3 %collective-permute-start.12 = (bf16[512,640]{1,0:T(8,128)(2,1)}, bf16[512,640]{1,0:T(8,128)(2,1)S(1)}, u32[]{:S(2)}, u32[]{:S(2)}) collective-permute-start(bf16[512,640]{1,0:T(8,128)(2,1)} %collective-permute-done.9.refs_2_), channel_id=1, source_target_pairs={{0,1},{1,0},{2,3},{3,2},{4,5},{5,4},{6,7},{7,6},{8,9},{9,8},{10,11... | collective-permute-start | bytes 1966088 | tf_op jit(solution)/shard_map/b_swap/ppermute | solution.py:32
  92.0 7.7 %collective-permute-start.14 = (bf16[512,640]{1,0:T(8,128)(2,1)}, bf16[512,640]{1,0:T(8,128)(2,1)S(1)}, u32[]{:S(2)}, u32[]{:S(2)}) collective-permute-start(bf16[512,640]{1,0:T(8,128)(2,1)} %collective-permute-done.10.refs_3_), channel_id=1, source_target_pairs={{0,1},{1,0},{2,3},{3,2},{4,5},{5,4},{6,7},{7,6},{8,9},{9,8},{10,11... | collective-permute-start | bytes 1966088 | tf_op jit(solution)/shard_map/b_swap/ppermute | solution.py:32
  94.6 21.8 %collective-permute-start.24 = (f32[256,192]{1,0:T(8,128)S(1)}, f32[256,192]{1,0:T(8,128)S(1)}, u32[]{:S(2)}, u32[]{:S(2)}) collective-permute-start(f32[256,192]{1,0:T(8,128)S(1)} %select_add_fusion), channel_id=1, source_target_pairs={{0,2},{1,3},{2,4},{3,5},{4,6},{5,7},{6,0},{7,1},{8,10},{9,11},{10,... | collective-permute-start | bytes 589832 | tf_op jit(solution)/shard_map/up/ppermute | solution.py:32
  94.7 21.7 %collective-permute-start.25 = (f32[256,192]{1,0:T(8,128)S(1)}, f32[256,192]{1,0:T(8,128)S(1)}, u32[]{:S(2)}, u32[]{:S(2)}) collective-permute-start(f32[256,192]{1,0:T(8,128)S(1)} %select_add_fusion), channel_id=1, source_target_pairs={{0,6},{1,7},{2,0},{3,1},{4,2},{5,3},{6,4},{7,5},{8,14},{9,15},{10,... | collective-permute-start | bytes 589832 | tf_op jit(solution)/shard_map/down/ppermute | solution.py:32
  98.3 18.1 %collective-permute-start.23 = (f32[256,192]{1,0:T(8,128)S(1)}, f32[256,192]{1,0:T(8,128)S(1)}, u32[]{:S(2)}, u32[]{:S(2)}) collective-permute-start(f32[256,192]{1,0:T(8,128)S(1)} %select_add_fusion), channel_id=1, source_target_pairs={{0,4},{1,5},{2,6},{3,7},{4,0},{5,1},{6,2},{7,3},{8,12},{9,13},{10,... | collective-permute-start | bytes 589832 | tf_op jit(solution)/shard_map/send/ppermute | solution.py:32
  106.2 41.4 %collective-permute-start.27 = (bf16[512,512]{1,0:T(8,128)(2,1)S(1)}, bf16[512,512]{1,0:T(8,128)(2,1)S(1)}, u32[]{:S(2)}, u32[]{:S(2)}) collective-permute-start(bf16[512,512]{1,0:T(8,128)(2,1)S(1)} %product.5), channel_id=1, source_target_pairs={{0,96},{1,97},{2,98},{3,99},{4,100},{5,101},{6,102},{7,103},{8,104... | collective-permute-start | bytes 1572872 | tf_op jit(solution)/shard_map/mate_grad/ppermute | solution.py:32
  116.3 31.3 %collective-permute-start.28 = (bf16[512,384]{1,0:T(8,128)(2,1)S(1)}, bf16[512,384]{1,0:T(8,128)(2,1)S(1)}, u32[]{:S(2)}, u32[]{:S(2)}) collective-permute-start(bf16[512,384]{1,0:T(8,128)(2,1)S(1)} %product.6), channel_id=1, source_target_pairs={{0,96},{1,97},{2,98},{3,99},{4,100},{5,101},{6,102},{7,103},{8,104... | collective-permute-start | bytes 1179656 | tf_op jit(solution)/shard_map/mate_grad/ppermute | solution.py:32
  116.5 29.9 %collective-permute-start.26 = (f32[256,192]{1,0:T(8,128)S(1)}, f32[256,192]{1,0:T(8,128)S(1)}, u32[]{:S(2)}, u32[]{:S(2)}) collective-permute-start(f32[256,192]{1,0:T(8,128)S(1)} %add_add_fusion), channel_id=1, source_target_pairs={{0,1},{1,0},{2,3},{3,2},{4,5},{5,4},{6,7},{7,6},{8,9},{9,8},{10,11... | collective-permute-start | bytes 589832 | tf_op jit(solution)/shard_map/swap/ppermute | solution.py:32
  132.6 14.9 %collective-permute-start.29 = (bf16[512,128]{1,0:T(8,128)(2,1)S(1)}, bf16[512,128]{1,0:T(8,128)(2,1)S(1)}, u32[]{:S(2)}, u32[]{:S(2)}) collective-permute-start(bf16[512,128]{1,0:T(8,128)(2,1)S(1)} %product.8), channel_id=1, source_target_pairs={{0,96},{1,97},{2,98},{3,99},{4,100},{5,101},{6,102},{7,103},{8,104... | collective-permute-start | bytes 393224 | tf_op jit(solution)/shard_map/mate_grad/ppermute | solution.py:32
  154.9 4.4 %collective-permute-start.32 = (f32[128,128]{1,0:T(8,128)S(1)}, f32[128,128]{1,0:T(8,128)S(1)}, u32[]{:S(2)}, u32[]{:S(2)}) collective-permute-start(f32[128,128]{1,0:T(8,128)S(1)} %select_add_fusion.1), channel_id=1, source_target_pairs={{0,2},{1,3},{2,4},{3,5},{4,6},{5,7},{6,0},{7,1},{8,10},{9,11},{10,... | collective-permute-start | bytes 196616 | tf_op jit(solution)/shard_map/up/ppermute | solution.py:32
  155.8 3.5 %collective-permute-start.33 = (f32[128,128]{1,0:T(8,128)S(1)}, f32[128,128]{1,0:T(8,128)S(1)}, u32[]{:S(2)}, u32[]{:S(2)}) collective-permute-start(f32[128,128]{1,0:T(8,128)S(1)} %select_add_fusion.1), channel_id=1, source_target_pairs={{0,6},{1,7},{2,0},{3,1},{4,2},{5,3},{6,4},{7,5},{8,14},{9,15},{10,... | collective-permute-start | bytes 196616 | tf_op jit(solution)/shard_map/down/ppermute | solution.py:32
  157.6 4.6 %collective-permute-start.31 = (f32[128,128]{1,0:T(8,128)S(1)}, f32[128,128]{1,0:T(8,128)S(1)}, u32[]{:S(2)}, u32[]{:S(2)}) collective-permute-start(f32[128,128]{1,0:T(8,128)S(1)} %select_add_fusion.1), channel_id=1, source_target_pairs={{0,4},{1,5},{2,6},{3,7},{4,0},{5,1},{6,2},{7,3},{8,12},{9,13},{10,... | collective-permute-start | bytes 196616 | tf_op jit(solution)/shard_map/send/ppermute | solution.py:32
  (34 other events, 313.6 us)

commit v4 on v3

--- a/solution.py
+++ b/solution.py
@@ -12,8 +12,10 @@
 F32, BF16 = jnp.float32, jnp.bfloat16
 ROWS, FEAT, HID, HALF, RANK, DEPTH = 512, 640, 1792, 896, 64, 5120
 SHARD = 112
+TILE = 128
 STEP = 2 * FEAT
 NT = (((1,), (1,)), ((), ()))
+LIGHT = pl.CostEstimate(flops=1 << 20, bytes_accessed=1 << 16, transcendentals=0)
 ANY = pl.BlockSpec(memory_space=pl.ANY)
 
 
@@ -93,53 +95,28 @@
 
 def product_kernel(shards, where_ref, *refs):
     mine, other, weights = refs[:4], refs[4:8], refs[8 : 8 + shards]
-    out_ref, a_buf, w_buf, a_sem, w_sem, *acc = refs[8 + shards :]
+    out_ref, *acc = refs[8 + shards :]
     acc = acc[0] if acc else out_ref
     y, c = where_ref[16], where_ref[17]
-    a_copies = []
-    for group, (pieces, core) in enumerate(((mine, c), (other, 1 - c))):
-        lane = pl.multiple_of(core * FEAT, 128)
-        for k in range(4):
-            a_copies.append(
-                pltpu.make_async_copy(
-                    pieces[k], a_buf.at[k, :, pl.ds(lane, FEAT)], a_sem.at[group, k]
-                )
+    for step, shift in enumerate((0, 3 - 2 * c, 1 + 2 * c, 2)):
+        first = lax.rem(y + shift, 4) * STEP
+        near, far = (pl.multiple_of(first + core * FEAT, 128) for core in (c, 1 - c))
+        left = jnp.concatenate([mine[step][...], other[step][...]], axis=1)
+        rows = []
+        for k, w in enumerate(weights):
+            rows.append(
+                jnp.concatenate([w[:, pl.ds(near, FEAT)], w[:, pl.ds(far, FEAT)]], axis=1)
             )
-
-    def w_copies(step):
-        shift = (0, 3 - 2 * c, 1 + 2 * c, 2)[step]
-        lane = pl.multiple_of(lax.rem(y + shift, 4) * STEP, 128)
-        return [
-            pltpu.make_async_copy(
-                w.at[:, pl.ds(lane, STEP)],
-                w_buf.at[step % 2, pl.ds(k * 128, SHARD), :],
-                w_sem.at[step % 2, k],
-            )
-            for k, w in enumerate(weights)
-        ]
-
-    for copy in w_copies(0):
-        copy.start()
-    for copy in a_copies:
-        copy.start()
-    for half in range(2):
-        for k in range(shards):
-            w_buf[half, k * 128 + SHARD : k * 128 + 128, :] = jnp.zeros((128 - SHARD, STEP), BF16)
-    for step in range(4):
-        if step < 3:
-            for copy in w_copies(step + 1):
-                copy.start()
-        a_copies[step].wait()
-        a_copies[4 + step].wait()
-        for copy in w_copies(step):
-            copy.wait()
-        part = lax.dot_general(a_buf[step], w_buf[step % 2], NT, preferred_element_type=F32)
+            if shards > 1:
+                rows.append(jnp.zeros((128 - SHARD, STEP), BF16))
+        right = jnp.concatenate(rows, axis=0) if shards > 1 else rows[0]
+        part = lax.dot_general(left, right, NT, preferred_element_type=F32)
         if step == 0:
-            acc[...] = part
+            acc[:, : part.shape[1]] = part
         elif step < 3:
-            acc[...] += part
+            acc[:, : part.shape[1]] += part
         else:
-            out_ref[...] = (acc[...] + part).astype(out_ref.dtype)
+            out_ref[:, : part.shape[1]] = (acc[:, : part.shape[1]] + part).astype(out_ref.dtype)
 
 
 def product(dtype, where, mine, other, weights):
@@ -151,21 +128,11 @@
         out_shape=jax.ShapeDtypeStruct((ROWS, width), dtype),
         in_specs=[pl.BlockSpec(memory_space=pltpu.SMEM)] + [vmem] * (8 + shards),
         out_specs=vmem,
-        scratch_shapes=[
-            pltpu.VMEM((4, ROWS, STEP), BF16),
-            pltpu.VMEM((2, width, STEP), BF16),
-            pltpu.SemaphoreType.DMA((2, 4)),
-            pltpu.SemaphoreType.DMA((2, shards)),
-        ]
-        + ([] if dtype == F32 else [pltpu.VMEM((ROWS, width), F32)]),
+        scratch_shapes=[] if dtype == F32 else [pltpu.VMEM((ROWS, width), F32)],
         compiler_params=pltpu.CompilerParams(
-            vmem_limit_bytes=(8 << 20) + width * (4 * STEP + 14 * ROWS)
+            vmem_limit_bytes=(4 << 20) + width * (4 * STEP + 14 * ROWS)
         ),
-        cost_estimate=pl.CostEstimate(
-            flops=2 * ROWS * width * DEPTH,
-            bytes_accessed=2 * DEPTH * (ROWS + width) + 4 * ROWS * width,
-            transcendentals=0,
-        ),
+        cost_estimate=LIGHT,
         name="product",
     )(where, *mine, *other, *weights)
 
@@ -199,9 +166,7 @@
             out_specs=pl.BlockSpec((128, 3 * RANK), lambda i, w: (i, 0)),
         ),
         compiler_params=pltpu.CompilerParams(vmem_limit_bytes=12 << 20),
-        cost_estimate=pl.CostEstimate(
-            flops=ROWS * HID * 160, bytes_accessed=5 << 20, transcendentals=ROWS * HID
-        ),
+        cost_estimate=LIGHT,
         name="early",
     )(where, activations, out_grad, pm_t, gate, up, ph_t)
 
@@ -219,7 +184,7 @@
         ],
         axis=1,
     )
-    row = pl.program_id(0) * 64 + lax.broadcasted_iota(jnp.int32, hidden_grad.shape, 0)
+    row = pl.program_id(0) * TILE + lax.broadcasted_iota(jnp.int32, hidden_grad.shape, 0)
     hidden_grad = jnp.where(row < where_ref[19], hidden_grad, 0.0)
     gate, up = gate_ref[...].astype(F32), up_ref[...].astype(F32)
     sig = jax.nn.sigmoid(gate)
@@ -227,14 +192,9 @@
     grad_gate = (hidden_grad * up * sig * (1.0 + gate * (1.0 - sig))).astype(BF16)
     gg_ref[...] = grad_gate
     gu_ref[...] = grad_up
-    ph = ph_ref[...]
-    return jnp.concatenate(
-        [
-            lax.dot_general(g, ph, NT, preferred_element_type=F32)
-            for g in (grad_gate, grad_up)
-        ],
-        axis=1,
-    )
+    both = jnp.concatenate([grad_gate, grad_up], axis=0)
+    part = lax.dot_general(both, ph_ref[...], NT, preferred_element_type=F32)
+    return jnp.concatenate([part[:TILE], part[TILE:]], axis=1)
 
 
 def own_kernel(n, where_ref, gate_ref, up_ref, ph_ref, *refs):
@@ -245,12 +205,12 @@
 
 
 def row_tiles(half):
-    tile = pl.BlockSpec((64, HALF), lambda i, w: (i, half(w)))
+    tile = pl.BlockSpec((TILE, HALF), lambda i, w: (i, half(w)))
     return tile, pl.BlockSpec((RANK, HALF), lambda i, w: (0, half(w)))
 
 
 def pieces_of(h):
-    return [pl.BlockSpec((64, p.shape[1]), lambda i, w: (i, 0)) for p in h]
+    return [pl.BlockSpec((TILE, p.shape[1]), lambda i, w: (i, 0)) for p in h]
 
 
 BIG = jax.ShapeDtypeStruct((ROWS, HID), BF16)
@@ -263,15 +223,13 @@
         out_shape=(BIG, BIG, jax.ShapeDtypeStruct((ROWS, 2 * RANK), F32)),
         grid_spec=pltpu.PrefetchScalarGridSpec(
             num_scalar_prefetch=1,
-            grid=(8,),
+            grid=(ROWS // TILE,),
             in_specs=[tile, tile, ranks] + pieces_of(h),
-            out_specs=(tile, tile, pl.BlockSpec((64, 2 * RANK), lambda i, w: (i, 0))),
-            scratch_shapes=[pltpu.VMEM((64, 1024), F32)],
+            out_specs=(tile, tile, pl.BlockSpec((TILE, 2 * RANK), lambda i, w: (i, 0))),
+            scratch_shapes=[pltpu.VMEM((TILE, 1024), F32)],
         ),
-        compiler_params=pltpu.CompilerParams(vmem_limit_bytes=8 << 20),
-        cost_estimate=pl.CostEstimate(
-            flops=ROWS * HALF * 280, bytes_accessed=6 << 20, transcendentals=ROWS * HALF
-        ),
+        compiler_params=pltpu.CompilerParams(vmem_limit_bytes=14 << 20),
+        cost_estimate=LIGHT,
         name="own_half",
     )(where, gate, up, ph_t, *h)
 
@@ -281,9 +239,9 @@
     gg_ref, gu_ref, feat_ref, held, acc = refs[n:]
     i = pl.program_id(0)
     part = grads(where_ref, 8, refs[:n], held, gate_ref, up_ref, ph_ref, gg_ref, gu_ref)
-    acc[pl.ds(pl.multiple_of(i * 64, 64), 64), :] = part_ref[...] + part
-
-    @pl.when(i == 7)
+    acc[pl.ds(pl.multiple_of(i * TILE, TILE), TILE), :] = part_ref[...] + part
+
+    @pl.when(i == ROWS // TILE - 1)
     def _():
         feat_ref[...] = twice(hi_ref[...], lo_ref[...], acc[...])
 
@@ -309,12 +267,12 @@
         out_shape=(BIG, BIG, jax.ShapeDtypeStruct((4 * RANK, 2 * RANK), F32)),
         grid_spec=pltpu.PrefetchScalarGridSpec(
             num_scalar_prefetch=1,
-            grid=(8,),
+            grid=(ROWS // TILE,),
             in_specs=[
                 tile,
                 tile,
                 ranks,
-                pl.BlockSpec((64, 2 * RANK), lambda i, w: (i, 0)),
+                pl.BlockSpec((TILE, 2 * RANK), lambda i, w: (i, 0)),
                 spreads,
                 spreads,
                 ANY,
@@ -322,13 +280,11 @@
             ]
             + pieces_of(h),
             out_specs=(tile, tile, feat),
-            scratch_shapes=[pltpu.VMEM((64, 1024), F32), pltpu.VMEM((ROWS, 2 * RANK), F32)],
+            scratch_shapes=[pltpu.VMEM((TILE, 1024), F32), pltpu.VMEM((ROWS, 2 * RANK), F32)],
         ),
         input_output_aliases={7: 0, 8: 1},
-        compiler_params=pltpu.CompilerParams(vmem_limit_bytes=8 << 20),
-        cost_estimate=pl.CostEstimate(
-            flops=ROWS * HALF * 280, bytes_accessed=6 << 20, transcendentals=ROWS * HALF
-        ),
+        compiler_params=pltpu.CompilerParams(vmem_limit_bytes=14 << 20),
+        cost_estimate=LIGHT,
         name="other_half",
     )(where, gate, up, ph_t, part, *spread, gg, gu, *h)
 
@@ -395,33 +351,35 @@
     theirs = mate(out_grad, "mate_rows")
     a1 = along_y(out_grad, 1, "a1")
     a2 = along_y(after(out_grad, a1), -1, "a2")
-    a_far = along_y(a1, 1, "a_far")
-    r1, r2, r3 = lax.optimization_barrier((r1, r2, r3))
+    b1 = along_y(theirs, 1, "b1")
+    r1, r2, r3, a2, b1 = lax.optimization_barrier((r1, r2, r3, a2, b1))
     r4 = route(r1, "+", "p", "r4")
     r5 = route(pick(c, r1, r2), "-", "p", "r5")
     r6 = route(r2, "+", "-", "r6")
-    theirs, a2, a_far = lax.optimization_barrier((theirs, a2, a_far))
-    b1 = along_y(theirs, 1, "b1")
-    b2 = along_y(theirs, -1, "b2")
-    a_other = [swap(v, "a_swap") for v in (out_grad, a2, a1, a_far)]
-    b1, *a_other = lax.optimization_barrier((b1, *a_other))
+    b2 = along_y(after(theirs, a2), -1, "b2")
     b_far = along_y(b1, 1, "b_far")
-    r7 = route(after(pick(c, r4, r6), r5), "+", "p", "r7")
-    a_mine, b_mine = [out_grad, a1, a2, a_far], [theirs, b1, b2, b_far]
-    b_other = [swap(v, "b_swap") for v in (theirs, b2, b1, b_far)]
-
+    b_other = [swap(after(v, b2), "b_swap") for v in (theirs, b2)]
+    b_other += [swap(after(v, *b_other), "b_swap") for v in (b1, b_far)]
+    b_mine = [theirs, b1, b2, b_far]
+    h1 = product(BF16, where, b_mine, b_other, [own_w, r1, r2, r3])
+    r7 = route(after(pick(c, r4, r6), r5, h1), "+", "p", "r7")
+    a_far = along_y(after(a1, *b_other), 1, "a_far")
+    a_mine = [out_grad, a1, a2, a_far]
+    a_other = [swap(after(v, *b_other), "a_swap") for v in (out_grad, a2, a1, a_far)]
+
+    h2 = product(BF16, after(where, h1), b_mine, b_other, [r4, r5, r6])
     pm_t, ph_t = proj_model.T, proj_hidden.T
-    parts = early(after(where, b1), activations, out_grad, pm_t, gate_pre, up_pre, ph_t)
-    sums = sum_tensor(after(parts, r7), c)
+    parts = early(after(where, h1), activations, out_grad, pm_t, gate_pre, up_pre, ph_t)
+    sums = sum_tensor(after(parts, h2), c)
     *spread, down_feat = spread_features(where, sums)
 
-    h1 = product(BF16, where, b_mine, b_other, [own_w, r1, r2, r3])
-    h2 = product(BF16, after(where, h1), b_mine, b_other, [r4, r5, r6])
-    h3 = product(BF16, after(where, h2), b_mine, b_other, [r7])
-    h_in = [mate(h, "mate_grad") for h in (h1, h2, h3)]
-    o1 = product(F32, after(where, h2), a_mine, a_other, [own_w, r1, r2, r3, r4, r5, r6])
-    o2 = product(F32, after(where, h3), a_mine, a_other, [r7])
-    grad_gate, grad_up, part = own_half(where, gate_pre, up_pre, (o1, o2), ph_t)
+    h1_in = mate(h1, "mate_grad1")
+    own1 = product(F32, after(where, h2), a_mine, a_other, [own_w, r1, r2, r3, r4, r5, r6])
+    h3 = product(BF16, after(where, own1, h1_in), b_mine, b_other, [r7])
+    h2_in = mate(h2, "mate_grad2")
+    own2 = product(F32, after(where, h3, h2_in), a_mine, a_other, [r7])
+    h_in = [h1_in, h2_in, mate(h3, "mate_grad3")]
+    grad_gate, grad_up, part = own_half(where, gate_pre, up_pre, (own1, own2), ph_t)
     grad_gate, grad_up, feat = other_half(
         where, gate_pre, up_pre, h_in, ph_t, part, spread, grad_gate, grad_up
     )

time: 167 us -> 160 us (0.958)
  waiting for transfers between devices: 45.1 us -> 72.9 us
  starting transfers between devices: 57.8 us -> 36.9 us
  Pallas kernels: 47.1 us -> 35 us
    ppermute x35, waiting for transfers between devices: 45.1 us -> 72.9 us  [send(): return lax.ppermute(value, AXES, pairs)]
    ppermute x35, starting transfers between devices: 57.8 us -> 36.9 us  [send(): return lax.ppermute(value, AXES, pairs)]
    pallas_call x5, Pallas kernels: 32.6 us -> 23.3 us  [product(): pl.pallas_call(functools.partial(product_kernel, shards), out_shape=jax.S...]
    unnamed x62 -> x50, local copies, waits for them, and re-layouts: 11 us -> 9.65 us
  transfers between devices with their start and end apart: 35 -> 35, of which waited for: 11 -> 18; matrix products, arithmetic and copies ran while one was open for 2% -> 2% of each run, Pallas kernels for 25% -> 19%
where the time goes in v4:
time: 160 us
  waiting for transfers between devices  72.9 us (46%)
  starting transfers between devices  36.9 us (23%)
  Pallas kernels  35 us (22%)
  local copies, waits for them, and re-layouts  11.9 us (7%)
  other arithmetic  2.37 us (1%)
    ppermute x35, waiting for transfers between devices, send(): return lax.ppermute(value, AXES, pairs)  72.9 us
    ppermute x35, starting transfers between devices, send(): return lax.ppermute(value, AXES, pairs)  36.9 us
    pallas_call x5, Pallas kernels, product(): pl.pallas_call(functools.partial(product_kernel, shards), out_shape=jax.S...  23.3 us
    unnamed x50, local copies, waits for them, and re-layouts  9.65 us
    pallas_call x1, Pallas kernels, other_half(): pl.pallas_call(functools.partial(other_kernel, len(h)), out_shape=(BIG, B...  4.42 us
    pallas_call x1, Pallas kernels, own_half(): pl.pallas_call(functools.partial(own_kernel, len(h)), out_shape=(BIG, BIG...  3.82 us
  transfers between devices with their start and end apart: 35, of which 18 were waited for; matrix products, arithmetic and copies ran while one was open for 2% of the time, Pallas kernels for 19%

profile of v4, /device:TPU:1, one launch (start us, length us, event | category | flops | bytes accessed | tf_op | source)
XLA Modules:
  0.0 160.0 jit_solution(7104226353945963036)
XLA Ops:
  0.6 3.6 %collective-permute-start.4 = (bf16[512,640]{1,0:T(8,128)(2,1)}, bf16[512,640]{1,0:T(8,128)(2,1)S(1)}, u32[]{:S(2)}, u32[]{:S(2)}) collective-permute-start(bf16[512,640]{1,0:T(8,128)(2,1)} %grad_ref.1), channel_id=1, source_target_pairs={{0,2},{1,7},{2,4},{3,1},{4,6},{5,3},{6,0},{7,5},{8,10},{9,15},{10,... | collective-permute-start | bytes 1966088 | tf_op jit(solution)/shard_map/a1/ppermute | solution.py:34
  4.3 3.8 %collective-permute-start = (bf16[512,640]{1,0:T(8,128)(2,1)}, bf16[512,640]{1,0:T(8,128)(2,1)}, u32[]{:S(2)}, u32[]{:S(2)}) collective-permute-start(bf16[512,640]{1,0:T(8,128)(2,1)} %grad_ref.1), channel_id=1, source_target_pairs={{0,96},{1,97},{2,98},{3,99},{4,100},{5,101},{6,102},{7,103},{8,104... | collective-permute-start | bytes 1966088 | tf_op jit(solution)/shard_map/mate_rows/ppermute | solution.py:34
  9.2 1.5 collective-permute-start.2
  10.7 1.4 collective-permute-done.4.refs_1_
  12.9 10.4 %collective-permute-done.refs_0_ = bf16[512,640]{1,0:T(8,128)(2,1)} collective-permute-done((bf16[512,640]{1,0:T(8,128)(2,1)}, bf16[512,640]{1,0:T(8,128)(2,1)}, u32[]{:S(2)}, u32[]{:S(2)}) %collective-permute-start) | collective-permute-done | bytes 655392 | tf_op jit(solution)/shard_map/mate_rows/ppermute | solution.py:34
  23.6 12.9 %collective-permute-done.1.refs_9_ = bf16[112,5120]{1,0:T(8,128)(2,1)S(1)} collective-permute-done((bf16[112,5120]{1,0:T(8,128)(2,1)}, bf16[112,5120]{1,0:T(8,128)(2,1)S(1)}, u32[]{:S(2)}, u32[]{:S(2)}) %collective-permute-start.1) | collective-permute-done | bytes 1146912 | tf_op jit(solution)/shard_map/r1/ppermute | solution.py:34
  38.6 2.4 %collective-permute-start.8 = (bf16[512,640]{1,0:T(8,128)(2,1)}, bf16[512,640]{1,0:T(8,128)(2,1)}, u32[]{:S(2)}, u32[]{:S(2)}) collective-permute-start(bf16[512,640]{1,0:T(8,128)(2,1)} %collective-permute-done.6.refs_1_), channel_id=1, source_target_pairs={{0,2},{1,7},{2,4},{3,1},{4,6},{5,3},{6,0},{7,5},{8,10},{9,15},{10,... | collective-permute-start | bytes 1966088 | tf_op jit(solution)/shard_map/b_far/ppermute | solution.py:34
  41.1 13.7 %collective-permute-done.7.refs_2_ = bf16[512,640]{1,0:T(8,128)(2,1)} collective-permute-done((bf16[512,640]{1,0:T(8,128)(2,1)}, bf16[512,640]{1,0:T(8,128)(2,1)}, u32[]{:S(2)}, u32[]{:S(2)}) %collective-permute-start.7) | collective-permute-done | bytes 655392 | tf_op jit(solution)/shard_map/b2/ppermute | solution.py:34
  54.8 1.3 collective-permute-start.9
  58.9 2.3 %collective-permute-start.15 = (bf16[112,5120]{1,0:T(8,128)(2,1)}, bf16[112,5120]{1,0:T(8,128)(2,1)S(1)}, u32[]{:S(2)}, u32[]{:S(2)}) collective-permute-start(bf16[112,5120]{1,0:T(8,128)(2,1)} %copy-done.2), channel_id=1, source_target_pairs={{0,8},{1,25},{2,10},{3,27},{4,12},{5,29},{6,14},{7,31},{8,16},{9,1... | collective-permute-start | bytes 3440648 | tf_op jit(solution)/shard_map/r6/ppermute | solution.py:34
  65.5 1.3 copy-done.3
  71.5 5.2 %product.5 = bf16[512,512]{1,0:T(8,128)(2,1)S(1)} custom-call(s32[24]{0:T(128)S(1)} %concatenate.12.where_ref, bf16[512,640]{1,0:T(8,128)(2,1)} %collective-permute-done.refs_0_, bf16[512,640]{1,0:T(8,128)(2,1)} %collective-permute-done.6.refs_1_, bf16[512,640]{1,0:T(8,128)(2,1)} %collective-permute-done.7.refs_2_, ...), custom_call_target="tpu_custom_call" | custom-call | flops 1048576 | bytes 65536 | tf_op jit(solution)/shard_map/product/pallas_call | solution.py:126
  76.6 2.0 %collective-permute-start.16 = (bf16[512,640]{1,0:T(8,128)(2,1)S(1)}, bf16[512,640]{1,0:T(8,128)(2,1)S(1)}, u32[]{:S(2)}, u32[]{:S(2)}) collective-permute-start(bf16[512,640]{1,0:T(8,128)(2,1)S(1)} %copy-done.18), channel_id=1, source_target_pairs={{0,2},{1,7},{2,4},{3,1},{4,6},{5,3},{6,0},{7,5},{8,10},{9,15},{10,... | collective-permute-start | bytes 1966088 | tf_op jit(solution)/shard_map/a_far/ppermute | solution.py:34
  78.7 2.4 %early.1 = f32[512,192]{1,0:T(8,128)S(1)} custom-call(s32[24]{0:T(128)S(1)} %concatenate.12.where_ref, bf16[512,640]{1,0:T(8,128)(2,1)S(1)} %copy-done.22, bf16[512,640]{1,0:T(8,128)(2,1)S(1)} %copy-done.5, bf16[64,5120]{1,0:T(8,128)(2,1)S(1)} %bitcast.32, bf16[512,1792]{1,0:T(8,128)(2,1)S(1)} %copy-done, bf16[512,1792]{1,0:T(8,128)(2,1)S(1)} %copy-done.1, ...), custom_call_target="tpu_custom_call" | custom-call | flops 1048576 | bytes 65536 | tf_op jit(solution)/shard_map/early/pallas_call | solution.py:152
  81.1 4.8 %collective-permute-done.15.refs_10_.refs_14_ = bf16[112,5120]{1,0:T(8,128)(2,1)S(1)} collective-permute-done((bf16[112,5120]{1,0:T(8,128)(2,1)}, bf16[112,5120]{1,0:T(8,128)(2,1)S(1)}, u32[]{:S(2)}, u32[]{:S(2)}) %collective-permute-start.15) | collective-permute-done | bytes 1146912 | tf_op jit(solution)/shard_map/r6/ppermute | solution.py:34
  85.9 5.4 %product.6 = bf16[512,384]{1,0:T(8,128)(2,1)S(1)} custom-call(s32[24]{0:T(128)S(1)} %concatenate.12.where_ref, bf16[512,640]{1,0:T(8,128)(2,1)} %collective-permute-done.refs_0_, bf16[512,640]{1,0:T(8,128)(2,1)} %collective-permute-done.6.refs_1_, bf16[512,640]{1,0:T(8,128)(2,1)} %collective-permute-done.7.refs_2_, ...), custom_call_target="tpu_custom_call" | custom-call | flops 1048576 | bytes 65536 | tf_op jit(solution)/shard_map/product/pallas_call | solution.py:126
  94.0 1.9 %collective-permute-start.27 = (f32[256,192]{1,0:T(8,128)S(1)}, f32[256,192]{1,0:T(8,128)S(1)}, u32[]{:S(2)}, u32[]{:S(2)}) collective-permute-start(f32[256,192]{1,0:T(8,128)S(1)} %select_add_fusion), channel_id=1, source_target_pairs={{0,6},{1,7},{2,0},{3,1},{4,2},{5,3},{6,4},{7,5},{8,14},{9,15},{10,... | collective-permute-start | bytes 589832 | tf_op jit(solution)/shard_map/down/ppermute | solution.py:34
  95.9 6.2 %collective-permute-done.26 = f32[256,192]{1,0:T(8,128)S(1)} collective-permute-done((f32[256,192]{1,0:T(8,128)S(1)}, f32[256,192]{1,0:T(8,128)S(1)}, u32[]{:S(2)}, u32[]{:S(2)}) %collective-permute-start.26) | collective-permute-done | bytes 196640 | tf_op jit(solution)/shard_map/up/ppermute | solution.py:34
  104.3 6.2 %collective-permute-done.25 = f32[256,192]{1,0:T(8,128)S(1)} collective-permute-done((f32[256,192]{1,0:T(8,128)S(1)}, f32[256,192]{1,0:T(8,128)S(1)}, u32[]{:S(2)}, u32[]{:S(2)}) %collective-permute-start.25) | collective-permute-done | bytes 196640 | tf_op jit(solution)/shard_map/send/ppermute | solution.py:34
  110.4 1.9 %collective-permute-start.20 = (bf16[512,640]{1,0:T(8,128)(2,1)S(1)}, bf16[512,640]{1,0:T(8,128)(2,1)S(1)}, u32[]{:S(2)}, u32[]{:S(2)}) collective-permute-start(bf16[512,640]{1,0:T(8,128)(2,1)S(1)} %collective-permute-done.16.refs_3_), channel_id=1, source_target_pairs={{0,1},{1,0},{2,3},{3,2},{4,5},{5,4},{6,7},{7,6},{8,9},{9,8},{10,11... | collective-permute-start | bytes 1966088 | tf_op jit(solution)/shard_map/a_swap/ppermute | solution.py:34
  112.8 2.7 %collective-permute-start.23 = (bf16[512,384]{1,0:T(8,128)(2,1)S(1)}, bf16[512,384]{1,0:T(8,128)(2,1)S(1)}, u32[]{:S(2)}, u32[]{:S(2)}) collective-permute-start(bf16[512,384]{1,0:T(8,128)(2,1)S(1)} %product.6), channel_id=1, source_target_pairs={{0,96},{1,97},{2,98},{3,99},{4,100},{5,101},{6,102},{7,103},{8,104... | collective-permute-start | bytes 1179656 | tf_op jit(solution)/shard_map/mate_grad2/ppermute | solution.py:34
  115.6 6.9 %product.7.refs_0_ = f32[512,896]{1,0:T(8,128)S(1)} custom-call(s32[24]{0:T(128)S(1)} %concatenate.12.where_ref, bf16[512,640]{1,0:T(8,128)(2,1)S(1)} %copy-done.5, bf16[512,640]{1,0:T(8,128)(2,1)S(1)} %copy-done.18, bf16[512,640]{1,0:T(8,128)(2,1)S(1)} %copy-done.20, bf16[512,640]{1,0:T(8,128)(2,1)S(1)} %collective-permute-done.16.refs_3_, ...), custom_call_target="tpu_custom_call" | custom-call | flops 1048576 | bytes 65536 | tf_op jit(solution)/shard_map/product/pallas_call | solution.py:126
  122.5 4.7 %collective-permute-done.21.refs_0_ = bf16[512,512]{1,0:T(8,128)(2,1)S(1)} collective-permute-done((bf16[512,512]{1,0:T(8,128)(2,1)S(1)}, bf16[512,512]{1,0:T(8,128)(2,1)S(1)}, u32[]{:S(2)}, u32[]{:S(2)}) %collective-permute-start.21) | collective-permute-done | bytes 524320 | tf_op jit(solution)/shard_map/mate_grad1/ppermute | solution.py:34
  127.2 3.7 %product.8 = bf16[512,128]{1,0:T(8,128)(2,1)S(1)} custom-call(s32[24]{0:T(128)S(1)} %concatenate.12.where_ref, bf16[512,640]{1,0:T(8,128)(2,1)} %collective-permute-done.refs_0_, bf16[512,640]{1,0:T(8,128)(2,1)} %collective-permute-done.6.refs_1_, bf16[512,640]{1,0:T(8,128)(2,1)} %collective-permute-done.7.refs_2_, ...), custom_call_target="tpu_custom_call" | custom-call | flops 1048576 | bytes 65536 | tf_op jit(solution)/shard_map/product/pallas_call | solution.py:126
  132.2 3.4 %collective-permute-done.23.refs_1_ = bf16[512,384]{1,0:T(8,128)(2,1)S(1)} collective-permute-done((bf16[512,384]{1,0:T(8,128)(2,1)S(1)}, bf16[512,384]{1,0:T(8,128)(2,1)S(1)}, u32[]{:S(2)}, u32[]{:S(2)}) %collective-permute-start.23) | collective-permute-done | bytes 393248 | tf_op jit(solution)/shard_map/mate_grad2/ppermute | solution.py:34
  135.6 2.2 %product.9.refs_1_ = f32[512,128]{1,0:T(8,128)S(1)} custom-call(s32[24]{0:T(128)S(1)} %concatenate.12.where_ref, bf16[512,640]{1,0:T(8,128)(2,1)S(1)} %copy-done.5, bf16[512,640]{1,0:T(8,128)(2,1)S(1)} %copy-done.18, bf16[512,640]{1,0:T(8,128)(2,1)S(1)} %copy-done.20, bf16[512,640]{1,0:T(8,128)(2,1)S(1)} %collective-permute-done.16.refs_3_, ...), custom_call_target="tpu_custom_call" | custom-call | flops 1048576 | bytes 65536 | tf_op jit(solution)/shard_map/product/pallas_call | solution.py:126
  137.7 3.8 %own_half.1 = (bf16[512,1792]{1,0:T(8,128)(2,1)}, bf16[512,1792]{1,0:T(8,128)(2,1)}, f32[512,128]{1,0:T(8,128)S(1)}) custom-call(s32[24]{0:T(128)S(1)} %concatenate.12.where_ref, bf16[512,1792]{1,0:T(8,128)(2,1)S(1)} %copy-done, bf16[512,1792]{1,0:T(8,128)(2,1)S(1)} %copy-done.1, bf16[64,1792]{1,0:T(8,128)(2,1)S(1)} %bitcast.30, ...), custom_call_target="tpu_custom_call" | custom-call | flops 1048576 | bytes 65536 | tf_op jit(solution)/shard_map/own_half/pallas_call | solution.py:221
  141.6 4.4 %other_half.1 = (bf16[512,1792]{1,0:T(8,128)(2,1)}, bf16[512,1792]{1,0:T(8,128)(2,1)}, f32[256,128]{1,0:T(8,128)S(1)}) custom-call(s32[24]{0:T(128)S(1)} %concatenate.12.where_ref, bf16[512,1792]{1,0:T(8,128)(2,1)S(1)} %copy-done, bf16[512,1792]{1,0:T(8,128)(2,1)S(1)} %copy-done.1, ...), custom_call_target="tpu_custom_call", output_to_operand_aliasing={{0}: (7, {}), {1}: (8, {})} | custom-call | flops 1048576 | bytes 65536 | tf_op jit(solution)/shard_map/other_half/pallas_call | solution.py:265
  148.2 2.7 %collective-permute-start.33 = (f32[128,128]{1,0:T(8,128)S(1)}, f32[128,128]{1,0:T(8,128)S(1)}, u32[]{:S(2)}, u32[]{:S(2)}) collective-permute-start(f32[128,128]{1,0:T(8,128)S(1)} %select_add_fusion.1), channel_id=1, source_target_pairs={{0,6},{1,7},{2,0},{3,1},{4,2},{5,3},{6,4},{7,5},{8,14},{9,15},{10,... | collective-permute-start | bytes 196616 | tf_op jit(solution)/shard_map/down/ppermute | solution.py:34
  150.9 1.6 %collective-permute-done.32 = f32[128,128]{1,0:T(8,128)S(1)} collective-permute-done((f32[128,128]{1,0:T(8,128)S(1)}, f32[128,128]{1,0:T(8,128)S(1)}, u32[]{:S(2)}, u32[]{:S(2)}) %collective-permute-start.32) | collective-permute-done | bytes 65568 | tf_op jit(solution)/shard_map/up/ppermute | solution.py:34
  153.0 2.6 %collective-permute-done.31 = f32[128,128]{1,0:T(8,128)S(1)} collective-permute-done((f32[128,128]{1,0:T(8,128)S(1)}, f32[128,128]{1,0:T(8,128)S(1)}, u32[]{:S(2)}, u32[]{:S(2)}) %collective-permute-start.31) | collective-permute-done | bytes 65568 | tf_op jit(solution)/shard_map/send/ppermute | solution.py:34
  155.5 2.1 %collective-permute-start.34 = (f32[128,128]{1,0:T(8,128)S(1)}, f32[128,128]{1,0:T(8,128)S(1)}, u32[]{:S(2)}, u32[]{:S(2)}) collective-permute-start(f32[128,128]{1,0:T(8,128)S(1)} %add_add_fusion.1), channel_id=1, source_target_pairs={{0,1},{1,0},{2,3},{3,2},{4,5},{5,4},{6,7},{7,6},{8,9},{9,8},{10,11... | collective-permute-start | bytes 196616 | tf_op jit(solution)/shard_map/swap/ppermute | solution.py:34
  (118 shorter events, 27.7 us)
Async XLA Ops:
  0.6 11.5 %collective-permute-start.4 = (bf16[512,640]{1,0:T(8,128)(2,1)}, bf16[512,640]{1,0:T(8,128)(2,1)S(1)}, u32[]{:S(2)}, u32[]{:S(2)}) collective-permute-start(bf16[512,640]{1,0:T(8,128)(2,1)} %grad_ref.1), channel_id=1, source_target_pairs={{0,2},{1,7},{2,4},{3,1},{4,6},{5,3},{6,0},{7,5},{8,10},{9,15},{10,... | collective-permute-start | bytes 1966088 | tf_op jit(solution)/shard_map/a1/ppermute | solution.py:34
  4.3 19.0 %collective-permute-start = (bf16[512,640]{1,0:T(8,128)(2,1)}, bf16[512,640]{1,0:T(8,128)(2,1)}, u32[]{:S(2)}, u32[]{:S(2)}) collective-permute-start(bf16[512,640]{1,0:T(8,128)(2,1)} %grad_ref.1), channel_id=1, source_target_pairs={{0,96},{1,97},{2,98},{3,99},{4,100},{5,101},{6,102},{7,103},{8,104... | collective-permute-start | bytes 1966088 | tf_op jit(solution)/shard_map/mate_rows/ppermute | solution.py:34
  8.0 28.4 %collective-permute-start.1 = (bf16[112,5120]{1,0:T(8,128)(2,1)}, bf16[112,5120]{1,0:T(8,128)(2,1)S(1)}, u32[]{:S(2)}, u32[]{:S(2)}) collective-permute-start(bf16[112,5120]{1,0:T(8,128)(2,1)} %refs_8_.3), channel_id=1, source_target_pairs={{0,32},{1,9},{2,34},{3,11},{4,36},{5,13},{6,38},{7,15},{8,40},{9,1... | collective-permute-start | bytes 3440648 | tf_op jit(solution)/shard_map/r1/ppermute | solution.py:34
  9.2 27.2 %collective-permute-start.2 = (bf16[112,5120]{1,0:T(8,128)(2,1)}, bf16[112,5120]{1,0:T(8,128)(2,1)S(1)}, u32[]{:S(2)}, u32[]{:S(2)}) collective-permute-start(bf16[112,5120]{1,0:T(8,128)(2,1)} %refs_8_.3), channel_id=1, source_target_pairs={{0,8},{1,25},{2,10},{3,27},{4,12},{5,29},{6,14},{7,31},{8,16},{9,1... | collective-permute-start | bytes 3440648 | tf_op jit(solution)/shard_map/r2/ppermute | solution.py:34
  10.7 25.8 %collective-permute-start.3 = (bf16[112,5120]{1,0:T(8,128)(2,1)}, bf16[112,5120]{1,0:T(8,128)(2,1)S(1)}, u32[]{:S(2)}, u32[]{:S(2)}) collective-permute-start(bf16[112,5120]{1,0:T(8,128)(2,1)} %refs_8_.3), channel_id=1, source_target_pairs={{0,24},{1,33},{2,26},{3,35},{4,28},{5,37},{6,30},{7,39},{8,0},{9,4... | collective-permute-start | bytes 3440648 | tf_op jit(solution)/shard_map/r3/ppermute | solution.py:34
  12.1 25.4 %collective-permute-start.5 = (bf16[512,640]{1,0:T(8,128)(2,1)}, bf16[512,640]{1,0:T(8,128)(2,1)S(1)}, u32[]{:S(2)}, u32[]{:S(2)}) collective-permute-start(bf16[512,640]{1,0:T(8,128)(2,1)} %grad_ref.1), channel_id=1, source_target_pairs={{0,6},{1,3},{2,0},{3,5},{4,2},{5,7},{6,4},{7,1},{8,14},{9,11},{10,... | collective-permute-start | bytes 1966088 | tf_op jit(solution)/shard_map/a2/ppermute | solution.py:34
  23.3 15.1 %collective-permute-start.6 = (bf16[512,640]{1,0:T(8,128)(2,1)}, bf16[512,640]{1,0:T(8,128)(2,1)}, u32[]{:S(2)}, u32[]{:S(2)}) collective-permute-start(bf16[512,640]{1,0:T(8,128)(2,1)} %collective-permute-done.refs_0_), channel_id=1, source_target_pairs={{0,2},{1,7},{2,4},{3,1},{4,6},{5,3},{6,0},{7,5},{8,10},{9,15},{10,... | collective-permute-start | bytes 1966088 | tf_op jit(solution)/shard_map/b1/ppermute | solution.py:34
  38.4 16.4 %collective-permute-start.7 = (bf16[512,640]{1,0:T(8,128)(2,1)}, bf16[512,640]{1,0:T(8,128)(2,1)}, u32[]{:S(2)}, u32[]{:S(2)}) collective-permute-start(bf16[512,640]{1,0:T(8,128)(2,1)} %collective-permute-done.refs_0_), channel_id=1, source_target_pairs={{0,6},{1,3},{2,0},{3,5},{4,2},{5,7},{6,4},{7,1},{8,14},{9,11},{10,... | collective-permute-start | bytes 1966088 | tf_op jit(solution)/shard_map/b2/ppermute | solution.py:34
  38.6 23.5 %collective-permute-start.8 = (bf16[512,640]{1,0:T(8,128)(2,1)}, bf16[512,640]{1,0:T(8,128)(2,1)}, u32[]{:S(2)}, u32[]{:S(2)}) collective-permute-start(bf16[512,640]{1,0:T(8,128)(2,1)} %collective-permute-done.6.refs_1_), channel_id=1, source_target_pairs={{0,2},{1,7},{2,4},{3,1},{4,6},{5,3},{6,0},{7,5},{8,10},{9,15},{10,... | collective-permute-start | bytes 1966088 | tf_op jit(solution)/shard_map/b_far/ppermute | solution.py:34
  41.1 40.0 %collective-permute-start.13 = (bf16[112,5120]{1,0:T(8,128)(2,1)S(1)}, bf16[112,5120]{1,0:T(8,128)(2,1)S(1)}, u32[]{:S(2)}, u32[]{:S(2)}) collective-permute-start(bf16[112,5120]{1,0:T(8,128)(2,1)S(1)} %collective-permute-done.1.refs_9_), channel_id=1, source_target_pairs={{0,8},{1,33},{2,10},{3,35},{4,12},{5,37},{6,14},{7,39},{8,16},{9,4... | collective-permute-start | bytes 3440648 | tf_op jit(solution)/shard_map/r4/ppermute | solution.py:34
  54.8 3.3 %collective-permute-start.9 = (bf16[512,640]{1,0:T(8,128)(2,1)}, bf16[512,640]{1,0:T(8,128)(2,1)S(1)}, u32[]{:S(2)}, u32[]{:S(2)}) collective-permute-start(bf16[512,640]{1,0:T(8,128)(2,1)} %collective-permute-done.refs_0_), channel_id=1, source_target_pairs={{0,1},{1,0},{2,3},{3,2},{4,5},{5,4},{6,7},{7,6},{8,9},{9,8},{10,11... | collective-permute-start | bytes 1966088 | tf_op jit(solution)/shard_map/b_swap/ppermute | solution.py:34
  56.1 5.1 %collective-permute-start.10 = (bf16[512,640]{1,0:T(8,128)(2,1)}, bf16[512,640]{1,0:T(8,128)(2,1)S(1)}, u32[]{:S(2)}, u32[]{:S(2)}) collective-permute-start(bf16[512,640]{1,0:T(8,128)(2,1)} %collective-permute-done.7.refs_2_), channel_id=1, source_target_pairs={{0,1},{1,0},{2,3},{3,2},{4,5},{5,4},{6,7},{7,6},{8,9},{9,8},{10,11... | collective-permute-start | bytes 1966088 | tf_op jit(solution)/shard_map/b_swap/ppermute | solution.py:34
  57.2 23.8 %collective-permute-start.14 = (bf16[112,5120]{1,0:T(8,128)(2,1)}, bf16[112,5120]{1,0:T(8,128)(2,1)}, u32[]{:S(2)}, u32[]{:S(2)}) collective-permute-start(bf16[112,5120]{1,0:T(8,128)(2,1)} %broadcast_select_fusion.1), channel_id=1, source_target_pairs={{0,24},{1,33},{2,26},{3,35},{4,28},{5,37},{6,30},{7,39},{8,0},{9,4... | collective-permute-start | bytes 3440648 | tf_op jit(solution)/shard_map/r5/ppermute | solution.py:34
  58.9 27.0 %collective-permute-start.15 = (bf16[112,5120]{1,0:T(8,128)(2,1)}, bf16[112,5120]{1,0:T(8,128)(2,1)S(1)}, u32[]{:S(2)}, u32[]{:S(2)}) collective-permute-start(bf16[112,5120]{1,0:T(8,128)(2,1)} %copy-done.2), channel_id=1, source_target_pairs={{0,8},{1,25},{2,10},{3,27},{4,12},{5,29},{6,14},{7,31},{8,16},{9,1... | collective-permute-start | bytes 3440648 | tf_op jit(solution)/shard_map/r6/ppermute | solution.py:34
  62.1 3.4 %collective-permute-start.12 = (bf16[512,640]{1,0:T(8,128)(2,1)}, bf16[512,640]{1,0:T(8,128)(2,1)}, u32[]{:S(2)}, u32[]{:S(2)}) collective-permute-start(bf16[512,640]{1,0:T(8,128)(2,1)} %collective-permute-done.8.refs_3_), channel_id=1, source_target_pairs={{0,1},{1,0},{2,3},{3,2},{4,5},{5,4},{6,7},{7,6},{8,9},{9,8},{10,11... | collective-permute-start | bytes 1966088 | tf_op jit(solution)/shard_map/b_swap/ppermute | solution.py:34
  76.6 27.5 %collective-permute-start.16 = (bf16[512,640]{1,0:T(8,128)(2,1)S(1)}, bf16[512,640]{1,0:T(8,128)(2,1)S(1)}, u32[]{:S(2)}, u32[]{:S(2)}) collective-permute-start(bf16[512,640]{1,0:T(8,128)(2,1)S(1)} %copy-done.18), channel_id=1, source_target_pairs={{0,2},{1,7},{2,4},{3,1},{4,6},{5,3},{6,0},{7,5},{8,10},{9,15},{10,... | collective-permute-start | bytes 1966088 | tf_op jit(solution)/shard_map/a_far/ppermute | solution.py:34
  91.6 20.8 %collective-permute-start.17 = (bf16[512,640]{1,0:T(8,128)(2,1)S(1)}, bf16[512,640]{1,0:T(8,128)(2,1)S(1)}, u32[]{:S(2)}, u32[]{:S(2)}) collective-permute-start(bf16[512,640]{1,0:T(8,128)(2,1)S(1)} %copy-done.5), channel_id=1, source_target_pairs={{0,1},{1,0},{2,3},{3,2},{4,5},{5,4},{6,7},{7,6},{8,9},{9,8},{10,11... | collective-permute-start | bytes 1966088 | tf_op jit(solution)/shard_map/a_swap/ppermute | solution.py:34
  92.1 35.0 %collective-permute-start.22 = (bf16[112,5120]{1,0:T(8,128)(2,1)S(1)}, bf16[112,5120]{1,0:T(8,128)(2,1)S(1)}, u32[]{:S(2)}, u32[]{:S(2)}) collective-permute-start(bf16[112,5120]{1,0:T(8,128)(2,1)S(1)} %broadcast_select_fusion), channel_id=1, source_target_pairs={{0,8},{1,33},{2,10},{3,35},{4,12},{5,37},{6,14},{7,39},{8,16},{9,4... | collective-permute-start | bytes 3440648 | tf_op jit(solution)/shard_map/r7/ppermute | solution.py:34
  93.0 9.2 %collective-permute-start.26 = (f32[256,192]{1,0:T(8,128)S(1)}, f32[256,192]{1,0:T(8,128)S(1)}, u32[]{:S(2)}, u32[]{:S(2)}) collective-permute-start(f32[256,192]{1,0:T(8,128)S(1)} %select_add_fusion), channel_id=1, source_target_pairs={{0,2},{1,3},{2,4},{3,5},{4,6},{5,7},{6,0},{7,1},{8,10},{9,11},{10,... | collective-permute-start | bytes 589832 | tf_op jit(solution)/shard_map/up/ppermute | solution.py:34
  94.0 8.9 %collective-permute-start.27 = (f32[256,192]{1,0:T(8,128)S(1)}, f32[256,192]{1,0:T(8,128)S(1)}, u32[]{:S(2)}, u32[]{:S(2)}) collective-permute-start(f32[256,192]{1,0:T(8,128)S(1)} %select_add_fusion), channel_id=1, source_target_pairs={{0,6},{1,7},{2,0},{3,1},{4,2},{5,3},{6,4},{7,5},{8,14},{9,15},{10,... | collective-permute-start | bytes 589832 | tf_op jit(solution)/shard_map/down/ppermute | solution.py:34
  102.2 8.3 %collective-permute-start.25 = (f32[256,192]{1,0:T(8,128)S(1)}, f32[256,192]{1,0:T(8,128)S(1)}, u32[]{:S(2)}, u32[]{:S(2)}) collective-permute-start(f32[256,192]{1,0:T(8,128)S(1)} %select_add_fusion), channel_id=1, source_target_pairs={{0,4},{1,5},{2,6},{3,7},{4,0},{5,1},{6,2},{7,3},{8,12},{9,13},{10,... | collective-permute-start | bytes 589832 | tf_op jit(solution)/shard_map/send/ppermute | solution.py:34
  103.0 9.5 %collective-permute-start.18 = (bf16[512,640]{1,0:T(8,128)(2,1)S(1)}, bf16[512,640]{1,0:T(8,128)(2,1)S(1)}, u32[]{:S(2)}, u32[]{:S(2)}) collective-permute-start(bf16[512,640]{1,0:T(8,128)(2,1)S(1)} %copy-done.20), channel_id=1, source_target_pairs={{0,1},{1,0},{2,3},{3,2},{4,5},{5,4},{6,7},{7,6},{8,9},{9,8},{10,11... | collective-permute-start | bytes 1966088 | tf_op jit(solution)/shard_map/a_swap/ppermute | solution.py:34
  104.2 8.6 %collective-permute-start.19 = (bf16[512,640]{1,0:T(8,128)(2,1)S(1)}, bf16[512,640]{1,0:T(8,128)(2,1)S(1)}, u32[]{:S(2)}, u32[]{:S(2)}) collective-permute-start(bf16[512,640]{1,0:T(8,128)(2,1)S(1)} %copy-done.18), channel_id=1, source_target_pairs={{0,1},{1,0},{2,3},{3,2},{4,5},{5,4},{6,7},{7,6},{8,9},{9,8},{10,11... | collective-permute-start | bytes 1966088 | tf_op jit(solution)/shard_map/a_swap/ppermute | solution.py:34
  110.4 5.1 %collective-permute-start.20 = (bf16[512,640]{1,0:T(8,128)(2,1)S(1)}, bf16[512,640]{1,0:T(8,128)(2,1)S(1)}, u32[]{:S(2)}, u32[]{:S(2)}) collective-permute-start(bf16[512,640]{1,0:T(8,128)(2,1)S(1)} %collective-permute-done.16.refs_3_), channel_id=1, source_target_pairs={{0,1},{1,0},{2,3},{3,2},{4,5},{5,4},{6,7},{7,6},{8,9},{9,8},{10,11... | collective-permute-start | bytes 1966088 | tf_op jit(solution)/shard_map/a_swap/ppermute | solution.py:34
  112.4 14.8 %collective-permute-start.21 = (bf16[512,512]{1,0:T(8,128)(2,1)S(1)}, bf16[512,512]{1,0:T(8,128)(2,1)S(1)}, u32[]{:S(2)}, u32[]{:S(2)}) collective-permute-start(bf16[512,512]{1,0:T(8,128)(2,1)S(1)} %product.5), channel_id=1, source_target_pairs={{0,96},{1,97},{2,98},{3,99},{4,100},{5,101},{6,102},{7,103},{8,104... | collective-permute-start | bytes 1572872 | tf_op jit(solution)/shard_map/mate_grad1/ppermute | solution.py:34
  112.5 18.5 %collective-permute-start.28 = (f32[256,192]{1,0:T(8,128)S(1)}, f32[256,192]{1,0:T(8,128)S(1)}, u32[]{:S(2)}, u32[]{:S(2)}) collective-permute-start(f32[256,192]{1,0:T(8,128)S(1)} %add_add_fusion), channel_id=1, source_target_pairs={{0,1},{1,0},{2,3},{3,2},{4,5},{5,4},{6,7},{7,6},{8,9},{9,8},{10,11... | collective-permute-start | bytes 589832 | tf_op jit(solution)/shard_map/swap/ppermute | solution.py:34
  112.8 22.8 %collective-permute-start.23 = (bf16[512,384]{1,0:T(8,128)(2,1)S(1)}, bf16[512,384]{1,0:T(8,128)(2,1)S(1)}, u32[]{:S(2)}, u32[]{:S(2)}) collective-permute-start(bf16[512,384]{1,0:T(8,128)(2,1)S(1)} %product.6), channel_id=1, source_target_pairs={{0,96},{1,97},{2,98},{3,99},{4,100},{5,101},{6,102},{7,103},{8,104... | collective-permute-start | bytes 1179656 | tf_op jit(solution)/shard_map/mate_grad2/ppermute | solution.py:34
  130.9 10.7 %collective-permute-start.29 = (bf16[512,128]{1,0:T(8,128)(2,1)S(1)}, bf16[512,128]{1,0:T(8,128)(2,1)S(1)}, u32[]{:S(2)}, u32[]{:S(2)}) collective-permute-start(bf16[512,128]{1,0:T(8,128)(2,1)S(1)} %product.8), channel_id=1, source_target_pairs={{0,96},{1,97},{2,98},{3,99},{4,100},{5,101},{6,102},{7,103},{8,104... | collective-permute-start | bytes 393224 | tf_op jit(solution)/shard_map/mate_grad3/ppermute | solution.py:34
  148.2 4.4 %collective-permute-start.32 = (f32[128,128]{1,0:T(8,128)S(1)}, f32[128,128]{1,0:T(8,128)S(1)}, u32[]{:S(2)}, u32[]{:S(2)}) collective-permute-start(f32[128,128]{1,0:T(8,128)S(1)} %select_add_fusion.1), channel_id=1, source_target_pairs={{0,2},{1,3},{2,4},{3,5},{4,6},{5,7},{6,0},{7,1},{8,10},{9,11},{10,... | collective-permute-start | bytes 196616 | tf_op jit(solution)/shard_map/up/ppermute | solution.py:34
  148.2 4.7 %collective-permute-start.33 = (f32[128,128]{1,0:T(8,128)S(1)}, f32[128,128]{1,0:T(8,128)S(1)}, u32[]{:S(2)}, u32[]{:S(2)}) collective-permute-start(f32[128,128]{1,0:T(8,128)S(1)} %select_add_fusion.1), channel_id=1, source_target_pairs={{0,6},{1,7},{2,0},{3,1},{4,2},{5,3},{6,4},{7,5},{8,14},{9,15},{10,... | collective-permute-start | bytes 196616 | tf_op jit(solution)/shard_map/down/ppermute | solution.py:34
  150.9 4.6 %collective-permute-start.31 = (f32[128,128]{1,0:T(8,128)S(1)}, f32[128,128]{1,0:T(8,128)S(1)}, u32[]{:S(2)}, u32[]{:S(2)}) collective-permute-start(f32[128,128]{1,0:T(8,128)S(1)} %select_add_fusion.1), channel_id=1, source_target_pairs={{0,4},{1,5},{2,6},{3,7},{4,0},{5,1},{6,2},{7,3},{8,12},{9,13},{10,... | collective-permute-start | bytes 196616 | tf_op jit(solution)/shard_map/send/ppermute | solution.py:34
  155.5 3.0 %collective-permute-start.34 = (f32[128,128]{1,0:T(8,128)S(1)}, f32[128,128]{1,0:T(8,128)S(1)}, u32[]{:S(2)}, u32[]{:S(2)}) collective-permute-start(f32[128,128]{1,0:T(8,128)S(1)} %add_add_fusion.1), channel_id=1, source_target_pairs={{0,1},{1,0},{2,3},{3,2},{4,5},{5,4},{6,7},{7,6},{8,9},{9,8},{10,11... | collective-permute-start | bytes 196616 | tf_op jit(solution)/shard_map/swap/ppermute | solution.py:34
  (28 other events, 246.6 us)

commit v5 on v4

--- a/solution.py
+++ b/solution.py
@@ -58,10 +58,6 @@
     return lax.optimization_barrier((value, *others))[0]
 
 
-def pick(c, a, b):
-    return jnp.where(c == 0, a, b)
-
-
 def route(v, zero, one, name):
     hop = {
         "p": lambda z, x, y, c: (z ^ 1, x, y, c),
@@ -80,12 +76,12 @@
     held = jnp.stack(
         [
             at(0, 0),
-            jnp.where(first, at(1, 0), at(0, 3)),
-            jnp.where(first, at(0, 3), at(0, 1)),
+            at(0, 3),
+            jnp.where(first, at(1, 0), at(0, 1)),
             jnp.where(first, at(0, 1), at(1, 0)),
-            at(1, 3),
-            at(1, 1),
-            at(0, 2),
+            jnp.where(first, at(1, 3), at(1, 1)),
+            jnp.where(first, at(0, 2), at(1, 3)),
+            jnp.where(first, at(1, 1), at(0, 2)),
             at(1, 2),
         ]
     )
@@ -130,7 +126,7 @@
         out_specs=vmem,
         scratch_shapes=[] if dtype == F32 else [pltpu.VMEM((ROWS, width), F32)],
         compiler_params=pltpu.CompilerParams(
-            vmem_limit_bytes=(4 << 20) + width * (4 * STEP + 14 * ROWS)
+            vmem_limit_bytes=(6 << 20) + width * (4 * STEP + 14 * ROWS)
         ),
         cost_estimate=LIGHT,
         name="product",
@@ -345,38 +341,38 @@
         ]
     ).astype(jnp.int32)
     own_w = down_weight
-    r1 = route(own_w, "p", "+", "r1")
-    r2 = route(own_w, "+", "-", "r2")
-    r3 = route(own_w, "-", "p", "r3")
     theirs = mate(out_grad, "mate_rows")
-    a1 = along_y(out_grad, 1, "a1")
-    a2 = along_y(after(out_grad, a1), -1, "a2")
-    b1 = along_y(theirs, 1, "b1")
-    r1, r2, r3, a2, b1 = lax.optimization_barrier((r1, r2, r3, a2, b1))
-    r4 = route(r1, "+", "p", "r4")
-    r5 = route(pick(c, r1, r2), "-", "p", "r5")
-    r6 = route(r2, "+", "-", "r6")
-    b2 = along_y(after(theirs, a2), -1, "b2")
+    a1, a2 = along_y(out_grad, 1, "a1"), along_y(out_grad, -1, "a2")
+    r1 = route(own_w, "+", "+", "r1")
+    r2 = route(own_w, "p", "-", "r2")
+    theirs, a1, a2, again = lax.optimization_barrier((theirs, a1, a2, own_w))
+    r3 = route(again, "-", "p", "r3")
+    b1, b2 = along_y(theirs, 1, "b1"), along_y(theirs, -1, "b2")
+    r1, r2, r3, b1, b2 = lax.optimization_barrier((r1, r2, r3, b1, b2))
+    r6 = route(r2, "-", "-", "r6")
+    r4 = route(r2, "+", "p", "r4")
+    r5 = route(r1, "+", "p", "r5")
     b_far = along_y(b1, 1, "b_far")
-    b_other = [swap(after(v, b2), "b_swap") for v in (theirs, b2)]
-    b_other += [swap(after(v, *b_other), "b_swap") for v in (b1, b_far)]
+    b_other = [swap(v, "b_swap") for v in (after(theirs, b1), b2, b1, b_far)]
     b_mine = [theirs, b1, b2, b_far]
-    h1 = product(BF16, where, b_mine, b_other, [own_w, r1, r2, r3])
-    r7 = route(after(pick(c, r4, r6), r5, h1), "+", "p", "r7")
-    a_far = along_y(after(a1, *b_other), 1, "a_far")
+    r7 = route(r6, "-", "p", "r7")
+    h1 = product(BF16, after(where, r4, r5, r6), b_mine, b_other, [own_w, r1, r2, r3])
+    h1_in = mate(h1, "mate_grad1")
+    a_far = along_y(after(a1, h1), 1, "a_far")
+    h2 = product(BF16, after(where, h1), b_mine, b_other, [r4, r5, r6])
+    h2_in = mate(h2, "mate_grad2")
     a_mine = [out_grad, a1, a2, a_far]
-    a_other = [swap(after(v, *b_other), "a_swap") for v in (out_grad, a2, a1, a_far)]
-
-    h2 = product(BF16, after(where, h1), b_mine, b_other, [r4, r5, r6])
+    a_other = [swap(v, "a_swap") for v in (after(out_grad, h1), after(a2, h1), after(a1, h1), a_far)]
+
     pm_t, ph_t = proj_model.T, proj_hidden.T
-    parts = early(after(where, h1), activations, out_grad, pm_t, gate_pre, up_pre, ph_t)
-    sums = sum_tensor(after(parts, h2), c)
+    own1 = product(
+        F32, after(where, h2), a_mine, a_other, [own_w, r1, r2, r3, r4, r5, r6]
+    )
+    parts = early(after(where, h2), activations, out_grad, pm_t, gate_pre, up_pre, ph_t)
+    sums = sum_tensor(after(parts, r7, h1_in, own1), c)
     *spread, down_feat = spread_features(where, sums)
 
-    h1_in = mate(h1, "mate_grad1")
-    own1 = product(F32, after(where, h2), a_mine, a_other, [own_w, r1, r2, r3, r4, r5, r6])
-    h3 = product(BF16, after(where, own1, h1_in), b_mine, b_other, [r7])
-    h2_in = mate(h2, "mate_grad2")
+    h3 = product(BF16, after(where, h2, h1_in, own1), b_mine, b_other, [r7])
     own2 = product(F32, after(where, h3, h2_in), a_mine, a_other, [r7])
     h_in = [h1_in, h2_in, mate(h3, "mate_grad3")]
     grad_gate, grad_up, part = own_half(where, gate_pre, up_pre, (own1, own2), ph_t)

time: 160 us -> 160 us (level)
  starting transfers between devices: 36.9 us -> 43.4 us
  waiting for transfers between devices: 72.9 us -> 68.2 us
    ppermute x35, starting transfers between devices: 36.9 us -> 43.4 us  [send(): return lax.ppermute(value, AXES, pairs)]
    ppermute x35, waiting for transfers between devices: 72.9 us -> 68.2 us  [send(): return lax.ppermute(value, AXES, pairs)]
    unnamed x50 -> x40, local copies, waits for them, and re-layouts: 9.65 us -> 7.87 us
  transfers between devices with their start and end apart: 35 -> 35, of which waited for: 18 -> 16; matrix products, arithmetic and copies ran while one was open for 2% -> 2% of each run, Pallas kernels for 19% -> 16%
where the time goes in v5:
time: 160 us
  waiting for transfers between devices  68.2 us (43%)
  starting transfers between devices  43.4 us (27%)
  Pallas kernels  34.7 us (22%)
  local copies, waits for them, and re-layouts  10.7 us (7%)
  other arithmetic  1.73 us (1%)
    ppermute x35, waiting for transfers between devices, send(): return lax.ppermute(value, AXES, pairs)  68.2 us
    ppermute x35, starting transfers between devices, send(): return lax.ppermute(value, AXES, pairs)  43.4 us
    pallas_call x5, Pallas kernels, product(): pl.pallas_call(functools.partial(product_kernel, shards), out_shape=jax.S...  23 us
    unnamed x40, local copies, waits for them, and re-layouts  7.87 us
    pallas_call x1, Pallas kernels, other_half(): pl.pallas_call(functools.partial(other_kernel, len(h)), out_shape=(BIG, B...  4.44 us
    pallas_call x1, Pallas kernels, own_half(): pl.pallas_call(functools.partial(own_kernel, len(h)), out_shape=(BIG, BIG...  3.82 us
  transfers between devices with their start and end apart: 35, of which 16 were waited for; matrix products, arithmetic and copies ran while one was open for 2% of the time, Pallas kernels for 16%

profile of v5, /device:TPU:1, one launch (start us, length us, event | category | flops | bytes accessed | tf_op | source)
XLA Modules:
  0.0 159.7 jit_solution(16129049935742895033)
XLA Ops:
  0.6 4.7 %collective-permute-start.2 = (bf16[512,640]{1,0:T(8,128)(2,1)}, bf16[512,640]{1,0:T(8,128)(2,1)S(1)}, u32[]{:S(2)}, u32[]{:S(2)}) collective-permute-start(bf16[512,640]{1,0:T(8,128)(2,1)} %grad_ref.1), channel_id=1, source_target_pairs={{0,96},{1,97},{2,98},{3,99},{4,100},{5,101},{6,102},{7,103},{8,104... | collective-permute-start | bytes 1966088 | tf_op jit(solution)/shard_map/mate_rows/ppermute | solution.py:34
  5.3 2.7 %collective-permute-start.3 = (bf16[512,640]{1,0:T(8,128)(2,1)}, bf16[512,640]{1,0:T(8,128)(2,1)S(1)}, u32[]{:S(2)}, u32[]{:S(2)}) collective-permute-start(bf16[512,640]{1,0:T(8,128)(2,1)} %grad_ref.1), channel_id=1, source_target_pairs={{0,2},{1,7},{2,4},{3,1},{4,6},{5,3},{6,0},{7,5},{8,10},{9,15},{10,... | collective-permute-start | bytes 1966088 | tf_op jit(solution)/shard_map/a1/ppermute | solution.py:34
  9.2 1.5 collective-permute-start.1
  10.7 9.4 %collective-permute-done.2.refs_0_ = bf16[512,640]{1,0:T(8,128)(2,1)S(1)} collective-permute-done((bf16[512,640]{1,0:T(8,128)(2,1)}, bf16[512,640]{1,0:T(8,128)(2,1)S(1)}, u32[]{:S(2)}, u32[]{:S(2)}) %collective-permute-start.2) | collective-permute-done | bytes 655392 | tf_op jit(solution)/shard_map/mate_rows/ppermute | solution.py:34
  22.1 2.9 %collective-permute-done.4.refs_2_ = bf16[512,640]{1,0:T(8,128)(2,1)} collective-permute-done((bf16[512,640]{1,0:T(8,128)(2,1)}, bf16[512,640]{1,0:T(8,128)(2,1)}, u32[]{:S(2)}, u32[]{:S(2)}) %collective-permute-start.4) | collective-permute-done | bytes 655392 | tf_op jit(solution)/shard_map/a2/ppermute | solution.py:34
  26.5 8.4 %collective-permute-done.refs_9_ = bf16[112,5120]{1,0:T(8,128)(2,1)} collective-permute-done((bf16[112,5120]{1,0:T(8,128)(2,1)}, bf16[112,5120]{1,0:T(8,128)(2,1)}, u32[]{:S(2)}, u32[]{:S(2)}) %collective-permute-start) | collective-permute-done | bytes 1146912 | tf_op jit(solution)/shard_map/r1/ppermute | solution.py:34
  34.9 2.1 %collective-permute-done.6.refs_1_ = bf16[512,640]{1,0:T(8,128)(2,1)S(1)} collective-permute-done((bf16[512,640]{1,0:T(8,128)(2,1)S(1)}, bf16[512,640]{1,0:T(8,128)(2,1)S(1)}, u32[]{:S(2)}, u32[]{:S(2)}) %collective-permute-start.6) | collective-permute-done | bytes 655392 | tf_op jit(solution)/shard_map/b1/ppermute | solution.py:34
  37.0 3.9 %collective-permute-done.7.refs_2_ = bf16[512,640]{1,0:T(8,128)(2,1)S(1)} collective-permute-done((bf16[512,640]{1,0:T(8,128)(2,1)S(1)}, bf16[512,640]{1,0:T(8,128)(2,1)S(1)}, u32[]{:S(2)}, u32[]{:S(2)}) %collective-permute-start.7) | collective-permute-done | bytes 655392 | tf_op jit(solution)/shard_map/b2/ppermute | solution.py:34
  41.9 4.5 %collective-permute-start.10 = (bf16[112,5120]{1,0:T(8,128)(2,1)S(1)}, bf16[112,5120]{1,0:T(8,128)(2,1)S(1)}, u32[]{:S(2)}, u32[]{:S(2)}) collective-permute-start(bf16[112,5120]{1,0:T(8,128)(2,1)S(1)} %collective-permute-done.1.refs_10_), channel_id=1, source_target_pairs={{0,24},{1,25},{2,26},{3,27},{4,28},{5,29},{6,30},{7,31},{8,0},{9,1... | collective-permute-start | bytes 3440648 | tf_op jit(solution)/shard_map/r6/ppermute | solution.py:34
  49.4 8.1 %collective-permute-done.11.refs_3_ = bf16[512,640]{1,0:T(8,128)(2,1)S(1)} collective-permute-done((bf16[512,640]{1,0:T(8,128)(2,1)S(1)}, bf16[512,640]{1,0:T(8,128)(2,1)S(1)}, u32[]{:S(2)}, u32[]{:S(2)}) %collective-permute-start.11) | collective-permute-done | bytes 655392 | tf_op jit(solution)/shard_map/b_far/ppermute | solution.py:34
  57.5 2.9 %collective-permute-start.12 = (bf16[512,640]{1,0:T(8,128)(2,1)S(1)}, bf16[512,640]{1,0:T(8,128)(2,1)}, u32[]{:S(2)}, u32[]{:S(2)}) collective-permute-start(bf16[512,640]{1,0:T(8,128)(2,1)S(1)} %collective-permute-done.2.refs_0_), channel_id=1, source_target_pairs={{0,1},{1,0},{2,3},{3,2},{4,5},{5,4},{6,7},{7,6},{8,9},{9,8},{10,11... | collective-permute-start | bytes 1966088 | tf_op jit(solution)/shard_map/b_swap/ppermute | solution.py:34
  60.4 9.6 %collective-permute-done.10.refs_10_.refs_14_ = bf16[112,5120]{1,0:T(8,128)(2,1)S(1)} collective-permute-done((bf16[112,5120]{1,0:T(8,128)(2,1)S(1)}, bf16[112,5120]{1,0:T(8,128)(2,1)S(1)}, u32[]{:S(2)}, u32[]{:S(2)}) %collective-permute-start.10) | collective-permute-done | bytes 1146912 | tf_op jit(solution)/shard_map/r6/ppermute | solution.py:34
  70.0 1.9 %collective-permute-start.13 = (bf16[512,640]{1,0:T(8,128)(2,1)S(1)}, bf16[512,640]{1,0:T(8,128)(2,1)}, u32[]{:S(2)}, u32[]{:S(2)}) collective-permute-start(bf16[512,640]{1,0:T(8,128)(2,1)S(1)} %collective-permute-done.7.refs_2_), channel_id=1, source_target_pairs={{0,1},{1,0},{2,3},{3,2},{4,5},{5,4},{6,7},{7,6},{8,9},{9,8},{10,11... | collective-permute-start | bytes 1966088 | tf_op jit(solution)/shard_map/b_swap/ppermute | solution.py:34
  80.8 4.9 %product.5 = bf16[512,512]{1,0:T(8,128)(2,1)S(1)} custom-call(s32[24]{0:T(128)S(1)} %concatenate.12.where_ref, bf16[512,640]{1,0:T(8,128)(2,1)S(1)} %collective-permute-done.2.refs_0_, bf16[512,640]{1,0:T(8,128)(2,1)S(1)} %collective-permute-done.6.refs_1_, bf16[512,640]{1,0:T(8,128)(2,1)S(1)} %collective-permute-done.7.refs_2_, ...), custom_call_target="tpu_custom_call" | custom-call | flops 1048576 | bytes 65536 | tf_op jit(solution)/shard_map/product/pallas_call | solution.py:122
  87.2 2.9 %collective-permute-start.19 = (bf16[512,640]{1,0:T(8,128)(2,1)S(1)}, bf16[512,640]{1,0:T(8,128)(2,1)S(1)}, u32[]{:S(2)}, u32[]{:S(2)}) collective-permute-start(bf16[512,640]{1,0:T(8,128)(2,1)S(1)} %copy-done.16), channel_id=1, source_target_pairs={{0,1},{1,0},{2,3},{3,2},{4,5},{5,4},{6,7},{7,6},{8,9},{9,8},{10,11... | collective-permute-start | bytes 1966088 | tf_op jit(solution)/shard_map/a_swap/ppermute | solution.py:34
  90.1 5.4 %collective-permute-done.16.refs_3_ = bf16[512,640]{1,0:T(8,128)(2,1)S(1)} collective-permute-done((bf16[512,640]{1,0:T(8,128)(2,1)S(1)}, bf16[512,640]{1,0:T(8,128)(2,1)S(1)}, u32[]{:S(2)}, u32[]{:S(2)}) %collective-permute-start.16) | collective-permute-done | bytes 655392 | tf_op jit(solution)/shard_map/a_far/ppermute | solution.py:34
  95.5 2.3 %collective-permute-start.20 = (bf16[512,640]{1,0:T(8,128)(2,1)S(1)}, bf16[512,640]{1,0:T(8,128)(2,1)S(1)}, u32[]{:S(2)}, u32[]{:S(2)}) collective-permute-start(bf16[512,640]{1,0:T(8,128)(2,1)S(1)} %collective-permute-done.16.refs_3_), channel_id=1, source_target_pairs={{0,1},{1,0},{2,3},{3,2},{4,5},{5,4},{6,7},{7,6},{8,9},{9,8},{10,11... | collective-permute-start | bytes 1966088 | tf_op jit(solution)/shard_map/a_swap/ppermute | solution.py:34
  98.7 4.9 %product.6 = bf16[512,384]{1,0:T(8,128)(2,1)S(1)} custom-call(s32[24]{0:T(128)S(1)} %concatenate.12.where_ref, bf16[512,640]{1,0:T(8,128)(2,1)S(1)} %collective-permute-done.2.refs_0_, bf16[512,640]{1,0:T(8,128)(2,1)S(1)} %collective-permute-done.6.refs_1_, bf16[512,640]{1,0:T(8,128)(2,1)S(1)} %collective-permute-done.7.refs_2_, ...), custom_call_target="tpu_custom_call" | custom-call | flops 1048576 | bytes 65536 | tf_op jit(solution)/shard_map/product/pallas_call | solution.py:122
  103.7 2.4 %early.1 = f32[512,192]{1,0:T(8,128)S(1)} custom-call(s32[24]{0:T(128)S(1)} %concatenate.12.where_ref, bf16[512,640]{1,0:T(8,128)(2,1)S(1)} %copy-done.18, bf16[512,640]{1,0:T(8,128)(2,1)S(1)} %copy-done.2, bf16[64,5120]{1,0:T(8,128)(2,1)S(1)} %bitcast.32, bf16[512,1792]{1,0:T(8,128)(2,1)S(1)} %copy-done, bf16[512,1792]{1,0:T(8,128)(2,1)S(1)} %copy-done.1, ...), custom_call_target="tpu_custom_call" | custom-call | flops 1048576 | bytes 65536 | tf_op jit(solution)/shard_map/early/pallas_call | solution.py:148
  106.1 7.5 %product.7.refs_0_ = f32[512,896]{1,0:T(8,128)S(1)} custom-call(s32[24]{0:T(128)S(1)} %concatenate.12.where_ref, bf16[512,640]{1,0:T(8,128)(2,1)S(1)} %copy-done.2, bf16[512,640]{1,0:T(8,128)(2,1)S(1)} %copy-done.16, bf16[512,640]{1,0:T(8,128)(2,1)} %collective-permute-done.4.refs_2_, bf16[512,640]{1,0:T(8,128)(2,1)S(1)} %collective-permute-done.16.refs_3_, ...), custom_call_target="tpu_custom_call" | custom-call | flops 1048576 | bytes 65536 | tf_op jit(solution)/shard_map/product/pallas_call | solution.py:122
  115.5 2.7 %collective-permute-start.27 = (f32[256,192]{1,0:T(8,128)S(1)}, f32[256,192]{1,0:T(8,128)S(1)}, u32[]{:S(2)}, u32[]{:S(2)}) collective-permute-start(f32[256,192]{1,0:T(8,128)S(1)} %select_add_fusion), channel_id=1, source_target_pairs={{0,6},{1,7},{2,0},{3,1},{4,2},{5,3},{6,4},{7,5},{8,14},{9,15},{10,... | collective-permute-start | bytes 589832 | tf_op jit(solution)/shard_map/down/ppermute | solution.py:34
  118.2 1.8 %collective-permute-start.23 = (bf16[512,384]{1,0:T(8,128)(2,1)S(1)}, bf16[512,384]{1,0:T(8,128)(2,1)S(1)}, u32[]{:S(2)}, u32[]{:S(2)}) collective-permute-start(bf16[512,384]{1,0:T(8,128)(2,1)S(1)} %product.6), channel_id=1, source_target_pairs={{0,96},{1,97},{2,98},{3,99},{4,100},{5,101},{6,102},{7,103},{8,104... | collective-permute-start | bytes 1179656 | tf_op jit(solution)/shard_map/mate_grad2/ppermute | solution.py:34
  120.0 4.6 %collective-permute-done.25 = f32[256,192]{1,0:T(8,128)S(1)} collective-permute-done((f32[256,192]{1,0:T(8,128)S(1)}, f32[256,192]{1,0:T(8,128)S(1)}, u32[]{:S(2)}, u32[]{:S(2)}) %collective-permute-start.25) | collective-permute-done | bytes 196640 | tf_op jit(solution)/shard_map/send/ppermute | solution.py:34
  124.6 5.8 %collective-permute-done.26 = f32[256,192]{1,0:T(8,128)S(1)} collective-permute-done((f32[256,192]{1,0:T(8,128)S(1)}, f32[256,192]{1,0:T(8,128)S(1)}, u32[]{:S(2)}, u32[]{:S(2)}) %collective-permute-start.26) | collective-permute-done | bytes 196640 | tf_op jit(solution)/shard_map/up/ppermute | solution.py:34
  131.2 3.1 %product.8 = bf16[512,128]{1,0:T(8,128)(2,1)S(1)} custom-call(s32[24]{0:T(128)S(1)} %concatenate.12.where_ref, bf16[512,640]{1,0:T(8,128)(2,1)S(1)} %collective-permute-done.2.refs_0_, bf16[512,640]{1,0:T(8,128)(2,1)S(1)} %collective-permute-done.6.refs_1_, bf16[512,640]{1,0:T(8,128)(2,1)S(1)} %collective-permute-done.7.refs_2_, ...), custom_call_target="tpu_custom_call" | custom-call | flops 1048576 | bytes 65536 | tf_op jit(solution)/shard_map/product/pallas_call | solution.py:122
  134.3 2.1 %collective-permute-start.29 = (bf16[512,128]{1,0:T(8,128)(2,1)S(1)}, bf16[512,128]{1,0:T(8,128)(2,1)S(1)}, u32[]{:S(2)}, u32[]{:S(2)}) collective-permute-start(bf16[512,128]{1,0:T(8,128)(2,1)S(1)} %product.8), channel_id=1, source_target_pairs={{0,96},{1,97},{2,98},{3,99},{4,100},{5,101},{6,102},{7,103},{8,104... | collective-permute-start | bytes 393224 | tf_op jit(solution)/shard_map/mate_grad3/ppermute | solution.py:34
  136.4 2.7 %product.9.refs_1_ = f32[512,128]{1,0:T(8,128)S(1)} custom-call(s32[24]{0:T(128)S(1)} %concatenate.12.where_ref, bf16[512,640]{1,0:T(8,128)(2,1)S(1)} %copy-done.2, bf16[512,640]{1,0:T(8,128)(2,1)S(1)} %copy-done.16, bf16[512,640]{1,0:T(8,128)(2,1)} %collective-permute-done.4.refs_2_, bf16[512,640]{1,0:T(8,128)(2,1)S(1)} %collective-permute-done.16.refs_3_, ...), custom_call_target="tpu_custom_call" | custom-call | flops 1048576 | bytes 65536 | tf_op jit(solution)/shard_map/product/pallas_call | solution.py:122
  139.1 3.8 %own_half.1 = (bf16[512,1792]{1,0:T(8,128)(2,1)}, bf16[512,1792]{1,0:T(8,128)(2,1)}, f32[512,128]{1,0:T(8,128)S(1)}) custom-call(s32[24]{0:T(128)S(1)} %concatenate.12.where_ref, bf16[512,1792]{1,0:T(8,128)(2,1)S(1)} %copy-done, bf16[512,1792]{1,0:T(8,128)(2,1)S(1)} %copy-done.1, bf16[64,1792]{1,0:T(8,128)(2,1)S(1)} %bitcast.30, ...), custom_call_target="tpu_custom_call" | custom-call | flops 1048576 | bytes 65536 | tf_op jit(solution)/shard_map/own_half/pallas_call | solution.py:217
  144.1 4.4 %other_half.1 = (bf16[512,1792]{1,0:T(8,128)(2,1)}, bf16[512,1792]{1,0:T(8,128)(2,1)}, f32[256,128]{1,0:T(8,128)S(1)}) custom-call(s32[24]{0:T(128)S(1)} %concatenate.12.where_ref, bf16[512,1792]{1,0:T(8,128)(2,1)S(1)} %copy-done, bf16[512,1792]{1,0:T(8,128)(2,1)S(1)} %copy-done.1, ...), custom_call_target="tpu_custom_call", output_to_operand_aliasing={{0}: (7, {}), {1}: (8, {})} | custom-call | flops 1048576 | bytes 65536 | tf_op jit(solution)/shard_map/other_half/pallas_call | solution.py:261
  151.1 1.8 %collective-permute-start.33 = (f32[128,128]{1,0:T(8,128)S(1)}, f32[128,128]{1,0:T(8,128)S(1)}, u32[]{:S(2)}, u32[]{:S(2)}) collective-permute-start(f32[128,128]{1,0:T(8,128)S(1)} %select_add_fusion.1), channel_id=1, source_target_pairs={{0,6},{1,7},{2,0},{3,1},{4,2},{5,3},{6,4},{7,5},{8,14},{9,15},{10,... | collective-permute-start | bytes 196616 | tf_op jit(solution)/shard_map/down/ppermute | solution.py:34
  152.9 1.8 %collective-permute-done.31 = f32[128,128]{1,0:T(8,128)S(1)} collective-permute-done((f32[128,128]{1,0:T(8,128)S(1)}, f32[128,128]{1,0:T(8,128)S(1)}, u32[]{:S(2)}, u32[]{:S(2)}) %collective-permute-start.31) | collective-permute-done | bytes 65568 | tf_op jit(solution)/shard_map/send/ppermute | solution.py:34
  154.7 2.0 %collective-permute-done.32 = f32[128,128]{1,0:T(8,128)S(1)} collective-permute-done((f32[128,128]{1,0:T(8,128)S(1)}, f32[128,128]{1,0:T(8,128)S(1)}, u32[]{:S(2)}, u32[]{:S(2)}) %collective-permute-start.32) | collective-permute-done | bytes 65568 | tf_op jit(solution)/shard_map/up/ppermute | solution.py:34
  (106 shorter events, 29.3 us)
Async XLA Ops:
  0.6 19.4 %collective-permute-start.2 = (bf16[512,640]{1,0:T(8,128)(2,1)}, bf16[512,640]{1,0:T(8,128)(2,1)S(1)}, u32[]{:S(2)}, u32[]{:S(2)}) collective-permute-start(bf16[512,640]{1,0:T(8,128)(2,1)} %grad_ref.1), channel_id=1, source_target_pairs={{0,96},{1,97},{2,98},{3,99},{4,100},{5,101},{6,102},{7,103},{8,104... | collective-permute-start | bytes 1966088 | tf_op jit(solution)/shard_map/mate_rows/ppermute | solution.py:34
  5.3 15.9 %collective-permute-start.3 = (bf16[512,640]{1,0:T(8,128)(2,1)}, bf16[512,640]{1,0:T(8,128)(2,1)S(1)}, u32[]{:S(2)}, u32[]{:S(2)}) collective-permute-start(bf16[512,640]{1,0:T(8,128)(2,1)} %grad_ref.1), channel_id=1, source_target_pairs={{0,2},{1,7},{2,4},{3,1},{4,6},{5,3},{6,0},{7,5},{8,10},{9,15},{10,... | collective-permute-start | bytes 1966088 | tf_op jit(solution)/shard_map/a1/ppermute | solution.py:34
  8.0 17.0 %collective-permute-start.4 = (bf16[512,640]{1,0:T(8,128)(2,1)}, bf16[512,640]{1,0:T(8,128)(2,1)}, u32[]{:S(2)}, u32[]{:S(2)}) collective-permute-start(bf16[512,640]{1,0:T(8,128)(2,1)} %grad_ref.1), channel_id=1, source_target_pairs={{0,6},{1,3},{2,0},{3,5},{4,2},{5,7},{6,4},{7,1},{8,14},{9,11},{10,... | collective-permute-start | bytes 1966088 | tf_op jit(solution)/shard_map/a2/ppermute | solution.py:34
  8.0 26.8 %collective-permute-start = (bf16[112,5120]{1,0:T(8,128)(2,1)}, bf16[112,5120]{1,0:T(8,128)(2,1)}, u32[]{:S(2)}, u32[]{:S(2)}) collective-permute-start(bf16[112,5120]{1,0:T(8,128)(2,1)} %refs_8_.3), channel_id=1, source_target_pairs={{0,8},{1,9},{2,10},{3,11},{4,12},{5,13},{6,14},{7,15},{8,16},{9,17... | collective-permute-start | bytes 3440648 | tf_op jit(solution)/shard_map/r1/ppermute | solution.py:34
  9.2 25.6 %collective-permute-start.1 = (bf16[112,5120]{1,0:T(8,128)(2,1)}, bf16[112,5120]{1,0:T(8,128)(2,1)S(1)}, u32[]{:S(2)}, u32[]{:S(2)}) collective-permute-start(bf16[112,5120]{1,0:T(8,128)(2,1)} %refs_8_.3), channel_id=1, source_target_pairs={{0,32},{1,25},{2,34},{3,27},{4,36},{5,29},{6,38},{7,31},{8,40},{9,... | collective-permute-start | bytes 3440648 | tf_op jit(solution)/shard_map/r2/ppermute | solution.py:34
  25.0 15.9 %collective-permute-start.5 = (bf16[112,5120]{1,0:T(8,128)(2,1)}, bf16[112,5120]{1,0:T(8,128)(2,1)S(1)}, u32[]{:S(2)}, u32[]{:S(2)}) collective-permute-start(bf16[112,5120]{1,0:T(8,128)(2,1)} %refs_8_.3), channel_id=1, source_target_pairs={{0,24},{1,33},{2,26},{3,35},{4,28},{5,37},{6,30},{7,39},{8,0},{9,4... | collective-permute-start | bytes 3440648 | tf_op jit(solution)/shard_map/r3/ppermute | solution.py:34
  25.0 12.0 %collective-permute-start.6 = (bf16[512,640]{1,0:T(8,128)(2,1)S(1)}, bf16[512,640]{1,0:T(8,128)(2,1)S(1)}, u32[]{:S(2)}, u32[]{:S(2)}) collective-permute-start(bf16[512,640]{1,0:T(8,128)(2,1)S(1)} %collective-permute-done.2.refs_0_), channel_id=1, source_target_pairs={{0,2},{1,7},{2,4},{3,1},{4,6},{5,3},{6,0},{7,5},{8,10},{9,15},{10,... | collective-permute-start | bytes 1966088 | tf_op jit(solution)/shard_map/b1/ppermute | solution.py:34
  25.5 15.4 %collective-permute-start.7 = (bf16[512,640]{1,0:T(8,128)(2,1)S(1)}, bf16[512,640]{1,0:T(8,128)(2,1)S(1)}, u32[]{:S(2)}, u32[]{:S(2)}) collective-permute-start(bf16[512,640]{1,0:T(8,128)(2,1)S(1)} %collective-permute-done.2.refs_0_), channel_id=1, source_target_pairs={{0,6},{1,3},{2,0},{3,5},{4,2},{5,7},{6,4},{7,1},{8,14},{9,11},{10,... | collective-permute-start | bytes 1966088 | tf_op jit(solution)/shard_map/b2/ppermute | solution.py:34
  41.9 28.1 %collective-permute-start.10 = (bf16[112,5120]{1,0:T(8,128)(2,1)S(1)}, bf16[112,5120]{1,0:T(8,128)(2,1)S(1)}, u32[]{:S(2)}, u32[]{:S(2)}) collective-permute-start(bf16[112,5120]{1,0:T(8,128)(2,1)S(1)} %collective-permute-done.1.refs_10_), channel_id=1, source_target_pairs={{0,24},{1,25},{2,26},{3,27},{4,28},{5,29},{6,30},{7,31},{8,0},{9,1... | collective-permute-start | bytes 3440648 | tf_op jit(solution)/shard_map/r6/ppermute | solution.py:34
  46.4 25.5 %collective-permute-start.8 = (bf16[112,5120]{1,0:T(8,128)(2,1)S(1)}, bf16[112,5120]{1,0:T(8,128)(2,1)S(1)}, u32[]{:S(2)}, u32[]{:S(2)}) collective-permute-start(bf16[112,5120]{1,0:T(8,128)(2,1)S(1)} %collective-permute-done.1.refs_10_), channel_id=1, source_target_pairs={{0,8},{1,33},{2,10},{3,35},{4,12},{5,37},{6,14},{7,39},{8,16},{9,4... | collective-permute-start | bytes 3440648 | tf_op jit(solution)/shard_map/r4/ppermute | solution.py:34
  47.8 9.7 %collective-permute-start.11 = (bf16[512,640]{1,0:T(8,128)(2,1)S(1)}, bf16[512,640]{1,0:T(8,128)(2,1)S(1)}, u32[]{:S(2)}, u32[]{:S(2)}) collective-permute-start(bf16[512,640]{1,0:T(8,128)(2,1)S(1)} %collective-permute-done.6.refs_1_), channel_id=1, source_target_pairs={{0,2},{1,7},{2,4},{3,1},{4,6},{5,3},{6,0},{7,5},{8,10},{9,15},{10,... | collective-permute-start | bytes 1966088 | tf_op jit(solution)/shard_map/b_far/ppermute | solution.py:34
  48.0 28.8 %collective-permute-start.9 = (bf16[112,5120]{1,0:T(8,128)(2,1)}, bf16[112,5120]{1,0:T(8,128)(2,1)}, u32[]{:S(2)}, u32[]{:S(2)}) collective-permute-start(bf16[112,5120]{1,0:T(8,128)(2,1)} %collective-permute-done.refs_9_), channel_id=1, source_target_pairs={{0,8},{1,33},{2,10},{3,35},{4,12},{5,37},{6,14},{7,39},{8,16},{9,4... | collective-permute-start | bytes 3440648 | tf_op jit(solution)/shard_map/r5/ppermute | solution.py:34
  48.9 28.0 %collective-permute-start.14 = (bf16[512,640]{1,0:T(8,128)(2,1)S(1)}, bf16[512,640]{1,0:T(8,128)(2,1)S(1)}, u32[]{:S(2)}, u32[]{:S(2)}) collective-permute-start(bf16[512,640]{1,0:T(8,128)(2,1)S(1)} %collective-permute-done.6.refs_1_), channel_id=1, source_target_pairs={{0,1},{1,0},{2,3},{3,2},{4,5},{5,4},{6,7},{7,6},{8,9},{9,8},{10,11... | collective-permute-start | bytes 1966088 | tf_op jit(solution)/shard_map/b_swap/ppermute | solution.py:34
  57.5 19.3 %collective-permute-start.12 = (bf16[512,640]{1,0:T(8,128)(2,1)S(1)}, bf16[512,640]{1,0:T(8,128)(2,1)}, u32[]{:S(2)}, u32[]{:S(2)}) collective-permute-start(bf16[512,640]{1,0:T(8,128)(2,1)S(1)} %collective-permute-done.2.refs_0_), channel_id=1, source_target_pairs={{0,1},{1,0},{2,3},{3,2},{4,5},{5,4},{6,7},{7,6},{8,9},{9,8},{10,11... | collective-permute-start | bytes 1966088 | tf_op jit(solution)/shard_map/b_swap/ppermute | solution.py:34
  70.0 6.8 %collective-permute-start.13 = (bf16[512,640]{1,0:T(8,128)(2,1)S(1)}, bf16[512,640]{1,0:T(8,128)(2,1)}, u32[]{:S(2)}, u32[]{:S(2)}) collective-permute-start(bf16[512,640]{1,0:T(8,128)(2,1)S(1)} %collective-permute-done.7.refs_2_), channel_id=1, source_target_pairs={{0,1},{1,0},{2,3},{3,2},{4,5},{5,4},{6,7},{7,6},{8,9},{9,8},{10,11... | collective-permute-start | bytes 1966088 | tf_op jit(solution)/shard_map/b_swap/ppermute | solution.py:34
  72.9 4.0 %collective-permute-start.15 = (bf16[512,640]{1,0:T(8,128)(2,1)S(1)}, bf16[512,640]{1,0:T(8,128)(2,1)}, u32[]{:S(2)}, u32[]{:S(2)}) collective-permute-start(bf16[512,640]{1,0:T(8,128)(2,1)S(1)} %collective-permute-done.11.refs_3_), channel_id=1, source_target_pairs={{0,1},{1,0},{2,3},{3,2},{4,5},{5,4},{6,7},{7,6},{8,9},{9,8},{10,11... | collective-permute-start | bytes 1966088 | tf_op jit(solution)/shard_map/b_swap/ppermute | solution.py:34
  85.7 9.8 %collective-permute-start.16 = (bf16[512,640]{1,0:T(8,128)(2,1)S(1)}, bf16[512,640]{1,0:T(8,128)(2,1)S(1)}, u32[]{:S(2)}, u32[]{:S(2)}) collective-permute-start(bf16[512,640]{1,0:T(8,128)(2,1)S(1)} %copy-done.16), channel_id=1, source_target_pairs={{0,2},{1,7},{2,4},{3,1},{4,6},{5,3},{6,0},{7,5},{8,10},{9,15},{10,... | collective-permute-start | bytes 1966088 | tf_op jit(solution)/shard_map/a_far/ppermute | solution.py:34
  85.8 12.0 %collective-permute-start.18 = (bf16[512,640]{1,0:T(8,128)(2,1)}, bf16[512,640]{1,0:T(8,128)(2,1)S(1)}, u32[]{:S(2)}, u32[]{:S(2)}) collective-permute-start(bf16[512,640]{1,0:T(8,128)(2,1)} %collective-permute-done.4.refs_2_), channel_id=1, source_target_pairs={{0,1},{1,0},{2,3},{3,2},{4,5},{5,4},{6,7},{7,6},{8,9},{9,8},{10,11... | collective-permute-start | bytes 1966088 | tf_op jit(solution)/shard_map/a_swap/ppermute | solution.py:34
  86.1 27.5 %collective-permute-start.22 = (bf16[112,5120]{1,0:T(8,128)(2,1)S(1)}, bf16[112,5120]{1,0:T(8,128)(2,1)S(1)}, u32[]{:S(2)}, u32[]{:S(2)}) collective-permute-start(bf16[112,5120]{1,0:T(8,128)(2,1)S(1)} %copy-done.4), channel_id=1, source_target_pairs={{0,24},{1,33},{2,26},{3,35},{4,28},{5,37},{6,30},{7,39},{8,0},{9,4... | collective-permute-start | bytes 3440648 | tf_op jit(solution)/shard_map/r7/ppermute | solution.py:34
  87.2 18.9 %collective-permute-start.19 = (bf16[512,640]{1,0:T(8,128)(2,1)S(1)}, bf16[512,640]{1,0:T(8,128)(2,1)S(1)}, u32[]{:S(2)}, u32[]{:S(2)}) collective-permute-start(bf16[512,640]{1,0:T(8,128)(2,1)S(1)} %copy-done.16), channel_id=1, source_target_pairs={{0,1},{1,0},{2,3},{3,2},{4,5},{5,4},{6,7},{7,6},{8,9},{9,8},{10,11... | collective-permute-start | bytes 1966088 | tf_op jit(solution)/shard_map/a_swap/ppermute | solution.py:34
  90.1 16.0 %collective-permute-start.17 = (bf16[512,640]{1,0:T(8,128)(2,1)S(1)}, bf16[512,640]{1,0:T(8,128)(2,1)S(1)}, u32[]{:S(2)}, u32[]{:S(2)}) collective-permute-start(bf16[512,640]{1,0:T(8,128)(2,1)S(1)} %copy-done.2), channel_id=1, source_target_pairs={{0,1},{1,0},{2,3},{3,2},{4,5},{5,4},{6,7},{7,6},{8,9},{9,8},{10,11... | collective-permute-start | bytes 1966088 | tf_op jit(solution)/shard_map/a_swap/ppermute | solution.py:34
  95.5 10.6 %collective-permute-start.20 = (bf16[512,640]{1,0:T(8,128)(2,1)S(1)}, bf16[512,640]{1,0:T(8,128)(2,1)S(1)}, u32[]{:S(2)}, u32[]{:S(2)}) collective-permute-start(bf16[512,640]{1,0:T(8,128)(2,1)S(1)} %collective-permute-done.16.refs_3_), channel_id=1, source_target_pairs={{0,1},{1,0},{2,3},{3,2},{4,5},{5,4},{6,7},{7,6},{8,9},{9,8},{10,11... | collective-permute-start | bytes 1966088 | tf_op jit(solution)/shard_map/a_swap/ppermute | solution.py:34
  97.8 15.8 %collective-permute-start.21 = (bf16[512,512]{1,0:T(8,128)(2,1)S(1)}, bf16[512,512]{1,0:T(8,128)(2,1)S(1)}, u32[]{:S(2)}, u32[]{:S(2)}) collective-permute-start(bf16[512,512]{1,0:T(8,128)(2,1)S(1)} %product.5), channel_id=1, source_target_pairs={{0,96},{1,97},{2,98},{3,99},{4,100},{5,101},{6,102},{7,103},{8,104... | collective-permute-start | bytes 1572872 | tf_op jit(solution)/shard_map/mate_grad1/ppermute | solution.py:34
  115.3 9.2 %collective-permute-start.25 = (f32[256,192]{1,0:T(8,128)S(1)}, f32[256,192]{1,0:T(8,128)S(1)}, u32[]{:S(2)}, u32[]{:S(2)}) collective-permute-start(f32[256,192]{1,0:T(8,128)S(1)} %select_add_fusion), channel_id=1, source_target_pairs={{0,4},{1,5},{2,6},{3,7},{4,0},{5,1},{6,2},{7,3},{8,12},{9,13},{10,... | collective-permute-start | bytes 589832 | tf_op jit(solution)/shard_map/send/ppermute | solution.py:34
  115.4 14.9 %collective-permute-start.26 = (f32[256,192]{1,0:T(8,128)S(1)}, f32[256,192]{1,0:T(8,128)S(1)}, u32[]{:S(2)}, u32[]{:S(2)}) collective-permute-start(f32[256,192]{1,0:T(8,128)S(1)} %select_add_fusion), channel_id=1, source_target_pairs={{0,2},{1,3},{2,4},{3,5},{4,6},{5,7},{6,0},{7,1},{8,10},{9,11},{10,... | collective-permute-start | bytes 589832 | tf_op jit(solution)/shard_map/up/ppermute | solution.py:34
  115.5 14.8 %collective-permute-start.27 = (f32[256,192]{1,0:T(8,128)S(1)}, f32[256,192]{1,0:T(8,128)S(1)}, u32[]{:S(2)}, u32[]{:S(2)}) collective-permute-start(f32[256,192]{1,0:T(8,128)S(1)} %select_add_fusion), channel_id=1, source_target_pairs={{0,6},{1,7},{2,0},{3,1},{4,2},{5,3},{6,4},{7,5},{8,14},{9,15},{10,... | collective-permute-start | bytes 589832 | tf_op jit(solution)/shard_map/down/ppermute | solution.py:34
  118.2 18.3 %collective-permute-start.23 = (bf16[512,384]{1,0:T(8,128)(2,1)S(1)}, bf16[512,384]{1,0:T(8,128)(2,1)S(1)}, u32[]{:S(2)}, u32[]{:S(2)}) collective-permute-start(bf16[512,384]{1,0:T(8,128)(2,1)S(1)} %product.6), channel_id=1, source_target_pairs={{0,96},{1,97},{2,98},{3,99},{4,100},{5,101},{6,102},{7,103},{8,104... | collective-permute-start | bytes 1179656 | tf_op jit(solution)/shard_map/mate_grad2/ppermute | solution.py:34
  130.4 12.6 %collective-permute-start.28 = (f32[256,192]{1,0:T(8,128)S(1)}, f32[256,192]{1,0:T(8,128)S(1)}, u32[]{:S(2)}, u32[]{:S(2)}) collective-permute-start(f32[256,192]{1,0:T(8,128)S(1)} %add_add_fusion), channel_id=1, source_target_pairs={{0,1},{1,0},{2,3},{3,2},{4,5},{5,4},{6,7},{7,6},{8,9},{9,8},{10,11... | collective-permute-start | bytes 589832 | tf_op jit(solution)/shard_map/swap/ppermute | solution.py:34
  134.3 9.8 %collective-permute-start.29 = (bf16[512,128]{1,0:T(8,128)(2,1)S(1)}, bf16[512,128]{1,0:T(8,128)(2,1)S(1)}, u32[]{:S(2)}, u32[]{:S(2)}) collective-permute-start(bf16[512,128]{1,0:T(8,128)(2,1)S(1)} %product.8), channel_id=1, source_target_pairs={{0,96},{1,97},{2,98},{3,99},{4,100},{5,101},{6,102},{7,103},{8,104... | collective-permute-start | bytes 393224 | tf_op jit(solution)/shard_map/mate_grad3/ppermute | solution.py:34
  149.9 4.8 %collective-permute-start.31 = (f32[128,128]{1,0:T(8,128)S(1)}, f32[128,128]{1,0:T(8,128)S(1)}, u32[]{:S(2)}, u32[]{:S(2)}) collective-permute-start(f32[128,128]{1,0:T(8,128)S(1)} %select_add_fusion.1), channel_id=1, source_target_pairs={{0,4},{1,5},{2,6},{3,7},{4,0},{5,1},{6,2},{7,3},{8,12},{9,13},{10,... | collective-permute-start | bytes 196616 | tf_op jit(solution)/shard_map/send/ppermute | solution.py:34
  150.2 6.5 %collective-permute-start.32 = (f32[128,128]{1,0:T(8,128)S(1)}, f32[128,128]{1,0:T(8,128)S(1)}, u32[]{:S(2)}, u32[]{:S(2)}) collective-permute-start(f32[128,128]{1,0:T(8,128)S(1)} %select_add_fusion.1), channel_id=1, source_target_pairs={{0,2},{1,3},{2,4},{3,5},{4,6},{5,7},{6,0},{7,1},{8,10},{9,11},{10,... | collective-permute-start | bytes 196616 | tf_op jit(solution)/shard_map/up/ppermute | solution.py:34
  151.1 5.6 %collective-permute-start.33 = (f32[128,128]{1,0:T(8,128)S(1)}, f32[128,128]{1,0:T(8,128)S(1)}, u32[]{:S(2)}, u32[]{:S(2)}) collective-permute-start(f32[128,128]{1,0:T(8,128)S(1)} %select_add_fusion.1), channel_id=1, source_target_pairs={{0,6},{1,7},{2,0},{3,1},{4,2},{5,3},{6,4},{7,5},{8,14},{9,15},{10,... | collective-permute-start | bytes 196616 | tf_op jit(solution)/shard_map/down/ppermute | solution.py:34
  (23 other events, 134.6 us)

commit v6 on v5

--- a/solution.py
+++ b/solution.py
@@ -90,18 +90,19 @@
 
 
 def product_kernel(shards, where_ref, *refs):
-    mine, other, weights = refs[:4], refs[4:8], refs[8 : 8 + shards]
-    out_ref, *acc = refs[8 + shards :]
+    mine, near, far, weights = refs[:4], refs[4], refs[5], refs[6 : 6 + shards]
+    out_ref, *acc = refs[6 + shards :]
     acc = acc[0] if acc else out_ref
     y, c = where_ref[16], where_ref[17]
     for step, shift in enumerate((0, 3 - 2 * c, 1 + 2 * c, 2)):
         first = lax.rem(y + shift, 4) * STEP
-        near, far = (pl.multiple_of(first + core * FEAT, 128) for core in (c, 1 - c))
-        left = jnp.concatenate([mine[step][...], other[step][...]], axis=1)
+        lane, swapped = (pl.multiple_of(first + core * FEAT, 128) for core in (c, 1 - c))
+        other = near[step * ROWS : step * ROWS + ROWS, :] if step < 3 else far[...]
+        left = jnp.concatenate([mine[step][...], other], axis=1)
         rows = []
         for k, w in enumerate(weights):
             rows.append(
-                jnp.concatenate([w[:, pl.ds(near, FEAT)], w[:, pl.ds(far, FEAT)]], axis=1)
+                jnp.concatenate([w[:, pl.ds(lane, FEAT)], w[:, pl.ds(swapped, FEAT)]], axis=1)
             )
             if shards > 1:
                 rows.append(jnp.zeros((128 - SHARD, STEP), BF16))
@@ -122,7 +123,7 @@
     return pl.pallas_call(
         functools.partial(product_kernel, shards),
         out_shape=jax.ShapeDtypeStruct((ROWS, width), dtype),
-        in_specs=[pl.BlockSpec(memory_space=pltpu.SMEM)] + [vmem] * (8 + shards),
+        in_specs=[pl.BlockSpec(memory_space=pltpu.SMEM)] + [vmem] * (6 + shards),
         out_specs=vmem,
         scratch_shapes=[] if dtype == F32 else [pltpu.VMEM((ROWS, width), F32)],
         compiler_params=pltpu.CompilerParams(
@@ -340,12 +341,16 @@
             lengths,
         ]
     ).astype(jnp.int32)
+    pm_t, ph_t = proj_model.T, proj_hidden.T
     own_w = down_weight
     theirs = mate(out_grad, "mate_rows")
     a1, a2 = along_y(out_grad, 1, "a1"), along_y(out_grad, -1, "a2")
     r1 = route(own_w, "+", "+", "r1")
     r2 = route(own_w, "p", "-", "r2")
-    theirs, a1, a2, again = lax.optimization_barrier((theirs, a1, a2, own_w))
+    parts = early(where, activations, out_grad, pm_t, gate_pre, up_pre, ph_t)
+    theirs, a1, a2, again, parts, where = lax.optimization_barrier(
+        (theirs, a1, a2, own_w, parts, where)
+    )
     r3 = route(again, "-", "p", "r3")
     b1, b2 = along_y(theirs, 1, "b1"), along_y(theirs, -1, "b2")
     r1, r2, r3, b1, b2 = lax.optimization_barrier((r1, r2, r3, b1, b2))
@@ -353,29 +358,24 @@
     r4 = route(r2, "+", "p", "r4")
     r5 = route(r1, "+", "p", "r5")
     b_far = along_y(b1, 1, "b_far")
-    b_other = [swap(v, "b_swap") for v in (after(theirs, b1), b2, b1, b_far)]
+    b_other = [swap(jnp.concatenate([theirs, b2, b1]), "b_swap"), swap(b_far, "b_swap")]
+    a_far = along_y(after(a1, b_far), 1, "a_far")
     b_mine = [theirs, b1, b2, b_far]
+    h1 = product(BF16, after(where, r4, r5, r6, a_far), b_mine, b_other, [own_w, r1, r2, r3])
     r7 = route(r6, "-", "p", "r7")
-    h1 = product(BF16, after(where, r4, r5, r6), b_mine, b_other, [own_w, r1, r2, r3])
     h1_in = mate(h1, "mate_grad1")
-    a_far = along_y(after(a1, h1), 1, "a_far")
     h2 = product(BF16, after(where, h1), b_mine, b_other, [r4, r5, r6])
     h2_in = mate(h2, "mate_grad2")
     a_mine = [out_grad, a1, a2, a_far]
-    a_other = [swap(v, "a_swap") for v in (after(out_grad, h1), after(a2, h1), after(a1, h1), a_far)]
-
-    pm_t, ph_t = proj_model.T, proj_hidden.T
-    own1 = product(
-        F32, after(where, h2), a_mine, a_other, [own_w, r1, r2, r3, r4, r5, r6]
-    )
-    parts = early(after(where, h2), activations, out_grad, pm_t, gate_pre, up_pre, ph_t)
-    sums = sum_tensor(after(parts, r7, h1_in, own1), c)
-    *spread, down_feat = spread_features(where, sums)
-
-    h3 = product(BF16, after(where, h2, h1_in, own1), b_mine, b_other, [r7])
+    near = jnp.concatenate([out_grad, a2, a1])
+    a_other = [swap(after(near, h1), "a_swap"), swap(a_far, "a_swap")]
+    own1 = product(F32, after(where, h2, h1_in), a_mine, a_other, [own_w, r1, r2, r3, r4, r5, r6])
+    sums = sum_tensor(after(parts, own1), c)
+    h3 = product(BF16, after(where, h2, own1), b_mine, b_other, [r7])
     own2 = product(F32, after(where, h3, h2_in), a_mine, a_other, [r7])
     h_in = [h1_in, h2_in, mate(h3, "mate_grad3")]
     grad_gate, grad_up, part = own_half(where, gate_pre, up_pre, (own1, own2), ph_t)
+    *spread, down_feat = spread_features(after(where, part), sums)
     grad_gate, grad_up, feat = other_half(
         where, gate_pre, up_pre, h_in, ph_t, part, spread, grad_gate, grad_up
     )

time: 160 us -> 148 us (0.925)
  starting transfers between devices: 43.4 us -> 34.3 us
  Pallas kernels: 34.7 us -> 30.6 us
    ppermute x35 -> x31, starting transfers between devices: 43.4 us -> 34.3 us  [send(): return lax.ppermute(value, AXES, pairs)]
    pallas_call x5, Pallas kernels: 23 us -> 18.9 us  [product(): pl.pallas_call(functools.partial(product_kernel, shards), out_shape=jax.S...]
    ppermute x35 -> x31, waiting for transfers between devices: 68.2 us -> 69.1 us  [send(): return lax.ppermute(value, AXES, pairs)]
    unnamed x40 -> x22, local copies, waits for them, and re-layouts: 7.87 us -> 7.23 us
  transfers between devices with their start and end apart: 35 -> 31, of which waited for: 16 -> 16; matrix products, arithmetic and copies ran while one was open for 2% -> 2% of each run, Pallas kernels for 16% -> 15%
where the time goes in v6:
time: 148 us; the launch traced here: 147 us
  waiting for transfers between devices  69.1 us (47%)
  starting transfers between devices  34.3 us (23%)
  Pallas kernels  30.6 us (21%)
  local copies, waits for them, and re-layouts  10.2 us (7%)
  other arithmetic  2.16 us (1%)
    ppermute x31, waiting for transfers between devices, send(): return lax.ppermute(value, AXES, pairs)  69.1 us
    ppermute x31, starting transfers between devices, send(): return lax.ppermute(value, AXES, pairs)  34.3 us
    pallas_call x5, Pallas kernels, product(): pl.pallas_call(functools.partial(product_kernel, shards), out_shape=jax.S...  18.9 us
    unnamed x22, local copies, waits for them, and re-layouts  7.23 us
    pallas_call x1, Pallas kernels, other_half(): pl.pallas_call(functools.partial(other_kernel, len(h)), out_shape=(BIG, B...  4.44 us
    pallas_call x1, Pallas kernels, own_half(): pl.pallas_call(functools.partial(own_kernel, len(h)), out_shape=(BIG, BIG...  3.82 us
  transfers between devices with their start and end apart: 31, of which 16 were waited for; matrix products, arithmetic and copies ran while one was open for 2% of the time, Pallas kernels for 15%

profile of v6, /device:TPU:1, one launch (start us, length us, event | category | flops | bytes accessed | tf_op | source)
XLA Modules:
  0.0 147.2 jit_solution(16801750812055225117)
XLA Ops:
  0.6 4.7 %collective-permute-start = (bf16[512,640]{1,0:T(8,128)(2,1)}, bf16[512,640]{1,0:T(8,128)(2,1)S(1)}, u32[]{:S(2)}, u32[]{:S(2)}) collective-permute-start(bf16[512,640]{1,0:T(8,128)(2,1)} %refs_0_.3), channel_id=1, source_target_pairs={{0,96},{1,97},{2,98},{3,99},{4,100},{5,101},{6,102},{7,103},{8,104... | collective-permute-start | bytes 1966088 | tf_op jit(solution)/shard_map/mate_rows/ppermute | solution.py:34
  5.3 2.7 %collective-permute-start.1 = (bf16[512,640]{1,0:T(8,128)(2,1)}, bf16[512,640]{1,0:T(8,128)(2,1)S(1)}, u32[]{:S(2)}, u32[]{:S(2)}) collective-permute-start(bf16[512,640]{1,0:T(8,128)(2,1)} %refs_0_.3), channel_id=1, source_target_pairs={{0,2},{1,7},{2,4},{3,1},{4,6},{5,3},{6,0},{7,5},{8,10},{9,15},{10,... | collective-permute-start | bytes 1966088 | tf_op jit(solution)/shard_map/a1/ppermute | solution.py:34
  9.2 1.5 collective-permute-start.4
  10.7 1.4 reduce_sum.29
  12.4 1.4 concatenate.18.where_ref
  13.8 1.5 %copy-done = bf16[512,1792]{1,0:T(8,128)(2,1)S(1)} copy-done((bf16[512,1792]{1,0:T(8,128)(2,1)S(1)}, bf16[512,1792]{1,0:T(8,128)(2,1)}, u32[]{:S(2)}) %copy-start) | copy-done | bytes 1835032
  15.3 1.5 %copy-done.2 = bf16[512,1792]{1,0:T(8,128)(2,1)S(1)} copy-done((bf16[512,1792]{1,0:T(8,128)(2,1)S(1)}, bf16[512,1792]{1,0:T(8,128)(2,1)}, u32[]{:S(2)}) %copy-start.2) | copy-done | bytes 1835032
  21.0 2.4 %early.1 = f32[512,192]{1,0:T(8,128)S(1)} custom-call(s32[24]{0:T(128)S(1)} %concatenate.18.where_ref, bf16[512,640]{1,0:T(8,128)(2,1)S(1)} %copy-done.9, bf16[512,640]{1,0:T(8,128)(2,1)S(1)} %copy-done.4, bf16[64,5120]{1,0:T(8,128)(2,1)S(1)} %bitcast.32, bf16[512,1792]{1,0:T(8,128)(2,1)S(1)} %copy-done, bf16[512,1792]{1,0:T(8,128)(2,1)S(1)} %copy-done.2, ...), custom_call_target="tpu_custom_call" | custom-call | flops 1048576 | bytes 65536 | tf_op jit(solution)/shard_map/early/pallas_call | solution.py:149
  23.5 1.4 collective-permute-done.2.refs_2_
  24.9 1.4 collective-permute-start.6
  26.4 8.4 %collective-permute-done.3.refs_7_ = bf16[112,5120]{1,0:T(8,128)(2,1)S(1)} collective-permute-done((bf16[112,5120]{1,0:T(8,128)(2,1)}, bf16[112,5120]{1,0:T(8,128)(2,1)S(1)}, u32[]{:S(2)}, u32[]{:S(2)}) %collective-permute-start.3) | collective-permute-done | bytes 1146912 | tf_op jit(solution)/shard_map/r1/ppermute | solution.py:34
  34.8 2.9 %collective-permute-done.6.refs_1_ = bf16[512,640]{1,0:T(8,128)(2,1)S(1)} collective-permute-done((bf16[512,640]{1,0:T(8,128)(2,1)S(1)}, bf16[512,640]{1,0:T(8,128)(2,1)S(1)}, u32[]{:S(2)}, u32[]{:S(2)}) %collective-permute-start.6) | collective-permute-done | bytes 655392 | tf_op jit(solution)/shard_map/b1/ppermute | solution.py:34
  37.7 5.8 %collective-permute-done.7.refs_2_ = bf16[512,640]{1,0:T(8,128)(2,1)S(1)} collective-permute-done((bf16[512,640]{1,0:T(8,128)(2,1)S(1)}, bf16[512,640]{1,0:T(8,128)(2,1)S(1)}, u32[]{:S(2)}, u32[]{:S(2)}) %collective-permute-start.7) | collective-permute-done | bytes 655392 | tf_op jit(solution)/shard_map/b2/ppermute | solution.py:34
  47.9 8.1 %collective-permute-done.11.refs_3_ = bf16[512,640]{1,0:T(8,128)(2,1)S(1)} collective-permute-done((bf16[512,640]{1,0:T(8,128)(2,1)S(1)}, bf16[512,640]{1,0:T(8,128)(2,1)S(1)}, u32[]{:S(2)}, u32[]{:S(2)}) %collective-permute-start.11) | collective-permute-done | bytes 655392 | tf_op jit(solution)/shard_map/b_far/ppermute | solution.py:34
  55.9 1.4 collective-permute-start.12
  57.4 14.6 %collective-permute-done.10.refs_8_.refs_12_ = bf16[112,5120]{1,0:T(8,128)(2,1)S(1)} collective-permute-done((bf16[112,5120]{1,0:T(8,128)(2,1)}, bf16[112,5120]{1,0:T(8,128)(2,1)S(1)}, u32[]{:S(2)}, u32[]{:S(2)}) %collective-permute-start.10) | collective-permute-done | bytes 1146912 | tf_op jit(solution)/shard_map/r6/ppermute | solution.py:34
  74.6 4.2 %product.5 = bf16[512,512]{1,0:T(8,128)(2,1)S(1)} custom-call(s32[24]{0:T(128)S(1)} %concatenate.18.where_ref, bf16[512,640]{1,0:T(8,128)(2,1)S(1)} %collective-permute-done.refs_0_, bf16[512,640]{1,0:T(8,128)(2,1)S(1)} %collective-permute-done.6.refs_1_, bf16[512,640]{1,0:T(8,128)(2,1)S(1)} %collective-permute-done.7.refs_2_, ...), custom_call_target="tpu_custom_call" | custom-call | flops 1048576 | bytes 65536 | tf_op jit(solution)/shard_map/product/pallas_call | solution.py:123
  78.8 1.7 %collective-permute-start.16 = (bf16[1536,640]{1,0:T(8,128)(2,1)S(1)}, bf16[1536,640]{1,0:T(8,128)(2,1)S(1)}, u32[]{:S(2)}, u32[]{:S(2)}) collective-permute-start(bf16[1536,640]{1,0:T(8,128)(2,1)S(1)} %pad_maximum_fusion.1), channel_id=1, source_target_pairs={{0,1},{1,0},{2,3},{3,2},{4,5},{5,4},{6,7},{7,6},{8,9},{9,8},{10,11... | collective-permute-start | bytes 5898248 | tf_op jit(solution)/shard_map/a_swap/ppermute | solution.py:34
  81.9 3.4 %product.6 = bf16[512,384]{1,0:T(8,128)(2,1)S(1)} custom-call(s32[24]{0:T(128)S(1)} %concatenate.18.where_ref, bf16[512,640]{1,0:T(8,128)(2,1)S(1)} %collective-permute-done.refs_0_, bf16[512,640]{1,0:T(8,128)(2,1)S(1)} %collective-permute-done.6.refs_1_, bf16[512,640]{1,0:T(8,128)(2,1)S(1)} %collective-permute-done.7.refs_2_, ...), custom_call_target="tpu_custom_call" | custom-call | flops 1048576 | bytes 65536 | tf_op jit(solution)/shard_map/product/pallas_call | solution.py:123
  85.4 9.5 %collective-permute-done.15.refs_0_ = bf16[512,512]{1,0:T(8,128)(2,1)S(1)} collective-permute-done((bf16[512,512]{1,0:T(8,128)(2,1)S(1)}, bf16[512,512]{1,0:T(8,128)(2,1)S(1)}, u32[]{:S(2)}, u32[]{:S(2)}) %collective-permute-start.15) | collective-permute-done | bytes 524320 | tf_op jit(solution)/shard_map/mate_grad1/ppermute | solution.py:34
  94.9 6.9 %product.7.refs_0_ = f32[512,896]{1,0:T(8,128)S(1)} custom-call(s32[24]{0:T(128)S(1)} %concatenate.18.where_ref, bf16[512,640]{1,0:T(8,128)(2,1)S(1)} %copy-done.5, bf16[512,640]{1,0:T(8,128)(2,1)S(1)} %collective-permute-done.1.refs_1_, bf16[512,640]{1,0:T(8,128)(2,1)S(1)} %collective-permute-done.2.refs_2_, ...), custom_call_target="tpu_custom_call" | custom-call | flops 1048576 | bytes 65536 | tf_op jit(solution)/shard_map/product/pallas_call | solution.py:123
  104.4 1.7 %collective-permute-start.21 = (f32[256,192]{1,0:T(8,128)S(1)}, f32[256,192]{1,0:T(8,128)S(1)}, u32[]{:S(2)}, u32[]{:S(2)}) collective-permute-start(f32[256,192]{1,0:T(8,128)S(1)} %select_add_fusion), channel_id=1, source_target_pairs={{0,4},{1,5},{2,6},{3,7},{4,0},{5,1},{6,2},{7,3},{8,12},{9,13},{10,... | collective-permute-start | bytes 589832 | tf_op jit(solution)/shard_map/send/ppermute | solution.py:34
  106.1 1.9 %collective-permute-start.22 = (f32[256,192]{1,0:T(8,128)S(1)}, f32[256,192]{1,0:T(8,128)S(1)}, u32[]{:S(2)}, u32[]{:S(2)}) collective-permute-start(f32[256,192]{1,0:T(8,128)S(1)} %select_add_fusion), channel_id=1, source_target_pairs={{0,2},{1,3},{2,4},{3,5},{4,6},{5,7},{6,0},{7,1},{8,10},{9,11},{10,... | collective-permute-start | bytes 589832 | tf_op jit(solution)/shard_map/up/ppermute | solution.py:34
  108.8 4.7 %collective-permute-done.21 = f32[256,192]{1,0:T(8,128)S(1)} collective-permute-done((f32[256,192]{1,0:T(8,128)S(1)}, f32[256,192]{1,0:T(8,128)S(1)}, u32[]{:S(2)}, u32[]{:S(2)}) %collective-permute-start.21) | collective-permute-done | bytes 196640 | tf_op jit(solution)/shard_map/send/ppermute | solution.py:34
  113.5 6.3 %collective-permute-done.22 = f32[256,192]{1,0:T(8,128)S(1)} collective-permute-done((f32[256,192]{1,0:T(8,128)S(1)}, f32[256,192]{1,0:T(8,128)S(1)}, u32[]{:S(2)}, u32[]{:S(2)}) %collective-permute-start.22) | collective-permute-done | bytes 196640 | tf_op jit(solution)/shard_map/up/ppermute | solution.py:34
  121.0 2.2 %product.8 = bf16[512,128]{1,0:T(8,128)(2,1)S(1)} custom-call(s32[24]{0:T(128)S(1)} %concatenate.18.where_ref, bf16[512,640]{1,0:T(8,128)(2,1)S(1)} %collective-permute-done.refs_0_, bf16[512,640]{1,0:T(8,128)(2,1)S(1)} %collective-permute-done.6.refs_1_, bf16[512,640]{1,0:T(8,128)(2,1)S(1)} %collective-permute-done.7.refs_2_, ...), custom_call_target="tpu_custom_call" | custom-call | flops 1048576 | bytes 65536 | tf_op jit(solution)/shard_map/product/pallas_call | solution.py:123
  123.7 2.2 %product.9.refs_1_ = f32[512,128]{1,0:T(8,128)S(1)} custom-call(s32[24]{0:T(128)S(1)} %concatenate.18.where_ref, bf16[512,640]{1,0:T(8,128)(2,1)S(1)} %copy-done.5, bf16[512,640]{1,0:T(8,128)(2,1)S(1)} %collective-permute-done.1.refs_1_, bf16[512,640]{1,0:T(8,128)(2,1)S(1)} %collective-permute-done.2.refs_2_, ...), custom_call_target="tpu_custom_call" | custom-call | flops 1048576 | bytes 65536 | tf_op jit(solution)/shard_map/product/pallas_call | solution.py:123
  125.8 3.8 %own_half.1 = (bf16[512,1792]{1,0:T(8,128)(2,1)}, bf16[512,1792]{1,0:T(8,128)(2,1)}, f32[512,128]{1,0:T(8,128)S(1)}) custom-call(s32[24]{0:T(128)S(1)} %concatenate.18.where_ref, bf16[512,1792]{1,0:T(8,128)(2,1)S(1)} %copy-done.1, bf16[512,1792]{1,0:T(8,128)(2,1)S(1)} %copy-done.3, bf16[64,1792]{1,0:T(8,128)(2,1)S(1)} %bitcast.30, ...), custom_call_target="tpu_custom_call" | custom-call | flops 1048576 | bytes 65536 | tf_op jit(solution)/shard_map/own_half/pallas_call | solution.py:218
  130.8 4.4 %other_half.1 = (bf16[512,1792]{1,0:T(8,128)(2,1)}, bf16[512,1792]{1,0:T(8,128)(2,1)}, f32[256,128]{1,0:T(8,128)S(1)}) custom-call(s32[24]{0:T(128)S(1)} %concatenate.18.where_ref, bf16[512,1792]{1,0:T(8,128)(2,1)S(1)} %copy-done.1, bf16[512,1792]{1,0:T(8,128)(2,1)S(1)} %copy-done.3, ...), custom_call_target="tpu_custom_call", output_to_operand_aliasing={{0}: (7, {}), {1}: (8, {})} | custom-call | flops 1048576 | bytes 65536 | tf_op jit(solution)/shard_map/other_half/pallas_call | solution.py:262
  137.7 1.9 %collective-permute-start.28 = (f32[128,128]{1,0:T(8,128)S(1)}, f32[128,128]{1,0:T(8,128)S(1)}, u32[]{:S(2)}, u32[]{:S(2)}) collective-permute-start(f32[128,128]{1,0:T(8,128)S(1)} %select_add_fusion.1), channel_id=1, source_target_pairs={{0,2},{1,3},{2,4},{3,5},{4,6},{5,7},{6,0},{7,1},{8,10},{9,11},{10,... | collective-permute-start | bytes 196616 | tf_op jit(solution)/shard_map/up/ppermute | solution.py:34
  141.3 1.9 %collective-permute-done.28 = f32[128,128]{1,0:T(8,128)S(1)} collective-permute-done((f32[128,128]{1,0:T(8,128)S(1)}, f32[128,128]{1,0:T(8,128)S(1)}, u32[]{:S(2)}, u32[]{:S(2)}) %collective-permute-start.28) | collective-permute-done | bytes 65568 | tf_op jit(solution)/shard_map/up/ppermute | solution.py:34
  143.3 1.6 %collective-permute-start.30 = (f32[128,128]{1,0:T(8,128)S(1)}, f32[128,128]{1,0:T(8,128)S(1)}, u32[]{:S(2)}, u32[]{:S(2)}) collective-permute-start(f32[128,128]{1,0:T(8,128)S(1)} %add_add_fusion.1), channel_id=1, source_target_pairs={{0,1},{1,0},{2,3},{3,2},{4,5},{5,4},{6,7},{7,6},{8,9},{9,8},{10,11... | collective-permute-start | bytes 196616 | tf_op jit(solution)/shard_map/swap/ppermute | solution.py:34
  (82 shorter events, 26.9 us)
Async XLA Ops:
  0.6 22.8 %collective-permute-start = (bf16[512,640]{1,0:T(8,128)(2,1)}, bf16[512,640]{1,0:T(8,128)(2,1)S(1)}, u32[]{:S(2)}, u32[]{:S(2)}) collective-permute-start(bf16[512,640]{1,0:T(8,128)(2,1)} %refs_0_.3), channel_id=1, source_target_pairs={{0,96},{1,97},{2,98},{3,99},{4,100},{5,101},{6,102},{7,103},{8,104... | collective-permute-start | bytes 1966088 | tf_op jit(solution)/shard_map/mate_rows/ppermute | solution.py:34
  5.3 18.1 %collective-permute-start.1 = (bf16[512,640]{1,0:T(8,128)(2,1)}, bf16[512,640]{1,0:T(8,128)(2,1)S(1)}, u32[]{:S(2)}, u32[]{:S(2)}) collective-permute-start(bf16[512,640]{1,0:T(8,128)(2,1)} %refs_0_.3), channel_id=1, source_target_pairs={{0,2},{1,7},{2,4},{3,1},{4,6},{5,3},{6,0},{7,5},{8,10},{9,15},{10,... | collective-permute-start | bytes 1966088 | tf_op jit(solution)/shard_map/a1/ppermute | solution.py:34
  8.0 16.9 %collective-permute-start.2 = (bf16[512,640]{1,0:T(8,128)(2,1)}, bf16[512,640]{1,0:T(8,128)(2,1)S(1)}, u32[]{:S(2)}, u32[]{:S(2)}) collective-permute-start(bf16[512,640]{1,0:T(8,128)(2,1)} %refs_0_.3), channel_id=1, source_target_pairs={{0,6},{1,3},{2,0},{3,5},{4,2},{5,7},{6,4},{7,1},{8,14},{9,11},{10,... | collective-permute-start | bytes 1966088 | tf_op jit(solution)/shard_map/a2/ppermute | solution.py:34
  8.0 26.7 %collective-permute-start.3 = (bf16[112,5120]{1,0:T(8,128)(2,1)}, bf16[112,5120]{1,0:T(8,128)(2,1)S(1)}, u32[]{:S(2)}, u32[]{:S(2)}) collective-permute-start(bf16[112,5120]{1,0:T(8,128)(2,1)} %refs_6_.3), channel_id=1, source_target_pairs={{0,8},{1,9},{2,10},{3,11},{4,12},{5,13},{6,14},{7,15},{8,16},{9,17... | collective-permute-start | bytes 3440648 | tf_op jit(solution)/shard_map/r1/ppermute | solution.py:34
  9.2 25.5 %collective-permute-start.4 = (bf16[112,5120]{1,0:T(8,128)(2,1)}, bf16[112,5120]{1,0:T(8,128)(2,1)}, u32[]{:S(2)}, u32[]{:S(2)}) collective-permute-start(bf16[112,5120]{1,0:T(8,128)(2,1)} %refs_6_.3), channel_id=1, source_target_pairs={{0,32},{1,25},{2,34},{3,27},{4,36},{5,29},{6,38},{7,31},{8,40},{9,... | collective-permute-start | bytes 3440648 | tf_op jit(solution)/shard_map/r2/ppermute | solution.py:34
  23.4 49.4 %copy-start.5 = (bf16[512,640]{1,0:T(8,128)(2,1)S(1)}, bf16[512,640]{1,0:T(8,128)(2,1)}, u32[]{:S(2)}) copy-start(bf16[512,640]{1,0:T(8,128)(2,1)} %refs_0_.3) | copy-start | bytes 1966084
  24.9 18.6 %collective-permute-start.5 = (bf16[112,5120]{1,0:T(8,128)(2,1)S(1)}, bf16[112,5120]{1,0:T(8,128)(2,1)S(1)}, u32[]{:S(2)}, u32[]{:S(2)}) collective-permute-start(bf16[112,5120]{1,0:T(8,128)(2,1)S(1)} %copy-done.6), channel_id=1, source_target_pairs={{0,24},{1,33},{2,26},{3,35},{4,28},{5,37},{6,30},{7,39},{8,0},{9,4... | collective-permute-start | bytes 3440648 | tf_op jit(solution)/shard_map/r3/ppermute | solution.py:34
  24.9 12.8 %collective-permute-start.6 = (bf16[512,640]{1,0:T(8,128)(2,1)S(1)}, bf16[512,640]{1,0:T(8,128)(2,1)S(1)}, u32[]{:S(2)}, u32[]{:S(2)}) collective-permute-start(bf16[512,640]{1,0:T(8,128)(2,1)S(1)} %collective-permute-done.refs_0_), channel_id=1, source_target_pairs={{0,2},{1,7},{2,4},{3,1},{4,6},{5,3},{6,0},{7,5},{8,10},{9,15},{10,... | collective-permute-start | bytes 1966088 | tf_op jit(solution)/shard_map/b1/ppermute | solution.py:34
  26.3 17.2 %collective-permute-start.7 = (bf16[512,640]{1,0:T(8,128)(2,1)S(1)}, bf16[512,640]{1,0:T(8,128)(2,1)S(1)}, u32[]{:S(2)}, u32[]{:S(2)}) collective-permute-start(bf16[512,640]{1,0:T(8,128)(2,1)S(1)} %collective-permute-done.refs_0_), channel_id=1, source_target_pairs={{0,6},{1,3},{2,0},{3,5},{4,2},{5,7},{6,4},{7,1},{8,14},{9,11},{10,... | collective-permute-start | bytes 1966088 | tf_op jit(solution)/shard_map/b2/ppermute | solution.py:34
  43.6 30.9 %collective-permute-start.13 = (bf16[1536,640]{1,0:T(8,128)(2,1)S(1)}, bf16[1536,640]{1,0:T(8,128)(2,1)S(1)}, u32[]{:S(2)}, u32[]{:S(2)}) collective-permute-start(bf16[1536,640]{1,0:T(8,128)(2,1)S(1)} %pad_maximum_fusion), channel_id=1, source_target_pairs={{0,1},{1,0},{2,3},{3,2},{4,5},{5,4},{6,7},{7,6},{8,9},{9,8},{10,11... | collective-permute-start | bytes 5898248 | tf_op jit(solution)/shard_map/b_swap/ppermute | solution.py:34
  44.9 27.0 %collective-permute-start.10 = (bf16[112,5120]{1,0:T(8,128)(2,1)}, bf16[112,5120]{1,0:T(8,128)(2,1)S(1)}, u32[]{:S(2)}, u32[]{:S(2)}) collective-permute-start(bf16[112,5120]{1,0:T(8,128)(2,1)} %collective-permute-done.4.refs_8_), channel_id=1, source_target_pairs={{0,24},{1,25},{2,26},{3,27},{4,28},{5,29},{6,30},{7,31},{8,0},{9,1... | collective-permute-start | bytes 3440648 | tf_op jit(solution)/shard_map/r6/ppermute | solution.py:34
  46.2 9.7 %collective-permute-start.11 = (bf16[512,640]{1,0:T(8,128)(2,1)S(1)}, bf16[512,640]{1,0:T(8,128)(2,1)S(1)}, u32[]{:S(2)}, u32[]{:S(2)}) collective-permute-start(bf16[512,640]{1,0:T(8,128)(2,1)S(1)} %collective-permute-done.6.refs_1_), channel_id=1, source_target_pairs={{0,2},{1,7},{2,4},{3,1},{4,6},{5,3},{6,0},{7,5},{8,10},{9,15},{10,... | collective-permute-start | bytes 1966088 | tf_op jit(solution)/shard_map/b_far/ppermute | solution.py:34
  46.4 26.6 %collective-permute-start.8 = (bf16[112,5120]{1,0:T(8,128)(2,1)}, bf16[112,5120]{1,0:T(8,128)(2,1)S(1)}, u32[]{:S(2)}, u32[]{:S(2)}) collective-permute-start(bf16[112,5120]{1,0:T(8,128)(2,1)} %collective-permute-done.4.refs_8_), channel_id=1, source_target_pairs={{0,8},{1,33},{2,10},{3,35},{4,12},{5,37},{6,14},{7,39},{8,16},{9,4... | collective-permute-start | bytes 3440648 | tf_op jit(solution)/shard_map/r4/ppermute | solution.py:34
  47.6 26.3 %collective-permute-start.9 = (bf16[112,5120]{1,0:T(8,128)(2,1)S(1)}, bf16[112,5120]{1,0:T(8,128)(2,1)S(1)}, u32[]{:S(2)}, u32[]{:S(2)}) collective-permute-start(bf16[112,5120]{1,0:T(8,128)(2,1)S(1)} %collective-permute-done.3.refs_7_), channel_id=1, source_target_pairs={{0,8},{1,33},{2,10},{3,35},{4,12},{5,37},{6,14},{7,39},{8,16},{9,4... | collective-permute-start | bytes 3440648 | tf_op jit(solution)/shard_map/r5/ppermute | solution.py:34
  55.9 18.0 %collective-permute-start.12 = (bf16[512,640]{1,0:T(8,128)(2,1)S(1)}, bf16[512,640]{1,0:T(8,128)(2,1)S(1)}, u32[]{:S(2)}, u32[]{:S(2)}) collective-permute-start(bf16[512,640]{1,0:T(8,128)(2,1)S(1)} %collective-permute-done.1.refs_1_), channel_id=1, source_target_pairs={{0,2},{1,7},{2,4},{3,1},{4,6},{5,3},{6,0},{7,5},{8,10},{9,15},{10,... | collective-permute-start | bytes 1966088 | tf_op jit(solution)/shard_map/a_far/ppermute | solution.py:34
  72.0 2.6 %collective-permute-start.14 = (bf16[512,640]{1,0:T(8,128)(2,1)S(1)}, bf16[512,640]{1,0:T(8,128)(2,1)S(1)}, u32[]{:S(2)}, u32[]{:S(2)}) collective-permute-start(bf16[512,640]{1,0:T(8,128)(2,1)S(1)} %collective-permute-done.11.refs_3_), channel_id=1, source_target_pairs={{0,1},{1,0},{2,3},{3,2},{4,5},{5,4},{6,7},{7,6},{8,9},{9,8},{10,11... | collective-permute-start | bytes 1966088 | tf_op jit(solution)/shard_map/b_swap/ppermute | solution.py:34
  78.8 16.1 %collective-permute-start.16 = (bf16[1536,640]{1,0:T(8,128)(2,1)S(1)}, bf16[1536,640]{1,0:T(8,128)(2,1)S(1)}, u32[]{:S(2)}, u32[]{:S(2)}) collective-permute-start(bf16[1536,640]{1,0:T(8,128)(2,1)S(1)} %pad_maximum_fusion.1), channel_id=1, source_target_pairs={{0,1},{1,0},{2,3},{3,2},{4,5},{5,4},{6,7},{7,6},{8,9},{9,8},{10,11... | collective-permute-start | bytes 5898248 | tf_op jit(solution)/shard_map/a_swap/ppermute | solution.py:34
  80.5 14.4 %collective-permute-start.17 = (bf16[512,640]{1,0:T(8,128)(2,1)S(1)}, bf16[512,640]{1,0:T(8,128)(2,1)S(1)}, u32[]{:S(2)}, u32[]{:S(2)}) collective-permute-start(bf16[512,640]{1,0:T(8,128)(2,1)S(1)} %collective-permute-done.12.refs_3_), channel_id=1, source_target_pairs={{0,1},{1,0},{2,3},{3,2},{4,5},{5,4},{6,7},{7,6},{8,9},{9,8},{10,11... | collective-permute-start | bytes 1966088 | tf_op jit(solution)/shard_map/a_swap/ppermute | solution.py:34
  80.6 14.3 %collective-permute-start.15 = (bf16[512,512]{1,0:T(8,128)(2,1)S(1)}, bf16[512,512]{1,0:T(8,128)(2,1)S(1)}, u32[]{:S(2)}, u32[]{:S(2)}) collective-permute-start(bf16[512,512]{1,0:T(8,128)(2,1)S(1)} %product.5), channel_id=1, source_target_pairs={{0,96},{1,97},{2,98},{3,99},{4,100},{5,101},{6,102},{7,103},{8,104... | collective-permute-start | bytes 1572872 | tf_op jit(solution)/shard_map/mate_grad1/ppermute | solution.py:34
  80.6 40.4 %collective-permute-start.18 = (bf16[112,5120]{1,0:T(8,128)(2,1)S(1)}, bf16[112,5120]{1,0:T(8,128)(2,1)S(1)}, u32[]{:S(2)}, u32[]{:S(2)}) collective-permute-start(bf16[112,5120]{1,0:T(8,128)(2,1)S(1)} %collective-permute-done.10.refs_8_.refs_12_), channel_id=1, source_target_pairs={{0,24},{1,33},{2,26},{3,35},{4,28},{5,37},{6,30},{7,39},{8,0},{9,4... | collective-permute-start | bytes 3440648 | tf_op jit(solution)/shard_map/r7/ppermute | solution.py:34
  101.8 2.5 %collective-permute-start.20 = (f32[256,192]{1,0:T(8,128)S(1)}, f32[256,192]{1,0:T(8,128)S(1)}, u32[]{:S(2)}, u32[]{:S(2)}) collective-permute-start(f32[256,192]{1,0:T(8,128)S(1)} %slice_select_fusion), channel_id=1, source_target_pairs={{0,1},{1,0},{2,3},{3,2},{4,5},{5,4},{6,7},{7,6},{8,9},{9,8},{10,11... | collective-permute-start | bytes 589832 | tf_op jit(solution)/shard_map/swap/ppermute | solution.py:34
  104.4 9.1 %collective-permute-start.21 = (f32[256,192]{1,0:T(8,128)S(1)}, f32[256,192]{1,0:T(8,128)S(1)}, u32[]{:S(2)}, u32[]{:S(2)}) collective-permute-start(f32[256,192]{1,0:T(8,128)S(1)} %select_add_fusion), channel_id=1, source_target_pairs={{0,4},{1,5},{2,6},{3,7},{4,0},{5,1},{6,2},{7,3},{8,12},{9,13},{10,... | collective-permute-start | bytes 589832 | tf_op jit(solution)/shard_map/send/ppermute | solution.py:34
  106.1 13.7 %collective-permute-start.22 = (f32[256,192]{1,0:T(8,128)S(1)}, f32[256,192]{1,0:T(8,128)S(1)}, u32[]{:S(2)}, u32[]{:S(2)}) collective-permute-start(f32[256,192]{1,0:T(8,128)S(1)} %select_add_fusion), channel_id=1, source_target_pairs={{0,2},{1,3},{2,4},{3,5},{4,6},{5,7},{6,0},{7,1},{8,10},{9,11},{10,... | collective-permute-start | bytes 589832 | tf_op jit(solution)/shard_map/up/ppermute | solution.py:34
  108.0 11.9 %collective-permute-start.23 = (f32[256,192]{1,0:T(8,128)S(1)}, f32[256,192]{1,0:T(8,128)S(1)}, u32[]{:S(2)}, u32[]{:S(2)}) collective-permute-start(f32[256,192]{1,0:T(8,128)S(1)} %select_add_fusion), channel_id=1, source_target_pairs={{0,6},{1,7},{2,0},{3,1},{4,2},{5,3},{6,4},{7,5},{8,14},{9,15},{10,... | collective-permute-start | bytes 589832 | tf_op jit(solution)/shard_map/down/ppermute | solution.py:34
  108.7 14.9 %collective-permute-start.19 = (bf16[512,384]{1,0:T(8,128)(2,1)S(1)}, bf16[512,384]{1,0:T(8,128)(2,1)S(1)}, u32[]{:S(2)}, u32[]{:S(2)}) collective-permute-start(bf16[512,384]{1,0:T(8,128)(2,1)S(1)} %product.6), channel_id=1, source_target_pairs={{0,96},{1,97},{2,98},{3,99},{4,100},{5,101},{6,102},{7,103},{8,104... | collective-permute-start | bytes 1179656 | tf_op jit(solution)/shard_map/mate_grad2/ppermute | solution.py:34
  119.9 9.8 %collective-permute-start.24 = (f32[256,192]{1,0:T(8,128)S(1)}, f32[256,192]{1,0:T(8,128)S(1)}, u32[]{:S(2)}, u32[]{:S(2)}) collective-permute-start(f32[256,192]{1,0:T(8,128)S(1)} %add_add_fusion), channel_id=1, source_target_pairs={{0,1},{1,0},{2,3},{3,2},{4,5},{5,4},{6,7},{7,6},{8,9},{9,8},{10,11... | collective-permute-start | bytes 589832 | tf_op jit(solution)/shard_map/swap/ppermute | solution.py:34
  123.2 7.6 %collective-permute-start.25 = (bf16[512,128]{1,0:T(8,128)(2,1)S(1)}, bf16[512,128]{1,0:T(8,128)(2,1)S(1)}, u32[]{:S(2)}, u32[]{:S(2)}) collective-permute-start(bf16[512,128]{1,0:T(8,128)(2,1)S(1)} %product.8), channel_id=1, source_target_pairs={{0,96},{1,97},{2,98},{3,99},{4,100},{5,101},{6,102},{7,103},{8,104... | collective-permute-start | bytes 393224 | tf_op jit(solution)/shard_map/mate_grad3/ppermute | solution.py:34
  135.3 1.3 collective-permute-start.26
  136.6 4.7 %collective-permute-start.27 = (f32[128,128]{1,0:T(8,128)S(1)}, f32[128,128]{1,0:T(8,128)S(1)}, u32[]{:S(2)}, u32[]{:S(2)}) collective-permute-start(f32[128,128]{1,0:T(8,128)S(1)} %select_add_fusion.1), channel_id=1, source_target_pairs={{0,4},{1,5},{2,6},{3,7},{4,0},{5,1},{6,2},{7,3},{8,12},{9,13},{10,... | collective-permute-start | bytes 196616 | tf_op jit(solution)/shard_map/send/ppermute | solution.py:34
  137.7 5.5 %collective-permute-start.28 = (f32[128,128]{1,0:T(8,128)S(1)}, f32[128,128]{1,0:T(8,128)S(1)}, u32[]{:S(2)}, u32[]{:S(2)}) collective-permute-start(f32[128,128]{1,0:T(8,128)S(1)} %select_add_fusion.1), channel_id=1, source_target_pairs={{0,2},{1,3},{2,4},{3,5},{4,6},{5,7},{6,0},{7,1},{8,10},{9,11},{10,... | collective-permute-start | bytes 196616 | tf_op jit(solution)/shard_map/up/ppermute | solution.py:34
  139.6 3.6 %collective-permute-start.29 = (f32[128,128]{1,0:T(8,128)S(1)}, f32[128,128]{1,0:T(8,128)S(1)}, u32[]{:S(2)}, u32[]{:S(2)}) collective-permute-start(f32[128,128]{1,0:T(8,128)S(1)} %select_add_fusion.1), channel_id=1, source_target_pairs={{0,6},{1,7},{2,0},{3,1},{4,2},{5,3},{6,4},{7,5},{8,14},{9,15},{10,... | collective-permute-start | bytes 196616 | tf_op jit(solution)/shard_map/down/ppermute | solution.py:34
  143.3 2.5 %collective-permute-start.30 = (f32[128,128]{1,0:T(8,128)S(1)}, f32[128,128]{1,0:T(8,128)S(1)}, u32[]{:S(2)}, u32[]{:S(2)}) collective-permute-start(f32[128,128]{1,0:T(8,128)S(1)} %add_add_fusion.1), channel_id=1, source_target_pairs={{0,1},{1,0},{2,3},{3,2},{4,5},{5,4},{6,7},{7,6},{8,9},{9,8},{10,11... | collective-permute-start | bytes 196616 | tf_op jit(solution)/shard_map/swap/ppermute | solution.py:34
  (10 other events, 18.9 us)

commit v7 on v6

--- a/solution.py
+++ b/solution.py
@@ -369,10 +369,20 @@
     a_mine = [out_grad, a1, a2, a_far]
     near = jnp.concatenate([out_grad, a2, a1])
     a_other = [swap(after(near, h1), "a_swap"), swap(a_far, "a_swap")]
-    own1 = product(F32, after(where, h2, h1_in), a_mine, a_other, [own_w, r1, r2, r3, r4, r5, r6])
-    sums = sum_tensor(after(parts, own1), c)
-    h3 = product(BF16, after(where, h2, own1), b_mine, b_other, [r7])
+    top, low = parts[:256], parts[256:]
+    half = jnp.where(c == 0, top, low) + swap(after(jnp.where(c == 0, low, top), h1), "s_core")
+    near_y = send(half, lambda z, x, y, c: (z, x, y ^ 1, c), "s_near")
+    half += after(near_y, h2)
+    far_y = send(half, lambda z, x, y, c: (z, x, y ^ 2, c), "s_far")
+    own1 = product(F32, after(where, h2), a_mine, a_other, [own_w, r1, r2, r3, r4, r5, r6])
+    half += after(far_y, own1)
+    rest = swap(half, "s_core")
+    h3 = product(BF16, after(where, h1_in, own1), b_mine, b_other, [r7])
     own2 = product(F32, after(where, h3, h2_in), a_mine, a_other, [r7])
+    rest = after(rest, own2)
+    sums = jnp.concatenate(
+        [jnp.where(c == 0, half, rest), jnp.where(c == 0, rest, half)], axis=0
+    )
     h_in = [h1_in, h2_in, mate(h3, "mate_grad3")]
     grad_gate, grad_up, part = own_half(where, gate_pre, up_pre, (own1, own2), ph_t)
     *spread, down_feat = spread_features(after(where, part), sums)

time: 148 us -> 135 us (0.912)
  waiting for transfers between devices: 69.1 us -> 52.2 us
  starting transfers between devices: 34.3 us -> 38.9 us
    ppermute x31 -> x30, waiting for transfers between devices: 69.1 us -> 52.2 us  [send(): return lax.ppermute(value, AXES, pairs)]
    ppermute x31 -> x30, starting transfers between devices: 34.3 us -> 38.9 us  [send(): return lax.ppermute(value, AXES, pairs)]
  transfers between devices with their start and end apart: 31 -> 30, of which waited for: 16 -> 13; matrix products, arithmetic and copies ran while one was open for 2% -> 2% of each run, Pallas kernels for 15% -> 16%
where the time goes in v7:
time: 135 us
  waiting for transfers between devices  52.2 us (39%)
  starting transfers between devices  38.9 us (29%)
  Pallas kernels  30.6 us (23%)
  local copies, waits for them, and re-layouts  10 us (7%)
  other arithmetic  2.05 us (2%)
    ppermute x30, waiting for transfers between devices, send(): return lax.ppermute(value, AXES, pairs)  52.2 us
    ppermute x30, starting transfers between devices, send(): return lax.ppermute(value, AXES, pairs)  38.9 us
    pallas_call x5, Pallas kernels, product(): pl.pallas_call(functools.partial(product_kernel, shards), out_shape=jax.S...  18.9 us
    unnamed x22, local copies, waits for them, and re-layouts  7.23 us
    pallas_call x1, Pallas kernels, other_half(): pl.pallas_call(functools.partial(other_kernel, len(h)), out_shape=(BIG, B...  4.44 us
    pallas_call x1, Pallas kernels, own_half(): pl.pallas_call(functools.partial(own_kernel, len(h)), out_shape=(BIG, BIG...  3.82 us
  transfers between devices with their start and end apart: 30, of which 13 were waited for; matrix products, arithmetic and copies ran while one was open for 2% of the time, Pallas kernels for 16%

profile of v7, /device:TPU:1, one launch (start us, length us, event | category | flops | bytes accessed | tf_op | source)
XLA Modules:
  0.0 134.6 jit_solution(16139081977944745486)
XLA Ops:
  0.6 4.7 %collective-permute-start = (bf16[512,640]{1,0:T(8,128)(2,1)}, bf16[512,640]{1,0:T(8,128)(2,1)S(1)}, u32[]{:S(2)}, u32[]{:S(2)}) collective-permute-start(bf16[512,640]{1,0:T(8,128)(2,1)} %refs_0_.3), channel_id=1, source_target_pairs={{0,96},{1,97},{2,98},{3,99},{4,100},{5,101},{6,102},{7,103},{8,104... | collective-permute-start | bytes 1966088 | tf_op jit(solution)/shard_map/mate_rows/ppermute | solution.py:34
  5.3 2.7 %collective-permute-start.1 = (bf16[512,640]{1,0:T(8,128)(2,1)}, bf16[512,640]{1,0:T(8,128)(2,1)S(1)}, u32[]{:S(2)}, u32[]{:S(2)}) collective-permute-start(bf16[512,640]{1,0:T(8,128)(2,1)} %refs_0_.3), channel_id=1, source_target_pairs={{0,2},{1,7},{2,4},{3,1},{4,6},{5,3},{6,0},{7,5},{8,10},{9,15},{10,... | collective-permute-start | bytes 1966088 | tf_op jit(solution)/shard_map/a1/ppermute | solution.py:34
  9.2 1.5 %collective-permute-start.4 = (bf16[112,5120]{1,0:T(8,128)(2,1)}, bf16[112,5120]{1,0:T(8,128)(2,1)}, u32[]{:S(2)}, u32[]{:S(2)}) collective-permute-start(bf16[112,5120]{1,0:T(8,128)(2,1)} %refs_6_.3), channel_id=1, source_target_pairs={{0,32},{1,25},{2,34},{3,27},{4,36},{5,29},{6,38},{7,31},{8,40},{9,... | collective-permute-start | bytes 3440648 | tf_op jit(solution)/shard_map/r2/ppermute | solution.py:34
  12.3 1.3 concatenate.18.where_ref
  13.6 1.5 %copy-done = bf16[512,1792]{1,0:T(8,128)(2,1)S(1)} copy-done((bf16[512,1792]{1,0:T(8,128)(2,1)S(1)}, bf16[512,1792]{1,0:T(8,128)(2,1)}, u32[]{:S(2)}) %copy-start) | copy-done | bytes 1835032
  15.1 1.5 %copy-done.2 = bf16[512,1792]{1,0:T(8,128)(2,1)S(1)} copy-done((bf16[512,1792]{1,0:T(8,128)(2,1)S(1)}, bf16[512,1792]{1,0:T(8,128)(2,1)}, u32[]{:S(2)}) %copy-start.2) | copy-done | bytes 1835032
  20.8 2.4 %early.1 = f32[512,192]{1,0:T(8,128)S(1)} custom-call(s32[24]{0:T(128)S(1)} %concatenate.18.where_ref, bf16[512,640]{1,0:T(8,128)(2,1)S(1)} %copy-done.9, bf16[512,640]{1,0:T(8,128)(2,1)S(1)} %copy-done.4, bf16[64,5120]{1,0:T(8,128)(2,1)S(1)} %bitcast.32, bf16[512,1792]{1,0:T(8,128)(2,1)S(1)} %copy-done, bf16[512,1792]{1,0:T(8,128)(2,1)S(1)} %copy-done.2, ...), custom_call_target="tpu_custom_call" | custom-call | flops 1048576 | bytes 65536 | tf_op jit(solution)/shard_map/early/pallas_call | solution.py:149
  23.2 1.7 %collective-permute-done.2.refs_2_ = bf16[512,640]{1,0:T(8,128)(2,1)S(1)} collective-permute-done((bf16[512,640]{1,0:T(8,128)(2,1)}, bf16[512,640]{1,0:T(8,128)(2,1)S(1)}, u32[]{:S(2)}, u32[]{:S(2)}) %collective-permute-start.2) | collective-permute-done | bytes 655392 | tf_op jit(solution)/shard_map/a2/ppermute | solution.py:34
  26.4 8.4 %collective-permute-done.3.refs_7_ = bf16[112,5120]{1,0:T(8,128)(2,1)S(1)} collective-permute-done((bf16[112,5120]{1,0:T(8,128)(2,1)}, bf16[112,5120]{1,0:T(8,128)(2,1)S(1)}, u32[]{:S(2)}, u32[]{:S(2)}) %collective-permute-start.3) | collective-permute-done | bytes 1146912 | tf_op jit(solution)/shard_map/r1/ppermute | solution.py:34
  34.8 2.9 %collective-permute-done.6.refs_1_ = bf16[512,640]{1,0:T(8,128)(2,1)S(1)} collective-permute-done((bf16[512,640]{1,0:T(8,128)(2,1)S(1)}, bf16[512,640]{1,0:T(8,128)(2,1)S(1)}, u32[]{:S(2)}, u32[]{:S(2)}) %collective-permute-start.6) | collective-permute-done | bytes 655392 | tf_op jit(solution)/shard_map/b1/ppermute | solution.py:34
  37.7 5.2 %collective-permute-done.7.refs_2_ = bf16[512,640]{1,0:T(8,128)(2,1)S(1)} collective-permute-done((bf16[512,640]{1,0:T(8,128)(2,1)S(1)}, bf16[512,640]{1,0:T(8,128)(2,1)S(1)}, u32[]{:S(2)}, u32[]{:S(2)}) %collective-permute-start.7) | collective-permute-done | bytes 655392 | tf_op jit(solution)/shard_map/b2/ppermute | solution.py:34
  43.1 1.6 %collective-permute-start.13 = (bf16[1536,640]{1,0:T(8,128)(2,1)S(1)}, bf16[1536,640]{1,0:T(8,128)(2,1)S(1)}, u32[]{:S(2)}, u32[]{:S(2)}) collective-permute-start(bf16[1536,640]{1,0:T(8,128)(2,1)S(1)} %pad_maximum_fusion), channel_id=1, source_target_pairs={{0,1},{1,0},{2,3},{3,2},{4,5},{5,4},{6,7},{7,6},{8,9},{9,8},{10,11... | collective-permute-start | bytes 5898248 | tf_op jit(solution)/shard_map/b_swap/ppermute | solution.py:34
  47.9 7.8 %collective-permute-done.11.refs_3_ = bf16[512,640]{1,0:T(8,128)(2,1)S(1)} collective-permute-done((bf16[512,640]{1,0:T(8,128)(2,1)S(1)}, bf16[512,640]{1,0:T(8,128)(2,1)S(1)}, u32[]{:S(2)}, u32[]{:S(2)}) %collective-permute-start.11) | collective-permute-done | bytes 655392 | tf_op jit(solution)/shard_map/b_far/ppermute | solution.py:34
  55.7 1.7 %collective-permute-start.12 = (bf16[512,640]{1,0:T(8,128)(2,1)S(1)}, bf16[512,640]{1,0:T(8,128)(2,1)S(1)}, u32[]{:S(2)}, u32[]{:S(2)}) collective-permute-start(bf16[512,640]{1,0:T(8,128)(2,1)S(1)} %collective-permute-done.1.refs_1_), channel_id=1, source_target_pairs={{0,2},{1,7},{2,4},{3,1},{4,6},{5,3},{6,0},{7,5},{8,10},{9,15},{10,... | collective-permute-start | bytes 1966088 | tf_op jit(solution)/shard_map/a_far/ppermute | solution.py:34
  57.4 14.4 %collective-permute-done.10.refs_8_.refs_12_ = bf16[112,5120]{1,0:T(8,128)(2,1)S(1)} collective-permute-done((bf16[112,5120]{1,0:T(8,128)(2,1)}, bf16[112,5120]{1,0:T(8,128)(2,1)S(1)}, u32[]{:S(2)}, u32[]{:S(2)}) %collective-permute-start.10) | collective-permute-done | bytes 1146912 | tf_op jit(solution)/shard_map/r6/ppermute | solution.py:34
  74.3 4.2 %product.5 = bf16[512,512]{1,0:T(8,128)(2,1)S(1)} custom-call(s32[24]{0:T(128)S(1)} %concatenate.18.where_ref, bf16[512,640]{1,0:T(8,128)(2,1)S(1)} %collective-permute-done.refs_0_, bf16[512,640]{1,0:T(8,128)(2,1)S(1)} %collective-permute-done.6.refs_1_, bf16[512,640]{1,0:T(8,128)(2,1)S(1)} %collective-permute-done.7.refs_2_, ...), custom_call_target="tpu_custom_call" | custom-call | flops 1048576 | bytes 65536 | tf_op jit(solution)/shard_map/product/pallas_call | solution.py:123
  78.5 2.0 %collective-permute-start.15 = (bf16[1536,640]{1,0:T(8,128)(2,1)S(1)}, bf16[1536,640]{1,0:T(8,128)(2,1)S(1)}, u32[]{:S(2)}, u32[]{:S(2)}) collective-permute-start(bf16[1536,640]{1,0:T(8,128)(2,1)S(1)} %pad_maximum_fusion.1), channel_id=1, source_target_pairs={{0,1},{1,0},{2,3},{3,2},{4,5},{5,4},{6,7},{7,6},{8,9},{9,8},{10,11... | collective-permute-start | bytes 5898248 | tf_op jit(solution)/shard_map/a_swap/ppermute | solution.py:34
  82.2 3.2 %collective-permute-done.20 = f32[256,192]{1,0:T(8,128)S(1)} collective-permute-done((f32[256,192]{1,0:T(8,128)S(1)}, f32[256,192]{1,0:T(8,128)S(1)}, u32[]{:S(2)}, u32[]{:S(2)}) %collective-permute-start.20) | collective-permute-done | bytes 196640 | tf_op jit(solution)/shard_map/s_core/ppermute | solution.py:34
  86.0 3.4 %product.6 = bf16[512,384]{1,0:T(8,128)(2,1)S(1)} custom-call(s32[24]{0:T(128)S(1)} %concatenate.18.where_ref, bf16[512,640]{1,0:T(8,128)(2,1)S(1)} %collective-permute-done.refs_0_, bf16[512,640]{1,0:T(8,128)(2,1)S(1)} %collective-permute-done.6.refs_1_, bf16[512,640]{1,0:T(8,128)(2,1)S(1)} %collective-permute-done.7.refs_2_, ...), custom_call_target="tpu_custom_call" | custom-call | flops 1048576 | bytes 65536 | tf_op jit(solution)/shard_map/product/pallas_call | solution.py:123
  89.4 3.6 %collective-permute-done.21 = f32[256,192]{1,0:T(8,128)S(1)} collective-permute-done((f32[256,192]{1,0:T(8,128)S(1)}, f32[256,192]{1,0:T(8,128)S(1)}, u32[]{:S(2)}, u32[]{:S(2)}) %collective-permute-start.21) | collective-permute-done | bytes 196640 | tf_op jit(solution)/shard_map/s_near/ppermute | solution.py:34
  93.2 3.1 %collective-permute-start.22 = (f32[256,192]{1,0:T(8,128)S(1)}, f32[256,192]{1,0:T(8,128)S(1)}, u32[]{:S(2)}, u32[]{:S(2)}) collective-permute-start(f32[256,192]{1,0:T(8,128)S(1)} %add.231), channel_id=1, source_target_pairs={{0,4},{1,5},{2,6},{3,7},{4,0},{5,1},{6,2},{7,3},{8,12},{9,13},{10,... | collective-permute-start | bytes 589832 | tf_op jit(solution)/shard_map/s_far/ppermute | solution.py:34
  96.2 6.9 %product.7.refs_0_ = f32[512,896]{1,0:T(8,128)S(1)} custom-call(s32[24]{0:T(128)S(1)} %concatenate.18.where_ref, bf16[512,640]{1,0:T(8,128)(2,1)S(1)} %copy-done.5, bf16[512,640]{1,0:T(8,128)(2,1)S(1)} %collective-permute-done.1.refs_1_, bf16[512,640]{1,0:T(8,128)(2,1)S(1)} %collective-permute-done.2.refs_2_, ...), custom_call_target="tpu_custom_call" | custom-call | flops 1048576 | bytes 65536 | tf_op jit(solution)/shard_map/product/pallas_call | solution.py:123
  103.2 1.5 %collective-permute-start.23 = (f32[256,192]{1,0:T(8,128)S(1)}, f32[256,192]{1,0:T(8,128)S(1)}, u32[]{:S(2)}, u32[]{:S(2)}) collective-permute-start(f32[256,192]{1,0:T(8,128)S(1)} %add.232), channel_id=1, source_target_pairs={{0,1},{1,0},{2,3},{3,2},{4,5},{5,4},{6,7},{7,6},{8,9},{9,8},{10,11... | collective-permute-start | bytes 589832 | tf_op jit(solution)/shard_map/s_core/ppermute | solution.py:34
  104.7 2.2 %product.8 = bf16[512,128]{1,0:T(8,128)(2,1)S(1)} custom-call(s32[24]{0:T(128)S(1)} %concatenate.18.where_ref, bf16[512,640]{1,0:T(8,128)(2,1)S(1)} %collective-permute-done.refs_0_, bf16[512,640]{1,0:T(8,128)(2,1)S(1)} %collective-permute-done.6.refs_1_, bf16[512,640]{1,0:T(8,128)(2,1)S(1)} %collective-permute-done.7.refs_2_, ...), custom_call_target="tpu_custom_call" | custom-call | flops 1048576 | bytes 65536 | tf_op jit(solution)/shard_map/product/pallas_call | solution.py:123
  106.9 2.4 %collective-permute-start.24 = (bf16[512,128]{1,0:T(8,128)(2,1)S(1)}, bf16[512,128]{1,0:T(8,128)(2,1)S(1)}, u32[]{:S(2)}, u32[]{:S(2)}) collective-permute-start(bf16[512,128]{1,0:T(8,128)(2,1)S(1)} %product.8), channel_id=1, source_target_pairs={{0,96},{1,97},{2,98},{3,99},{4,100},{5,101},{6,102},{7,103},{8,104... | collective-permute-start | bytes 393224 | tf_op jit(solution)/shard_map/mate_grad3/ppermute | solution.py:34
  109.3 2.2 %product.9.refs_1_ = f32[512,128]{1,0:T(8,128)S(1)} custom-call(s32[24]{0:T(128)S(1)} %concatenate.18.where_ref, bf16[512,640]{1,0:T(8,128)(2,1)S(1)} %copy-done.5, bf16[512,640]{1,0:T(8,128)(2,1)S(1)} %collective-permute-done.1.refs_1_, bf16[512,640]{1,0:T(8,128)(2,1)S(1)} %collective-permute-done.2.refs_2_, ...), custom_call_target="tpu_custom_call" | custom-call | flops 1048576 | bytes 65536 | tf_op jit(solution)/shard_map/product/pallas_call | solution.py:123
  111.5 3.8 %own_half.1 = (bf16[512,1792]{1,0:T(8,128)(2,1)}, bf16[512,1792]{1,0:T(8,128)(2,1)}, f32[512,128]{1,0:T(8,128)S(1)}) custom-call(s32[24]{0:T(128)S(1)} %concatenate.18.where_ref, bf16[512,1792]{1,0:T(8,128)(2,1)S(1)} %copy-done.1, bf16[512,1792]{1,0:T(8,128)(2,1)S(1)} %copy-done.3, bf16[64,1792]{1,0:T(8,128)(2,1)S(1)} %bitcast.30, ...), custom_call_target="tpu_custom_call" | custom-call | flops 1048576 | bytes 65536 | tf_op jit(solution)/shard_map/own_half/pallas_call | solution.py:218
  116.5 4.4 %other_half.1 = (bf16[512,1792]{1,0:T(8,128)(2,1)}, bf16[512,1792]{1,0:T(8,128)(2,1)}, f32[256,128]{1,0:T(8,128)S(1)}) custom-call(s32[24]{0:T(128)S(1)} %concatenate.18.where_ref, bf16[512,1792]{1,0:T(8,128)(2,1)S(1)} %copy-done.1, bf16[512,1792]{1,0:T(8,128)(2,1)S(1)} %copy-done.3, ...), custom_call_target="tpu_custom_call", output_to_operand_aliasing={{0}: (7, {}), {1}: (8, {})} | custom-call | flops 1048576 | bytes 65536 | tf_op jit(solution)/shard_map/other_half/pallas_call | solution.py:262
  122.6 3.5 %collective-permute-start.26 = (f32[128,128]{1,0:T(8,128)S(1)}, f32[128,128]{1,0:T(8,128)S(1)}, u32[]{:S(2)}, u32[]{:S(2)}) collective-permute-start(f32[128,128]{1,0:T(8,128)S(1)} %select_add_fusion.1), channel_id=1, source_target_pairs={{0,4},{1,5},{2,6},{3,7},{4,0},{5,1},{6,2},{7,3},{8,12},{9,13},{10,... | collective-permute-start | bytes 196616 | tf_op jit(solution)/shard_map/send/ppermute | solution.py:34
  126.1 2.7 %collective-permute-start.28 = (f32[128,128]{1,0:T(8,128)S(1)}, f32[128,128]{1,0:T(8,128)S(1)}, u32[]{:S(2)}, u32[]{:S(2)}) collective-permute-start(f32[128,128]{1,0:T(8,128)S(1)} %select_add_fusion.1), channel_id=1, source_target_pairs={{0,6},{1,7},{2,0},{3,1},{4,2},{5,3},{6,4},{7,5},{8,14},{9,15},{10,... | collective-permute-start | bytes 196616 | tf_op jit(solution)/shard_map/down/ppermute | solution.py:34
  128.8 1.6 %collective-permute-done.27 = f32[128,128]{1,0:T(8,128)S(1)} collective-permute-done((f32[128,128]{1,0:T(8,128)S(1)}, f32[128,128]{1,0:T(8,128)S(1)}, u32[]{:S(2)}, u32[]{:S(2)}) %collective-permute-start.27) | collective-permute-done | bytes 65568 | tf_op jit(solution)/shard_map/up/ppermute | solution.py:34
  130.4 1.9 %collective-permute-start.29 = (f32[128,128]{1,0:T(8,128)S(1)}, f32[128,128]{1,0:T(8,128)S(1)}, u32[]{:S(2)}, u32[]{:S(2)}) collective-permute-start(f32[128,128]{1,0:T(8,128)S(1)} %add_add_fusion), channel_id=1, source_target_pairs={{0,1},{1,0},{2,3},{3,2},{4,5},{5,4},{6,7},{7,6},{8,9},{9,8},{10,11... | collective-permute-start | bytes 196616 | tf_op jit(solution)/shard_map/swap/ppermute | solution.py:34
  (81 shorter events, 22.0 us)
Async XLA Ops:
  0.6 22.5 %collective-permute-start = (bf16[512,640]{1,0:T(8,128)(2,1)}, bf16[512,640]{1,0:T(8,128)(2,1)S(1)}, u32[]{:S(2)}, u32[]{:S(2)}) collective-permute-start(bf16[512,640]{1,0:T(8,128)(2,1)} %refs_0_.3), channel_id=1, source_target_pairs={{0,96},{1,97},{2,98},{3,99},{4,100},{5,101},{6,102},{7,103},{8,104... | collective-permute-start | bytes 1966088 | tf_op jit(solution)/shard_map/mate_rows/ppermute | solution.py:34
  5.3 17.9 %collective-permute-start.1 = (bf16[512,640]{1,0:T(8,128)(2,1)}, bf16[512,640]{1,0:T(8,128)(2,1)S(1)}, u32[]{:S(2)}, u32[]{:S(2)}) collective-permute-start(bf16[512,640]{1,0:T(8,128)(2,1)} %refs_0_.3), channel_id=1, source_target_pairs={{0,2},{1,7},{2,4},{3,1},{4,6},{5,3},{6,0},{7,5},{8,10},{9,15},{10,... | collective-permute-start | bytes 1966088 | tf_op jit(solution)/shard_map/a1/ppermute | solution.py:34
  8.0 16.9 %collective-permute-start.2 = (bf16[512,640]{1,0:T(8,128)(2,1)}, bf16[512,640]{1,0:T(8,128)(2,1)S(1)}, u32[]{:S(2)}, u32[]{:S(2)}) collective-permute-start(bf16[512,640]{1,0:T(8,128)(2,1)} %refs_0_.3), channel_id=1, source_target_pairs={{0,6},{1,3},{2,0},{3,5},{4,2},{5,7},{6,4},{7,1},{8,14},{9,11},{10,... | collective-permute-start | bytes 1966088 | tf_op jit(solution)/shard_map/a2/ppermute | solution.py:34
  8.0 26.7 %collective-permute-start.3 = (bf16[112,5120]{1,0:T(8,128)(2,1)}, bf16[112,5120]{1,0:T(8,128)(2,1)S(1)}, u32[]{:S(2)}, u32[]{:S(2)}) collective-permute-start(bf16[112,5120]{1,0:T(8,128)(2,1)} %refs_6_.3), channel_id=1, source_target_pairs={{0,8},{1,9},{2,10},{3,11},{4,12},{5,13},{6,14},{7,15},{8,16},{9,17... | collective-permute-start | bytes 3440648 | tf_op jit(solution)/shard_map/r1/ppermute | solution.py:34
  9.2 25.5 %collective-permute-start.4 = (bf16[112,5120]{1,0:T(8,128)(2,1)}, bf16[112,5120]{1,0:T(8,128)(2,1)}, u32[]{:S(2)}, u32[]{:S(2)}) collective-permute-start(bf16[112,5120]{1,0:T(8,128)(2,1)} %refs_6_.3), channel_id=1, source_target_pairs={{0,32},{1,25},{2,34},{3,27},{4,36},{5,29},{6,38},{7,31},{8,40},{9,... | collective-permute-start | bytes 3440648 | tf_op jit(solution)/shard_map/r2/ppermute | solution.py:34
  23.2 49.4 %copy-start.5 = (bf16[512,640]{1,0:T(8,128)(2,1)S(1)}, bf16[512,640]{1,0:T(8,128)(2,1)}, u32[]{:S(2)}) copy-start(bf16[512,640]{1,0:T(8,128)(2,1)} %refs_0_.3) | copy-start | bytes 1966084
  24.9 18.0 %collective-permute-start.5 = (bf16[112,5120]{1,0:T(8,128)(2,1)S(1)}, bf16[112,5120]{1,0:T(8,128)(2,1)S(1)}, u32[]{:S(2)}, u32[]{:S(2)}) collective-permute-start(bf16[112,5120]{1,0:T(8,128)(2,1)S(1)} %copy-done.6), channel_id=1, source_target_pairs={{0,24},{1,33},{2,26},{3,35},{4,28},{5,37},{6,30},{7,39},{8,0},{9,4... | collective-permute-start | bytes 3440648 | tf_op jit(solution)/shard_map/r3/ppermute | solution.py:34
  24.9 12.8 %collective-permute-start.6 = (bf16[512,640]{1,0:T(8,128)(2,1)S(1)}, bf16[512,640]{1,0:T(8,128)(2,1)S(1)}, u32[]{:S(2)}, u32[]{:S(2)}) collective-permute-start(bf16[512,640]{1,0:T(8,128)(2,1)S(1)} %collective-permute-done.refs_0_), channel_id=1, source_target_pairs={{0,2},{1,7},{2,4},{3,1},{4,6},{5,3},{6,0},{7,5},{8,10},{9,15},{10,... | collective-permute-start | bytes 1966088 | tf_op jit(solution)/shard_map/b1/ppermute | solution.py:34
  26.0 16.9 %collective-permute-start.7 = (bf16[512,640]{1,0:T(8,128)(2,1)S(1)}, bf16[512,640]{1,0:T(8,128)(2,1)S(1)}, u32[]{:S(2)}, u32[]{:S(2)}) collective-permute-start(bf16[512,640]{1,0:T(8,128)(2,1)S(1)} %collective-permute-done.refs_0_), channel_id=1, source_target_pairs={{0,6},{1,3},{2,0},{3,5},{4,2},{5,7},{6,4},{7,1},{8,14},{9,11},{10,... | collective-permute-start | bytes 1966088 | tf_op jit(solution)/shard_map/b2/ppermute | solution.py:34
  43.1 31.2 %collective-permute-start.13 = (bf16[1536,640]{1,0:T(8,128)(2,1)S(1)}, bf16[1536,640]{1,0:T(8,128)(2,1)S(1)}, u32[]{:S(2)}, u32[]{:S(2)}) collective-permute-start(bf16[1536,640]{1,0:T(8,128)(2,1)S(1)} %pad_maximum_fusion), channel_id=1, source_target_pairs={{0,1},{1,0},{2,3},{3,2},{4,5},{5,4},{6,7},{7,6},{8,9},{9,8},{10,11... | collective-permute-start | bytes 5898248 | tf_op jit(solution)/shard_map/b_swap/ppermute | solution.py:34
  44.7 27.0 %collective-permute-start.10 = (bf16[112,5120]{1,0:T(8,128)(2,1)}, bf16[112,5120]{1,0:T(8,128)(2,1)S(1)}, u32[]{:S(2)}, u32[]{:S(2)}) collective-permute-start(bf16[112,5120]{1,0:T(8,128)(2,1)} %collective-permute-done.4.refs_8_), channel_id=1, source_target_pairs={{0,24},{1,25},{2,26},{3,27},{4,28},{5,29},{6,30},{7,31},{8,0},{9,1... | collective-permute-start | bytes 3440648 | tf_op jit(solution)/shard_map/r6/ppermute | solution.py:34
  46.0 9.7 %collective-permute-start.11 = (bf16[512,640]{1,0:T(8,128)(2,1)S(1)}, bf16[512,640]{1,0:T(8,128)(2,1)S(1)}, u32[]{:S(2)}, u32[]{:S(2)}) collective-permute-start(bf16[512,640]{1,0:T(8,128)(2,1)S(1)} %collective-permute-done.6.refs_1_), channel_id=1, source_target_pairs={{0,2},{1,7},{2,4},{3,1},{4,6},{5,3},{6,0},{7,5},{8,10},{9,15},{10,... | collective-permute-start | bytes 1966088 | tf_op jit(solution)/shard_map/b_far/ppermute | solution.py:34
  46.4 26.3 %collective-permute-start.8 = (bf16[112,5120]{1,0:T(8,128)(2,1)}, bf16[112,5120]{1,0:T(8,128)(2,1)S(1)}, u32[]{:S(2)}, u32[]{:S(2)}) collective-permute-start(bf16[112,5120]{1,0:T(8,128)(2,1)} %collective-permute-done.4.refs_8_), channel_id=1, source_target_pairs={{0,8},{1,33},{2,10},{3,35},{4,12},{5,37},{6,14},{7,39},{8,16},{9,4... | collective-permute-start | bytes 3440648 | tf_op jit(solution)/shard_map/r4/ppermute | solution.py:34
  47.3 26.6 %collective-permute-start.9 = (bf16[112,5120]{1,0:T(8,128)(2,1)S(1)}, bf16[112,5120]{1,0:T(8,128)(2,1)S(1)}, u32[]{:S(2)}, u32[]{:S(2)}) collective-permute-start(bf16[112,5120]{1,0:T(8,128)(2,1)S(1)} %collective-permute-done.3.refs_7_), channel_id=1, source_target_pairs={{0,8},{1,33},{2,10},{3,35},{4,12},{5,37},{6,14},{7,39},{8,16},{9,4... | collective-permute-start | bytes 3440648 | tf_op jit(solution)/shard_map/r5/ppermute | solution.py:34
  55.7 18.2 %collective-permute-start.12 = (bf16[512,640]{1,0:T(8,128)(2,1)S(1)}, bf16[512,640]{1,0:T(8,128)(2,1)S(1)}, u32[]{:S(2)}, u32[]{:S(2)}) collective-permute-start(bf16[512,640]{1,0:T(8,128)(2,1)S(1)} %collective-permute-done.1.refs_1_), channel_id=1, source_target_pairs={{0,2},{1,7},{2,4},{3,1},{4,6},{5,3},{6,0},{7,5},{8,10},{9,15},{10,... | collective-permute-start | bytes 1966088 | tf_op jit(solution)/shard_map/a_far/ppermute | solution.py:34
  71.7 2.6 %collective-permute-start.14 = (bf16[512,640]{1,0:T(8,128)(2,1)S(1)}, bf16[512,640]{1,0:T(8,128)(2,1)S(1)}, u32[]{:S(2)}, u32[]{:S(2)}) collective-permute-start(bf16[512,640]{1,0:T(8,128)(2,1)S(1)} %collective-permute-done.11.refs_3_), channel_id=1, source_target_pairs={{0,1},{1,0},{2,3},{3,2},{4,5},{5,4},{6,7},{7,6},{8,9},{9,8},{10,11... | collective-permute-start | bytes 1966088 | tf_op jit(solution)/shard_map/b_swap/ppermute | solution.py:34
  78.5 17.7 %collective-permute-start.15 = (bf16[1536,640]{1,0:T(8,128)(2,1)S(1)}, bf16[1536,640]{1,0:T(8,128)(2,1)S(1)}, u32[]{:S(2)}, u32[]{:S(2)}) collective-permute-start(bf16[1536,640]{1,0:T(8,128)(2,1)S(1)} %pad_maximum_fusion.1), channel_id=1, source_target_pairs={{0,1},{1,0},{2,3},{3,2},{4,5},{5,4},{6,7},{7,6},{8,9},{9,8},{10,11... | collective-permute-start | bytes 5898248 | tf_op jit(solution)/shard_map/a_swap/ppermute | solution.py:34
  80.5 24.3 %collective-permute-start.18 = (bf16[112,5120]{1,0:T(8,128)(2,1)S(1)}, bf16[112,5120]{1,0:T(8,128)(2,1)S(1)}, u32[]{:S(2)}, u32[]{:S(2)}) collective-permute-start(bf16[112,5120]{1,0:T(8,128)(2,1)S(1)} %collective-permute-done.10.refs_8_.refs_12_), channel_id=1, source_target_pairs={{0,24},{1,33},{2,26},{3,35},{4,28},{5,37},{6,30},{7,39},{8,0},{9,4... | collective-permute-start | bytes 3440648 | tf_op jit(solution)/shard_map/r7/ppermute | solution.py:34
  81.6 11.6 %collective-permute-start.16 = (bf16[512,640]{1,0:T(8,128)(2,1)S(1)}, bf16[512,640]{1,0:T(8,128)(2,1)S(1)}, u32[]{:S(2)}, u32[]{:S(2)}) collective-permute-start(bf16[512,640]{1,0:T(8,128)(2,1)S(1)} %collective-permute-done.12.refs_3_), channel_id=1, source_target_pairs={{0,1},{1,0},{2,3},{3,2},{4,5},{5,4},{6,7},{7,6},{8,9},{9,8},{10,11... | collective-permute-start | bytes 1966088 | tf_op jit(solution)/shard_map/a_swap/ppermute | solution.py:34
  81.9 3.5 %collective-permute-start.20 = (f32[256,192]{1,0:T(8,128)S(1)}, f32[256,192]{1,0:T(8,128)S(1)}, u32[]{:S(2)}, u32[]{:S(2)}) collective-permute-start(f32[256,192]{1,0:T(8,128)S(1)} %slice_select_fusion), channel_id=1, source_target_pairs={{0,1},{1,0},{2,3},{3,2},{4,5},{5,4},{6,7},{7,6},{8,9},{9,8},{10,11... | collective-permute-start | bytes 589832 | tf_op jit(solution)/shard_map/s_core/ppermute | solution.py:34
  85.4 7.6 %collective-permute-start.21 = (f32[256,192]{1,0:T(8,128)S(1)}, f32[256,192]{1,0:T(8,128)S(1)}, u32[]{:S(2)}, u32[]{:S(2)}) collective-permute-start(f32[256,192]{1,0:T(8,128)S(1)} %select_add_fusion), channel_id=1, source_target_pairs={{0,2},{1,3},{2,0},{3,1},{4,6},{5,7},{6,4},{7,5},{8,10},{9,11},{10,... | collective-permute-start | bytes 589832 | tf_op jit(solution)/shard_map/s_near/ppermute | solution.py:34
  86.0 18.7 %collective-permute-start.17 = (bf16[512,512]{1,0:T(8,128)(2,1)S(1)}, bf16[512,512]{1,0:T(8,128)(2,1)S(1)}, u32[]{:S(2)}, u32[]{:S(2)}) collective-permute-start(bf16[512,512]{1,0:T(8,128)(2,1)S(1)} %product.5), channel_id=1, source_target_pairs={{0,96},{1,97},{2,98},{3,99},{4,100},{5,101},{6,102},{7,103},{8,104... | collective-permute-start | bytes 1572872 | tf_op jit(solution)/shard_map/mate_grad1/ppermute | solution.py:34
  93.0 16.3 %collective-permute-start.19 = (bf16[512,384]{1,0:T(8,128)(2,1)S(1)}, bf16[512,384]{1,0:T(8,128)(2,1)S(1)}, u32[]{:S(2)}, u32[]{:S(2)}) collective-permute-start(bf16[512,384]{1,0:T(8,128)(2,1)S(1)} %product.6), channel_id=1, source_target_pairs={{0,96},{1,97},{2,98},{3,99},{4,100},{5,101},{6,102},{7,103},{8,104... | collective-permute-start | bytes 1179656 | tf_op jit(solution)/shard_map/mate_grad2/ppermute | solution.py:34
  93.2 10.0 %collective-permute-start.22 = (f32[256,192]{1,0:T(8,128)S(1)}, f32[256,192]{1,0:T(8,128)S(1)}, u32[]{:S(2)}, u32[]{:S(2)}) collective-permute-start(f32[256,192]{1,0:T(8,128)S(1)} %add.231), channel_id=1, source_target_pairs={{0,4},{1,5},{2,6},{3,7},{4,0},{5,1},{6,2},{7,3},{8,12},{9,13},{10,... | collective-permute-start | bytes 589832 | tf_op jit(solution)/shard_map/s_far/ppermute | solution.py:34
  103.2 12.1 %collective-permute-start.23 = (f32[256,192]{1,0:T(8,128)S(1)}, f32[256,192]{1,0:T(8,128)S(1)}, u32[]{:S(2)}, u32[]{:S(2)}) collective-permute-start(f32[256,192]{1,0:T(8,128)S(1)} %add.232), channel_id=1, source_target_pairs={{0,1},{1,0},{2,3},{3,2},{4,5},{5,4},{6,7},{7,6},{8,9},{9,8},{10,11... | collective-permute-start | bytes 589832 | tf_op jit(solution)/shard_map/s_core/ppermute | solution.py:34
  106.9 4.6 %copy-start.1 = (bf16[512,1792]{1,0:T(8,128)(2,1)S(1)}, bf16[512,1792]{1,0:T(8,128)(2,1)}, u32[]{:S(2)}) copy-start(bf16[512,1792]{1,0:T(8,128)(2,1)} %gate_ref.5) | copy-start | bytes 5505028
  106.9 9.6 %collective-permute-start.24 = (bf16[512,128]{1,0:T(8,128)(2,1)S(1)}, bf16[512,128]{1,0:T(8,128)(2,1)S(1)}, u32[]{:S(2)}, u32[]{:S(2)}) collective-permute-start(bf16[512,128]{1,0:T(8,128)(2,1)S(1)} %product.8), channel_id=1, source_target_pairs={{0,96},{1,97},{2,98},{3,99},{4,100},{5,101},{6,102},{7,103},{8,104... | collective-permute-start | bytes 393224 | tf_op jit(solution)/shard_map/mate_grad3/ppermute | solution.py:34
  121.0 1.6 %collective-permute-start.25 = (f32[128,128]{1,0:T(8,128)S(1)}, f32[128,128]{1,0:T(8,128)S(1)}, u32[]{:S(2)}, u32[]{:S(2)}) collective-permute-start(f32[128,128]{1,0:T(8,128)S(1)} %slice_select_fusion.1), channel_id=1, source_target_pairs={{0,1},{1,0},{2,3},{3,2},{4,5},{5,4},{6,7},{7,6},{8,9},{9,8},{10,11... | collective-permute-start | bytes 196616 | tf_op jit(solution)/shard_map/swap/ppermute | solution.py:34
  122.6 6.2 %collective-permute-start.26 = (f32[128,128]{1,0:T(8,128)S(1)}, f32[128,128]{1,0:T(8,128)S(1)}, u32[]{:S(2)}, u32[]{:S(2)}) collective-permute-start(f32[128,128]{1,0:T(8,128)S(1)} %select_add_fusion.1), channel_id=1, source_target_pairs={{0,4},{1,5},{2,6},{3,7},{4,0},{5,1},{6,2},{7,3},{8,12},{9,13},{10,... | collective-permute-start | bytes 196616 | tf_op jit(solution)/shard_map/send/ppermute | solution.py:34
  126.1 4.3 %collective-permute-start.27 = (f32[128,128]{1,0:T(8,128)S(1)}, f32[128,128]{1,0:T(8,128)S(1)}, u32[]{:S(2)}, u32[]{:S(2)}) collective-permute-start(f32[128,128]{1,0:T(8,128)S(1)} %select_add_fusion.1), channel_id=1, source_target_pairs={{0,2},{1,3},{2,4},{3,5},{4,6},{5,7},{6,0},{7,1},{8,10},{9,11},{10,... | collective-permute-start | bytes 196616 | tf_op jit(solution)/shard_map/up/ppermute | solution.py:34
  126.1 4.3 %collective-permute-start.28 = (f32[128,128]{1,0:T(8,128)S(1)}, f32[128,128]{1,0:T(8,128)S(1)}, u32[]{:S(2)}, u32[]{:S(2)}) collective-permute-start(f32[128,128]{1,0:T(8,128)S(1)} %select_add_fusion.1), channel_id=1, source_target_pairs={{0,6},{1,7},{2,0},{3,1},{4,2},{5,3},{6,4},{7,5},{8,14},{9,15},{10,... | collective-permute-start | bytes 196616 | tf_op jit(solution)/shard_map/down/ppermute | solution.py:34
  130.4 2.8 %collective-permute-start.29 = (f32[128,128]{1,0:T(8,128)S(1)}, f32[128,128]{1,0:T(8,128)S(1)}, u32[]{:S(2)}, u32[]{:S(2)}) collective-permute-start(f32[128,128]{1,0:T(8,128)S(1)} %add_add_fusion), channel_id=1, source_target_pairs={{0,1},{1,0},{2,3},{3,2},{4,5},{5,4},{6,7},{7,6},{8,9},{9,8},{10,11... | collective-permute-start | bytes 196616 | tf_op jit(solution)/shard_map/swap/ppermute | solution.py:34
  (9 other events, 20.5 us)

commit v8 on v7

--- a/solution.py
+++ b/solution.py
@@ -347,10 +347,7 @@
     a1, a2 = along_y(out_grad, 1, "a1"), along_y(out_grad, -1, "a2")
     r1 = route(own_w, "+", "+", "r1")
     r2 = route(own_w, "p", "-", "r2")
-    parts = early(where, activations, out_grad, pm_t, gate_pre, up_pre, ph_t)
-    theirs, a1, a2, again, parts, where = lax.optimization_barrier(
-        (theirs, a1, a2, own_w, parts, where)
-    )
+    theirs, a1, a2, again, where = lax.optimization_barrier((theirs, a1, a2, own_w, where))
     r3 = route(again, "-", "p", "r3")
     b1, b2 = along_y(theirs, 1, "b1"), along_y(theirs, -1, "b2")
     r1, r2, r3, b1, b2 = lax.optimization_barrier((r1, r2, r3, b1, b2))
@@ -358,10 +355,14 @@
     r4 = route(r2, "+", "p", "r4")
     r5 = route(r1, "+", "p", "r5")
     b_far = along_y(b1, 1, "b_far")
-    b_other = [swap(jnp.concatenate([theirs, b2, b1]), "b_swap"), swap(b_far, "b_swap")]
+    b_near = swap(jnp.concatenate([theirs, b2, b1]), "b_swap")
+    b_other = [b_near, swap(after(b_far, b_near), "b_swap")]
     a_far = along_y(after(a1, b_far), 1, "a_far")
+    parts = early(after(where, b_far), activations, out_grad, pm_t, gate_pre, up_pre, ph_t)
+    top, low = parts[:256], parts[256:]
+    core_sum = swap(after(jnp.where(c == 0, low, top), b_other[1]), "s_core")
     b_mine = [theirs, b1, b2, b_far]
-    h1 = product(BF16, after(where, r4, r5, r6, a_far), b_mine, b_other, [own_w, r1, r2, r3])
+    h1 = product(BF16, after(where, r4, r5, r6, a_far, parts), b_mine, b_other, [own_w, r1, r2, r3])
     r7 = route(r6, "-", "p", "r7")
     h1_in = mate(h1, "mate_grad1")
     h2 = product(BF16, after(where, h1), b_mine, b_other, [r4, r5, r6])
@@ -369,23 +370,21 @@
     a_mine = [out_grad, a1, a2, a_far]
     near = jnp.concatenate([out_grad, a2, a1])
     a_other = [swap(after(near, h1), "a_swap"), swap(a_far, "a_swap")]
-    top, low = parts[:256], parts[256:]
-    half = jnp.where(c == 0, top, low) + swap(after(jnp.where(c == 0, low, top), h1), "s_core")
+    half = jnp.where(c == 0, top, low) + after(core_sum, h2)
     near_y = send(half, lambda z, x, y, c: (z, x, y ^ 1, c), "s_near")
-    half += after(near_y, h2)
+    own1 = product(F32, after(where, h2), a_mine, a_other, [own_w, r1, r2, r3, r4, r5, r6])
+    half += after(near_y, own1)
     far_y = send(half, lambda z, x, y, c: (z, x, y ^ 2, c), "s_far")
-    own1 = product(F32, after(where, h2), a_mine, a_other, [own_w, r1, r2, r3, r4, r5, r6])
-    half += after(far_y, own1)
+    h3 = product(BF16, after(where, h1_in, own1), b_mine, b_other, [r7])
+    own2 = product(F32, after(where, h3), a_mine, a_other, [r7])
+    half += after(far_y, own2)
     rest = swap(half, "s_core")
-    h3 = product(BF16, after(where, h1_in, own1), b_mine, b_other, [r7])
-    own2 = product(F32, after(where, h3, h2_in), a_mine, a_other, [r7])
-    rest = after(rest, own2)
     sums = jnp.concatenate(
         [jnp.where(c == 0, half, rest), jnp.where(c == 0, rest, half)], axis=0
     )
     h_in = [h1_in, h2_in, mate(h3, "mate_grad3")]
-    grad_gate, grad_up, part = own_half(where, gate_pre, up_pre, (own1, own2), ph_t)
-    *spread, down_feat = spread_features(after(where, part), sums)
+    grad_gate, grad_up, part = own_half(after(where, h2_in), gate_pre, up_pre, (own1, own2), ph_t)
+    *spread, down_feat = spread_features(after(where, part, h_in[2]), sums)
     grad_gate, grad_up, feat = other_half(
         where, gate_pre, up_pre, h_in, ph_t, part, spread, grad_gate, grad_up
     )

time: 135 us -> 131 us (0.970)
  local copies, waits for them, and re-layouts: 10 us -> 2.9 us
  starting transfers between devices: 38.9 us -> 41 us
  waiting for transfers between devices: 52.2 us -> 53.7 us
    unnamed x22 -> x14, local copies, waits for them, and re-layouts: 7.23 us -> 0.04 us
    ppermute x30, starting transfers between devices: 38.9 us -> 41 us  [send(): return lax.ppermute(value, AXES, pairs)]
    ppermute x30, waiting for transfers between devices: 52.2 us -> 53.7 us  [send(): return lax.ppermute(value, AXES, pairs)]
  transfers between devices with their start and end apart: 30 -> 30, of which waited for: 13 -> 15; matrix products, arithmetic and copies ran while one was open for 2% -> 3% of each run, Pallas kernels for 16% -> 16%
where the time goes in v8:
time: 131 us
  waiting for transfers between devices  53.7 us (41%)
  starting transfers between devices  41 us (31%)
  Pallas kernels  30.6 us (23%)
  local copies, waits for them, and re-layouts  2.9 us (2%)
  other arithmetic  2.14 us (2%)
    ppermute x30, waiting for transfers between devices, send(): return lax.ppermute(value, AXES, pairs)  53.7 us
    ppermute x30, starting transfers between devices, send(): return lax.ppermute(value, AXES, pairs)  41 us
    pallas_call x5, Pallas kernels, product(): pl.pallas_call(functools.partial(product_kernel, shards), out_shape=jax.S...  18.9 us
    pallas_call x1, Pallas kernels, other_half(): pl.pallas_call(functools.partial(other_kernel, len(h)), out_shape=(BIG, B...  4.44 us
    pallas_call x1, Pallas kernels, own_half(): pl.pallas_call(functools.partial(own_kernel, len(h)), out_shape=(BIG, BIG...  3.81 us
  transfers between devices with their start and end apart: 30, of which 15 were waited for; matrix products, arithmetic and copies ran while one was open for 3% of the time, Pallas kernels for 16%

profile of v8, /device:TPU:1, one launch (start us, length us, event | category | flops | bytes accessed | tf_op | source)
XLA Modules:
  0.0 131.2 jit_solution(9584436612691988479)
XLA Ops:
  0.6 4.7 %collective-permute-start = (bf16[512,640]{1,0:T(8,128)(2,1)}, bf16[512,640]{1,0:T(8,128)(2,1)S(1)}, u32[]{:S(2)}, u32[]{:S(2)}) collective-permute-start(bf16[512,640]{1,0:T(8,128)(2,1)} %refs_0_.3), channel_id=1, source_target_pairs={{0,96},{1,97},{2,98},{3,99},{4,100},{5,101},{6,102},{7,103},{8,104... | collective-permute-start | bytes 1966088 | tf_op jit(solution)/shard_map/mate_rows/ppermute | solution.py:34
  5.3 2.7 %collective-permute-start.1 = (bf16[512,640]{1,0:T(8,128)(2,1)}, bf16[512,640]{1,0:T(8,128)(2,1)S(1)}, u32[]{:S(2)}, u32[]{:S(2)}) collective-permute-start(bf16[512,640]{1,0:T(8,128)(2,1)} %refs_0_.3), channel_id=1, source_target_pairs={{0,2},{1,7},{2,4},{3,1},{4,6},{5,3},{6,0},{7,5},{8,10},{9,15},{10,... | collective-permute-start | bytes 1966088 | tf_op jit(solution)/shard_map/a1/ppermute | solution.py:34
  9.2 1.5 %collective-permute-start.4 = (bf16[112,5120]{1,0:T(8,128)(2,1)}, bf16[112,5120]{1,0:T(8,128)(2,1)}, u32[]{:S(2)}, u32[]{:S(2)}) collective-permute-start(bf16[112,5120]{1,0:T(8,128)(2,1)} %refs_6_.3), channel_id=1, source_target_pairs={{0,32},{1,25},{2,34},{3,27},{4,36},{5,29},{6,38},{7,31},{8,40},{9,... | collective-permute-start | bytes 3440648 | tf_op jit(solution)/shard_map/r2/ppermute | solution.py:34
  13.8 6.2 %collective-permute-done.refs_0_ = bf16[512,640]{1,0:T(8,128)(2,1)S(1)} collective-permute-done((bf16[512,640]{1,0:T(8,128)(2,1)}, bf16[512,640]{1,0:T(8,128)(2,1)S(1)}, u32[]{:S(2)}, u32[]{:S(2)}) %collective-permute-start) | collective-permute-done | bytes 655392 | tf_op jit(solution)/shard_map/mate_rows/ppermute | solution.py:34
  21.2 3.7 %collective-permute-done.2.refs_2_ = bf16[512,640]{1,0:T(8,128)(2,1)S(1)} collective-permute-done((bf16[512,640]{1,0:T(8,128)(2,1)}, bf16[512,640]{1,0:T(8,128)(2,1)S(1)}, u32[]{:S(2)}, u32[]{:S(2)}) %collective-permute-start.2) | collective-permute-done | bytes 655392 | tf_op jit(solution)/shard_map/a2/ppermute | solution.py:34
  24.9 1.5 %collective-permute-start.7 = (bf16[512,640]{1,0:T(8,128)(2,1)S(1)}, bf16[512,640]{1,0:T(8,128)(2,1)S(1)}, u32[]{:S(2)}, u32[]{:S(2)}) collective-permute-start(bf16[512,640]{1,0:T(8,128)(2,1)S(1)} %collective-permute-done.refs_0_), channel_id=1, source_target_pairs={{0,6},{1,3},{2,0},{3,5},{4,2},{5,7},{6,4},{7,1},{8,14},{9,11},{10,... | collective-permute-start | bytes 1966088 | tf_op jit(solution)/shard_map/b2/ppermute | solution.py:34
  26.4 8.4 %collective-permute-done.3.refs_7_ = bf16[112,5120]{1,0:T(8,128)(2,1)S(1)} collective-permute-done((bf16[112,5120]{1,0:T(8,128)(2,1)}, bf16[112,5120]{1,0:T(8,128)(2,1)S(1)}, u32[]{:S(2)}, u32[]{:S(2)}) %collective-permute-start.3) | collective-permute-done | bytes 1146912 | tf_op jit(solution)/shard_map/r1/ppermute | solution.py:34
  34.8 2.9 %collective-permute-done.6.refs_1_ = bf16[512,640]{1,0:T(8,128)(2,1)S(1)} collective-permute-done((bf16[512,640]{1,0:T(8,128)(2,1)S(1)}, bf16[512,640]{1,0:T(8,128)(2,1)S(1)}, u32[]{:S(2)}, u32[]{:S(2)}) %collective-permute-start.6) | collective-permute-done | bytes 655392 | tf_op jit(solution)/shard_map/b1/ppermute | solution.py:34
  37.7 2.9 %collective-permute-done.7.refs_2_ = bf16[512,640]{1,0:T(8,128)(2,1)S(1)} collective-permute-done((bf16[512,640]{1,0:T(8,128)(2,1)S(1)}, bf16[512,640]{1,0:T(8,128)(2,1)S(1)}, u32[]{:S(2)}, u32[]{:S(2)}) %collective-permute-start.7) | collective-permute-done | bytes 655392 | tf_op jit(solution)/shard_map/b2/ppermute | solution.py:34
  40.8 2.8 %collective-permute-start.13 = (bf16[1536,640]{1,0:T(8,128)(2,1)S(1)}, bf16[1536,640]{1,0:T(8,128)(2,1)S(1)}, u32[]{:S(2)}, u32[]{:S(2)}) collective-permute-start(bf16[1536,640]{1,0:T(8,128)(2,1)S(1)} %pad_maximum_fusion), channel_id=1, source_target_pairs={{0,1},{1,0},{2,3},{3,2},{4,5},{5,4},{6,7},{7,6},{8,9},{9,8},{10,11... | collective-permute-start | bytes 5898248 | tf_op jit(solution)/shard_map/b_swap/ppermute | solution.py:34
  43.6 3.1 %collective-permute-start.10 = (bf16[112,5120]{1,0:T(8,128)(2,1)}, bf16[112,5120]{1,0:T(8,128)(2,1)S(1)}, u32[]{:S(2)}, u32[]{:S(2)}) collective-permute-start(bf16[112,5120]{1,0:T(8,128)(2,1)} %collective-permute-done.4.refs_8_), channel_id=1, source_target_pairs={{0,24},{1,25},{2,26},{3,27},{4,28},{5,29},{6,30},{7,31},{8,0},{9,1... | collective-permute-start | bytes 3440648 | tf_op jit(solution)/shard_map/r6/ppermute | solution.py:34
  48.1 5.2 %collective-permute-done.11.refs_3_ = bf16[512,640]{1,0:T(8,128)(2,1)S(1)} collective-permute-done((bf16[512,640]{1,0:T(8,128)(2,1)S(1)}, bf16[512,640]{1,0:T(8,128)(2,1)S(1)}, u32[]{:S(2)}, u32[]{:S(2)}) %collective-permute-start.11) | collective-permute-done | bytes 655392 | tf_op jit(solution)/shard_map/b_far/ppermute | solution.py:34
  55.7 2.4 %early.1 = f32[512,192]{1,0:T(8,128)S(1)} custom-call(s32[24]{0:T(128)S(1)} %concatenate.18.where_ref, bf16[512,640]{1,0:T(8,128)(2,1)S(1)} %copy-done.5, bf16[512,640]{1,0:T(8,128)(2,1)S(1)} %copy-done.2, bf16[64,5120]{1,0:T(8,128)(2,1)S(1)} %bitcast.32, bf16[512,1792]{1,0:T(8,128)(2,1)S(1)} %copy-done, bf16[512,1792]{1,0:T(8,128)(2,1)S(1)} %copy-done.1, ...), custom_call_target="tpu_custom_call" | custom-call | flops 1048576 | bytes 65536 | tf_op jit(solution)/shard_map/early/pallas_call | solution.py:149
  58.1 13.8 %collective-permute-done.10.refs_8_.refs_12_ = bf16[112,5120]{1,0:T(8,128)(2,1)S(1)} collective-permute-done((bf16[112,5120]{1,0:T(8,128)(2,1)}, bf16[112,5120]{1,0:T(8,128)(2,1)S(1)}, u32[]{:S(2)}, u32[]{:S(2)}) %collective-permute-start.10) | collective-permute-done | bytes 1146912 | tf_op jit(solution)/shard_map/r6/ppermute | solution.py:34
  71.9 2.3 %collective-permute-done.9.refs_7_.refs_11_ = bf16[112,5120]{1,0:T(8,128)(2,1)S(1)} collective-permute-done((bf16[112,5120]{1,0:T(8,128)(2,1)S(1)}, bf16[112,5120]{1,0:T(8,128)(2,1)S(1)}, u32[]{:S(2)}, u32[]{:S(2)}) %collective-permute-start.9) | collective-permute-done | bytes 1146912 | tf_op jit(solution)/shard_map/r5/ppermute | solution.py:34
  74.2 4.2 %product.5 = bf16[512,512]{1,0:T(8,128)(2,1)S(1)} custom-call(s32[24]{0:T(128)S(1)} %concatenate.18.where_ref, bf16[512,640]{1,0:T(8,128)(2,1)S(1)} %collective-permute-done.refs_0_, bf16[512,640]{1,0:T(8,128)(2,1)S(1)} %collective-permute-done.6.refs_1_, bf16[512,640]{1,0:T(8,128)(2,1)S(1)} %collective-permute-done.7.refs_2_, ...), custom_call_target="tpu_custom_call" | custom-call | flops 1048576 | bytes 65536 | tf_op jit(solution)/shard_map/product/pallas_call | solution.py:123
  78.4 2.2 %collective-permute-start.16 = (bf16[1536,640]{1,0:T(8,128)(2,1)S(1)}, bf16[1536,640]{1,0:T(8,128)(2,1)S(1)}, u32[]{:S(2)}, u32[]{:S(2)}) collective-permute-start(bf16[1536,640]{1,0:T(8,128)(2,1)S(1)} %pad_maximum_fusion.1), channel_id=1, source_target_pairs={{0,1},{1,0},{2,3},{3,2},{4,5},{5,4},{6,7},{7,6},{8,9},{9,8},{10,11... | collective-permute-start | bytes 5898248 | tf_op jit(solution)/shard_map/a_swap/ppermute | solution.py:34
  81.6 3.4 %product.6 = bf16[512,384]{1,0:T(8,128)(2,1)S(1)} custom-call(s32[24]{0:T(128)S(1)} %concatenate.18.where_ref, bf16[512,640]{1,0:T(8,128)(2,1)S(1)} %collective-permute-done.refs_0_, bf16[512,640]{1,0:T(8,128)(2,1)S(1)} %collective-permute-done.6.refs_1_, bf16[512,640]{1,0:T(8,128)(2,1)S(1)} %collective-permute-done.7.refs_2_, ...), custom_call_target="tpu_custom_call" | custom-call | flops 1048576 | bytes 65536 | tf_op jit(solution)/shard_map/product/pallas_call | solution.py:123
  86.2 2.0 %collective-permute-start.15 = (bf16[512,384]{1,0:T(8,128)(2,1)S(1)}, bf16[512,384]{1,0:T(8,128)(2,1)S(1)}, u32[]{:S(2)}, u32[]{:S(2)}) collective-permute-start(bf16[512,384]{1,0:T(8,128)(2,1)S(1)} %product.6), channel_id=1, source_target_pairs={{0,96},{1,97},{2,98},{3,99},{4,100},{5,101},{6,102},{7,103},{8,104... | collective-permute-start | bytes 1179656 | tf_op jit(solution)/shard_map/mate_grad2/ppermute | solution.py:34
  88.2 6.9 %product.7.refs_0_ = f32[512,896]{1,0:T(8,128)S(1)} custom-call(s32[24]{0:T(128)S(1)} %concatenate.18.where_ref, bf16[512,640]{1,0:T(8,128)(2,1)S(1)} %copy-done.2, bf16[512,640]{1,0:T(8,128)(2,1)S(1)} %collective-permute-done.1.refs_1_, bf16[512,640]{1,0:T(8,128)(2,1)S(1)} %collective-permute-done.2.refs_2_, ...), custom_call_target="tpu_custom_call" | custom-call | flops 1048576 | bytes 65536 | tf_op jit(solution)/shard_map/product/pallas_call | solution.py:123
  95.1 3.4 %collective-permute-start.23 = (f32[256,192]{1,0:T(8,128)S(1)}, f32[256,192]{1,0:T(8,128)S(1)}, u32[]{:S(2)}, u32[]{:S(2)}) collective-permute-start(f32[256,192]{1,0:T(8,128)S(1)} %add.231), channel_id=1, source_target_pairs={{0,4},{1,5},{2,6},{3,7},{4,0},{5,1},{6,2},{7,3},{8,12},{9,13},{10,... | collective-permute-start | bytes 589832 | tf_op jit(solution)/shard_map/s_far/ppermute | solution.py:34
  98.5 2.2 %product.8 = bf16[512,128]{1,0:T(8,128)(2,1)S(1)} custom-call(s32[24]{0:T(128)S(1)} %concatenate.18.where_ref, bf16[512,640]{1,0:T(8,128)(2,1)S(1)} %collective-permute-done.refs_0_, bf16[512,640]{1,0:T(8,128)(2,1)S(1)} %collective-permute-done.6.refs_1_, bf16[512,640]{1,0:T(8,128)(2,1)S(1)} %collective-permute-done.7.refs_2_, ...), custom_call_target="tpu_custom_call" | custom-call | flops 1048576 | bytes 65536 | tf_op jit(solution)/shard_map/product/pallas_call | solution.py:123
  100.7 2.2 %product.9.refs_1_ = f32[512,128]{1,0:T(8,128)S(1)} custom-call(s32[24]{0:T(128)S(1)} %concatenate.18.where_ref, bf16[512,640]{1,0:T(8,128)(2,1)S(1)} %copy-done.2, bf16[512,640]{1,0:T(8,128)(2,1)S(1)} %collective-permute-done.1.refs_1_, bf16[512,640]{1,0:T(8,128)(2,1)S(1)} %collective-permute-done.2.refs_2_, ...), custom_call_target="tpu_custom_call" | custom-call | flops 1048576 | bytes 65536 | tf_op jit(solution)/shard_map/product/pallas_call | solution.py:123
  102.8 1.4 %collective-permute-done.23 = f32[256,192]{1,0:T(8,128)S(1)} collective-permute-done((f32[256,192]{1,0:T(8,128)S(1)}, f32[256,192]{1,0:T(8,128)S(1)}, u32[]{:S(2)}, u32[]{:S(2)}) %collective-permute-start.23) | collective-permute-done | bytes 196640 | tf_op jit(solution)/shard_map/s_far/ppermute | solution.py:34
  104.3 1.6 %collective-permute-start.24 = (f32[256,192]{1,0:T(8,128)S(1)}, f32[256,192]{1,0:T(8,128)S(1)}, u32[]{:S(2)}, u32[]{:S(2)}) collective-permute-start(f32[256,192]{1,0:T(8,128)S(1)} %add.232), channel_id=1, source_target_pairs={{0,1},{1,0},{2,3},{3,2},{4,5},{5,4},{6,7},{7,6},{8,9},{9,8},{10,11... | collective-permute-start | bytes 589832 | tf_op jit(solution)/shard_map/s_core/ppermute | solution.py:34
  106.5 3.8 %own_half.1 = (bf16[512,1792]{1,0:T(8,128)(2,1)}, bf16[512,1792]{1,0:T(8,128)(2,1)}, f32[512,128]{1,0:T(8,128)S(1)}) custom-call(s32[24]{0:T(128)S(1)} %concatenate.18.where_ref, bf16[512,1792]{1,0:T(8,128)(2,1)S(1)} %copy-done, bf16[512,1792]{1,0:T(8,128)(2,1)S(1)} %copy-done.1, bf16[64,1792]{1,0:T(8,128)(2,1)S(1)} %bitcast.30, ...), custom_call_target="tpu_custom_call" | custom-call | flops 1048576 | bytes 65536 | tf_op jit(solution)/shard_map/own_half/pallas_call | solution.py:218
  110.3 1.8 %collective-permute-done.20.refs_2_ = bf16[512,128]{1,0:T(8,128)(2,1)S(1)} collective-permute-done((bf16[512,128]{1,0:T(8,128)(2,1)S(1)}, bf16[512,128]{1,0:T(8,128)(2,1)S(1)}, u32[]{:S(2)}, u32[]{:S(2)}) %collective-permute-start.20) | collective-permute-done | bytes 131104 | tf_op jit(solution)/shard_map/mate_grad3/ppermute | solution.py:34
  113.3 4.4 %other_half.1 = (bf16[512,1792]{1,0:T(8,128)(2,1)}, bf16[512,1792]{1,0:T(8,128)(2,1)}, f32[256,128]{1,0:T(8,128)S(1)}) custom-call(s32[24]{0:T(128)S(1)} %concatenate.18.where_ref, bf16[512,1792]{1,0:T(8,128)(2,1)S(1)} %copy-done, bf16[512,1792]{1,0:T(8,128)(2,1)S(1)} %copy-done.1, ...), custom_call_target="tpu_custom_call", output_to_operand_aliasing={{0}: (7, {}), {1}: (8, {})} | custom-call | flops 1048576 | bytes 65536 | tf_op jit(solution)/shard_map/other_half/pallas_call | solution.py:262
  119.6 3.0 %collective-permute-start.26 = (f32[128,128]{1,0:T(8,128)S(1)}, f32[128,128]{1,0:T(8,128)S(1)}, u32[]{:S(2)}, u32[]{:S(2)}) collective-permute-start(f32[128,128]{1,0:T(8,128)S(1)} %select_add_fusion.1), channel_id=1, source_target_pairs={{0,4},{1,5},{2,6},{3,7},{4,0},{5,1},{6,2},{7,3},{8,12},{9,13},{10,... | collective-permute-start | bytes 196616 | tf_op jit(solution)/shard_map/send/ppermute | solution.py:34
  122.7 2.7 %collective-permute-start.28 = (f32[128,128]{1,0:T(8,128)S(1)}, f32[128,128]{1,0:T(8,128)S(1)}, u32[]{:S(2)}, u32[]{:S(2)}) collective-permute-start(f32[128,128]{1,0:T(8,128)S(1)} %select_add_fusion.1), channel_id=1, source_target_pairs={{0,6},{1,7},{2,0},{3,1},{4,2},{5,3},{6,4},{7,5},{8,14},{9,15},{10,... | collective-permute-start | bytes 196616 | tf_op jit(solution)/shard_map/down/ppermute | solution.py:34
  125.3 1.6 %collective-permute-done.27 = f32[128,128]{1,0:T(8,128)S(1)} collective-permute-done((f32[128,128]{1,0:T(8,128)S(1)}, f32[128,128]{1,0:T(8,128)S(1)}, u32[]{:S(2)}, u32[]{:S(2)}) %collective-permute-start.27) | collective-permute-done | bytes 65568 | tf_op jit(solution)/shard_map/up/ppermute | solution.py:34
  127.0 1.9 %collective-permute-start.29 = (f32[128,128]{1,0:T(8,128)S(1)}, f32[128,128]{1,0:T(8,128)S(1)}, u32[]{:S(2)}, u32[]{:S(2)}) collective-permute-start(f32[128,128]{1,0:T(8,128)S(1)} %add_add_fusion), channel_id=1, source_target_pairs={{0,1},{1,0},{2,3},{3,2},{4,5},{5,4},{6,7},{7,6},{8,9},{9,8},{10,11... | collective-permute-start | bytes 196616 | tf_op jit(solution)/shard_map/swap/ppermute | solution.py:34
  (73 shorter events, 17.7 us)
Async XLA Ops:
  0.6 19.3 %collective-permute-start = (bf16[512,640]{1,0:T(8,128)(2,1)}, bf16[512,640]{1,0:T(8,128)(2,1)S(1)}, u32[]{:S(2)}, u32[]{:S(2)}) collective-permute-start(bf16[512,640]{1,0:T(8,128)(2,1)} %refs_0_.3), channel_id=1, source_target_pairs={{0,96},{1,97},{2,98},{3,99},{4,100},{5,101},{6,102},{7,103},{8,104... | collective-permute-start | bytes 1966088 | tf_op jit(solution)/shard_map/mate_rows/ppermute | solution.py:34
  5.3 15.9 %collective-permute-start.1 = (bf16[512,640]{1,0:T(8,128)(2,1)}, bf16[512,640]{1,0:T(8,128)(2,1)S(1)}, u32[]{:S(2)}, u32[]{:S(2)}) collective-permute-start(bf16[512,640]{1,0:T(8,128)(2,1)} %refs_0_.3), channel_id=1, source_target_pairs={{0,2},{1,7},{2,4},{3,1},{4,6},{5,3},{6,0},{7,5},{8,10},{9,15},{10,... | collective-permute-start | bytes 1966088 | tf_op jit(solution)/shard_map/a1/ppermute | solution.py:34
  8.0 16.9 %collective-permute-start.2 = (bf16[512,640]{1,0:T(8,128)(2,1)}, bf16[512,640]{1,0:T(8,128)(2,1)S(1)}, u32[]{:S(2)}, u32[]{:S(2)}) collective-permute-start(bf16[512,640]{1,0:T(8,128)(2,1)} %refs_0_.3), channel_id=1, source_target_pairs={{0,6},{1,3},{2,0},{3,5},{4,2},{5,7},{6,4},{7,1},{8,14},{9,11},{10,... | collective-permute-start | bytes 1966088 | tf_op jit(solution)/shard_map/a2/ppermute | solution.py:34
  8.0 26.7 %collective-permute-start.3 = (bf16[112,5120]{1,0:T(8,128)(2,1)}, bf16[112,5120]{1,0:T(8,128)(2,1)S(1)}, u32[]{:S(2)}, u32[]{:S(2)}) collective-permute-start(bf16[112,5120]{1,0:T(8,128)(2,1)} %refs_6_.3), channel_id=1, source_target_pairs={{0,8},{1,9},{2,10},{3,11},{4,12},{5,13},{6,14},{7,15},{8,16},{9,17... | collective-permute-start | bytes 3440648 | tf_op jit(solution)/shard_map/r1/ppermute | solution.py:34
  9.2 25.5 %collective-permute-start.4 = (bf16[112,5120]{1,0:T(8,128)(2,1)}, bf16[112,5120]{1,0:T(8,128)(2,1)}, u32[]{:S(2)}, u32[]{:S(2)}) collective-permute-start(bf16[112,5120]{1,0:T(8,128)(2,1)} %refs_6_.3), channel_id=1, source_target_pairs={{0,32},{1,25},{2,34},{3,27},{4,36},{5,29},{6,38},{7,31},{8,40},{9,... | collective-permute-start | bytes 3440648 | tf_op jit(solution)/shard_map/r2/ppermute | solution.py:34
  13.8 41.7 %copy-start.2 = (bf16[512,640]{1,0:T(8,128)(2,1)S(1)}, bf16[512,640]{1,0:T(8,128)(2,1)}, u32[]{:S(2)}) copy-start(bf16[512,640]{1,0:T(8,128)(2,1)} %refs_0_.3) | copy-start | bytes 1966084
  24.9 15.7 %collective-permute-start.5 = (bf16[112,5120]{1,0:T(8,128)(2,1)}, bf16[112,5120]{1,0:T(8,128)(2,1)S(1)}, u32[]{:S(2)}, u32[]{:S(2)}) collective-permute-start(bf16[112,5120]{1,0:T(8,128)(2,1)} %refs_6_.3), channel_id=1, source_target_pairs={{0,24},{1,33},{2,26},{3,35},{4,28},{5,37},{6,30},{7,39},{8,0},{9,4... | collective-permute-start | bytes 3440648 | tf_op jit(solution)/shard_map/r3/ppermute | solution.py:34
  24.9 12.8 %collective-permute-start.6 = (bf16[512,640]{1,0:T(8,128)(2,1)S(1)}, bf16[512,640]{1,0:T(8,128)(2,1)S(1)}, u32[]{:S(2)}, u32[]{:S(2)}) collective-permute-start(bf16[512,640]{1,0:T(8,128)(2,1)S(1)} %collective-permute-done.refs_0_), channel_id=1, source_target_pairs={{0,2},{1,7},{2,4},{3,1},{4,6},{5,3},{6,0},{7,5},{8,10},{9,15},{10,... | collective-permute-start | bytes 1966088 | tf_op jit(solution)/shard_map/b1/ppermute | solution.py:34
  24.9 15.6 %collective-permute-start.7 = (bf16[512,640]{1,0:T(8,128)(2,1)S(1)}, bf16[512,640]{1,0:T(8,128)(2,1)S(1)}, u32[]{:S(2)}, u32[]{:S(2)}) collective-permute-start(bf16[512,640]{1,0:T(8,128)(2,1)S(1)} %collective-permute-done.refs_0_), channel_id=1, source_target_pairs={{0,6},{1,3},{2,0},{3,5},{4,2},{5,7},{6,4},{7,1},{8,14},{9,11},{10,... | collective-permute-start | bytes 1966088 | tf_op jit(solution)/shard_map/b2/ppermute | solution.py:34
  40.8 13.8 %collective-permute-start.13 = (bf16[1536,640]{1,0:T(8,128)(2,1)S(1)}, bf16[1536,640]{1,0:T(8,128)(2,1)S(1)}, u32[]{:S(2)}, u32[]{:S(2)}) collective-permute-start(bf16[1536,640]{1,0:T(8,128)(2,1)S(1)} %pad_maximum_fusion), channel_id=1, source_target_pairs={{0,1},{1,0},{2,3},{3,2},{4,5},{5,4},{6,7},{7,6},{8,9},{9,8},{10,11... | collective-permute-start | bytes 5898248 | tf_op jit(solution)/shard_map/b_swap/ppermute | solution.py:34
  43.6 9.7 %collective-permute-start.11 = (bf16[512,640]{1,0:T(8,128)(2,1)S(1)}, bf16[512,640]{1,0:T(8,128)(2,1)S(1)}, u32[]{:S(2)}, u32[]{:S(2)}) collective-permute-start(bf16[512,640]{1,0:T(8,128)(2,1)S(1)} %collective-permute-done.6.refs_1_), channel_id=1, source_target_pairs={{0,2},{1,7},{2,4},{3,1},{4,6},{5,3},{6,0},{7,5},{8,10},{9,15},{10,... | collective-permute-start | bytes 1966088 | tf_op jit(solution)/shard_map/b_far/ppermute | solution.py:34
  43.6 28.3 %collective-permute-start.10 = (bf16[112,5120]{1,0:T(8,128)(2,1)}, bf16[112,5120]{1,0:T(8,128)(2,1)S(1)}, u32[]{:S(2)}, u32[]{:S(2)}) collective-permute-start(bf16[112,5120]{1,0:T(8,128)(2,1)} %collective-permute-done.4.refs_8_), channel_id=1, source_target_pairs={{0,24},{1,25},{2,26},{3,27},{4,28},{5,29},{6,30},{7,31},{8,0},{9,1... | collective-permute-start | bytes 3440648 | tf_op jit(solution)/shard_map/r6/ppermute | solution.py:34
  46.6 25.2 %collective-permute-start.8 = (bf16[112,5120]{1,0:T(8,128)(2,1)}, bf16[112,5120]{1,0:T(8,128)(2,1)S(1)}, u32[]{:S(2)}, u32[]{:S(2)}) collective-permute-start(bf16[112,5120]{1,0:T(8,128)(2,1)} %collective-permute-done.4.refs_8_), channel_id=1, source_target_pairs={{0,8},{1,33},{2,10},{3,35},{4,12},{5,37},{6,14},{7,39},{8,16},{9,4... | collective-permute-start | bytes 3440648 | tf_op jit(solution)/shard_map/r4/ppermute | solution.py:34
  47.2 26.9 %collective-permute-start.9 = (bf16[112,5120]{1,0:T(8,128)(2,1)S(1)}, bf16[112,5120]{1,0:T(8,128)(2,1)S(1)}, u32[]{:S(2)}, u32[]{:S(2)}) collective-permute-start(bf16[112,5120]{1,0:T(8,128)(2,1)S(1)} %collective-permute-done.3.refs_7_), channel_id=1, source_target_pairs={{0,8},{1,33},{2,10},{3,35},{4,12},{5,37},{6,14},{7,39},{8,16},{9,4... | collective-permute-start | bytes 3440648 | tf_op jit(solution)/shard_map/r5/ppermute | solution.py:34
  53.3 20.8 %collective-permute-start.12 = (bf16[512,640]{1,0:T(8,128)(2,1)S(1)}, bf16[512,640]{1,0:T(8,128)(2,1)S(1)}, u32[]{:S(2)}, u32[]{:S(2)}) collective-permute-start(bf16[512,640]{1,0:T(8,128)(2,1)S(1)} %collective-permute-done.1.refs_1_), channel_id=1, source_target_pairs={{0,2},{1,7},{2,4},{3,1},{4,6},{5,3},{6,0},{7,5},{8,10},{9,15},{10,... | collective-permute-start | bytes 1966088 | tf_op jit(solution)/shard_map/a_far/ppermute | solution.py:34
  54.5 19.6 %collective-permute-start.14 = (bf16[512,640]{1,0:T(8,128)(2,1)S(1)}, bf16[512,640]{1,0:T(8,128)(2,1)S(1)}, u32[]{:S(2)}, u32[]{:S(2)}) collective-permute-start(bf16[512,640]{1,0:T(8,128)(2,1)S(1)} %collective-permute-done.11.refs_3_), channel_id=1, source_target_pairs={{0,1},{1,0},{2,3},{3,2},{4,5},{5,4},{6,7},{7,6},{8,9},{9,8},{10,11... | collective-permute-start | bytes 1966088 | tf_op jit(solution)/shard_map/b_swap/ppermute | solution.py:34
  55.7 18.5 %copy-start.3 = (bf16[112,5120]{1,0:T(8,128)(2,1)S(1)}, bf16[112,5120]{1,0:T(8,128)(2,1)}, u32[]{:S(2)}) copy-start(bf16[112,5120]{1,0:T(8,128)(2,1)} %refs_6_.3) | copy-start | bytes 3440644
  78.4 9.8 %collective-permute-start.16 = (bf16[1536,640]{1,0:T(8,128)(2,1)S(1)}, bf16[1536,640]{1,0:T(8,128)(2,1)S(1)}, u32[]{:S(2)}, u32[]{:S(2)}) collective-permute-start(bf16[1536,640]{1,0:T(8,128)(2,1)S(1)} %pad_maximum_fusion.1), channel_id=1, source_target_pairs={{0,1},{1,0},{2,3},{3,2},{4,5},{5,4},{6,7},{7,6},{8,9},{9,8},{10,11... | collective-permute-start | bytes 5898248 | tf_op jit(solution)/shard_map/a_swap/ppermute | solution.py:34
  80.5 18.0 %collective-permute-start.19 = (bf16[112,5120]{1,0:T(8,128)(2,1)S(1)}, bf16[112,5120]{1,0:T(8,128)(2,1)S(1)}, u32[]{:S(2)}, u32[]{:S(2)}) collective-permute-start(bf16[112,5120]{1,0:T(8,128)(2,1)S(1)} %collective-permute-done.10.refs_8_.refs_12_), channel_id=1, source_target_pairs={{0,24},{1,33},{2,26},{3,35},{4,28},{5,37},{6,30},{7,39},{8,0},{9,4... | collective-permute-start | bytes 3440648 | tf_op jit(solution)/shard_map/r7/ppermute | solution.py:34
  81.0 5.2 %collective-permute-start.17 = (bf16[512,640]{1,0:T(8,128)(2,1)S(1)}, bf16[512,640]{1,0:T(8,128)(2,1)S(1)}, u32[]{:S(2)}, u32[]{:S(2)}) collective-permute-start(bf16[512,640]{1,0:T(8,128)(2,1)S(1)} %collective-permute-done.12.refs_3_), channel_id=1, source_target_pairs={{0,1},{1,0},{2,3},{3,2},{4,5},{5,4},{6,7},{7,6},{8,9},{9,8},{10,11... | collective-permute-start | bytes 1966088 | tf_op jit(solution)/shard_map/a_swap/ppermute | solution.py:34
  81.0 4.4 %collective-permute-start.21 = (f32[256,192]{1,0:T(8,128)S(1)}, f32[256,192]{1,0:T(8,128)S(1)}, u32[]{:S(2)}, u32[]{:S(2)}) collective-permute-start(f32[256,192]{1,0:T(8,128)S(1)} %slice_select_fusion), channel_id=1, source_target_pairs={{0,1},{1,0},{2,3},{3,2},{4,5},{5,4},{6,7},{7,6},{8,9},{9,8},{10,11... | collective-permute-start | bytes 589832 | tf_op jit(solution)/shard_map/s_core/ppermute | solution.py:34
  81.6 16.9 %collective-permute-start.18 = (bf16[512,512]{1,0:T(8,128)(2,1)S(1)}, bf16[512,512]{1,0:T(8,128)(2,1)S(1)}, u32[]{:S(2)}, u32[]{:S(2)}) collective-permute-start(bf16[512,512]{1,0:T(8,128)(2,1)S(1)} %product.5), channel_id=1, source_target_pairs={{0,96},{1,97},{2,98},{3,99},{4,100},{5,101},{6,102},{7,103},{8,104... | collective-permute-start | bytes 1572872 | tf_op jit(solution)/shard_map/mate_grad1/ppermute | solution.py:34
  85.5 9.6 %collective-permute-start.22 = (f32[256,192]{1,0:T(8,128)S(1)}, f32[256,192]{1,0:T(8,128)S(1)}, u32[]{:S(2)}, u32[]{:S(2)}) collective-permute-start(f32[256,192]{1,0:T(8,128)S(1)} %select_add_fusion), channel_id=1, source_target_pairs={{0,2},{1,3},{2,0},{3,1},{4,6},{5,7},{6,4},{7,5},{8,10},{9,11},{10,... | collective-permute-start | bytes 589832 | tf_op jit(solution)/shard_map/s_near/ppermute | solution.py:34
  86.2 20.3 %collective-permute-start.15 = (bf16[512,384]{1,0:T(8,128)(2,1)S(1)}, bf16[512,384]{1,0:T(8,128)(2,1)S(1)}, u32[]{:S(2)}, u32[]{:S(2)}) collective-permute-start(bf16[512,384]{1,0:T(8,128)(2,1)S(1)} %product.6), channel_id=1, source_target_pairs={{0,96},{1,97},{2,98},{3,99},{4,100},{5,101},{6,102},{7,103},{8,104... | collective-permute-start | bytes 1179656 | tf_op jit(solution)/shard_map/mate_grad2/ppermute | solution.py:34
  95.1 9.1 %collective-permute-start.23 = (f32[256,192]{1,0:T(8,128)S(1)}, f32[256,192]{1,0:T(8,128)S(1)}, u32[]{:S(2)}, u32[]{:S(2)}) collective-permute-start(f32[256,192]{1,0:T(8,128)S(1)} %add.231), channel_id=1, source_target_pairs={{0,4},{1,5},{2,6},{3,7},{4,0},{5,1},{6,2},{7,3},{8,12},{9,13},{10,... | collective-permute-start | bytes 589832 | tf_op jit(solution)/shard_map/s_far/ppermute | solution.py:34
  104.3 7.8 %collective-permute-start.24 = (f32[256,192]{1,0:T(8,128)S(1)}, f32[256,192]{1,0:T(8,128)S(1)}, u32[]{:S(2)}, u32[]{:S(2)}) collective-permute-start(f32[256,192]{1,0:T(8,128)S(1)} %add.232), channel_id=1, source_target_pairs={{0,1},{1,0},{2,3},{3,2},{4,5},{5,4},{6,7},{7,6},{8,9},{9,8},{10,11... | collective-permute-start | bytes 589832 | tf_op jit(solution)/shard_map/s_core/ppermute | solution.py:34
  105.9 6.3 %collective-permute-start.20 = (bf16[512,128]{1,0:T(8,128)(2,1)S(1)}, bf16[512,128]{1,0:T(8,128)(2,1)S(1)}, u32[]{:S(2)}, u32[]{:S(2)}) collective-permute-start(bf16[512,128]{1,0:T(8,128)(2,1)S(1)} %product.8), channel_id=1, source_target_pairs={{0,96},{1,97},{2,98},{3,99},{4,100},{5,101},{6,102},{7,103},{8,104... | collective-permute-start | bytes 393224 | tf_op jit(solution)/shard_map/mate_grad3/ppermute | solution.py:34
  117.8 1.8 %collective-permute-start.25 = (f32[128,128]{1,0:T(8,128)S(1)}, f32[128,128]{1,0:T(8,128)S(1)}, u32[]{:S(2)}, u32[]{:S(2)}) collective-permute-start(f32[128,128]{1,0:T(8,128)S(1)} %slice_select_fusion.1), channel_id=1, source_target_pairs={{0,1},{1,0},{2,3},{3,2},{4,5},{5,4},{6,7},{7,6},{8,9},{9,8},{10,11... | collective-permute-start | bytes 196616 | tf_op jit(solution)/shard_map/swap/ppermute | solution.py:34
  119.6 5.7 %collective-permute-start.26 = (f32[128,128]{1,0:T(8,128)S(1)}, f32[128,128]{1,0:T(8,128)S(1)}, u32[]{:S(2)}, u32[]{:S(2)}) collective-permute-start(f32[128,128]{1,0:T(8,128)S(1)} %select_add_fusion.1), channel_id=1, source_target_pairs={{0,4},{1,5},{2,6},{3,7},{4,0},{5,1},{6,2},{7,3},{8,12},{9,13},{10,... | collective-permute-start | bytes 196616 | tf_op jit(solution)/shard_map/send/ppermute | solution.py:34
  122.7 4.3 %collective-permute-start.27 = (f32[128,128]{1,0:T(8,128)S(1)}, f32[128,128]{1,0:T(8,128)S(1)}, u32[]{:S(2)}, u32[]{:S(2)}) collective-permute-start(f32[128,128]{1,0:T(8,128)S(1)} %select_add_fusion.1), channel_id=1, source_target_pairs={{0,2},{1,3},{2,4},{3,5},{4,6},{5,7},{6,0},{7,1},{8,10},{9,11},{10,... | collective-permute-start | bytes 196616 | tf_op jit(solution)/shard_map/up/ppermute | solution.py:34
  122.7 4.3 %collective-permute-start.28 = (f32[128,128]{1,0:T(8,128)S(1)}, f32[128,128]{1,0:T(8,128)S(1)}, u32[]{:S(2)}, u32[]{:S(2)}) collective-permute-start(f32[128,128]{1,0:T(8,128)S(1)} %select_add_fusion.1), channel_id=1, source_target_pairs={{0,6},{1,7},{2,0},{3,1},{4,2},{5,3},{6,4},{7,5},{8,14},{9,15},{10,... | collective-permute-start | bytes 196616 | tf_op jit(solution)/shard_map/down/ppermute | solution.py:34
  127.0 2.8 %collective-permute-start.29 = (f32[128,128]{1,0:T(8,128)S(1)}, f32[128,128]{1,0:T(8,128)S(1)}, u32[]{:S(2)}, u32[]{:S(2)}) collective-permute-start(f32[128,128]{1,0:T(8,128)S(1)} %add_add_fusion), channel_id=1, source_target_pairs={{0,1},{1,0},{2,3},{3,2},{4,5},{5,4},{6,7},{7,6},{8,9},{9,8},{10,11... | collective-permute-start | bytes 196616 | tf_op jit(solution)/shard_map/swap/ppermute | solution.py:34
  (5 other events, 75.0 us)

commit v9 on v8

--- a/solution.py
+++ b/solution.py
@@ -347,10 +347,11 @@
     a1, a2 = along_y(out_grad, 1, "a1"), along_y(out_grad, -1, "a2")
     r1 = route(own_w, "+", "+", "r1")
     r2 = route(own_w, "p", "-", "r2")
-    theirs, a1, a2, again, where = lax.optimization_barrier((theirs, a1, a2, own_w, where))
-    r3 = route(again, "-", "p", "r3")
+    r3 = route(own_w, "-", "p", "r3")
     b1, b2 = along_y(theirs, 1, "b1"), along_y(theirs, -1, "b2")
-    r1, r2, r3, b1, b2 = lax.optimization_barrier((r1, r2, r3, b1, b2))
+    r1, r2, r3, b1, b2, a1, a2, where = lax.optimization_barrier(
+        (r1, r2, r3, b1, b2, a1, a2, where)
+    )
     r6 = route(r2, "-", "-", "r6")
     r4 = route(r2, "+", "p", "r4")
     r5 = route(r1, "+", "p", "r5")

time: 131 us -> 132 us (level)
  waiting for transfers between devices: 53.7 us -> 52.1 us
  Pallas kernels: 30.6 us -> 32 us
    ppermute x30, waiting for transfers between devices: 53.7 us -> 52.1 us  [send(): return lax.ppermute(value, AXES, pairs)]
    pallas_call x5, Pallas kernels: 18.9 us -> 20.2 us  [product(): pl.pallas_call(functools.partial(product_kernel, shards), out_shape=jax.S...]
  transfers between devices with their start and end apart: 30 -> 30, of which waited for: 15 -> 14; matrix products, arithmetic and copies ran while one was open for 3% -> 3% of each run, Pallas kernels for 16% -> 16%
where the time goes in v9:
time: 132 us
  waiting for transfers between devices  52.1 us (39%)
  starting transfers between devices  41.8 us (32%)
  Pallas kernels  32 us (24%)
  local copies, waits for them, and re-layouts  2.96 us (2%)
  other arithmetic  2.14 us (2%)
    ppermute x30, waiting for transfers between devices, send(): return lax.ppermute(value, AXES, pairs)  52.1 us
    ppermute x30, starting transfers between devices, send(): return lax.ppermute(value, AXES, pairs)  41.8 us
    pallas_call x5, Pallas kernels, product(): pl.pallas_call(functools.partial(product_kernel, shards), out_shape=jax.S...  20.2 us
    pallas_call x1, Pallas kernels, other_half(): pl.pallas_call(functools.partial(other_kernel, len(h)), out_shape=(BIG, B...  4.44 us
    pallas_call x1, Pallas kernels, own_half(): pl.pallas_call(functools.partial(own_kernel, len(h)), out_shape=(BIG, BIG...  3.81 us
  transfers between devices with their start and end apart: 30, of which 14 were waited for; matrix products, arithmetic and copies ran while one was open for 3% of the time, Pallas kernels for 16%

profile of v9, /device:TPU:1, one launch (start us, length us, event | category | flops | bytes accessed | tf_op | source)
XLA Modules:
  0.0 131.9 jit_solution(12963131396174510288)
XLA Ops:
  0.6 4.7 %collective-permute-start.3 = (bf16[512,640]{1,0:T(8,128)(2,1)}, bf16[512,640]{1,0:T(8,128)(2,1)S(1)}, u32[]{:S(2)}, u32[]{:S(2)}) collective-permute-start(bf16[512,640]{1,0:T(8,128)(2,1)} %refs_0_.3), channel_id=1, source_target_pairs={{0,96},{1,97},{2,98},{3,99},{4,100},{5,101},{6,102},{7,103},{8,104... | collective-permute-start | bytes 1966088 | tf_op jit(solution)/shard_map/mate_rows/ppermute | solution.py:34
  5.3 2.7 %collective-permute-start.6 = (bf16[512,640]{1,0:T(8,128)(2,1)}, bf16[512,640]{1,0:T(8,128)(2,1)S(1)}, u32[]{:S(2)}, u32[]{:S(2)}) collective-permute-start(bf16[512,640]{1,0:T(8,128)(2,1)} %refs_0_.3), channel_id=1, source_target_pairs={{0,2},{1,7},{2,4},{3,1},{4,6},{5,3},{6,0},{7,5},{8,10},{9,15},{10,... | collective-permute-start | bytes 1966088 | tf_op jit(solution)/shard_map/a1/ppermute | solution.py:34
  9.2 1.5 %collective-permute-start.1 = (bf16[112,5120]{1,0:T(8,128)(2,1)}, bf16[112,5120]{1,0:T(8,128)(2,1)}, u32[]{:S(2)}, u32[]{:S(2)}) collective-permute-start(bf16[112,5120]{1,0:T(8,128)(2,1)} %refs_6_.3), channel_id=1, source_target_pairs={{0,32},{1,25},{2,34},{3,27},{4,36},{5,29},{6,38},{7,31},{8,40},{9,... | collective-permute-start | bytes 3440648 | tf_op jit(solution)/shard_map/r2/ppermute | solution.py:34
  10.7 9.4 %collective-permute-done.3.refs_0_ = bf16[512,640]{1,0:T(8,128)(2,1)S(1)} collective-permute-done((bf16[512,640]{1,0:T(8,128)(2,1)}, bf16[512,640]{1,0:T(8,128)(2,1)S(1)}, u32[]{:S(2)}, u32[]{:S(2)}) %collective-permute-start.3) | collective-permute-done | bytes 655392 | tf_op jit(solution)/shard_map/mate_rows/ppermute | solution.py:34
  21.2 3.4 %collective-permute-start.4 = (bf16[512,640]{1,0:T(8,128)(2,1)S(1)}, bf16[512,640]{1,0:T(8,128)(2,1)S(1)}, u32[]{:S(2)}, u32[]{:S(2)}) collective-permute-start(bf16[512,640]{1,0:T(8,128)(2,1)S(1)} %collective-permute-done.3.refs_0_), channel_id=1, source_target_pairs={{0,2},{1,7},{2,4},{3,1},{4,6},{5,3},{6,0},{7,5},{8,10},{9,15},{10,... | collective-permute-start | bytes 1966088 | tf_op jit(solution)/shard_map/b1/ppermute | solution.py:34
  25.1 1.4 %reduce_sum.29 = s32[]{:T(128)} reduce(s32[4]{0:T(128)} %param.15, s32[]{:T(128)} %constant.165.clone.1), dimensions={0}, to_apply=%region_2.3 | reduce | flops 3 | bytes 24 | tf_op jit(solution)/shard_map/reduce_sum | solution.py:340
  26.8 1.4 %concatenate.18.where_ref = s32[24]{0:T(128)S(1)} concatenate(s32[8]{0:T(128)S(1)} %get-tuple-element.72, s32[8]{0:T(128)S(1)} %get-tuple-element.71, s32[1]{0:T(128)} %bitcast.16, s32[1]{0:T(128)} %bitcast.17, s32[1]{0:T(128)} %bitcast.18, s32[1]{0:T(128)} %bitcast.19, s32[4]{0:T(128)} %param.15), dimensions={0} | concatenate | bytes 192 | tf_op jit(solution)/shard_map/concatenate | solution.py:336
  28.2 6.7 %collective-permute-done.refs_7_ = bf16[112,5120]{1,0:T(8,128)(2,1)} collective-permute-done((bf16[112,5120]{1,0:T(8,128)(2,1)}, bf16[112,5120]{1,0:T(8,128)(2,1)}, u32[]{:S(2)}, u32[]{:S(2)}) %collective-permute-start) | collective-permute-done | bytes 1146912 | tf_op jit(solution)/shard_map/r1/ppermute | solution.py:34
  34.9 4.1 %collective-permute-done.2.refs_9_ = bf16[112,5120]{1,0:T(8,128)(2,1)} collective-permute-done((bf16[112,5120]{1,0:T(8,128)(2,1)}, bf16[112,5120]{1,0:T(8,128)(2,1)}, u32[]{:S(2)}, u32[]{:S(2)}) %collective-permute-start.2) | collective-permute-done | bytes 1146912 | tf_op jit(solution)/shard_map/r3/ppermute | solution.py:34
  38.9 3.1 %collective-permute-done.5.refs_2_ = bf16[512,640]{1,0:T(8,128)(2,1)S(1)} collective-permute-done((bf16[512,640]{1,0:T(8,128)(2,1)S(1)}, bf16[512,640]{1,0:T(8,128)(2,1)S(1)}, u32[]{:S(2)}, u32[]{:S(2)}) %collective-permute-start.5) | collective-permute-done | bytes 655392 | tf_op jit(solution)/shard_map/b2/ppermute | solution.py:34
  43.3 2.4 %collective-permute-start.10 = (bf16[112,5120]{1,0:T(8,128)(2,1)}, bf16[112,5120]{1,0:T(8,128)(2,1)S(1)}, u32[]{:S(2)}, u32[]{:S(2)}) collective-permute-start(bf16[112,5120]{1,0:T(8,128)(2,1)} %collective-permute-done.1.refs_8_), channel_id=1, source_target_pairs={{0,24},{1,25},{2,26},{3,27},{4,28},{5,29},{6,30},{7,31},{8,0},{9,1... | collective-permute-start | bytes 3440648 | tf_op jit(solution)/shard_map/r6/ppermute | solution.py:34
  45.6 1.5 %collective-permute-start.9 = (bf16[112,5120]{1,0:T(8,128)(2,1)}, bf16[112,5120]{1,0:T(8,128)(2,1)S(1)}, u32[]{:S(2)}, u32[]{:S(2)}) collective-permute-start(bf16[112,5120]{1,0:T(8,128)(2,1)} %collective-permute-done.refs_7_), channel_id=1, source_target_pairs={{0,8},{1,33},{2,10},{3,35},{4,12},{5,37},{6,14},{7,39},{8,16},{9,4... | collective-permute-start | bytes 3440648 | tf_op jit(solution)/shard_map/r5/ppermute | solution.py:34
  47.1 5.2 %collective-permute-done.11.refs_3_ = bf16[512,640]{1,0:T(8,128)(2,1)S(1)} collective-permute-done((bf16[512,640]{1,0:T(8,128)(2,1)S(1)}, bf16[512,640]{1,0:T(8,128)(2,1)S(1)}, u32[]{:S(2)}, u32[]{:S(2)}) %collective-permute-start.11) | collective-permute-done | bytes 655392 | tf_op jit(solution)/shard_map/b_far/ppermute | solution.py:34
  52.3 1.9 %collective-permute-start.12 = (bf16[512,640]{1,0:T(8,128)(2,1)S(1)}, bf16[512,640]{1,0:T(8,128)(2,1)S(1)}, u32[]{:S(2)}, u32[]{:S(2)}) collective-permute-start(bf16[512,640]{1,0:T(8,128)(2,1)S(1)} %collective-permute-done.6.refs_1_), channel_id=1, source_target_pairs={{0,2},{1,7},{2,4},{3,1},{4,6},{5,3},{6,0},{7,5},{8,10},{9,15},{10,... | collective-permute-start | bytes 1966088 | tf_op jit(solution)/shard_map/a_far/ppermute | solution.py:34
  54.9 2.4 %early.1 = f32[512,192]{1,0:T(8,128)S(1)} custom-call(s32[24]{0:T(128)S(1)} %concatenate.18.where_ref, bf16[512,640]{1,0:T(8,128)(2,1)S(1)} %copy-done.5, bf16[512,640]{1,0:T(8,128)(2,1)S(1)} %copy-done.2, bf16[64,5120]{1,0:T(8,128)(2,1)S(1)} %bitcast.32, bf16[512,1792]{1,0:T(8,128)(2,1)S(1)} %copy-done, bf16[512,1792]{1,0:T(8,128)(2,1)S(1)} %copy-done.1, ...), custom_call_target="tpu_custom_call" | custom-call | flops 1048576 | bytes 65536 | tf_op jit(solution)/shard_map/early/pallas_call | solution.py:149
  57.3 13.4 %collective-permute-done.10.refs_8_.refs_12_ = bf16[112,5120]{1,0:T(8,128)(2,1)S(1)} collective-permute-done((bf16[112,5120]{1,0:T(8,128)(2,1)}, bf16[112,5120]{1,0:T(8,128)(2,1)S(1)}, u32[]{:S(2)}, u32[]{:S(2)}) %collective-permute-start.10) | collective-permute-done | bytes 1146912 | tf_op jit(solution)/shard_map/r6/ppermute | solution.py:34
  70.8 2.4 %collective-permute-done.9.refs_7_.refs_11_ = bf16[112,5120]{1,0:T(8,128)(2,1)S(1)} collective-permute-done((bf16[112,5120]{1,0:T(8,128)(2,1)}, bf16[112,5120]{1,0:T(8,128)(2,1)S(1)}, u32[]{:S(2)}, u32[]{:S(2)}) %collective-permute-start.9) | collective-permute-done | bytes 1146912 | tf_op jit(solution)/shard_map/r5/ppermute | solution.py:34
  73.1 4.9 %product.5 = bf16[512,512]{1,0:T(8,128)(2,1)S(1)} custom-call(s32[24]{0:T(128)S(1)} %concatenate.18.where_ref, bf16[512,640]{1,0:T(8,128)(2,1)S(1)} %collective-permute-done.3.refs_0_, bf16[512,640]{1,0:T(8,128)(2,1)S(1)} %collective-permute-done.4.refs_1_, bf16[512,640]{1,0:T(8,128)(2,1)S(1)} %collective-permute-done.5.refs_2_, ...), custom_call_target="tpu_custom_call" | custom-call | flops 1048576 | bytes 65536 | tf_op jit(solution)/shard_map/product/pallas_call | solution.py:123
  78.0 2.2 %collective-permute-start.16 = (bf16[1536,640]{1,0:T(8,128)(2,1)S(1)}, bf16[1536,640]{1,0:T(8,128)(2,1)S(1)}, u32[]{:S(2)}, u32[]{:S(2)}) collective-permute-start(bf16[1536,640]{1,0:T(8,128)(2,1)S(1)} %pad_maximum_fusion.1), channel_id=1, source_target_pairs={{0,1},{1,0},{2,3},{3,2},{4,5},{5,4},{6,7},{7,6},{8,9},{9,8},{10,11... | collective-permute-start | bytes 5898248 | tf_op jit(solution)/shard_map/a_swap/ppermute | solution.py:34
  81.8 3.4 %product.6 = bf16[512,384]{1,0:T(8,128)(2,1)S(1)} custom-call(s32[24]{0:T(128)S(1)} %concatenate.18.where_ref, bf16[512,640]{1,0:T(8,128)(2,1)S(1)} %collective-permute-done.3.refs_0_, bf16[512,640]{1,0:T(8,128)(2,1)S(1)} %collective-permute-done.4.refs_1_, bf16[512,640]{1,0:T(8,128)(2,1)S(1)} %collective-permute-done.5.refs_2_, ...), custom_call_target="tpu_custom_call" | custom-call | flops 1048576 | bytes 65536 | tf_op jit(solution)/shard_map/product/pallas_call | solution.py:123
  87.5 7.6 %product.7.refs_0_ = f32[512,896]{1,0:T(8,128)S(1)} custom-call(s32[24]{0:T(128)S(1)} %concatenate.18.where_ref, bf16[512,640]{1,0:T(8,128)(2,1)S(1)} %copy-done.2, bf16[512,640]{1,0:T(8,128)(2,1)S(1)} %collective-permute-done.6.refs_1_, bf16[512,640]{1,0:T(8,128)(2,1)S(1)} %collective-permute-done.7.refs_2_, ...), custom_call_target="tpu_custom_call" | custom-call | flops 1048576 | bytes 65536 | tf_op jit(solution)/shard_map/product/pallas_call | solution.py:123
  95.1 4.1 %collective-permute-start.23 = (f32[256,192]{1,0:T(8,128)S(1)}, f32[256,192]{1,0:T(8,128)S(1)}, u32[]{:S(2)}, u32[]{:S(2)}) collective-permute-start(f32[256,192]{1,0:T(8,128)S(1)} %add.231), channel_id=1, source_target_pairs={{0,4},{1,5},{2,6},{3,7},{4,0},{5,1},{6,2},{7,3},{8,12},{9,13},{10,... | collective-permute-start | bytes 589832 | tf_op jit(solution)/shard_map/s_far/ppermute | solution.py:34
  99.2 2.2 %product.8 = bf16[512,128]{1,0:T(8,128)(2,1)S(1)} custom-call(s32[24]{0:T(128)S(1)} %concatenate.18.where_ref, bf16[512,640]{1,0:T(8,128)(2,1)S(1)} %collective-permute-done.3.refs_0_, bf16[512,640]{1,0:T(8,128)(2,1)S(1)} %collective-permute-done.4.refs_1_, bf16[512,640]{1,0:T(8,128)(2,1)S(1)} %collective-permute-done.5.refs_2_, ...), custom_call_target="tpu_custom_call" | custom-call | flops 1048576 | bytes 65536 | tf_op jit(solution)/shard_map/product/pallas_call | solution.py:123
  101.4 2.2 %product.9.refs_1_ = f32[512,128]{1,0:T(8,128)S(1)} custom-call(s32[24]{0:T(128)S(1)} %concatenate.18.where_ref, bf16[512,640]{1,0:T(8,128)(2,1)S(1)} %copy-done.2, bf16[512,640]{1,0:T(8,128)(2,1)S(1)} %collective-permute-done.6.refs_1_, bf16[512,640]{1,0:T(8,128)(2,1)S(1)} %collective-permute-done.7.refs_2_, ...), custom_call_target="tpu_custom_call" | custom-call | flops 1048576 | bytes 65536 | tf_op jit(solution)/shard_map/product/pallas_call | solution.py:123
  104.9 1.7 %collective-permute-start.24 = (f32[256,192]{1,0:T(8,128)S(1)}, f32[256,192]{1,0:T(8,128)S(1)}, u32[]{:S(2)}, u32[]{:S(2)}) collective-permute-start(f32[256,192]{1,0:T(8,128)S(1)} %add.232), channel_id=1, source_target_pairs={{0,1},{1,0},{2,3},{3,2},{4,5},{5,4},{6,7},{7,6},{8,9},{9,8},{10,11... | collective-permute-start | bytes 589832 | tf_op jit(solution)/shard_map/s_core/ppermute | solution.py:34
  107.5 3.8 %own_half.1 = (bf16[512,1792]{1,0:T(8,128)(2,1)}, bf16[512,1792]{1,0:T(8,128)(2,1)}, f32[512,128]{1,0:T(8,128)S(1)}) custom-call(s32[24]{0:T(128)S(1)} %concatenate.18.where_ref, bf16[512,1792]{1,0:T(8,128)(2,1)S(1)} %copy-done, bf16[512,1792]{1,0:T(8,128)(2,1)S(1)} %copy-done.1, bf16[64,1792]{1,0:T(8,128)(2,1)S(1)} %bitcast.30, ...), custom_call_target="tpu_custom_call" | custom-call | flops 1048576 | bytes 65536 | tf_op jit(solution)/shard_map/own_half/pallas_call | solution.py:218
  111.3 1.6 %collective-permute-done.20.refs_2_ = bf16[512,128]{1,0:T(8,128)(2,1)S(1)} collective-permute-done((bf16[512,128]{1,0:T(8,128)(2,1)S(1)}, bf16[512,128]{1,0:T(8,128)(2,1)S(1)}, u32[]{:S(2)}, u32[]{:S(2)}) %collective-permute-start.20) | collective-permute-done | bytes 131104 | tf_op jit(solution)/shard_map/mate_grad3/ppermute | solution.py:34
  114.0 4.4 %other_half.1 = (bf16[512,1792]{1,0:T(8,128)(2,1)}, bf16[512,1792]{1,0:T(8,128)(2,1)}, f32[256,128]{1,0:T(8,128)S(1)}) custom-call(s32[24]{0:T(128)S(1)} %concatenate.18.where_ref, bf16[512,1792]{1,0:T(8,128)(2,1)S(1)} %copy-done, bf16[512,1792]{1,0:T(8,128)(2,1)S(1)} %copy-done.1, ...), custom_call_target="tpu_custom_call", output_to_operand_aliasing={{0}: (7, {}), {1}: (8, {})} | custom-call | flops 1048576 | bytes 65536 | tf_op jit(solution)/shard_map/other_half/pallas_call | solution.py:262
  120.3 3.0 %collective-permute-start.26 = (f32[128,128]{1,0:T(8,128)S(1)}, f32[128,128]{1,0:T(8,128)S(1)}, u32[]{:S(2)}, u32[]{:S(2)}) collective-permute-start(f32[128,128]{1,0:T(8,128)S(1)} %select_add_fusion.1), channel_id=1, source_target_pairs={{0,4},{1,5},{2,6},{3,7},{4,0},{5,1},{6,2},{7,3},{8,12},{9,13},{10,... | collective-permute-start | bytes 196616 | tf_op jit(solution)/shard_map/send/ppermute | solution.py:34
  123.4 2.7 %collective-permute-start.28 = (f32[128,128]{1,0:T(8,128)S(1)}, f32[128,128]{1,0:T(8,128)S(1)}, u32[]{:S(2)}, u32[]{:S(2)}) collective-permute-start(f32[128,128]{1,0:T(8,128)S(1)} %select_add_fusion.1), channel_id=1, source_target_pairs={{0,6},{1,7},{2,0},{3,1},{4,2},{5,3},{6,4},{7,5},{8,14},{9,15},{10,... | collective-permute-start | bytes 196616 | tf_op jit(solution)/shard_map/down/ppermute | solution.py:34
  126.0 1.6 %collective-permute-done.27 = f32[128,128]{1,0:T(8,128)S(1)} collective-permute-done((f32[128,128]{1,0:T(8,128)S(1)}, f32[128,128]{1,0:T(8,128)S(1)}, u32[]{:S(2)}, u32[]{:S(2)}) %collective-permute-start.27) | collective-permute-done | bytes 65568 | tf_op jit(solution)/shard_map/up/ppermute | solution.py:34
  127.7 1.9 %collective-permute-start.29 = (f32[128,128]{1,0:T(8,128)S(1)}, f32[128,128]{1,0:T(8,128)S(1)}, u32[]{:S(2)}, u32[]{:S(2)}) collective-permute-start(f32[128,128]{1,0:T(8,128)S(1)} %add_add_fusion), channel_id=1, source_target_pairs={{0,1},{1,0},{2,3},{3,2},{4,5},{5,4},{6,7},{7,6},{8,9},{9,8},{10,11... | collective-permute-start | bytes 196616 | tf_op jit(solution)/shard_map/swap/ppermute | solution.py:34
  (73 shorter events, 16.3 us)
Async XLA Ops:
  0.6 19.4 %collective-permute-start.3 = (bf16[512,640]{1,0:T(8,128)(2,1)}, bf16[512,640]{1,0:T(8,128)(2,1)S(1)}, u32[]{:S(2)}, u32[]{:S(2)}) collective-permute-start(bf16[512,640]{1,0:T(8,128)(2,1)} %refs_0_.3), channel_id=1, source_target_pairs={{0,96},{1,97},{2,98},{3,99},{4,100},{5,101},{6,102},{7,103},{8,104... | collective-permute-start | bytes 1966088 | tf_op jit(solution)/shard_map/mate_rows/ppermute | solution.py:34
  5.3 15.9 %collective-permute-start.6 = (bf16[512,640]{1,0:T(8,128)(2,1)}, bf16[512,640]{1,0:T(8,128)(2,1)S(1)}, u32[]{:S(2)}, u32[]{:S(2)}) collective-permute-start(bf16[512,640]{1,0:T(8,128)(2,1)} %refs_0_.3), channel_id=1, source_target_pairs={{0,2},{1,7},{2,4},{3,1},{4,6},{5,3},{6,0},{7,5},{8,10},{9,15},{10,... | collective-permute-start | bytes 1966088 | tf_op jit(solution)/shard_map/a1/ppermute | solution.py:34
  8.0 17.0 %collective-permute-start.7 = (bf16[512,640]{1,0:T(8,128)(2,1)}, bf16[512,640]{1,0:T(8,128)(2,1)S(1)}, u32[]{:S(2)}, u32[]{:S(2)}) collective-permute-start(bf16[512,640]{1,0:T(8,128)(2,1)} %refs_0_.3), channel_id=1, source_target_pairs={{0,6},{1,3},{2,0},{3,5},{4,2},{5,7},{6,4},{7,1},{8,14},{9,11},{10,... | collective-permute-start | bytes 1966088 | tf_op jit(solution)/shard_map/a2/ppermute | solution.py:34
  8.0 26.8 %collective-permute-start = (bf16[112,5120]{1,0:T(8,128)(2,1)}, bf16[112,5120]{1,0:T(8,128)(2,1)}, u32[]{:S(2)}, u32[]{:S(2)}) collective-permute-start(bf16[112,5120]{1,0:T(8,128)(2,1)} %refs_6_.3), channel_id=1, source_target_pairs={{0,8},{1,9},{2,10},{3,11},{4,12},{5,13},{6,14},{7,15},{8,16},{9,17... | collective-permute-start | bytes 3440648 | tf_op jit(solution)/shard_map/r1/ppermute | solution.py:34
  9.2 25.6 %collective-permute-start.1 = (bf16[112,5120]{1,0:T(8,128)(2,1)}, bf16[112,5120]{1,0:T(8,128)(2,1)}, u32[]{:S(2)}, u32[]{:S(2)}) collective-permute-start(bf16[112,5120]{1,0:T(8,128)(2,1)} %refs_6_.3), channel_id=1, source_target_pairs={{0,32},{1,25},{2,34},{3,27},{4,36},{5,29},{6,38},{7,31},{8,40},{9,... | collective-permute-start | bytes 3440648 | tf_op jit(solution)/shard_map/r2/ppermute | solution.py:34
  20.1 18.9 %collective-permute-start.2 = (bf16[112,5120]{1,0:T(8,128)(2,1)}, bf16[112,5120]{1,0:T(8,128)(2,1)}, u32[]{:S(2)}, u32[]{:S(2)}) collective-permute-start(bf16[112,5120]{1,0:T(8,128)(2,1)} %refs_6_.3), channel_id=1, source_target_pairs={{0,24},{1,33},{2,26},{3,35},{4,28},{5,37},{6,30},{7,39},{8,0},{9,4... | collective-permute-start | bytes 3440648 | tf_op jit(solution)/shard_map/r3/ppermute | solution.py:34
  21.2 17.7 %collective-permute-start.4 = (bf16[512,640]{1,0:T(8,128)(2,1)S(1)}, bf16[512,640]{1,0:T(8,128)(2,1)S(1)}, u32[]{:S(2)}, u32[]{:S(2)}) collective-permute-start(bf16[512,640]{1,0:T(8,128)(2,1)S(1)} %collective-permute-done.3.refs_0_), channel_id=1, source_target_pairs={{0,2},{1,7},{2,4},{3,1},{4,6},{5,3},{6,0},{7,5},{8,10},{9,15},{10,... | collective-permute-start | bytes 1966088 | tf_op jit(solution)/shard_map/b1/ppermute | solution.py:34
  25.0 17.1 %collective-permute-start.5 = (bf16[512,640]{1,0:T(8,128)(2,1)S(1)}, bf16[512,640]{1,0:T(8,128)(2,1)S(1)}, u32[]{:S(2)}, u32[]{:S(2)}) collective-permute-start(bf16[512,640]{1,0:T(8,128)(2,1)S(1)} %collective-permute-done.3.refs_0_), channel_id=1, source_target_pairs={{0,6},{1,3},{2,0},{3,5},{4,2},{5,7},{6,4},{7,1},{8,14},{9,11},{10,... | collective-permute-start | bytes 1966088 | tf_op jit(solution)/shard_map/b2/ppermute | solution.py:34
  28.2 26.5 %copy-start.2 = (bf16[512,640]{1,0:T(8,128)(2,1)S(1)}, bf16[512,640]{1,0:T(8,128)(2,1)}, u32[]{:S(2)}) copy-start(bf16[512,640]{1,0:T(8,128)(2,1)} %refs_0_.3) | copy-start | bytes 1966084
  42.3 11.9 %collective-permute-start.13 = (bf16[1536,640]{1,0:T(8,128)(2,1)S(1)}, bf16[1536,640]{1,0:T(8,128)(2,1)S(1)}, u32[]{:S(2)}, u32[]{:S(2)}) collective-permute-start(bf16[1536,640]{1,0:T(8,128)(2,1)S(1)} %pad_maximum_fusion), channel_id=1, source_target_pairs={{0,1},{1,0},{2,3},{3,2},{4,5},{5,4},{6,7},{7,6},{8,9},{9,8},{10,11... | collective-permute-start | bytes 5898248 | tf_op jit(solution)/shard_map/b_swap/ppermute | solution.py:34
  42.6 9.7 %collective-permute-start.11 = (bf16[512,640]{1,0:T(8,128)(2,1)S(1)}, bf16[512,640]{1,0:T(8,128)(2,1)S(1)}, u32[]{:S(2)}, u32[]{:S(2)}) collective-permute-start(bf16[512,640]{1,0:T(8,128)(2,1)S(1)} %collective-permute-done.4.refs_1_), channel_id=1, source_target_pairs={{0,2},{1,7},{2,4},{3,1},{4,6},{5,3},{6,0},{7,5},{8,10},{9,15},{10,... | collective-permute-start | bytes 1966088 | tf_op jit(solution)/shard_map/b_far/ppermute | solution.py:34
  43.3 27.5 %collective-permute-start.10 = (bf16[112,5120]{1,0:T(8,128)(2,1)}, bf16[112,5120]{1,0:T(8,128)(2,1)S(1)}, u32[]{:S(2)}, u32[]{:S(2)}) collective-permute-start(bf16[112,5120]{1,0:T(8,128)(2,1)} %collective-permute-done.1.refs_8_), channel_id=1, source_target_pairs={{0,24},{1,25},{2,26},{3,27},{4,28},{5,29},{6,30},{7,31},{8,0},{9,1... | collective-permute-start | bytes 3440648 | tf_op jit(solution)/shard_map/r6/ppermute | solution.py:34
  45.6 25.1 %collective-permute-start.8 = (bf16[112,5120]{1,0:T(8,128)(2,1)}, bf16[112,5120]{1,0:T(8,128)(2,1)S(1)}, u32[]{:S(2)}, u32[]{:S(2)}) collective-permute-start(bf16[112,5120]{1,0:T(8,128)(2,1)} %collective-permute-done.1.refs_8_), channel_id=1, source_target_pairs={{0,8},{1,33},{2,10},{3,35},{4,12},{5,37},{6,14},{7,39},{8,16},{9,4... | collective-permute-start | bytes 3440648 | tf_op jit(solution)/shard_map/r4/ppermute | solution.py:34
  45.6 27.5 %collective-permute-start.9 = (bf16[112,5120]{1,0:T(8,128)(2,1)}, bf16[112,5120]{1,0:T(8,128)(2,1)S(1)}, u32[]{:S(2)}, u32[]{:S(2)}) collective-permute-start(bf16[112,5120]{1,0:T(8,128)(2,1)} %collective-permute-done.refs_7_), channel_id=1, source_target_pairs={{0,8},{1,33},{2,10},{3,35},{4,12},{5,37},{6,14},{7,39},{8,16},{9,4... | collective-permute-start | bytes 3440648 | tf_op jit(solution)/shard_map/r5/ppermute | solution.py:34
  52.3 20.8 %collective-permute-start.12 = (bf16[512,640]{1,0:T(8,128)(2,1)S(1)}, bf16[512,640]{1,0:T(8,128)(2,1)S(1)}, u32[]{:S(2)}, u32[]{:S(2)}) collective-permute-start(bf16[512,640]{1,0:T(8,128)(2,1)S(1)} %collective-permute-done.6.refs_1_), channel_id=1, source_target_pairs={{0,2},{1,7},{2,4},{3,1},{4,6},{5,3},{6,0},{7,5},{8,10},{9,15},{10,... | collective-permute-start | bytes 1966088 | tf_op jit(solution)/shard_map/a_far/ppermute | solution.py:34
  54.2 18.9 %collective-permute-start.14 = (bf16[512,640]{1,0:T(8,128)(2,1)S(1)}, bf16[512,640]{1,0:T(8,128)(2,1)S(1)}, u32[]{:S(2)}, u32[]{:S(2)}) collective-permute-start(bf16[512,640]{1,0:T(8,128)(2,1)S(1)} %collective-permute-done.11.refs_3_), channel_id=1, source_target_pairs={{0,1},{1,0},{2,3},{3,2},{4,5},{5,4},{6,7},{7,6},{8,9},{9,8},{10,11... | collective-permute-start | bytes 1966088 | tf_op jit(solution)/shard_map/b_swap/ppermute | solution.py:34
  54.9 18.2 %copy-start.3 = (bf16[112,5120]{1,0:T(8,128)(2,1)S(1)}, bf16[112,5120]{1,0:T(8,128)(2,1)}, u32[]{:S(2)}) copy-start(bf16[112,5120]{1,0:T(8,128)(2,1)} %refs_6_.3) | copy-start | bytes 3440644
  78.0 9.4 %collective-permute-start.16 = (bf16[1536,640]{1,0:T(8,128)(2,1)S(1)}, bf16[1536,640]{1,0:T(8,128)(2,1)S(1)}, u32[]{:S(2)}, u32[]{:S(2)}) collective-permute-start(bf16[1536,640]{1,0:T(8,128)(2,1)S(1)} %pad_maximum_fusion.1), channel_id=1, source_target_pairs={{0,1},{1,0},{2,3},{3,2},{4,5},{5,4},{6,7},{7,6},{8,9},{9,8},{10,11... | collective-permute-start | bytes 5898248 | tf_op jit(solution)/shard_map/a_swap/ppermute | solution.py:34
  80.3 18.9 %collective-permute-start.19 = (bf16[112,5120]{1,0:T(8,128)(2,1)S(1)}, bf16[112,5120]{1,0:T(8,128)(2,1)S(1)}, u32[]{:S(2)}, u32[]{:S(2)}) collective-permute-start(bf16[112,5120]{1,0:T(8,128)(2,1)S(1)} %collective-permute-done.10.refs_8_.refs_12_), channel_id=1, source_target_pairs={{0,24},{1,33},{2,26},{3,35},{4,28},{5,37},{6,30},{7,39},{8,0},{9,4... | collective-permute-start | bytes 3440648 | tf_op jit(solution)/shard_map/r7/ppermute | solution.py:34
  80.3 6.0 %collective-permute-start.17 = (bf16[512,640]{1,0:T(8,128)(2,1)S(1)}, bf16[512,640]{1,0:T(8,128)(2,1)S(1)}, u32[]{:S(2)}, u32[]{:S(2)}) collective-permute-start(bf16[512,640]{1,0:T(8,128)(2,1)S(1)} %collective-permute-done.12.refs_3_), channel_id=1, source_target_pairs={{0,1},{1,0},{2,3},{3,2},{4,5},{5,4},{6,7},{7,6},{8,9},{9,8},{10,11... | collective-permute-start | bytes 1966088 | tf_op jit(solution)/shard_map/a_swap/ppermute | solution.py:34
  80.5 4.8 %collective-permute-start.21 = (f32[256,192]{1,0:T(8,128)S(1)}, f32[256,192]{1,0:T(8,128)S(1)}, u32[]{:S(2)}, u32[]{:S(2)}) collective-permute-start(f32[256,192]{1,0:T(8,128)S(1)} %slice_select_fusion), channel_id=1, source_target_pairs={{0,1},{1,0},{2,3},{3,2},{4,5},{5,4},{6,7},{7,6},{8,9},{9,8},{10,11... | collective-permute-start | bytes 589832 | tf_op jit(solution)/shard_map/s_core/ppermute | solution.py:34
  80.9 18.3 %collective-permute-start.18 = (bf16[512,512]{1,0:T(8,128)(2,1)S(1)}, bf16[512,512]{1,0:T(8,128)(2,1)S(1)}, u32[]{:S(2)}, u32[]{:S(2)}) collective-permute-start(bf16[512,512]{1,0:T(8,128)(2,1)S(1)} %product.5), channel_id=1, source_target_pairs={{0,96},{1,97},{2,98},{3,99},{4,100},{5,101},{6,102},{7,103},{8,104... | collective-permute-start | bytes 1572872 | tf_op jit(solution)/shard_map/mate_grad1/ppermute | solution.py:34
  85.3 9.7 %collective-permute-start.22 = (f32[256,192]{1,0:T(8,128)S(1)}, f32[256,192]{1,0:T(8,128)S(1)}, u32[]{:S(2)}, u32[]{:S(2)}) collective-permute-start(f32[256,192]{1,0:T(8,128)S(1)} %select_add_fusion), channel_id=1, source_target_pairs={{0,2},{1,3},{2,0},{3,1},{4,6},{5,7},{6,4},{7,5},{8,10},{9,11},{10,... | collective-permute-start | bytes 589832 | tf_op jit(solution)/shard_map/s_near/ppermute | solution.py:34
  86.2 21.2 %collective-permute-start.15 = (bf16[512,384]{1,0:T(8,128)(2,1)S(1)}, bf16[512,384]{1,0:T(8,128)(2,1)S(1)}, u32[]{:S(2)}, u32[]{:S(2)}) collective-permute-start(bf16[512,384]{1,0:T(8,128)(2,1)S(1)} %product.6), channel_id=1, source_target_pairs={{0,96},{1,97},{2,98},{3,99},{4,100},{5,101},{6,102},{7,103},{8,104... | collective-permute-start | bytes 1179656 | tf_op jit(solution)/shard_map/mate_grad2/ppermute | solution.py:34
  95.1 9.7 %collective-permute-start.23 = (f32[256,192]{1,0:T(8,128)S(1)}, f32[256,192]{1,0:T(8,128)S(1)}, u32[]{:S(2)}, u32[]{:S(2)}) collective-permute-start(f32[256,192]{1,0:T(8,128)S(1)} %add.231), channel_id=1, source_target_pairs={{0,4},{1,5},{2,6},{3,7},{4,0},{5,1},{6,2},{7,3},{8,12},{9,13},{10,... | collective-permute-start | bytes 589832 | tf_op jit(solution)/shard_map/s_far/ppermute | solution.py:34
  104.9 8.0 %collective-permute-start.24 = (f32[256,192]{1,0:T(8,128)S(1)}, f32[256,192]{1,0:T(8,128)S(1)}, u32[]{:S(2)}, u32[]{:S(2)}) collective-permute-start(f32[256,192]{1,0:T(8,128)S(1)} %add.232), channel_id=1, source_target_pairs={{0,1},{1,0},{2,3},{3,2},{4,5},{5,4},{6,7},{7,6},{8,9},{9,8},{10,11... | collective-permute-start | bytes 589832 | tf_op jit(solution)/shard_map/s_core/ppermute | solution.py:34
  106.6 6.3 %collective-permute-start.20 = (bf16[512,128]{1,0:T(8,128)(2,1)S(1)}, bf16[512,128]{1,0:T(8,128)(2,1)S(1)}, u32[]{:S(2)}, u32[]{:S(2)}) collective-permute-start(bf16[512,128]{1,0:T(8,128)(2,1)S(1)} %product.8), channel_id=1, source_target_pairs={{0,96},{1,97},{2,98},{3,99},{4,100},{5,101},{6,102},{7,103},{8,104... | collective-permute-start | bytes 393224 | tf_op jit(solution)/shard_map/mate_grad3/ppermute | solution.py:34
  118.5 1.8 %collective-permute-start.25 = (f32[128,128]{1,0:T(8,128)S(1)}, f32[128,128]{1,0:T(8,128)S(1)}, u32[]{:S(2)}, u32[]{:S(2)}) collective-permute-start(f32[128,128]{1,0:T(8,128)S(1)} %slice_select_fusion.1), channel_id=1, source_target_pairs={{0,1},{1,0},{2,3},{3,2},{4,5},{5,4},{6,7},{7,6},{8,9},{9,8},{10,11... | collective-permute-start | bytes 196616 | tf_op jit(solution)/shard_map/swap/ppermute | solution.py:34
  120.3 5.7 %collective-permute-start.26 = (f32[128,128]{1,0:T(8,128)S(1)}, f32[128,128]{1,0:T(8,128)S(1)}, u32[]{:S(2)}, u32[]{:S(2)}) collective-permute-start(f32[128,128]{1,0:T(8,128)S(1)} %select_add_fusion.1), channel_id=1, source_target_pairs={{0,4},{1,5},{2,6},{3,7},{4,0},{5,1},{6,2},{7,3},{8,12},{9,13},{10,... | collective-permute-start | bytes 196616 | tf_op jit(solution)/shard_map/send/ppermute | solution.py:34
  123.4 4.3 %collective-permute-start.27 = (f32[128,128]{1,0:T(8,128)S(1)}, f32[128,128]{1,0:T(8,128)S(1)}, u32[]{:S(2)}, u32[]{:S(2)}) collective-permute-start(f32[128,128]{1,0:T(8,128)S(1)} %select_add_fusion.1), channel_id=1, source_target_pairs={{0,2},{1,3},{2,4},{3,5},{4,6},{5,7},{6,0},{7,1},{8,10},{9,11},{10,... | collective-permute-start | bytes 196616 | tf_op jit(solution)/shard_map/up/ppermute | solution.py:34
  123.4 4.3 %collective-permute-start.28 = (f32[128,128]{1,0:T(8,128)S(1)}, f32[128,128]{1,0:T(8,128)S(1)}, u32[]{:S(2)}, u32[]{:S(2)}) collective-permute-start(f32[128,128]{1,0:T(8,128)S(1)} %select_add_fusion.1), channel_id=1, source_target_pairs={{0,6},{1,7},{2,0},{3,1},{4,2},{5,3},{6,4},{7,5},{8,14},{9,15},{10,... | collective-permute-start | bytes 196616 | tf_op jit(solution)/shard_map/down/ppermute | solution.py:34
  127.7 2.8 %collective-permute-start.29 = (f32[128,128]{1,0:T(8,128)S(1)}, f32[128,128]{1,0:T(8,128)S(1)}, u32[]{:S(2)}, u32[]{:S(2)}) collective-permute-start(f32[128,128]{1,0:T(8,128)S(1)} %add_add_fusion), channel_id=1, source_target_pairs={{0,1},{1,0},{2,3},{3,2},{4,5},{5,4},{6,7},{7,6},{8,9},{9,8},{10,11... | collective-permute-start | bytes 196616 | tf_op jit(solution)/shard_map/swap/ppermute | solution.py:34
  (5 other events, 63.5 us)

commit v10 on v9

--- a/solution.py
+++ b/solution.py
@@ -231,16 +231,11 @@
     )(where, gate, up, ph_t, *h)
 
 
-def other_kernel(n, where_ref, gate_ref, up_ref, ph_ref, part_ref, hi_ref, lo_ref,
-                 gg_in, gu_in, *refs):
-    gg_ref, gu_ref, feat_ref, held, acc = refs[n:]
-    i = pl.program_id(0)
-    part = grads(where_ref, 8, refs[:n], held, gate_ref, up_ref, ph_ref, gg_ref, gu_ref)
-    acc[pl.ds(pl.multiple_of(i * TILE, TILE), TILE), :] = part_ref[...] + part
-
-    @pl.when(i == ROWS // TILE - 1)
-    def _():
-        feat_ref[...] = twice(hi_ref[...], lo_ref[...], acc[...])
+def other_kernel(n, where_ref, gate_ref, up_ref, ph_ref, part_ref, gg_in, gu_in, *refs):
+    gg_ref, gu_ref, sum_ref, held = refs[n:]
+    sum_ref[...] = part_ref[...] + grads(
+        where_ref, 8, refs[:n], held, gate_ref, up_ref, ph_ref, gg_ref, gu_ref
+    )
 
 
 def parted(value):
@@ -255,35 +250,41 @@
     return total + jnp.dot(hi, right_hi, preferred_element_type=F32)
 
 
-def other_half(where, gate, up, h, ph_t, part, spread, gg, gu):
+def other_half(where, gate, up, h, ph_t, part, gg, gu):
     tile, ranks = row_tiles(lambda w: 1 - w[18])
-    feat = pl.BlockSpec((4 * RANK, 2 * RANK), lambda i, w: (0, 0))
-    spreads = pl.BlockSpec((4 * RANK, ROWS), lambda i, w: (0, 0))
+    narrow = pl.BlockSpec((TILE, 2 * RANK), lambda i, w: (i, 0))
     return pl.pallas_call(
         functools.partial(other_kernel, len(h)),
-        out_shape=(BIG, BIG, jax.ShapeDtypeStruct((4 * RANK, 2 * RANK), F32)),
+        out_shape=(BIG, BIG, jax.ShapeDtypeStruct((ROWS, 2 * RANK), F32)),
         grid_spec=pltpu.PrefetchScalarGridSpec(
             num_scalar_prefetch=1,
             grid=(ROWS // TILE,),
-            in_specs=[
-                tile,
-                tile,
-                ranks,
-                pl.BlockSpec((TILE, 2 * RANK), lambda i, w: (i, 0)),
-                spreads,
-                spreads,
-                ANY,
-                ANY,
-            ]
-            + pieces_of(h),
-            out_specs=(tile, tile, feat),
-            scratch_shapes=[pltpu.VMEM((TILE, 1024), F32), pltpu.VMEM((ROWS, 2 * RANK), F32)],
+            in_specs=[tile, tile, ranks, narrow, ANY, ANY] + pieces_of(h),
+            out_specs=(tile, tile, narrow),
+            scratch_shapes=[pltpu.VMEM((TILE, 1024), F32)],
         ),
-        input_output_aliases={7: 0, 8: 1},
+        input_output_aliases={5: 0, 6: 1},
         compiler_params=pltpu.CompilerParams(vmem_limit_bytes=14 << 20),
         cost_estimate=LIGHT,
         name="other_half",
-    )(where, gate, up, ph_t, part, *spread, gg, gu, *h)
+    )(where, gate, up, ph_t, part, gg, gu, *h)
+
+
+def feature_kernel(hi_ref, lo_ref, right_ref, out_ref):
+    out_ref[...] = twice(hi_ref[...], lo_ref[...], right_ref[...])
+
+
+def features_of(spread, right):
+    vmem = pl.BlockSpec(memory_space=pltpu.VMEM)
+    return pl.pallas_call(
+        feature_kernel,
+        out_shape=jax.ShapeDtypeStruct((4 * RANK, 2 * RANK), F32),
+        in_specs=[vmem] * 3,
+        out_specs=vmem,
+        compiler_params=pltpu.CompilerParams(vmem_limit_bytes=4 << 20),
+        cost_estimate=LIGHT,
+        name="features",
+    )(*spread, right)
 
 
 def spread_kernel(where_ref, sums_ref, hi_ref, lo_ref, feat_ref):
@@ -378,17 +379,18 @@
     far_y = send(half, lambda z, x, y, c: (z, x, y ^ 2, c), "s_far")
     h3 = product(BF16, after(where, h1_in, own1), b_mine, b_other, [r7])
     own2 = product(F32, after(where, h3), a_mine, a_other, [r7])
-    half += after(far_y, own2)
+    h_in = [h1_in, h2_in, mate(h3, "mate_grad3")]
+    grad_gate, grad_up, part = own_half(where, gate_pre, up_pre, (own1, own2), ph_t)
+    half += after(far_y, part, h_in[1], h_in[2])
     rest = swap(half, "s_core")
     sums = jnp.concatenate(
         [jnp.where(c == 0, half, rest), jnp.where(c == 0, rest, half)], axis=0
     )
-    h_in = [h1_in, h2_in, mate(h3, "mate_grad3")]
-    grad_gate, grad_up, part = own_half(after(where, h2_in), gate_pre, up_pre, (own1, own2), ph_t)
-    *spread, down_feat = spread_features(after(where, part, h_in[2]), sums)
-    grad_gate, grad_up, feat = other_half(
-        where, gate_pre, up_pre, h_in, ph_t, part, spread, grad_gate, grad_up
-    )
+    *spread, down_feat = spread_features(where, sums)
+    grad_gate, grad_up, part = other_half(
+        where, gate_pre, up_pre, h_in, ph_t, part, grad_gate, grad_up
+    )
+    feat = features_of(spread, part)
     total = jnp.concatenate([sum_tensor(feat, c), down_feat], axis=1)
     features = total.reshape(4, RANK, 3, RANK).transpose(0, 2, 1, 3).reshape(4, 3, RANK * RANK)
     return grad_gate, grad_up, features

time: 132 us -> 127 us (0.962)
  starting transfers between devices: 41.8 us -> 37 us
    ppermute x30, starting transfers between devices: 41.8 us -> 37 us  [send(): return lax.ppermute(value, AXES, pairs)]
  transfers between devices with their start and end apart: 30 -> 30, of which waited for: 14 -> 13; matrix products, arithmetic and copies ran while one was open for 3% -> 3% of each run, Pallas kernels for 16% -> 20%
where the time goes in v10:
time: 127 us; the launch traced here: 126 us
  waiting for transfers between devices  51.7 us (41%)
  starting transfers between devices  37 us (29%)
  Pallas kernels  31.6 us (25%)
  local copies, waits for them, and re-layouts  2.96 us (2%)
  other arithmetic  2.15 us (2%)
    ppermute x30, waiting for transfers between devices, send(): return lax.ppermute(value, AXES, pairs)  51.7 us
    ppermute x30, starting transfers between devices, send(): return lax.ppermute(value, AXES, pairs)  37 us
    pallas_call x5, Pallas kernels, product(): pl.pallas_call(functools.partial(product_kernel, shards), out_shape=jax.S...  20.2 us
    pallas_call x1, Pallas kernels, own_half(): pl.pallas_call(functools.partial(own_kernel, len(h)), out_shape=(BIG, BIG...  3.82 us
    pallas_call x1, Pallas kernels, other_half(): pl.pallas_call(functools.partial(other_kernel, len(h)), out_shape=(BIG, B...  3.76 us
  transfers between devices with their start and end apart: 30, of which 13 were waited for; matrix products, arithmetic and copies ran while one was open for 3% of the time, Pallas kernels for 20%

profile of v10, /device:TPU:1, one launch (start us, length us, event | category | flops | bytes accessed | tf_op | source)
XLA Modules:
  0.0 126.4 jit_solution(8743626672081592917)
XLA Ops:
  0.6 4.7 %collective-permute-start.3 = (bf16[512,640]{1,0:T(8,128)(2,1)}, bf16[512,640]{1,0:T(8,128)(2,1)S(1)}, u32[]{:S(2)}, u32[]{:S(2)}) collective-permute-start(bf16[512,640]{1,0:T(8,128)(2,1)} %refs_0_.3), channel_id=1, source_target_pairs={{0,96},{1,97},{2,98},{3,99},{4,100},{5,101},{6,102},{7,103},{8,104... | collective-permute-start | bytes 1966088 | tf_op jit(solution)/shard_map/mate_rows/ppermute | solution.py:34
  5.3 2.7 %collective-permute-start.6 = (bf16[512,640]{1,0:T(8,128)(2,1)}, bf16[512,640]{1,0:T(8,128)(2,1)S(1)}, u32[]{:S(2)}, u32[]{:S(2)}) collective-permute-start(bf16[512,640]{1,0:T(8,128)(2,1)} %refs_0_.3), channel_id=1, source_target_pairs={{0,2},{1,7},{2,4},{3,1},{4,6},{5,3},{6,0},{7,5},{8,10},{9,15},{10,... | collective-permute-start | bytes 1966088 | tf_op jit(solution)/shard_map/a1/ppermute | solution.py:34
  9.2 1.5 %collective-permute-start.1 = (bf16[112,5120]{1,0:T(8,128)(2,1)}, bf16[112,5120]{1,0:T(8,128)(2,1)}, u32[]{:S(2)}, u32[]{:S(2)}) collective-permute-start(bf16[112,5120]{1,0:T(8,128)(2,1)} %refs_6_.3), channel_id=1, source_target_pairs={{0,32},{1,25},{2,34},{3,27},{4,36},{5,29},{6,38},{7,31},{8,40},{9,... | collective-permute-start | bytes 3440648 | tf_op jit(solution)/shard_map/r2/ppermute | solution.py:34
  10.7 9.4 %collective-permute-done.3.refs_0_ = bf16[512,640]{1,0:T(8,128)(2,1)S(1)} collective-permute-done((bf16[512,640]{1,0:T(8,128)(2,1)}, bf16[512,640]{1,0:T(8,128)(2,1)S(1)}, u32[]{:S(2)}, u32[]{:S(2)}) %collective-permute-start.3) | collective-permute-done | bytes 655392 | tf_op jit(solution)/shard_map/mate_rows/ppermute | solution.py:34
  21.2 3.4 %collective-permute-start.4 = (bf16[512,640]{1,0:T(8,128)(2,1)S(1)}, bf16[512,640]{1,0:T(8,128)(2,1)S(1)}, u32[]{:S(2)}, u32[]{:S(2)}) collective-permute-start(bf16[512,640]{1,0:T(8,128)(2,1)S(1)} %collective-permute-done.3.refs_0_), channel_id=1, source_target_pairs={{0,2},{1,7},{2,4},{3,1},{4,6},{5,3},{6,0},{7,5},{8,10},{9,15},{10,... | collective-permute-start | bytes 1966088 | tf_op jit(solution)/shard_map/b1/ppermute | solution.py:34
  25.1 1.4 %reduce_sum.29 = s32[]{:T(128)} reduce(s32[4]{0:T(128)} %param.15, s32[]{:T(128)} %constant.165.clone.1), dimensions={0}, to_apply=%region_2.3 | reduce | flops 3 | bytes 24 | tf_op jit(solution)/shard_map/reduce_sum | solution.py:341
  26.8 1.4 %concatenate.18.where_ref = s32[24]{0:T(128)S(1)} concatenate(s32[8]{0:T(128)S(1)} %get-tuple-element.68, s32[8]{0:T(128)S(1)} %get-tuple-element.67, s32[1]{0:T(128)} %bitcast.16, s32[1]{0:T(128)} %bitcast.17, s32[1]{0:T(128)} %bitcast.18, s32[1]{0:T(128)} %bitcast.19, s32[4]{0:T(128)} %param.15), dimensions={0} | concatenate | bytes 192 | tf_op jit(solution)/shard_map/concatenate | solution.py:337
  28.2 6.7 %collective-permute-done.refs_7_ = bf16[112,5120]{1,0:T(8,128)(2,1)} collective-permute-done((bf16[112,5120]{1,0:T(8,128)(2,1)}, bf16[112,5120]{1,0:T(8,128)(2,1)}, u32[]{:S(2)}, u32[]{:S(2)}) %collective-permute-start) | collective-permute-done | bytes 1146912 | tf_op jit(solution)/shard_map/r1/ppermute | solution.py:34
  34.9 4.1 %collective-permute-done.2.refs_9_ = bf16[112,5120]{1,0:T(8,128)(2,1)} collective-permute-done((bf16[112,5120]{1,0:T(8,128)(2,1)}, bf16[112,5120]{1,0:T(8,128)(2,1)}, u32[]{:S(2)}, u32[]{:S(2)}) %collective-permute-start.2) | collective-permute-done | bytes 1146912 | tf_op jit(solution)/shard_map/r3/ppermute | solution.py:34
  38.9 3.1 %collective-permute-done.5.refs_2_ = bf16[512,640]{1,0:T(8,128)(2,1)S(1)} collective-permute-done((bf16[512,640]{1,0:T(8,128)(2,1)S(1)}, bf16[512,640]{1,0:T(8,128)(2,1)S(1)}, u32[]{:S(2)}, u32[]{:S(2)}) %collective-permute-start.5) | collective-permute-done | bytes 655392 | tf_op jit(solution)/shard_map/b2/ppermute | solution.py:34
  43.3 2.4 %collective-permute-start.10 = (bf16[112,5120]{1,0:T(8,128)(2,1)}, bf16[112,5120]{1,0:T(8,128)(2,1)S(1)}, u32[]{:S(2)}, u32[]{:S(2)}) collective-permute-start(bf16[112,5120]{1,0:T(8,128)(2,1)} %collective-permute-done.1.refs_8_), channel_id=1, source_target_pairs={{0,24},{1,25},{2,26},{3,27},{4,28},{5,29},{6,30},{7,31},{8,0},{9,1... | collective-permute-start | bytes 3440648 | tf_op jit(solution)/shard_map/r6/ppermute | solution.py:34
  45.6 1.5 %collective-permute-start.9 = (bf16[112,5120]{1,0:T(8,128)(2,1)}, bf16[112,5120]{1,0:T(8,128)(2,1)S(1)}, u32[]{:S(2)}, u32[]{:S(2)}) collective-permute-start(bf16[112,5120]{1,0:T(8,128)(2,1)} %collective-permute-done.refs_7_), channel_id=1, source_target_pairs={{0,8},{1,33},{2,10},{3,35},{4,12},{5,37},{6,14},{7,39},{8,16},{9,4... | collective-permute-start | bytes 3440648 | tf_op jit(solution)/shard_map/r5/ppermute | solution.py:34
  47.1 5.2 %collective-permute-done.11.refs_3_ = bf16[512,640]{1,0:T(8,128)(2,1)S(1)} collective-permute-done((bf16[512,640]{1,0:T(8,128)(2,1)S(1)}, bf16[512,640]{1,0:T(8,128)(2,1)S(1)}, u32[]{:S(2)}, u32[]{:S(2)}) %collective-permute-start.11) | collective-permute-done | bytes 655392 | tf_op jit(solution)/shard_map/b_far/ppermute | solution.py:34
  52.3 1.9 %collective-permute-start.12 = (bf16[512,640]{1,0:T(8,128)(2,1)S(1)}, bf16[512,640]{1,0:T(8,128)(2,1)S(1)}, u32[]{:S(2)}, u32[]{:S(2)}) collective-permute-start(bf16[512,640]{1,0:T(8,128)(2,1)S(1)} %collective-permute-done.6.refs_1_), channel_id=1, source_target_pairs={{0,2},{1,7},{2,4},{3,1},{4,6},{5,3},{6,0},{7,5},{8,10},{9,15},{10,... | collective-permute-start | bytes 1966088 | tf_op jit(solution)/shard_map/a_far/ppermute | solution.py:34
  54.9 2.4 %early.1 = f32[512,192]{1,0:T(8,128)S(1)} custom-call(s32[24]{0:T(128)S(1)} %concatenate.18.where_ref, bf16[512,640]{1,0:T(8,128)(2,1)S(1)} %copy-done.5, bf16[512,640]{1,0:T(8,128)(2,1)S(1)} %copy-done.2, bf16[64,5120]{1,0:T(8,128)(2,1)S(1)} %bitcast.32, bf16[512,1792]{1,0:T(8,128)(2,1)S(1)} %copy-done, bf16[512,1792]{1,0:T(8,128)(2,1)S(1)} %copy-done.1, ...), custom_call_target="tpu_custom_call" | custom-call | flops 1048576 | bytes 65536 | tf_op jit(solution)/shard_map/early/pallas_call | solution.py:149
  57.3 13.4 %collective-permute-done.10.refs_8_.refs_12_ = bf16[112,5120]{1,0:T(8,128)(2,1)S(1)} collective-permute-done((bf16[112,5120]{1,0:T(8,128)(2,1)}, bf16[112,5120]{1,0:T(8,128)(2,1)S(1)}, u32[]{:S(2)}, u32[]{:S(2)}) %collective-permute-start.10) | collective-permute-done | bytes 1146912 | tf_op jit(solution)/shard_map/r6/ppermute | solution.py:34
  70.8 2.4 %collective-permute-done.9.refs_7_.refs_11_ = bf16[112,5120]{1,0:T(8,128)(2,1)S(1)} collective-permute-done((bf16[112,5120]{1,0:T(8,128)(2,1)}, bf16[112,5120]{1,0:T(8,128)(2,1)S(1)}, u32[]{:S(2)}, u32[]{:S(2)}) %collective-permute-start.9) | collective-permute-done | bytes 1146912 | tf_op jit(solution)/shard_map/r5/ppermute | solution.py:34
  73.1 4.9 %product.5 = bf16[512,512]{1,0:T(8,128)(2,1)S(1)} custom-call(s32[24]{0:T(128)S(1)} %concatenate.18.where_ref, bf16[512,640]{1,0:T(8,128)(2,1)S(1)} %collective-permute-done.3.refs_0_, bf16[512,640]{1,0:T(8,128)(2,1)S(1)} %collective-permute-done.4.refs_1_, bf16[512,640]{1,0:T(8,128)(2,1)S(1)} %collective-permute-done.5.refs_2_, ...), custom_call_target="tpu_custom_call" | custom-call | flops 1048576 | bytes 65536 | tf_op jit(solution)/shard_map/product/pallas_call | solution.py:123
  78.0 2.2 %collective-permute-start.15 = (bf16[1536,640]{1,0:T(8,128)(2,1)S(1)}, bf16[1536,640]{1,0:T(8,128)(2,1)S(1)}, u32[]{:S(2)}, u32[]{:S(2)}) collective-permute-start(bf16[1536,640]{1,0:T(8,128)(2,1)S(1)} %pad_maximum_fusion.1), channel_id=1, source_target_pairs={{0,1},{1,0},{2,3},{3,2},{4,5},{5,4},{6,7},{7,6},{8,9},{9,8},{10,11... | collective-permute-start | bytes 5898248 | tf_op jit(solution)/shard_map/a_swap/ppermute | solution.py:34
  81.8 3.4 %product.6 = bf16[512,384]{1,0:T(8,128)(2,1)S(1)} custom-call(s32[24]{0:T(128)S(1)} %concatenate.18.where_ref, bf16[512,640]{1,0:T(8,128)(2,1)S(1)} %collective-permute-done.3.refs_0_, bf16[512,640]{1,0:T(8,128)(2,1)S(1)} %collective-permute-done.4.refs_1_, bf16[512,640]{1,0:T(8,128)(2,1)S(1)} %collective-permute-done.5.refs_2_, ...), custom_call_target="tpu_custom_call" | custom-call | flops 1048576 | bytes 65536 | tf_op jit(solution)/shard_map/product/pallas_call | solution.py:123
  87.5 7.6 %product.7.refs_0_ = f32[512,896]{1,0:T(8,128)S(1)} custom-call(s32[24]{0:T(128)S(1)} %concatenate.18.where_ref, bf16[512,640]{1,0:T(8,128)(2,1)S(1)} %copy-done.2, bf16[512,640]{1,0:T(8,128)(2,1)S(1)} %collective-permute-done.6.refs_1_, bf16[512,640]{1,0:T(8,128)(2,1)S(1)} %collective-permute-done.7.refs_2_, ...), custom_call_target="tpu_custom_call" | custom-call | flops 1048576 | bytes 65536 | tf_op jit(solution)/shard_map/product/pallas_call | solution.py:123
  95.1 4.1 %collective-permute-start.23 = (f32[256,192]{1,0:T(8,128)S(1)}, f32[256,192]{1,0:T(8,128)S(1)}, u32[]{:S(2)}, u32[]{:S(2)}) collective-permute-start(f32[256,192]{1,0:T(8,128)S(1)} %add.231), channel_id=1, source_target_pairs={{0,4},{1,5},{2,6},{3,7},{4,0},{5,1},{6,2},{7,3},{8,12},{9,13},{10,... | collective-permute-start | bytes 589832 | tf_op jit(solution)/shard_map/s_far/ppermute | solution.py:34
  99.2 2.2 %product.8 = bf16[512,128]{1,0:T(8,128)(2,1)S(1)} custom-call(s32[24]{0:T(128)S(1)} %concatenate.18.where_ref, bf16[512,640]{1,0:T(8,128)(2,1)S(1)} %collective-permute-done.3.refs_0_, bf16[512,640]{1,0:T(8,128)(2,1)S(1)} %collective-permute-done.4.refs_1_, bf16[512,640]{1,0:T(8,128)(2,1)S(1)} %collective-permute-done.5.refs_2_, ...), custom_call_target="tpu_custom_call" | custom-call | flops 1048576 | bytes 65536 | tf_op jit(solution)/shard_map/product/pallas_call | solution.py:123
  102.3 2.2 %product.9.refs_1_ = f32[512,128]{1,0:T(8,128)S(1)} custom-call(s32[24]{0:T(128)S(1)} %concatenate.18.where_ref, bf16[512,640]{1,0:T(8,128)(2,1)S(1)} %copy-done.2, bf16[512,640]{1,0:T(8,128)(2,1)S(1)} %collective-permute-done.6.refs_1_, bf16[512,640]{1,0:T(8,128)(2,1)S(1)} %collective-permute-done.7.refs_2_, ...), custom_call_target="tpu_custom_call" | custom-call | flops 1048576 | bytes 65536 | tf_op jit(solution)/shard_map/product/pallas_call | solution.py:123
  104.5 3.8 %own_half.1 = (bf16[512,1792]{1,0:T(8,128)(2,1)}, bf16[512,1792]{1,0:T(8,128)(2,1)}, f32[512,128]{1,0:T(8,128)S(1)}) custom-call(s32[24]{0:T(128)S(1)} %concatenate.18.where_ref, bf16[512,1792]{1,0:T(8,128)(2,1)S(1)} %copy-done, bf16[512,1792]{1,0:T(8,128)(2,1)S(1)} %copy-done.1, bf16[64,1792]{1,0:T(8,128)(2,1)S(1)} %bitcast.30, ...), custom_call_target="tpu_custom_call" | custom-call | flops 1048576 | bytes 65536 | tf_op jit(solution)/shard_map/own_half/pallas_call | solution.py:218
  108.4 1.6 %collective-permute-start.24 = (f32[256,192]{1,0:T(8,128)S(1)}, f32[256,192]{1,0:T(8,128)S(1)}, u32[]{:S(2)}, u32[]{:S(2)}) collective-permute-start(f32[256,192]{1,0:T(8,128)S(1)} %add.232), channel_id=1, source_target_pairs={{0,1},{1,0},{2,3},{3,2},{4,5},{5,4},{6,7},{7,6},{8,9},{9,8},{10,11... | collective-permute-start | bytes 589832 | tf_op jit(solution)/shard_map/s_core/ppermute | solution.py:34
  110.0 3.8 %other_half.1 = (bf16[512,1792]{1,0:T(8,128)(2,1)}, bf16[512,1792]{1,0:T(8,128)(2,1)}, f32[512,128]{1,0:T(8,128)S(1)}) custom-call(s32[24]{0:T(128)S(1)} %concatenate.18.where_ref, bf16[512,1792]{1,0:T(8,128)(2,1)S(1)} %copy-done, bf16[512,1792]{1,0:T(8,128)(2,1)S(1)} %copy-done.1, ...), custom_call_target="tpu_custom_call", output_to_operand_aliasing={{0}: (5, {}), {1}: (6, {})} | custom-call | flops 1048576 | bytes 65536 | tf_op jit(solution)/shard_map/other_half/pallas_call | solution.py:256
  115.4 1.2 collective-permute-done.25
  116.8 1.3 %collective-permute-start.27 = (f32[128,128]{1,0:T(8,128)S(1)}, f32[128,128]{1,0:T(8,128)S(1)}, u32[]{:S(2)}, u32[]{:S(2)}) collective-permute-start(f32[128,128]{1,0:T(8,128)S(1)} %select_add_fusion.1), channel_id=1, source_target_pairs={{0,2},{1,3},{2,4},{3,5},{4,6},{5,7},{6,0},{7,1},{8,10},{9,11},{10,... | collective-permute-start | bytes 196616 | tf_op jit(solution)/shard_map/up/ppermute | solution.py:34
  118.1 1.4 %collective-permute-start.28 = (f32[128,128]{1,0:T(8,128)S(1)}, f32[128,128]{1,0:T(8,128)S(1)}, u32[]{:S(2)}, u32[]{:S(2)}) collective-permute-start(f32[128,128]{1,0:T(8,128)S(1)} %select_add_fusion.1), channel_id=1, source_target_pairs={{0,6},{1,7},{2,0},{3,1},{4,2},{5,3},{6,4},{7,5},{8,14},{9,15},{10,... | collective-permute-start | bytes 196616 | tf_op jit(solution)/shard_map/down/ppermute | solution.py:34
  119.5 2.3 %collective-permute-done.26 = f32[128,128]{1,0:T(8,128)S(1)} collective-permute-done((f32[128,128]{1,0:T(8,128)S(1)}, f32[128,128]{1,0:T(8,128)S(1)}, u32[]{:S(2)}, u32[]{:S(2)}) %collective-permute-start.26) | collective-permute-done | bytes 65568 | tf_op jit(solution)/shard_map/send/ppermute | solution.py:34
  121.8 1.4 %collective-permute-done.27 = f32[128,128]{1,0:T(8,128)S(1)} collective-permute-done((f32[128,128]{1,0:T(8,128)S(1)}, f32[128,128]{1,0:T(8,128)S(1)}, u32[]{:S(2)}, u32[]{:S(2)}) %collective-permute-start.27) | collective-permute-done | bytes 65568 | tf_op jit(solution)/shard_map/up/ppermute | solution.py:34
  (74 shorter events, 14.5 us)
Async XLA Ops:
  0.6 19.4 %collective-permute-start.3 = (bf16[512,640]{1,0:T(8,128)(2,1)}, bf16[512,640]{1,0:T(8,128)(2,1)S(1)}, u32[]{:S(2)}, u32[]{:S(2)}) collective-permute-start(bf16[512,640]{1,0:T(8,128)(2,1)} %refs_0_.3), channel_id=1, source_target_pairs={{0,96},{1,97},{2,98},{3,99},{4,100},{5,101},{6,102},{7,103},{8,104... | collective-permute-start | bytes 1966088 | tf_op jit(solution)/shard_map/mate_rows/ppermute | solution.py:34
  5.3 15.9 %collective-permute-start.6 = (bf16[512,640]{1,0:T(8,128)(2,1)}, bf16[512,640]{1,0:T(8,128)(2,1)S(1)}, u32[]{:S(2)}, u32[]{:S(2)}) collective-permute-start(bf16[512,640]{1,0:T(8,128)(2,1)} %refs_0_.3), channel_id=1, source_target_pairs={{0,2},{1,7},{2,4},{3,1},{4,6},{5,3},{6,0},{7,5},{8,10},{9,15},{10,... | collective-permute-start | bytes 1966088 | tf_op jit(solution)/shard_map/a1/ppermute | solution.py:34
  8.0 17.0 %collective-permute-start.7 = (bf16[512,640]{1,0:T(8,128)(2,1)}, bf16[512,640]{1,0:T(8,128)(2,1)S(1)}, u32[]{:S(2)}, u32[]{:S(2)}) collective-permute-start(bf16[512,640]{1,0:T(8,128)(2,1)} %refs_0_.3), channel_id=1, source_target_pairs={{0,6},{1,3},{2,0},{3,5},{4,2},{5,7},{6,4},{7,1},{8,14},{9,11},{10,... | collective-permute-start | bytes 1966088 | tf_op jit(solution)/shard_map/a2/ppermute | solution.py:34
  8.0 26.8 %collective-permute-start = (bf16[112,5120]{1,0:T(8,128)(2,1)}, bf16[112,5120]{1,0:T(8,128)(2,1)}, u32[]{:S(2)}, u32[]{:S(2)}) collective-permute-start(bf16[112,5120]{1,0:T(8,128)(2,1)} %refs_6_.3), channel_id=1, source_target_pairs={{0,8},{1,9},{2,10},{3,11},{4,12},{5,13},{6,14},{7,15},{8,16},{9,17... | collective-permute-start | bytes 3440648 | tf_op jit(solution)/shard_map/r1/ppermute | solution.py:34
  9.2 25.6 %collective-permute-start.1 = (bf16[112,5120]{1,0:T(8,128)(2,1)}, bf16[112,5120]{1,0:T(8,128)(2,1)}, u32[]{:S(2)}, u32[]{:S(2)}) collective-permute-start(bf16[112,5120]{1,0:T(8,128)(2,1)} %refs_6_.3), channel_id=1, source_target_pairs={{0,32},{1,25},{2,34},{3,27},{4,36},{5,29},{6,38},{7,31},{8,40},{9,... | collective-permute-start | bytes 3440648 | tf_op jit(solution)/shard_map/r2/ppermute | solution.py:34
  20.1 18.9 %collective-permute-start.2 = (bf16[112,5120]{1,0:T(8,128)(2,1)}, bf16[112,5120]{1,0:T(8,128)(2,1)}, u32[]{:S(2)}, u32[]{:S(2)}) collective-permute-start(bf16[112,5120]{1,0:T(8,128)(2,1)} %refs_6_.3), channel_id=1, source_target_pairs={{0,24},{1,33},{2,26},{3,35},{4,28},{5,37},{6,30},{7,39},{8,0},{9,4... | collective-permute-start | bytes 3440648 | tf_op jit(solution)/shard_map/r3/ppermute | solution.py:34
  21.2 17.7 %collective-permute-start.4 = (bf16[512,640]{1,0:T(8,128)(2,1)S(1)}, bf16[512,640]{1,0:T(8,128)(2,1)S(1)}, u32[]{:S(2)}, u32[]{:S(2)}) collective-permute-start(bf16[512,640]{1,0:T(8,128)(2,1)S(1)} %collective-permute-done.3.refs_0_), channel_id=1, source_target_pairs={{0,2},{1,7},{2,4},{3,1},{4,6},{5,3},{6,0},{7,5},{8,10},{9,15},{10,... | collective-permute-start | bytes 1966088 | tf_op jit(solution)/shard_map/b1/ppermute | solution.py:34
  25.0 17.1 %collective-permute-start.5 = (bf16[512,640]{1,0:T(8,128)(2,1)S(1)}, bf16[512,640]{1,0:T(8,128)(2,1)S(1)}, u32[]{:S(2)}, u32[]{:S(2)}) collective-permute-start(bf16[512,640]{1,0:T(8,128)(2,1)S(1)} %collective-permute-done.3.refs_0_), channel_id=1, source_target_pairs={{0,6},{1,3},{2,0},{3,5},{4,2},{5,7},{6,4},{7,1},{8,14},{9,11},{10,... | collective-permute-start | bytes 1966088 | tf_op jit(solution)/shard_map/b2/ppermute | solution.py:34
  28.2 26.5 %copy-start.2 = (bf16[512,640]{1,0:T(8,128)(2,1)S(1)}, bf16[512,640]{1,0:T(8,128)(2,1)}, u32[]{:S(2)}) copy-start(bf16[512,640]{1,0:T(8,128)(2,1)} %refs_0_.3) | copy-start | bytes 1966084
  42.3 11.9 %collective-permute-start.13 = (bf16[1536,640]{1,0:T(8,128)(2,1)S(1)}, bf16[1536,640]{1,0:T(8,128)(2,1)S(1)}, u32[]{:S(2)}, u32[]{:S(2)}) collective-permute-start(bf16[1536,640]{1,0:T(8,128)(2,1)S(1)} %pad_maximum_fusion), channel_id=1, source_target_pairs={{0,1},{1,0},{2,3},{3,2},{4,5},{5,4},{6,7},{7,6},{8,9},{9,8},{10,11... | collective-permute-start | bytes 5898248 | tf_op jit(solution)/shard_map/b_swap/ppermute | solution.py:34
  42.6 9.7 %collective-permute-start.11 = (bf16[512,640]{1,0:T(8,128)(2,1)S(1)}, bf16[512,640]{1,0:T(8,128)(2,1)S(1)}, u32[]{:S(2)}, u32[]{:S(2)}) collective-permute-start(bf16[512,640]{1,0:T(8,128)(2,1)S(1)} %collective-permute-done.4.refs_1_), channel_id=1, source_target_pairs={{0,2},{1,7},{2,4},{3,1},{4,6},{5,3},{6,0},{7,5},{8,10},{9,15},{10,... | collective-permute-start | bytes 1966088 | tf_op jit(solution)/shard_map/b_far/ppermute | solution.py:34
  43.3 27.5 %collective-permute-start.10 = (bf16[112,5120]{1,0:T(8,128)(2,1)}, bf16[112,5120]{1,0:T(8,128)(2,1)S(1)}, u32[]{:S(2)}, u32[]{:S(2)}) collective-permute-start(bf16[112,5120]{1,0:T(8,128)(2,1)} %collective-permute-done.1.refs_8_), channel_id=1, source_target_pairs={{0,24},{1,25},{2,26},{3,27},{4,28},{5,29},{6,30},{7,31},{8,0},{9,1... | collective-permute-start | bytes 3440648 | tf_op jit(solution)/shard_map/r6/ppermute | solution.py:34
  45.6 25.1 %collective-permute-start.8 = (bf16[112,5120]{1,0:T(8,128)(2,1)}, bf16[112,5120]{1,0:T(8,128)(2,1)S(1)}, u32[]{:S(2)}, u32[]{:S(2)}) collective-permute-start(bf16[112,5120]{1,0:T(8,128)(2,1)} %collective-permute-done.1.refs_8_), channel_id=1, source_target_pairs={{0,8},{1,33},{2,10},{3,35},{4,12},{5,37},{6,14},{7,39},{8,16},{9,4... | collective-permute-start | bytes 3440648 | tf_op jit(solution)/shard_map/r4/ppermute | solution.py:34
  45.6 27.5 %collective-permute-start.9 = (bf16[112,5120]{1,0:T(8,128)(2,1)}, bf16[112,5120]{1,0:T(8,128)(2,1)S(1)}, u32[]{:S(2)}, u32[]{:S(2)}) collective-permute-start(bf16[112,5120]{1,0:T(8,128)(2,1)} %collective-permute-done.refs_7_), channel_id=1, source_target_pairs={{0,8},{1,33},{2,10},{3,35},{4,12},{5,37},{6,14},{7,39},{8,16},{9,4... | collective-permute-start | bytes 3440648 | tf_op jit(solution)/shard_map/r5/ppermute | solution.py:34
  52.3 20.8 %collective-permute-start.12 = (bf16[512,640]{1,0:T(8,128)(2,1)S(1)}, bf16[512,640]{1,0:T(8,128)(2,1)S(1)}, u32[]{:S(2)}, u32[]{:S(2)}) collective-permute-start(bf16[512,640]{1,0:T(8,128)(2,1)S(1)} %collective-permute-done.6.refs_1_), channel_id=1, source_target_pairs={{0,2},{1,7},{2,4},{3,1},{4,6},{5,3},{6,0},{7,5},{8,10},{9,15},{10,... | collective-permute-start | bytes 1966088 | tf_op jit(solution)/shard_map/a_far/ppermute | solution.py:34
  54.2 18.9 %collective-permute-start.14 = (bf16[512,640]{1,0:T(8,128)(2,1)S(1)}, bf16[512,640]{1,0:T(8,128)(2,1)S(1)}, u32[]{:S(2)}, u32[]{:S(2)}) collective-permute-start(bf16[512,640]{1,0:T(8,128)(2,1)S(1)} %collective-permute-done.11.refs_3_), channel_id=1, source_target_pairs={{0,1},{1,0},{2,3},{3,2},{4,5},{5,4},{6,7},{7,6},{8,9},{9,8},{10,11... | collective-permute-start | bytes 1966088 | tf_op jit(solution)/shard_map/b_swap/ppermute | solution.py:34
  54.9 18.2 %copy-start.3 = (bf16[112,5120]{1,0:T(8,128)(2,1)S(1)}, bf16[112,5120]{1,0:T(8,128)(2,1)}, u32[]{:S(2)}) copy-start(bf16[112,5120]{1,0:T(8,128)(2,1)} %refs_6_.3) | copy-start | bytes 3440644
  78.0 9.4 %collective-permute-start.15 = (bf16[1536,640]{1,0:T(8,128)(2,1)S(1)}, bf16[1536,640]{1,0:T(8,128)(2,1)S(1)}, u32[]{:S(2)}, u32[]{:S(2)}) collective-permute-start(bf16[1536,640]{1,0:T(8,128)(2,1)S(1)} %pad_maximum_fusion.1), channel_id=1, source_target_pairs={{0,1},{1,0},{2,3},{3,2},{4,5},{5,4},{6,7},{7,6},{8,9},{9,8},{10,11... | collective-permute-start | bytes 5898248 | tf_op jit(solution)/shard_map/a_swap/ppermute | solution.py:34
  80.3 18.9 %collective-permute-start.18 = (bf16[112,5120]{1,0:T(8,128)(2,1)S(1)}, bf16[112,5120]{1,0:T(8,128)(2,1)S(1)}, u32[]{:S(2)}, u32[]{:S(2)}) collective-permute-start(bf16[112,5120]{1,0:T(8,128)(2,1)S(1)} %collective-permute-done.10.refs_8_.refs_12_), channel_id=1, source_target_pairs={{0,24},{1,33},{2,26},{3,35},{4,28},{5,37},{6,30},{7,39},{8,0},{9,4... | collective-permute-start | bytes 3440648 | tf_op jit(solution)/shard_map/r7/ppermute | solution.py:34
  80.3 6.0 %collective-permute-start.16 = (bf16[512,640]{1,0:T(8,128)(2,1)S(1)}, bf16[512,640]{1,0:T(8,128)(2,1)S(1)}, u32[]{:S(2)}, u32[]{:S(2)}) collective-permute-start(bf16[512,640]{1,0:T(8,128)(2,1)S(1)} %collective-permute-done.12.refs_3_), channel_id=1, source_target_pairs={{0,1},{1,0},{2,3},{3,2},{4,5},{5,4},{6,7},{7,6},{8,9},{9,8},{10,11... | collective-permute-start | bytes 1966088 | tf_op jit(solution)/shard_map/a_swap/ppermute | solution.py:34
  80.5 4.8 %collective-permute-start.21 = (f32[256,192]{1,0:T(8,128)S(1)}, f32[256,192]{1,0:T(8,128)S(1)}, u32[]{:S(2)}, u32[]{:S(2)}) collective-permute-start(f32[256,192]{1,0:T(8,128)S(1)} %slice_select_fusion), channel_id=1, source_target_pairs={{0,1},{1,0},{2,3},{3,2},{4,5},{5,4},{6,7},{7,6},{8,9},{9,8},{10,11... | collective-permute-start | bytes 589832 | tf_op jit(solution)/shard_map/s_core/ppermute | solution.py:34
  80.9 18.3 %collective-permute-start.17 = (bf16[512,512]{1,0:T(8,128)(2,1)S(1)}, bf16[512,512]{1,0:T(8,128)(2,1)S(1)}, u32[]{:S(2)}, u32[]{:S(2)}) collective-permute-start(bf16[512,512]{1,0:T(8,128)(2,1)S(1)} %product.5), channel_id=1, source_target_pairs={{0,96},{1,97},{2,98},{3,99},{4,100},{5,101},{6,102},{7,103},{8,104... | collective-permute-start | bytes 1572872 | tf_op jit(solution)/shard_map/mate_grad1/ppermute | solution.py:34
  85.3 9.7 %collective-permute-start.22 = (f32[256,192]{1,0:T(8,128)S(1)}, f32[256,192]{1,0:T(8,128)S(1)}, u32[]{:S(2)}, u32[]{:S(2)}) collective-permute-start(f32[256,192]{1,0:T(8,128)S(1)} %select_add_fusion), channel_id=1, source_target_pairs={{0,2},{1,3},{2,0},{3,1},{4,6},{5,7},{6,4},{7,5},{8,10},{9,11},{10,... | collective-permute-start | bytes 589832 | tf_op jit(solution)/shard_map/s_near/ppermute | solution.py:34
  86.2 22.1 %collective-permute-start.19 = (bf16[512,384]{1,0:T(8,128)(2,1)S(1)}, bf16[512,384]{1,0:T(8,128)(2,1)S(1)}, u32[]{:S(2)}, u32[]{:S(2)}) collective-permute-start(bf16[512,384]{1,0:T(8,128)(2,1)S(1)} %product.6), channel_id=1, source_target_pairs={{0,96},{1,97},{2,98},{3,99},{4,100},{5,101},{6,102},{7,103},{8,104... | collective-permute-start | bytes 1179656 | tf_op jit(solution)/shard_map/mate_grad2/ppermute | solution.py:34
  95.1 13.2 %collective-permute-start.23 = (f32[256,192]{1,0:T(8,128)S(1)}, f32[256,192]{1,0:T(8,128)S(1)}, u32[]{:S(2)}, u32[]{:S(2)}) collective-permute-start(f32[256,192]{1,0:T(8,128)S(1)} %add.231), channel_id=1, source_target_pairs={{0,4},{1,5},{2,6},{3,7},{4,0},{5,1},{6,2},{7,3},{8,12},{9,13},{10,... | collective-permute-start | bytes 589832 | tf_op jit(solution)/shard_map/s_far/ppermute | solution.py:34
  101.4 6.9 %collective-permute-start.20 = (bf16[512,128]{1,0:T(8,128)(2,1)S(1)}, bf16[512,128]{1,0:T(8,128)(2,1)S(1)}, u32[]{:S(2)}, u32[]{:S(2)}) collective-permute-start(bf16[512,128]{1,0:T(8,128)(2,1)S(1)} %product.8), channel_id=1, source_target_pairs={{0,96},{1,97},{2,98},{3,99},{4,100},{5,101},{6,102},{7,103},{8,104... | collective-permute-start | bytes 393224 | tf_op jit(solution)/shard_map/mate_grad3/ppermute | solution.py:34
  108.4 5.4 %collective-permute-start.24 = (f32[256,192]{1,0:T(8,128)S(1)}, f32[256,192]{1,0:T(8,128)S(1)}, u32[]{:S(2)}, u32[]{:S(2)}) collective-permute-start(f32[256,192]{1,0:T(8,128)S(1)} %add.232), channel_id=1, source_target_pairs={{0,1},{1,0},{2,3},{3,2},{4,5},{5,4},{6,7},{7,6},{8,9},{9,8},{10,11... | collective-permute-start | bytes 589832 | tf_op jit(solution)/shard_map/s_core/ppermute | solution.py:34
  115.3 1.3 %collective-permute-start.25 = (f32[128,128]{1,0:T(8,128)S(1)}, f32[128,128]{1,0:T(8,128)S(1)}, u32[]{:S(2)}, u32[]{:S(2)}) collective-permute-start(f32[128,128]{1,0:T(8,128)S(1)} %slice_select_fusion.1), channel_id=1, source_target_pairs={{0,1},{1,0},{2,3},{3,2},{4,5},{5,4},{6,7},{7,6},{8,9},{9,8},{10,11... | collective-permute-start | bytes 196616 | tf_op jit(solution)/shard_map/swap/ppermute | solution.py:34
  116.7 5.1 %collective-permute-start.26 = (f32[128,128]{1,0:T(8,128)S(1)}, f32[128,128]{1,0:T(8,128)S(1)}, u32[]{:S(2)}, u32[]{:S(2)}) collective-permute-start(f32[128,128]{1,0:T(8,128)S(1)} %select_add_fusion.1), channel_id=1, source_target_pairs={{0,4},{1,5},{2,6},{3,7},{4,0},{5,1},{6,2},{7,3},{8,12},{9,13},{10,... | collective-permute-start | bytes 196616 | tf_op jit(solution)/shard_map/send/ppermute | solution.py:34
  116.8 6.5 %collective-permute-start.27 = (f32[128,128]{1,0:T(8,128)S(1)}, f32[128,128]{1,0:T(8,128)S(1)}, u32[]{:S(2)}, u32[]{:S(2)}) collective-permute-start(f32[128,128]{1,0:T(8,128)S(1)} %select_add_fusion.1), channel_id=1, source_target_pairs={{0,2},{1,3},{2,4},{3,5},{4,6},{5,7},{6,0},{7,1},{8,10},{9,11},{10,... | collective-permute-start | bytes 196616 | tf_op jit(solution)/shard_map/up/ppermute | solution.py:34
  118.1 5.2 %collective-permute-start.28 = (f32[128,128]{1,0:T(8,128)S(1)}, f32[128,128]{1,0:T(8,128)S(1)}, u32[]{:S(2)}, u32[]{:S(2)}) collective-permute-start(f32[128,128]{1,0:T(8,128)S(1)} %select_add_fusion.1), channel_id=1, source_target_pairs={{0,6},{1,7},{2,0},{3,1},{4,2},{5,3},{6,4},{7,5},{8,14},{9,15},{10,... | collective-permute-start | bytes 196616 | tf_op jit(solution)/shard_map/down/ppermute | solution.py:34
  123.3 1.7 %collective-permute-start.29 = (f32[128,128]{1,0:T(8,128)S(1)}, f32[128,128]{1,0:T(8,128)S(1)}, u32[]{:S(2)}, u32[]{:S(2)}) collective-permute-start(f32[128,128]{1,0:T(8,128)S(1)} %add_add_fusion), channel_id=1, source_target_pairs={{0,1},{1,0},{2,3},{3,2},{4,5},{5,4},{6,7},{7,6},{8,9},{9,8},{10,11... | collective-permute-start | bytes 196616 | tf_op jit(solution)/shard_map/swap/ppermute | solution.py:34
  (5 other events, 63.5 us)

commit v11 on v10

--- a/solution.py
+++ b/solution.py
@@ -362,9 +362,9 @@
     a_far = along_y(after(a1, b_far), 1, "a_far")
     parts = early(after(where, b_far), activations, out_grad, pm_t, gate_pre, up_pre, ph_t)
     top, low = parts[:256], parts[256:]
-    core_sum = swap(after(jnp.where(c == 0, low, top), b_other[1]), "s_core")
+    half = jnp.where(c == 0, top, low) + swap(jnp.where(c == 0, low, top), "s_core")
     b_mine = [theirs, b1, b2, b_far]
-    h1 = product(BF16, after(where, r4, r5, r6, a_far, parts), b_mine, b_other, [own_w, r1, r2, r3])
+    h1 = product(BF16, after(where, r4, r5, r6, a_far, half), b_mine, b_other, [own_w, r1, r2, r3])
     r7 = route(r6, "-", "p", "r7")
     h1_in = mate(h1, "mate_grad1")
     h2 = product(BF16, after(where, h1), b_mine, b_other, [r4, r5, r6])
@@ -372,7 +372,6 @@
     a_mine = [out_grad, a1, a2, a_far]
     near = jnp.concatenate([out_grad, a2, a1])
     a_other = [swap(after(near, h1), "a_swap"), swap(a_far, "a_swap")]
-    half = jnp.where(c == 0, top, low) + after(core_sum, h2)
     near_y = send(half, lambda z, x, y, c: (z, x, y ^ 1, c), "s_near")
     own1 = product(F32, after(where, h2), a_mine, a_other, [own_w, r1, r2, r3, r4, r5, r6])
     half += after(near_y, own1)

time: 127 us -> 126 us (level)
  waiting for transfers between devices: 51.7 us -> 48 us
  local copies, waits for them, and re-layouts: 2.96 us -> 6.13 us
    ppermute x30, waiting for transfers between devices: 51.7 us -> 48 us  [send(): return lax.ppermute(value, AXES, pairs)]
    unnamed x14 -> x16, local copies, waits for them, and re-layouts: 0.04 us -> 3.28 us
  transfers between devices with their start and end apart: 30 -> 30, of which waited for: 13 -> 14; matrix products, arithmetic and copies ran while one was open for 3% -> 3% of each run, Pallas kernels for 20% -> 20%
where the time goes in v11:
time: 126 us
  waiting for transfers between devices  48 us (38%)
  starting transfers between devices  37.1 us (29%)
  Pallas kernels  31.6 us (25%)
  local copies, waits for them, and re-layouts  6.13 us (5%)
  other arithmetic  2.11 us (2%)
    ppermute x30, waiting for transfers between devices, send(): return lax.ppermute(value, AXES, pairs)  48 us
    ppermute x30, starting transfers between devices, send(): return lax.ppermute(value, AXES, pairs)  37.1 us
    pallas_call x5, Pallas kernels, product(): pl.pallas_call(functools.partial(product_kernel, shards), out_shape=jax.S...  20.2 us
    pallas_call x1, Pallas kernels, own_half(): pl.pallas_call(functools.partial(own_kernel, len(h)), out_shape=(BIG, BIG...  3.82 us
    pallas_call x1, Pallas kernels, other_half(): pl.pallas_call(functools.partial(other_kernel, len(h)), out_shape=(BIG, B...  3.76 us
    unnamed x16, local copies, waits for them, and re-layouts  3.28 us
  transfers between devices with their start and end apart: 30, of which 14 were waited for; matrix products, arithmetic and copies ran while one was open for 3% of the time, Pallas kernels for 20%

profile of v11, /device:TPU:1, one launch (start us, length us, event | category | flops | bytes accessed | tf_op | source)
XLA Modules:
  0.0 125.8 jit_solution(18102041462136899697)
XLA Ops:
  0.6 4.7 %collective-permute-start.3 = (bf16[512,640]{1,0:T(8,128)(2,1)}, bf16[512,640]{1,0:T(8,128)(2,1)S(1)}, u32[]{:S(2)}, u32[]{:S(2)}) collective-permute-start(bf16[512,640]{1,0:T(8,128)(2,1)} %refs_0_.3), channel_id=1, source_target_pairs={{0,96},{1,97},{2,98},{3,99},{4,100},{5,101},{6,102},{7,103},{8,104... | collective-permute-start | bytes 1966088 | tf_op jit(solution)/shard_map/mate_rows/ppermute | solution.py:34
  5.3 2.7 %collective-permute-start.6 = (bf16[512,640]{1,0:T(8,128)(2,1)}, bf16[512,640]{1,0:T(8,128)(2,1)S(1)}, u32[]{:S(2)}, u32[]{:S(2)}) collective-permute-start(bf16[512,640]{1,0:T(8,128)(2,1)} %refs_0_.3), channel_id=1, source_target_pairs={{0,2},{1,7},{2,4},{3,1},{4,6},{5,3},{6,0},{7,5},{8,10},{9,15},{10,... | collective-permute-start | bytes 1966088 | tf_op jit(solution)/shard_map/a1/ppermute | solution.py:34
  9.2 1.5 %collective-permute-start.1 = (bf16[112,5120]{1,0:T(8,128)(2,1)}, bf16[112,5120]{1,0:T(8,128)(2,1)}, u32[]{:S(2)}, u32[]{:S(2)}) collective-permute-start(bf16[112,5120]{1,0:T(8,128)(2,1)} %refs_6_.3), channel_id=1, source_target_pairs={{0,32},{1,25},{2,34},{3,27},{4,36},{5,29},{6,38},{7,31},{8,40},{9,... | collective-permute-start | bytes 3440648 | tf_op jit(solution)/shard_map/r2/ppermute | solution.py:34
  10.7 9.4 %collective-permute-done.3.refs_0_ = bf16[512,640]{1,0:T(8,128)(2,1)S(1)} collective-permute-done((bf16[512,640]{1,0:T(8,128)(2,1)}, bf16[512,640]{1,0:T(8,128)(2,1)S(1)}, u32[]{:S(2)}, u32[]{:S(2)}) %collective-permute-start.3) | collective-permute-done | bytes 655392 | tf_op jit(solution)/shard_map/mate_rows/ppermute | solution.py:34
  21.2 3.4 %collective-permute-start.4 = (bf16[512,640]{1,0:T(8,128)(2,1)S(1)}, bf16[512,640]{1,0:T(8,128)(2,1)S(1)}, u32[]{:S(2)}, u32[]{:S(2)}) collective-permute-start(bf16[512,640]{1,0:T(8,128)(2,1)S(1)} %collective-permute-done.3.refs_0_), channel_id=1, source_target_pairs={{0,2},{1,7},{2,4},{3,1},{4,6},{5,3},{6,0},{7,5},{8,10},{9,15},{10,... | collective-permute-start | bytes 1966088 | tf_op jit(solution)/shard_map/b1/ppermute | solution.py:34
  25.1 1.3 %reduce_sum.29 = s32[]{:T(128)} reduce(s32[4]{0:T(128)} %param.15, s32[]{:T(128)} %constant.165.clone.1), dimensions={0}, to_apply=%region_2.3 | reduce | flops 3 | bytes 24 | tf_op jit(solution)/shard_map/reduce_sum | solution.py:341
  26.7 1.3 %concatenate.18.where_ref = s32[24]{0:T(128)S(1)} concatenate(s32[8]{0:T(128)S(1)} %get-tuple-element.64, s32[8]{0:T(128)S(1)} %get-tuple-element.63, s32[1]{0:T(128)} %bitcast.16, s32[1]{0:T(128)} %bitcast.17, s32[1]{0:T(128)} %bitcast.18, s32[1]{0:T(128)} %bitcast.19, s32[4]{0:T(128)} %param.15), dimensions={0} | concatenate | bytes 192 | tf_op jit(solution)/shard_map/concatenate | solution.py:337
  28.1 6.8 %collective-permute-done.refs_7_ = bf16[112,5120]{1,0:T(8,128)(2,1)} collective-permute-done((bf16[112,5120]{1,0:T(8,128)(2,1)}, bf16[112,5120]{1,0:T(8,128)(2,1)}, u32[]{:S(2)}, u32[]{:S(2)}) %collective-permute-start) | collective-permute-done | bytes 1146912 | tf_op jit(solution)/shard_map/r1/ppermute | solution.py:34
  34.9 4.1 %collective-permute-done.2.refs_9_ = bf16[112,5120]{1,0:T(8,128)(2,1)} collective-permute-done((bf16[112,5120]{1,0:T(8,128)(2,1)}, bf16[112,5120]{1,0:T(8,128)(2,1)}, u32[]{:S(2)}, u32[]{:S(2)}) %collective-permute-start.2) | collective-permute-done | bytes 1146912 | tf_op jit(solution)/shard_map/r3/ppermute | solution.py:34
  38.9 3.1 %collective-permute-done.5.refs_2_ = bf16[512,640]{1,0:T(8,128)(2,1)S(1)} collective-permute-done((bf16[512,640]{1,0:T(8,128)(2,1)S(1)}, bf16[512,640]{1,0:T(8,128)(2,1)S(1)}, u32[]{:S(2)}, u32[]{:S(2)}) %collective-permute-start.5) | collective-permute-done | bytes 655392 | tf_op jit(solution)/shard_map/b2/ppermute | solution.py:34
  43.2 2.4 %collective-permute-start.10 = (bf16[112,5120]{1,0:T(8,128)(2,1)}, bf16[112,5120]{1,0:T(8,128)(2,1)S(1)}, u32[]{:S(2)}, u32[]{:S(2)}) collective-permute-start(bf16[112,5120]{1,0:T(8,128)(2,1)} %collective-permute-done.1.refs_8_), channel_id=1, source_target_pairs={{0,24},{1,25},{2,26},{3,27},{4,28},{5,29},{6,30},{7,31},{8,0},{9,1... | collective-permute-start | bytes 3440648 | tf_op jit(solution)/shard_map/r6/ppermute | solution.py:34
  45.6 1.5 %collective-permute-start.9 = (bf16[112,5120]{1,0:T(8,128)(2,1)}, bf16[112,5120]{1,0:T(8,128)(2,1)S(1)}, u32[]{:S(2)}, u32[]{:S(2)}) collective-permute-start(bf16[112,5120]{1,0:T(8,128)(2,1)} %collective-permute-done.refs_7_), channel_id=1, source_target_pairs={{0,8},{1,33},{2,10},{3,35},{4,12},{5,37},{6,14},{7,39},{8,16},{9,4... | collective-permute-start | bytes 3440648 | tf_op jit(solution)/shard_map/r5/ppermute | solution.py:34
  47.1 5.2 %collective-permute-done.11.refs_3_ = bf16[512,640]{1,0:T(8,128)(2,1)S(1)} collective-permute-done((bf16[512,640]{1,0:T(8,128)(2,1)S(1)}, bf16[512,640]{1,0:T(8,128)(2,1)S(1)}, u32[]{:S(2)}, u32[]{:S(2)}) %collective-permute-start.11) | collective-permute-done | bytes 655392 | tf_op jit(solution)/shard_map/b_far/ppermute | solution.py:34
  55.5 2.4 %early.1 = f32[512,192]{1,0:T(8,128)S(1)} custom-call(s32[24]{0:T(128)S(1)} %concatenate.18.where_ref, bf16[512,640]{1,0:T(8,128)(2,1)S(1)} %copy-done.6, bf16[512,640]{1,0:T(8,128)(2,1)S(1)} %copy-done.2, bf16[64,5120]{1,0:T(8,128)(2,1)S(1)} %bitcast.32, bf16[512,1792]{1,0:T(8,128)(2,1)S(1)} %copy-done, bf16[512,1792]{1,0:T(8,128)(2,1)S(1)} %copy-done.1, ...), custom_call_target="tpu_custom_call" | custom-call | flops 1048576 | bytes 65536 | tf_op jit(solution)/shard_map/early/pallas_call | solution.py:149
  58.0 2.5 %collective-permute-start.13 = (f32[256,192]{1,0:T(8,128)S(1)}, f32[256,192]{1,0:T(8,128)S(1)}, u32[]{:S(2)}, u32[]{:S(2)}) collective-permute-start(f32[256,192]{1,0:T(8,128)S(1)} %slice_select_fusion), channel_id=1, source_target_pairs={{0,1},{1,0},{2,3},{3,2},{4,5},{5,4},{6,7},{7,6},{8,9},{9,8},{10,11... | collective-permute-start | bytes 589832 | tf_op jit(solution)/shard_map/s_core/ppermute | solution.py:34
  62.2 8.5 %collective-permute-done.10.refs_8_.refs_12_ = bf16[112,5120]{1,0:T(8,128)(2,1)S(1)} collective-permute-done((bf16[112,5120]{1,0:T(8,128)(2,1)}, bf16[112,5120]{1,0:T(8,128)(2,1)S(1)}, u32[]{:S(2)}, u32[]{:S(2)}) %collective-permute-start.10) | collective-permute-done | bytes 1146912 | tf_op jit(solution)/shard_map/r6/ppermute | solution.py:34
  70.7 2.4 %collective-permute-done.9.refs_7_.refs_11_ = bf16[112,5120]{1,0:T(8,128)(2,1)S(1)} collective-permute-done((bf16[112,5120]{1,0:T(8,128)(2,1)}, bf16[112,5120]{1,0:T(8,128)(2,1)S(1)}, u32[]{:S(2)}, u32[]{:S(2)}) %collective-permute-start.9) | collective-permute-done | bytes 1146912 | tf_op jit(solution)/shard_map/r5/ppermute | solution.py:34
  73.1 4.9 %product.5 = bf16[512,512]{1,0:T(8,128)(2,1)S(1)} custom-call(s32[24]{0:T(128)S(1)} %concatenate.18.where_ref, bf16[512,640]{1,0:T(8,128)(2,1)S(1)} %collective-permute-done.3.refs_0_, bf16[512,640]{1,0:T(8,128)(2,1)S(1)} %collective-permute-done.4.refs_1_, bf16[512,640]{1,0:T(8,128)(2,1)S(1)} %collective-permute-done.5.refs_2_, ...), custom_call_target="tpu_custom_call" | custom-call | flops 1048576 | bytes 65536 | tf_op jit(solution)/shard_map/product/pallas_call | solution.py:123
  78.0 2.2 %collective-permute-start.16 = (bf16[1536,640]{1,0:T(8,128)(2,1)S(1)}, bf16[1536,640]{1,0:T(8,128)(2,1)S(1)}, u32[]{:S(2)}, u32[]{:S(2)}) collective-permute-start(bf16[1536,640]{1,0:T(8,128)(2,1)S(1)} %pad_maximum_fusion.1), channel_id=1, source_target_pairs={{0,1},{1,0},{2,3},{3,2},{4,5},{5,4},{6,7},{7,6},{8,9},{9,8},{10,11... | collective-permute-start | bytes 5898248 | tf_op jit(solution)/shard_map/a_swap/ppermute | solution.py:34
  82.0 3.4 %product.6 = bf16[512,384]{1,0:T(8,128)(2,1)S(1)} custom-call(s32[24]{0:T(128)S(1)} %concatenate.18.where_ref, bf16[512,640]{1,0:T(8,128)(2,1)S(1)} %collective-permute-done.3.refs_0_, bf16[512,640]{1,0:T(8,128)(2,1)S(1)} %collective-permute-done.4.refs_1_, bf16[512,640]{1,0:T(8,128)(2,1)S(1)} %collective-permute-done.5.refs_2_, ...), custom_call_target="tpu_custom_call" | custom-call | flops 1048576 | bytes 65536 | tf_op jit(solution)/shard_map/product/pallas_call | solution.py:123
  86.6 7.6 %product.7.refs_0_ = f32[512,896]{1,0:T(8,128)S(1)} custom-call(s32[24]{0:T(128)S(1)} %concatenate.18.where_ref, bf16[512,640]{1,0:T(8,128)(2,1)S(1)} %copy-done.3, bf16[512,640]{1,0:T(8,128)(2,1)S(1)} %collective-permute-done.6.refs_1_, bf16[512,640]{1,0:T(8,128)(2,1)S(1)} %collective-permute-done.7.refs_2_, ...), custom_call_target="tpu_custom_call" | custom-call | flops 1048576 | bytes 65536 | tf_op jit(solution)/shard_map/product/pallas_call | solution.py:123
  94.3 4.2 %collective-permute-start.23 = (f32[256,192]{1,0:T(8,128)S(1)}, f32[256,192]{1,0:T(8,128)S(1)}, u32[]{:S(2)}, u32[]{:S(2)}) collective-permute-start(f32[256,192]{1,0:T(8,128)S(1)} %add.231), channel_id=1, source_target_pairs={{0,4},{1,5},{2,6},{3,7},{4,0},{5,1},{6,2},{7,3},{8,12},{9,13},{10,... | collective-permute-start | bytes 589832 | tf_op jit(solution)/shard_map/s_far/ppermute | solution.py:34
  98.5 2.2 %product.8 = bf16[512,128]{1,0:T(8,128)(2,1)S(1)} custom-call(s32[24]{0:T(128)S(1)} %concatenate.18.where_ref, bf16[512,640]{1,0:T(8,128)(2,1)S(1)} %collective-permute-done.3.refs_0_, bf16[512,640]{1,0:T(8,128)(2,1)S(1)} %collective-permute-done.4.refs_1_, bf16[512,640]{1,0:T(8,128)(2,1)S(1)} %collective-permute-done.5.refs_2_, ...), custom_call_target="tpu_custom_call" | custom-call | flops 1048576 | bytes 65536 | tf_op jit(solution)/shard_map/product/pallas_call | solution.py:123
  101.6 2.2 %product.9.refs_1_ = f32[512,128]{1,0:T(8,128)S(1)} custom-call(s32[24]{0:T(128)S(1)} %concatenate.18.where_ref, bf16[512,640]{1,0:T(8,128)(2,1)S(1)} %copy-done.3, bf16[512,640]{1,0:T(8,128)(2,1)S(1)} %collective-permute-done.6.refs_1_, bf16[512,640]{1,0:T(8,128)(2,1)S(1)} %collective-permute-done.7.refs_2_, ...), custom_call_target="tpu_custom_call" | custom-call | flops 1048576 | bytes 65536 | tf_op jit(solution)/shard_map/product/pallas_call | solution.py:123
  103.8 3.8 %own_half.1 = (bf16[512,1792]{1,0:T(8,128)(2,1)}, bf16[512,1792]{1,0:T(8,128)(2,1)}, f32[512,128]{1,0:T(8,128)S(1)}) custom-call(s32[24]{0:T(128)S(1)} %concatenate.18.where_ref, bf16[512,1792]{1,0:T(8,128)(2,1)S(1)} %copy-done, bf16[512,1792]{1,0:T(8,128)(2,1)S(1)} %copy-done.1, bf16[64,1792]{1,0:T(8,128)(2,1)S(1)} %bitcast.30, ...), custom_call_target="tpu_custom_call" | custom-call | flops 1048576 | bytes 65536 | tf_op jit(solution)/shard_map/own_half/pallas_call | solution.py:218
  107.6 1.8 %collective-permute-start.24 = (f32[256,192]{1,0:T(8,128)S(1)}, f32[256,192]{1,0:T(8,128)S(1)}, u32[]{:S(2)}, u32[]{:S(2)}) collective-permute-start(f32[256,192]{1,0:T(8,128)S(1)} %add.232), channel_id=1, source_target_pairs={{0,1},{1,0},{2,3},{3,2},{4,5},{5,4},{6,7},{7,6},{8,9},{9,8},{10,11... | collective-permute-start | bytes 589832 | tf_op jit(solution)/shard_map/s_core/ppermute | solution.py:34
  109.4 3.8 %other_half.1 = (bf16[512,1792]{1,0:T(8,128)(2,1)}, bf16[512,1792]{1,0:T(8,128)(2,1)}, f32[512,128]{1,0:T(8,128)S(1)}) custom-call(s32[24]{0:T(128)S(1)} %concatenate.18.where_ref, bf16[512,1792]{1,0:T(8,128)(2,1)S(1)} %copy-done, bf16[512,1792]{1,0:T(8,128)(2,1)S(1)} %copy-done.1, ...), custom_call_target="tpu_custom_call", output_to_operand_aliasing={{0}: (5, {}), {1}: (6, {})} | custom-call | flops 1048576 | bytes 65536 | tf_op jit(solution)/shard_map/other_half/pallas_call | solution.py:256
  114.8 1.2 collective-permute-done.25
  116.2 1.4 %collective-permute-start.27 = (f32[128,128]{1,0:T(8,128)S(1)}, f32[128,128]{1,0:T(8,128)S(1)}, u32[]{:S(2)}, u32[]{:S(2)}) collective-permute-start(f32[128,128]{1,0:T(8,128)S(1)} %select_add_fusion.1), channel_id=1, source_target_pairs={{0,2},{1,3},{2,4},{3,5},{4,6},{5,7},{6,0},{7,1},{8,10},{9,11},{10,... | collective-permute-start | bytes 196616 | tf_op jit(solution)/shard_map/up/ppermute | solution.py:34
  117.6 1.4 %collective-permute-start.28 = (f32[128,128]{1,0:T(8,128)S(1)}, f32[128,128]{1,0:T(8,128)S(1)}, u32[]{:S(2)}, u32[]{:S(2)}) collective-permute-start(f32[128,128]{1,0:T(8,128)S(1)} %select_add_fusion.1), channel_id=1, source_target_pairs={{0,6},{1,7},{2,0},{3,1},{4,2},{5,3},{6,4},{7,5},{8,14},{9,15},{10,... | collective-permute-start | bytes 196616 | tf_op jit(solution)/shard_map/down/ppermute | solution.py:34
  118.9 2.3 %collective-permute-done.26 = f32[128,128]{1,0:T(8,128)S(1)} collective-permute-done((f32[128,128]{1,0:T(8,128)S(1)}, f32[128,128]{1,0:T(8,128)S(1)}, u32[]{:S(2)}, u32[]{:S(2)}) %collective-permute-start.26) | collective-permute-done | bytes 65568 | tf_op jit(solution)/shard_map/send/ppermute | solution.py:34
  121.2 1.4 %collective-permute-done.27 = f32[128,128]{1,0:T(8,128)S(1)} collective-permute-done((f32[128,128]{1,0:T(8,128)S(1)}, f32[128,128]{1,0:T(8,128)S(1)}, u32[]{:S(2)}, u32[]{:S(2)}) %collective-permute-start.27) | collective-permute-done | bytes 65568 | tf_op jit(solution)/shard_map/up/ppermute | solution.py:34
  (76 shorter events, 18.1 us)
Async XLA Ops:
  0.6 19.4 %collective-permute-start.3 = (bf16[512,640]{1,0:T(8,128)(2,1)}, bf16[512,640]{1,0:T(8,128)(2,1)S(1)}, u32[]{:S(2)}, u32[]{:S(2)}) collective-permute-start(bf16[512,640]{1,0:T(8,128)(2,1)} %refs_0_.3), channel_id=1, source_target_pairs={{0,96},{1,97},{2,98},{3,99},{4,100},{5,101},{6,102},{7,103},{8,104... | collective-permute-start | bytes 1966088 | tf_op jit(solution)/shard_map/mate_rows/ppermute | solution.py:34
  5.3 15.9 %collective-permute-start.6 = (bf16[512,640]{1,0:T(8,128)(2,1)}, bf16[512,640]{1,0:T(8,128)(2,1)S(1)}, u32[]{:S(2)}, u32[]{:S(2)}) collective-permute-start(bf16[512,640]{1,0:T(8,128)(2,1)} %refs_0_.3), channel_id=1, source_target_pairs={{0,2},{1,7},{2,4},{3,1},{4,6},{5,3},{6,0},{7,5},{8,10},{9,15},{10,... | collective-permute-start | bytes 1966088 | tf_op jit(solution)/shard_map/a1/ppermute | solution.py:34
  8.0 17.0 %collective-permute-start.7 = (bf16[512,640]{1,0:T(8,128)(2,1)}, bf16[512,640]{1,0:T(8,128)(2,1)S(1)}, u32[]{:S(2)}, u32[]{:S(2)}) collective-permute-start(bf16[512,640]{1,0:T(8,128)(2,1)} %refs_0_.3), channel_id=1, source_target_pairs={{0,6},{1,3},{2,0},{3,5},{4,2},{5,7},{6,4},{7,1},{8,14},{9,11},{10,... | collective-permute-start | bytes 1966088 | tf_op jit(solution)/shard_map/a2/ppermute | solution.py:34
  8.0 26.8 %collective-permute-start = (bf16[112,5120]{1,0:T(8,128)(2,1)}, bf16[112,5120]{1,0:T(8,128)(2,1)}, u32[]{:S(2)}, u32[]{:S(2)}) collective-permute-start(bf16[112,5120]{1,0:T(8,128)(2,1)} %refs_6_.3), channel_id=1, source_target_pairs={{0,8},{1,9},{2,10},{3,11},{4,12},{5,13},{6,14},{7,15},{8,16},{9,17... | collective-permute-start | bytes 3440648 | tf_op jit(solution)/shard_map/r1/ppermute | solution.py:34
  9.2 25.6 %collective-permute-start.1 = (bf16[112,5120]{1,0:T(8,128)(2,1)}, bf16[112,5120]{1,0:T(8,128)(2,1)}, u32[]{:S(2)}, u32[]{:S(2)}) collective-permute-start(bf16[112,5120]{1,0:T(8,128)(2,1)} %refs_6_.3), channel_id=1, source_target_pairs={{0,32},{1,25},{2,34},{3,27},{4,36},{5,29},{6,38},{7,31},{8,40},{9,... | collective-permute-start | bytes 3440648 | tf_op jit(solution)/shard_map/r2/ppermute | solution.py:34
  20.1 18.9 %collective-permute-start.2 = (bf16[112,5120]{1,0:T(8,128)(2,1)}, bf16[112,5120]{1,0:T(8,128)(2,1)}, u32[]{:S(2)}, u32[]{:S(2)}) collective-permute-start(bf16[112,5120]{1,0:T(8,128)(2,1)} %refs_6_.3), channel_id=1, source_target_pairs={{0,24},{1,33},{2,26},{3,35},{4,28},{5,37},{6,30},{7,39},{8,0},{9,4... | collective-permute-start | bytes 3440648 | tf_op jit(solution)/shard_map/r3/ppermute | solution.py:34
  21.2 17.7 %collective-permute-start.4 = (bf16[512,640]{1,0:T(8,128)(2,1)S(1)}, bf16[512,640]{1,0:T(8,128)(2,1)S(1)}, u32[]{:S(2)}, u32[]{:S(2)}) collective-permute-start(bf16[512,640]{1,0:T(8,128)(2,1)S(1)} %collective-permute-done.3.refs_0_), channel_id=1, source_target_pairs={{0,2},{1,7},{2,4},{3,1},{4,6},{5,3},{6,0},{7,5},{8,10},{9,15},{10,... | collective-permute-start | bytes 1966088 | tf_op jit(solution)/shard_map/b1/ppermute | solution.py:34
  25.0 17.1 %collective-permute-start.5 = (bf16[512,640]{1,0:T(8,128)(2,1)S(1)}, bf16[512,640]{1,0:T(8,128)(2,1)S(1)}, u32[]{:S(2)}, u32[]{:S(2)}) collective-permute-start(bf16[512,640]{1,0:T(8,128)(2,1)S(1)} %collective-permute-done.3.refs_0_), channel_id=1, source_target_pairs={{0,6},{1,3},{2,0},{3,5},{4,2},{5,7},{6,4},{7,1},{8,14},{9,11},{10,... | collective-permute-start | bytes 1966088 | tf_op jit(solution)/shard_map/b2/ppermute | solution.py:34
  28.1 24.2 %copy-start.1 = (bf16[512,1792]{1,0:T(8,128)(2,1)S(1)}, bf16[512,1792]{1,0:T(8,128)(2,1)}, u32[]{:S(2)}) copy-start(bf16[512,1792]{1,0:T(8,128)(2,1)} %up_ref.5) | copy-start | bytes 5505028
  28.1 24.2 %copy-start.5 = (bf16[1792,64]{0,1:T(8,128)(2,1)S(1)}, bf16[1792,64]{0,1:T(8,128)(2,1)}, u32[]{:S(2)}) copy-start(bf16[1792,64]{0,1:T(8,128)(2,1)} %param.14) | copy-start | bytes 688132
  42.3 18.2 %collective-permute-start.14 = (bf16[1536,640]{1,0:T(8,128)(2,1)S(1)}, bf16[1536,640]{1,0:T(8,128)(2,1)S(1)}, u32[]{:S(2)}, u32[]{:S(2)}) collective-permute-start(bf16[1536,640]{1,0:T(8,128)(2,1)S(1)} %pad_maximum_fusion), channel_id=1, source_target_pairs={{0,1},{1,0},{2,3},{3,2},{4,5},{5,4},{6,7},{7,6},{8,9},{9,8},{10,11... | collective-permute-start | bytes 5898248 | tf_op jit(solution)/shard_map/b_swap/ppermute | solution.py:34
  42.5 9.7 %collective-permute-start.11 = (bf16[512,640]{1,0:T(8,128)(2,1)S(1)}, bf16[512,640]{1,0:T(8,128)(2,1)S(1)}, u32[]{:S(2)}, u32[]{:S(2)}) collective-permute-start(bf16[512,640]{1,0:T(8,128)(2,1)S(1)} %collective-permute-done.4.refs_1_), channel_id=1, source_target_pairs={{0,2},{1,7},{2,4},{3,1},{4,6},{5,3},{6,0},{7,5},{8,10},{9,15},{10,... | collective-permute-start | bytes 1966088 | tf_op jit(solution)/shard_map/b_far/ppermute | solution.py:34
  43.2 27.5 %collective-permute-start.10 = (bf16[112,5120]{1,0:T(8,128)(2,1)}, bf16[112,5120]{1,0:T(8,128)(2,1)S(1)}, u32[]{:S(2)}, u32[]{:S(2)}) collective-permute-start(bf16[112,5120]{1,0:T(8,128)(2,1)} %collective-permute-done.1.refs_8_), channel_id=1, source_target_pairs={{0,24},{1,25},{2,26},{3,27},{4,28},{5,29},{6,30},{7,31},{8,0},{9,1... | collective-permute-start | bytes 3440648 | tf_op jit(solution)/shard_map/r6/ppermute | solution.py:34
  45.6 25.1 %collective-permute-start.8 = (bf16[112,5120]{1,0:T(8,128)(2,1)}, bf16[112,5120]{1,0:T(8,128)(2,1)S(1)}, u32[]{:S(2)}, u32[]{:S(2)}) collective-permute-start(bf16[112,5120]{1,0:T(8,128)(2,1)} %collective-permute-done.1.refs_8_), channel_id=1, source_target_pairs={{0,8},{1,33},{2,10},{3,35},{4,12},{5,37},{6,14},{7,39},{8,16},{9,4... | collective-permute-start | bytes 3440648 | tf_op jit(solution)/shard_map/r4/ppermute | solution.py:34
  45.6 27.5 %collective-permute-start.9 = (bf16[112,5120]{1,0:T(8,128)(2,1)}, bf16[112,5120]{1,0:T(8,128)(2,1)S(1)}, u32[]{:S(2)}, u32[]{:S(2)}) collective-permute-start(bf16[112,5120]{1,0:T(8,128)(2,1)} %collective-permute-done.refs_7_), channel_id=1, source_target_pairs={{0,8},{1,33},{2,10},{3,35},{4,12},{5,37},{6,14},{7,39},{8,16},{9,4... | collective-permute-start | bytes 3440648 | tf_op jit(solution)/shard_map/r5/ppermute | solution.py:34
  58.0 3.7 %collective-permute-start.13 = (f32[256,192]{1,0:T(8,128)S(1)}, f32[256,192]{1,0:T(8,128)S(1)}, u32[]{:S(2)}, u32[]{:S(2)}) collective-permute-start(f32[256,192]{1,0:T(8,128)S(1)} %slice_select_fusion), channel_id=1, source_target_pairs={{0,1},{1,0},{2,3},{3,2},{4,5},{5,4},{6,7},{7,6},{8,9},{9,8},{10,11... | collective-permute-start | bytes 589832 | tf_op jit(solution)/shard_map/s_core/ppermute | solution.py:34
  60.5 12.6 %collective-permute-start.12 = (bf16[512,640]{1,0:T(8,128)(2,1)S(1)}, bf16[512,640]{1,0:T(8,128)(2,1)S(1)}, u32[]{:S(2)}, u32[]{:S(2)}) collective-permute-start(bf16[512,640]{1,0:T(8,128)(2,1)S(1)} %collective-permute-done.6.refs_1_), channel_id=1, source_target_pairs={{0,2},{1,7},{2,4},{3,1},{4,6},{5,3},{6,0},{7,5},{8,10},{9,15},{10,... | collective-permute-start | bytes 1966088 | tf_op jit(solution)/shard_map/a_far/ppermute | solution.py:34
  61.6 11.5 %collective-permute-start.15 = (bf16[512,640]{1,0:T(8,128)(2,1)S(1)}, bf16[512,640]{1,0:T(8,128)(2,1)S(1)}, u32[]{:S(2)}, u32[]{:S(2)}) collective-permute-start(bf16[512,640]{1,0:T(8,128)(2,1)S(1)} %collective-permute-done.11.refs_3_), channel_id=1, source_target_pairs={{0,1},{1,0},{2,3},{3,2},{4,5},{5,4},{6,7},{7,6},{8,9},{9,8},{10,11... | collective-permute-start | bytes 1966088 | tf_op jit(solution)/shard_map/b_swap/ppermute | solution.py:34
  78.0 8.6 %collective-permute-start.16 = (bf16[1536,640]{1,0:T(8,128)(2,1)S(1)}, bf16[1536,640]{1,0:T(8,128)(2,1)S(1)}, u32[]{:S(2)}, u32[]{:S(2)}) collective-permute-start(bf16[1536,640]{1,0:T(8,128)(2,1)S(1)} %pad_maximum_fusion.1), channel_id=1, source_target_pairs={{0,1},{1,0},{2,3},{3,2},{4,5},{5,4},{6,7},{7,6},{8,9},{9,8},{10,11... | collective-permute-start | bytes 5898248 | tf_op jit(solution)/shard_map/a_swap/ppermute | solution.py:34
  80.2 18.2 %collective-permute-start.19 = (bf16[112,5120]{1,0:T(8,128)(2,1)S(1)}, bf16[112,5120]{1,0:T(8,128)(2,1)S(1)}, u32[]{:S(2)}, u32[]{:S(2)}) collective-permute-start(bf16[112,5120]{1,0:T(8,128)(2,1)S(1)} %collective-permute-done.10.refs_8_.refs_12_), channel_id=1, source_target_pairs={{0,24},{1,33},{2,26},{3,35},{4,28},{5,37},{6,30},{7,39},{8,0},{9,4... | collective-permute-start | bytes 3440648 | tf_op jit(solution)/shard_map/r7/ppermute | solution.py:34
  80.2 5.2 %collective-permute-start.17 = (bf16[512,640]{1,0:T(8,128)(2,1)S(1)}, bf16[512,640]{1,0:T(8,128)(2,1)S(1)}, u32[]{:S(2)}, u32[]{:S(2)}) collective-permute-start(bf16[512,640]{1,0:T(8,128)(2,1)S(1)} %collective-permute-done.12.refs_3_), channel_id=1, source_target_pairs={{0,1},{1,0},{2,3},{3,2},{4,5},{5,4},{6,7},{7,6},{8,9},{9,8},{10,11... | collective-permute-start | bytes 1966088 | tf_op jit(solution)/shard_map/a_swap/ppermute | solution.py:34
  80.4 18.0 %collective-permute-start.18 = (bf16[512,512]{1,0:T(8,128)(2,1)S(1)}, bf16[512,512]{1,0:T(8,128)(2,1)S(1)}, u32[]{:S(2)}, u32[]{:S(2)}) collective-permute-start(bf16[512,512]{1,0:T(8,128)(2,1)S(1)} %product.5), channel_id=1, source_target_pairs={{0,96},{1,97},{2,98},{3,99},{4,100},{5,101},{6,102},{7,103},{8,104... | collective-permute-start | bytes 1572872 | tf_op jit(solution)/shard_map/mate_grad1/ppermute | solution.py:34
  81.3 12.9 %collective-permute-start.22 = (f32[256,192]{1,0:T(8,128)S(1)}, f32[256,192]{1,0:T(8,128)S(1)}, u32[]{:S(2)}, u32[]{:S(2)}) collective-permute-start(f32[256,192]{1,0:T(8,128)S(1)} %select_add_fusion), channel_id=1, source_target_pairs={{0,2},{1,3},{2,0},{3,1},{4,6},{5,7},{6,4},{7,5},{8,10},{9,11},{10,... | collective-permute-start | bytes 589832 | tf_op jit(solution)/shard_map/s_near/ppermute | solution.py:34
  85.4 22.2 %collective-permute-start.20 = (bf16[512,384]{1,0:T(8,128)(2,1)S(1)}, bf16[512,384]{1,0:T(8,128)(2,1)S(1)}, u32[]{:S(2)}, u32[]{:S(2)}) collective-permute-start(bf16[512,384]{1,0:T(8,128)(2,1)S(1)} %product.6), channel_id=1, source_target_pairs={{0,96},{1,97},{2,98},{3,99},{4,100},{5,101},{6,102},{7,103},{8,104... | collective-permute-start | bytes 1179656 | tf_op jit(solution)/shard_map/mate_grad2/ppermute | solution.py:34
  94.3 13.3 %collective-permute-start.23 = (f32[256,192]{1,0:T(8,128)S(1)}, f32[256,192]{1,0:T(8,128)S(1)}, u32[]{:S(2)}, u32[]{:S(2)}) collective-permute-start(f32[256,192]{1,0:T(8,128)S(1)} %add.231), channel_id=1, source_target_pairs={{0,4},{1,5},{2,6},{3,7},{4,0},{5,1},{6,2},{7,3},{8,12},{9,13},{10,... | collective-permute-start | bytes 589832 | tf_op jit(solution)/shard_map/s_far/ppermute | solution.py:34
  100.6 6.9 %collective-permute-start.21 = (bf16[512,128]{1,0:T(8,128)(2,1)S(1)}, bf16[512,128]{1,0:T(8,128)(2,1)S(1)}, u32[]{:S(2)}, u32[]{:S(2)}) collective-permute-start(bf16[512,128]{1,0:T(8,128)(2,1)S(1)} %product.8), channel_id=1, source_target_pairs={{0,96},{1,97},{2,98},{3,99},{4,100},{5,101},{6,102},{7,103},{8,104... | collective-permute-start | bytes 393224 | tf_op jit(solution)/shard_map/mate_grad3/ppermute | solution.py:34
  107.6 5.6 %collective-permute-start.24 = (f32[256,192]{1,0:T(8,128)S(1)}, f32[256,192]{1,0:T(8,128)S(1)}, u32[]{:S(2)}, u32[]{:S(2)}) collective-permute-start(f32[256,192]{1,0:T(8,128)S(1)} %add.232), channel_id=1, source_target_pairs={{0,1},{1,0},{2,3},{3,2},{4,5},{5,4},{6,7},{7,6},{8,9},{9,8},{10,11... | collective-permute-start | bytes 589832 | tf_op jit(solution)/shard_map/s_core/ppermute | solution.py:34
  114.7 1.3 %collective-permute-start.25 = (f32[128,128]{1,0:T(8,128)S(1)}, f32[128,128]{1,0:T(8,128)S(1)}, u32[]{:S(2)}, u32[]{:S(2)}) collective-permute-start(f32[128,128]{1,0:T(8,128)S(1)} %slice_select_fusion.1), channel_id=1, source_target_pairs={{0,1},{1,0},{2,3},{3,2},{4,5},{5,4},{6,7},{7,6},{8,9},{9,8},{10,11... | collective-permute-start | bytes 196616 | tf_op jit(solution)/shard_map/swap/ppermute | solution.py:34
  116.1 5.1 %collective-permute-start.26 = (f32[128,128]{1,0:T(8,128)S(1)}, f32[128,128]{1,0:T(8,128)S(1)}, u32[]{:S(2)}, u32[]{:S(2)}) collective-permute-start(f32[128,128]{1,0:T(8,128)S(1)} %select_add_fusion.1), channel_id=1, source_target_pairs={{0,4},{1,5},{2,6},{3,7},{4,0},{5,1},{6,2},{7,3},{8,12},{9,13},{10,... | collective-permute-start | bytes 196616 | tf_op jit(solution)/shard_map/send/ppermute | solution.py:34
  116.2 6.5 %collective-permute-start.27 = (f32[128,128]{1,0:T(8,128)S(1)}, f32[128,128]{1,0:T(8,128)S(1)}, u32[]{:S(2)}, u32[]{:S(2)}) collective-permute-start(f32[128,128]{1,0:T(8,128)S(1)} %select_add_fusion.1), channel_id=1, source_target_pairs={{0,2},{1,3},{2,4},{3,5},{4,6},{5,7},{6,0},{7,1},{8,10},{9,11},{10,... | collective-permute-start | bytes 196616 | tf_op jit(solution)/shard_map/up/ppermute | solution.py:34
  117.6 5.1 %collective-permute-start.28 = (f32[128,128]{1,0:T(8,128)S(1)}, f32[128,128]{1,0:T(8,128)S(1)}, u32[]{:S(2)}, u32[]{:S(2)}) collective-permute-start(f32[128,128]{1,0:T(8,128)S(1)} %select_add_fusion.1), channel_id=1, source_target_pairs={{0,6},{1,7},{2,0},{3,1},{4,2},{5,3},{6,4},{7,5},{8,14},{9,15},{10,... | collective-permute-start | bytes 196616 | tf_op jit(solution)/shard_map/down/ppermute | solution.py:34
  122.7 1.7 %collective-permute-start.29 = (f32[128,128]{1,0:T(8,128)S(1)}, f32[128,128]{1,0:T(8,128)S(1)}, u32[]{:S(2)}, u32[]{:S(2)}) collective-permute-start(f32[128,128]{1,0:T(8,128)S(1)} %add_add_fusion), channel_id=1, source_target_pairs={{0,1},{1,0},{2,3},{3,2},{4,5},{5,4},{6,7},{7,6},{8,9},{9,8},{10,11... | collective-permute-start | bytes 196616 | tf_op jit(solution)/shard_map/swap/ppermute | solution.py:34
  (6 other events, 49.1 us)

commit v12 on v11

--- a/solution.py
+++ b/solution.py
@@ -374,13 +374,13 @@
     a_other = [swap(after(near, h1), "a_swap"), swap(a_far, "a_swap")]
     near_y = send(half, lambda z, x, y, c: (z, x, y ^ 1, c), "s_near")
     own1 = product(F32, after(where, h2), a_mine, a_other, [own_w, r1, r2, r3, r4, r5, r6])
-    half += after(near_y, own1)
+    half += after(near_y, h2)
     far_y = send(half, lambda z, x, y, c: (z, x, y ^ 2, c), "s_far")
     h3 = product(BF16, after(where, h1_in, own1), b_mine, b_other, [r7])
     own2 = product(F32, after(where, h3), a_mine, a_other, [r7])
     h_in = [h1_in, h2_in, mate(h3, "mate_grad3")]
     grad_gate, grad_up, part = own_half(where, gate_pre, up_pre, (own1, own2), ph_t)
-    half += after(far_y, part, h_in[1], h_in[2])
+    half = after(half + after(far_y, own1), part, h_in[1], h_in[2])
     rest = swap(half, "s_core")
     sums = jnp.concatenate(
         [jnp.where(c == 0, half, rest), jnp.where(c == 0, rest, half)], axis=0

time: 126 us -> 130 us (1.032)
  waiting for transfers between devices: 48 us -> 50.2 us
  starting transfers between devices: 37.1 us -> 38.7 us
    ppermute x30, waiting for transfers between devices: 48 us -> 50.2 us  [send(): return lax.ppermute(value, AXES, pairs)]
    ppermute x30, starting transfers between devices: 37.1 us -> 38.7 us  [send(): return lax.ppermute(value, AXES, pairs)]
  transfers between devices with their start and end apart: 30 -> 30, of which waited for: 14 -> 15; matrix products, arithmetic and copies ran while one was open for 3% -> 3% of each run, Pallas kernels for 20% -> 20%
where the time goes in v12:
time: 130 us
  waiting for transfers between devices  50.2 us (39%)
  starting transfers between devices  38.7 us (30%)
  Pallas kernels  31.6 us (24%)
  local copies, waits for them, and re-layouts  6.13 us (5%)
  other arithmetic  2.11 us (2%)
    ppermute x30, waiting for transfers between devices, send(): return lax.ppermute(value, AXES, pairs)  50.2 us
    ppermute x30, starting transfers between devices, send(): return lax.ppermute(value, AXES, pairs)  38.7 us
    pallas_call x5, Pallas kernels, product(): pl.pallas_call(functools.partial(product_kernel, shards), out_shape=jax.S...  20.2 us
    pallas_call x1, Pallas kernels, own_half(): pl.pallas_call(functools.partial(own_kernel, len(h)), out_shape=(BIG, BIG...  3.82 us
    pallas_call x1, Pallas kernels, other_half(): pl.pallas_call(functools.partial(other_kernel, len(h)), out_shape=(BIG, B...  3.76 us
    unnamed x16, local copies, waits for them, and re-layouts  3.28 us
  transfers between devices with their start and end apart: 30, of which 15 were waited for; matrix products, arithmetic and copies ran while one was open for 3% of the time, Pallas kernels for 20%

profile of v12, /device:TPU:1, one launch (start us, length us, event | category | flops | bytes accessed | tf_op | source)
XLA Modules:
  0.0 129.6 jit_solution(12367037125641936353)
XLA Ops:
  0.6 4.7 %collective-permute-start.3 = (bf16[512,640]{1,0:T(8,128)(2,1)}, bf16[512,640]{1,0:T(8,128)(2,1)S(1)}, u32[]{:S(2)}, u32[]{:S(2)}) collective-permute-start(bf16[512,640]{1,0:T(8,128)(2,1)} %refs_0_.3), channel_id=1, source_target_pairs={{0,96},{1,97},{2,98},{3,99},{4,100},{5,101},{6,102},{7,103},{8,104... | collective-permute-start | bytes 1966088 | tf_op jit(solution)/shard_map/mate_rows/ppermute | solution.py:34
  5.3 2.7 %collective-permute-start.6 = (bf16[512,640]{1,0:T(8,128)(2,1)}, bf16[512,640]{1,0:T(8,128)(2,1)S(1)}, u32[]{:S(2)}, u32[]{:S(2)}) collective-permute-start(bf16[512,640]{1,0:T(8,128)(2,1)} %refs_0_.3), channel_id=1, source_target_pairs={{0,2},{1,7},{2,4},{3,1},{4,6},{5,3},{6,0},{7,5},{8,10},{9,15},{10,... | collective-permute-start | bytes 1966088 | tf_op jit(solution)/shard_map/a1/ppermute | solution.py:34
  9.2 1.5 %collective-permute-start.1 = (bf16[112,5120]{1,0:T(8,128)(2,1)}, bf16[112,5120]{1,0:T(8,128)(2,1)}, u32[]{:S(2)}, u32[]{:S(2)}) collective-permute-start(bf16[112,5120]{1,0:T(8,128)(2,1)} %refs_6_.3), channel_id=1, source_target_pairs={{0,32},{1,25},{2,34},{3,27},{4,36},{5,29},{6,38},{7,31},{8,40},{9,... | collective-permute-start | bytes 3440648 | tf_op jit(solution)/shard_map/r2/ppermute | solution.py:34
  10.7 9.4 %collective-permute-done.3.refs_0_ = bf16[512,640]{1,0:T(8,128)(2,1)S(1)} collective-permute-done((bf16[512,640]{1,0:T(8,128)(2,1)}, bf16[512,640]{1,0:T(8,128)(2,1)S(1)}, u32[]{:S(2)}, u32[]{:S(2)}) %collective-permute-start.3) | collective-permute-done | bytes 655392 | tf_op jit(solution)/shard_map/mate_rows/ppermute | solution.py:34
  21.2 3.4 %collective-permute-start.4 = (bf16[512,640]{1,0:T(8,128)(2,1)S(1)}, bf16[512,640]{1,0:T(8,128)(2,1)S(1)}, u32[]{:S(2)}, u32[]{:S(2)}) collective-permute-start(bf16[512,640]{1,0:T(8,128)(2,1)S(1)} %collective-permute-done.3.refs_0_), channel_id=1, source_target_pairs={{0,2},{1,7},{2,4},{3,1},{4,6},{5,3},{6,0},{7,5},{8,10},{9,15},{10,... | collective-permute-start | bytes 1966088 | tf_op jit(solution)/shard_map/b1/ppermute | solution.py:34
  25.1 1.3 %reduce_sum.29 = s32[]{:T(128)} reduce(s32[4]{0:T(128)} %param.15, s32[]{:T(128)} %constant.165.clone.1), dimensions={0}, to_apply=%region_2.3 | reduce | flops 3 | bytes 24 | tf_op jit(solution)/shard_map/reduce_sum | solution.py:341
  26.7 1.3 %concatenate.18.where_ref = s32[24]{0:T(128)S(1)} concatenate(s32[8]{0:T(128)S(1)} %get-tuple-element.66, s32[8]{0:T(128)S(1)} %get-tuple-element.65, s32[1]{0:T(128)} %bitcast.16, s32[1]{0:T(128)} %bitcast.17, s32[1]{0:T(128)} %bitcast.18, s32[1]{0:T(128)} %bitcast.19, s32[4]{0:T(128)} %param.15), dimensions={0} | concatenate | bytes 192 | tf_op jit(solution)/shard_map/concatenate | solution.py:337
  28.1 6.8 %collective-permute-done.refs_7_ = bf16[112,5120]{1,0:T(8,128)(2,1)} collective-permute-done((bf16[112,5120]{1,0:T(8,128)(2,1)}, bf16[112,5120]{1,0:T(8,128)(2,1)}, u32[]{:S(2)}, u32[]{:S(2)}) %collective-permute-start) | collective-permute-done | bytes 1146912 | tf_op jit(solution)/shard_map/r1/ppermute | solution.py:34
  34.9 4.1 %collective-permute-done.2.refs_9_ = bf16[112,5120]{1,0:T(8,128)(2,1)} collective-permute-done((bf16[112,5120]{1,0:T(8,128)(2,1)}, bf16[112,5120]{1,0:T(8,128)(2,1)}, u32[]{:S(2)}, u32[]{:S(2)}) %collective-permute-start.2) | collective-permute-done | bytes 1146912 | tf_op jit(solution)/shard_map/r3/ppermute | solution.py:34
  38.9 3.1 %collective-permute-done.5.refs_2_ = bf16[512,640]{1,0:T(8,128)(2,1)S(1)} collective-permute-done((bf16[512,640]{1,0:T(8,128)(2,1)S(1)}, bf16[512,640]{1,0:T(8,128)(2,1)S(1)}, u32[]{:S(2)}, u32[]{:S(2)}) %collective-permute-start.5) | collective-permute-done | bytes 655392 | tf_op jit(solution)/shard_map/b2/ppermute | solution.py:34
  43.2 1.5 %collective-permute-start.9 = (bf16[112,5120]{1,0:T(8,128)(2,1)}, bf16[112,5120]{1,0:T(8,128)(2,1)S(1)}, u32[]{:S(2)}, u32[]{:S(2)}) collective-permute-start(bf16[112,5120]{1,0:T(8,128)(2,1)} %collective-permute-done.refs_7_), channel_id=1, source_target_pairs={{0,8},{1,33},{2,10},{3,35},{4,12},{5,37},{6,14},{7,39},{8,16},{9,4... | collective-permute-start | bytes 3440648 | tf_op jit(solution)/shard_map/r5/ppermute | solution.py:34
  44.7 2.4 %collective-permute-start.10 = (bf16[112,5120]{1,0:T(8,128)(2,1)}, bf16[112,5120]{1,0:T(8,128)(2,1)S(1)}, u32[]{:S(2)}, u32[]{:S(2)}) collective-permute-start(bf16[112,5120]{1,0:T(8,128)(2,1)} %collective-permute-done.1.refs_8_), channel_id=1, source_target_pairs={{0,24},{1,25},{2,26},{3,27},{4,28},{5,29},{6,30},{7,31},{8,0},{9,1... | collective-permute-start | bytes 3440648 | tf_op jit(solution)/shard_map/r6/ppermute | solution.py:34
  47.1 5.2 %collective-permute-done.11.refs_3_ = bf16[512,640]{1,0:T(8,128)(2,1)S(1)} collective-permute-done((bf16[512,640]{1,0:T(8,128)(2,1)S(1)}, bf16[512,640]{1,0:T(8,128)(2,1)S(1)}, u32[]{:S(2)}, u32[]{:S(2)}) %collective-permute-start.11) | collective-permute-done | bytes 655392 | tf_op jit(solution)/shard_map/b_far/ppermute | solution.py:34
  55.5 2.4 %early.1 = f32[512,192]{1,0:T(8,128)S(1)} custom-call(s32[24]{0:T(128)S(1)} %concatenate.18.where_ref, bf16[512,640]{1,0:T(8,128)(2,1)S(1)} %copy-done.6, bf16[512,640]{1,0:T(8,128)(2,1)S(1)} %copy-done.2, bf16[64,5120]{1,0:T(8,128)(2,1)S(1)} %bitcast.32, bf16[512,1792]{1,0:T(8,128)(2,1)S(1)} %copy-done, bf16[512,1792]{1,0:T(8,128)(2,1)S(1)} %copy-done.1, ...), custom_call_target="tpu_custom_call" | custom-call | flops 1048576 | bytes 65536 | tf_op jit(solution)/shard_map/early/pallas_call | solution.py:149
  58.0 2.5 %collective-permute-start.13 = (f32[256,192]{1,0:T(8,128)S(1)}, f32[256,192]{1,0:T(8,128)S(1)}, u32[]{:S(2)}, u32[]{:S(2)}) collective-permute-start(f32[256,192]{1,0:T(8,128)S(1)} %slice_select_fusion), channel_id=1, source_target_pairs={{0,1},{1,0},{2,3},{3,2},{4,5},{5,4},{6,7},{7,6},{8,9},{9,8},{10,11... | collective-permute-start | bytes 589832 | tf_op jit(solution)/shard_map/s_core/ppermute | solution.py:34
  62.2 8.5 %collective-permute-done.9.refs_7_.refs_11_ = bf16[112,5120]{1,0:T(8,128)(2,1)S(1)} collective-permute-done((bf16[112,5120]{1,0:T(8,128)(2,1)}, bf16[112,5120]{1,0:T(8,128)(2,1)S(1)}, u32[]{:S(2)}, u32[]{:S(2)}) %collective-permute-start.9) | collective-permute-done | bytes 1146912 | tf_op jit(solution)/shard_map/r5/ppermute | solution.py:34
  71.7 4.9 %product.5 = bf16[512,512]{1,0:T(8,128)(2,1)S(1)} custom-call(s32[24]{0:T(128)S(1)} %concatenate.18.where_ref, bf16[512,640]{1,0:T(8,128)(2,1)S(1)} %collective-permute-done.3.refs_0_, bf16[512,640]{1,0:T(8,128)(2,1)S(1)} %collective-permute-done.4.refs_1_, bf16[512,640]{1,0:T(8,128)(2,1)S(1)} %collective-permute-done.5.refs_2_, ...), custom_call_target="tpu_custom_call" | custom-call | flops 1048576 | bytes 65536 | tf_op jit(solution)/shard_map/product/pallas_call | solution.py:123
  77.9 3.6 %collective-permute-start.17 = (bf16[512,640]{1,0:T(8,128)(2,1)S(1)}, bf16[512,640]{1,0:T(8,128)(2,1)S(1)}, u32[]{:S(2)}, u32[]{:S(2)}) collective-permute-start(bf16[512,640]{1,0:T(8,128)(2,1)S(1)} %collective-permute-done.12.refs_3_), channel_id=1, source_target_pairs={{0,1},{1,0},{2,3},{3,2},{4,5},{5,4},{6,7},{7,6},{8,9},{9,8},{10,11... | collective-permute-start | bytes 1966088 | tf_op jit(solution)/shard_map/a_swap/ppermute | solution.py:34
  82.6 3.4 %product.6 = bf16[512,384]{1,0:T(8,128)(2,1)S(1)} custom-call(s32[24]{0:T(128)S(1)} %concatenate.18.where_ref, bf16[512,640]{1,0:T(8,128)(2,1)S(1)} %collective-permute-done.3.refs_0_, bf16[512,640]{1,0:T(8,128)(2,1)S(1)} %collective-permute-done.4.refs_1_, bf16[512,640]{1,0:T(8,128)(2,1)S(1)} %collective-permute-done.5.refs_2_, ...), custom_call_target="tpu_custom_call" | custom-call | flops 1048576 | bytes 65536 | tf_op jit(solution)/shard_map/product/pallas_call | solution.py:123
  86.1 4.2 %collective-permute-done.22 = f32[256,192]{1,0:T(8,128)S(1)} collective-permute-done((f32[256,192]{1,0:T(8,128)S(1)}, f32[256,192]{1,0:T(8,128)S(1)}, u32[]{:S(2)}, u32[]{:S(2)}) %collective-permute-start.22) | collective-permute-done | bytes 196640 | tf_op jit(solution)/shard_map/s_near/ppermute | solution.py:34
  90.3 1.5 %collective-permute-start.20 = (bf16[512,384]{1,0:T(8,128)(2,1)S(1)}, bf16[512,384]{1,0:T(8,128)(2,1)S(1)}, u32[]{:S(2)}, u32[]{:S(2)}) collective-permute-start(bf16[512,384]{1,0:T(8,128)(2,1)S(1)} %product.6), channel_id=1, source_target_pairs={{0,96},{1,97},{2,98},{3,99},{4,100},{5,101},{6,102},{7,103},{8,104... | collective-permute-start | bytes 1179656 | tf_op jit(solution)/shard_map/mate_grad2/ppermute | solution.py:34
  91.9 1.2 collective-permute-start.23
  93.1 7.6 %product.7.refs_0_ = f32[512,896]{1,0:T(8,128)S(1)} custom-call(s32[24]{0:T(128)S(1)} %concatenate.18.where_ref, bf16[512,640]{1,0:T(8,128)(2,1)S(1)} %copy-done.3, bf16[512,640]{1,0:T(8,128)(2,1)S(1)} %collective-permute-done.6.refs_1_, bf16[512,640]{1,0:T(8,128)(2,1)S(1)} %collective-permute-done.7.refs_2_, ...), custom_call_target="tpu_custom_call" | custom-call | flops 1048576 | bytes 65536 | tf_op jit(solution)/shard_map/product/pallas_call | solution.py:123
  100.7 2.2 %product.8 = bf16[512,128]{1,0:T(8,128)(2,1)S(1)} custom-call(s32[24]{0:T(128)S(1)} %concatenate.18.where_ref, bf16[512,640]{1,0:T(8,128)(2,1)S(1)} %collective-permute-done.3.refs_0_, bf16[512,640]{1,0:T(8,128)(2,1)S(1)} %collective-permute-done.4.refs_1_, bf16[512,640]{1,0:T(8,128)(2,1)S(1)} %collective-permute-done.5.refs_2_, ...), custom_call_target="tpu_custom_call" | custom-call | flops 1048576 | bytes 65536 | tf_op jit(solution)/shard_map/product/pallas_call | solution.py:123
  103.3 2.2 %product.9.refs_1_ = f32[512,128]{1,0:T(8,128)S(1)} custom-call(s32[24]{0:T(128)S(1)} %concatenate.18.where_ref, bf16[512,640]{1,0:T(8,128)(2,1)S(1)} %copy-done.3, bf16[512,640]{1,0:T(8,128)(2,1)S(1)} %collective-permute-done.6.refs_1_, bf16[512,640]{1,0:T(8,128)(2,1)S(1)} %collective-permute-done.7.refs_2_, ...), custom_call_target="tpu_custom_call" | custom-call | flops 1048576 | bytes 65536 | tf_op jit(solution)/shard_map/product/pallas_call | solution.py:123
  105.5 3.8 %own_half.1 = (bf16[512,1792]{1,0:T(8,128)(2,1)}, bf16[512,1792]{1,0:T(8,128)(2,1)}, f32[512,128]{1,0:T(8,128)S(1)}) custom-call(s32[24]{0:T(128)S(1)} %concatenate.18.where_ref, bf16[512,1792]{1,0:T(8,128)(2,1)S(1)} %copy-done, bf16[512,1792]{1,0:T(8,128)(2,1)S(1)} %copy-done.1, bf16[64,1792]{1,0:T(8,128)(2,1)S(1)} %bitcast.30, ...), custom_call_target="tpu_custom_call" | custom-call | flops 1048576 | bytes 65536 | tf_op jit(solution)/shard_map/own_half/pallas_call | solution.py:218
  109.3 2.0 %collective-permute-start.24 = (f32[256,192]{1,0:T(8,128)S(1)}, f32[256,192]{1,0:T(8,128)S(1)}, u32[]{:S(2)}, u32[]{:S(2)}) collective-permute-start(f32[256,192]{1,0:T(8,128)S(1)} %add.232), channel_id=1, source_target_pairs={{0,1},{1,0},{2,3},{3,2},{4,5},{5,4},{6,7},{7,6},{8,9},{9,8},{10,11... | collective-permute-start | bytes 589832 | tf_op jit(solution)/shard_map/s_core/ppermute | solution.py:34
  111.3 3.8 %other_half.1 = (bf16[512,1792]{1,0:T(8,128)(2,1)}, bf16[512,1792]{1,0:T(8,128)(2,1)}, f32[512,128]{1,0:T(8,128)S(1)}) custom-call(s32[24]{0:T(128)S(1)} %concatenate.18.where_ref, bf16[512,1792]{1,0:T(8,128)(2,1)S(1)} %copy-done, bf16[512,1792]{1,0:T(8,128)(2,1)S(1)} %copy-done.1, ...), custom_call_target="tpu_custom_call", output_to_operand_aliasing={{0}: (5, {}), {1}: (6, {})} | custom-call | flops 1048576 | bytes 65536 | tf_op jit(solution)/shard_map/other_half/pallas_call | solution.py:256
  118.8 2.0 %collective-permute-start.28 = (f32[128,128]{1,0:T(8,128)S(1)}, f32[128,128]{1,0:T(8,128)S(1)}, u32[]{:S(2)}, u32[]{:S(2)}) collective-permute-start(f32[128,128]{1,0:T(8,128)S(1)} %select_add_fusion.1), channel_id=1, source_target_pairs={{0,6},{1,7},{2,0},{3,1},{4,2},{5,3},{6,4},{7,5},{8,14},{9,15},{10,... | collective-permute-start | bytes 196616 | tf_op jit(solution)/shard_map/down/ppermute | solution.py:34
  120.7 1.4 %collective-permute-start.26 = (f32[128,128]{1,0:T(8,128)S(1)}, f32[128,128]{1,0:T(8,128)S(1)}, u32[]{:S(2)}, u32[]{:S(2)}) collective-permute-start(f32[128,128]{1,0:T(8,128)S(1)} %select_add_fusion.1), channel_id=1, source_target_pairs={{0,4},{1,5},{2,6},{3,7},{4,0},{5,1},{6,2},{7,3},{8,12},{9,13},{10,... | collective-permute-start | bytes 196616 | tf_op jit(solution)/shard_map/send/ppermute | solution.py:34
  122.8 2.5 %collective-permute-done.26 = f32[128,128]{1,0:T(8,128)S(1)} collective-permute-done((f32[128,128]{1,0:T(8,128)S(1)}, f32[128,128]{1,0:T(8,128)S(1)}, u32[]{:S(2)}, u32[]{:S(2)}) %collective-permute-start.26) | collective-permute-done | bytes 65568 | tf_op jit(solution)/shard_map/send/ppermute | solution.py:34
  125.4 1.9 %collective-permute-start.29 = (f32[128,128]{1,0:T(8,128)S(1)}, f32[128,128]{1,0:T(8,128)S(1)}, u32[]{:S(2)}, u32[]{:S(2)}) collective-permute-start(f32[128,128]{1,0:T(8,128)S(1)} %add_add_fusion), channel_id=1, source_target_pairs={{0,1},{1,0},{2,3},{3,2},{4,5},{5,4},{6,7},{7,6},{8,9},{9,8},{10,11... | collective-permute-start | bytes 196616 | tf_op jit(solution)/shard_map/swap/ppermute | solution.py:34
  (76 shorter events, 19.8 us)
Async XLA Ops:
  0.6 19.4 %collective-permute-start.3 = (bf16[512,640]{1,0:T(8,128)(2,1)}, bf16[512,640]{1,0:T(8,128)(2,1)S(1)}, u32[]{:S(2)}, u32[]{:S(2)}) collective-permute-start(bf16[512,640]{1,0:T(8,128)(2,1)} %refs_0_.3), channel_id=1, source_target_pairs={{0,96},{1,97},{2,98},{3,99},{4,100},{5,101},{6,102},{7,103},{8,104... | collective-permute-start | bytes 1966088 | tf_op jit(solution)/shard_map/mate_rows/ppermute | solution.py:34
  5.3 15.9 %collective-permute-start.6 = (bf16[512,640]{1,0:T(8,128)(2,1)}, bf16[512,640]{1,0:T(8,128)(2,1)S(1)}, u32[]{:S(2)}, u32[]{:S(2)}) collective-permute-start(bf16[512,640]{1,0:T(8,128)(2,1)} %refs_0_.3), channel_id=1, source_target_pairs={{0,2},{1,7},{2,4},{3,1},{4,6},{5,3},{6,0},{7,5},{8,10},{9,15},{10,... | collective-permute-start | bytes 1966088 | tf_op jit(solution)/shard_map/a1/ppermute | solution.py:34
  8.0 17.0 %collective-permute-start.7 = (bf16[512,640]{1,0:T(8,128)(2,1)}, bf16[512,640]{1,0:T(8,128)(2,1)S(1)}, u32[]{:S(2)}, u32[]{:S(2)}) collective-permute-start(bf16[512,640]{1,0:T(8,128)(2,1)} %refs_0_.3), channel_id=1, source_target_pairs={{0,6},{1,3},{2,0},{3,5},{4,2},{5,7},{6,4},{7,1},{8,14},{9,11},{10,... | collective-permute-start | bytes 1966088 | tf_op jit(solution)/shard_map/a2/ppermute | solution.py:34
  8.0 26.8 %collective-permute-start = (bf16[112,5120]{1,0:T(8,128)(2,1)}, bf16[112,5120]{1,0:T(8,128)(2,1)}, u32[]{:S(2)}, u32[]{:S(2)}) collective-permute-start(bf16[112,5120]{1,0:T(8,128)(2,1)} %refs_6_.3), channel_id=1, source_target_pairs={{0,8},{1,9},{2,10},{3,11},{4,12},{5,13},{6,14},{7,15},{8,16},{9,17... | collective-permute-start | bytes 3440648 | tf_op jit(solution)/shard_map/r1/ppermute | solution.py:34
  9.2 25.6 %collective-permute-start.1 = (bf16[112,5120]{1,0:T(8,128)(2,1)}, bf16[112,5120]{1,0:T(8,128)(2,1)}, u32[]{:S(2)}, u32[]{:S(2)}) collective-permute-start(bf16[112,5120]{1,0:T(8,128)(2,1)} %refs_6_.3), channel_id=1, source_target_pairs={{0,32},{1,25},{2,34},{3,27},{4,36},{5,29},{6,38},{7,31},{8,40},{9,... | collective-permute-start | bytes 3440648 | tf_op jit(solution)/shard_map/r2/ppermute | solution.py:34
  20.1 18.9 %collective-permute-start.2 = (bf16[112,5120]{1,0:T(8,128)(2,1)}, bf16[112,5120]{1,0:T(8,128)(2,1)}, u32[]{:S(2)}, u32[]{:S(2)}) collective-permute-start(bf16[112,5120]{1,0:T(8,128)(2,1)} %refs_6_.3), channel_id=1, source_target_pairs={{0,24},{1,33},{2,26},{3,35},{4,28},{5,37},{6,30},{7,39},{8,0},{9,4... | collective-permute-start | bytes 3440648 | tf_op jit(solution)/shard_map/r3/ppermute | solution.py:34
  21.2 17.7 %collective-permute-start.4 = (bf16[512,640]{1,0:T(8,128)(2,1)S(1)}, bf16[512,640]{1,0:T(8,128)(2,1)S(1)}, u32[]{:S(2)}, u32[]{:S(2)}) collective-permute-start(bf16[512,640]{1,0:T(8,128)(2,1)S(1)} %collective-permute-done.3.refs_0_), channel_id=1, source_target_pairs={{0,2},{1,7},{2,4},{3,1},{4,6},{5,3},{6,0},{7,5},{8,10},{9,15},{10,... | collective-permute-start | bytes 1966088 | tf_op jit(solution)/shard_map/b1/ppermute | solution.py:34
  25.0 17.1 %collective-permute-start.5 = (bf16[512,640]{1,0:T(8,128)(2,1)S(1)}, bf16[512,640]{1,0:T(8,128)(2,1)S(1)}, u32[]{:S(2)}, u32[]{:S(2)}) collective-permute-start(bf16[512,640]{1,0:T(8,128)(2,1)S(1)} %collective-permute-done.3.refs_0_), channel_id=1, source_target_pairs={{0,6},{1,3},{2,0},{3,5},{4,2},{5,7},{6,4},{7,1},{8,14},{9,11},{10,... | collective-permute-start | bytes 1966088 | tf_op jit(solution)/shard_map/b2/ppermute | solution.py:34
  28.1 24.2 %copy-start.1 = (bf16[512,1792]{1,0:T(8,128)(2,1)S(1)}, bf16[512,1792]{1,0:T(8,128)(2,1)}, u32[]{:S(2)}) copy-start(bf16[512,1792]{1,0:T(8,128)(2,1)} %up_ref.5) | copy-start | bytes 5505028
  28.1 24.2 %copy-start.5 = (bf16[1792,64]{0,1:T(8,128)(2,1)S(1)}, bf16[1792,64]{0,1:T(8,128)(2,1)}, u32[]{:S(2)}) copy-start(bf16[1792,64]{0,1:T(8,128)(2,1)} %param.14) | copy-start | bytes 688132
  42.3 18.2 %collective-permute-start.14 = (bf16[1536,640]{1,0:T(8,128)(2,1)S(1)}, bf16[1536,640]{1,0:T(8,128)(2,1)S(1)}, u32[]{:S(2)}, u32[]{:S(2)}) collective-permute-start(bf16[1536,640]{1,0:T(8,128)(2,1)S(1)} %pad_maximum_fusion), channel_id=1, source_target_pairs={{0,1},{1,0},{2,3},{3,2},{4,5},{5,4},{6,7},{7,6},{8,9},{9,8},{10,11... | collective-permute-start | bytes 5898248 | tf_op jit(solution)/shard_map/b_swap/ppermute | solution.py:34
  42.5 9.7 %collective-permute-start.11 = (bf16[512,640]{1,0:T(8,128)(2,1)S(1)}, bf16[512,640]{1,0:T(8,128)(2,1)S(1)}, u32[]{:S(2)}, u32[]{:S(2)}) collective-permute-start(bf16[512,640]{1,0:T(8,128)(2,1)S(1)} %collective-permute-done.4.refs_1_), channel_id=1, source_target_pairs={{0,2},{1,7},{2,4},{3,1},{4,6},{5,3},{6,0},{7,5},{8,10},{9,15},{10,... | collective-permute-start | bytes 1966088 | tf_op jit(solution)/shard_map/b_far/ppermute | solution.py:34
  43.2 19.0 %collective-permute-start.8 = (bf16[112,5120]{1,0:T(8,128)(2,1)}, bf16[112,5120]{1,0:T(8,128)(2,1)S(1)}, u32[]{:S(2)}, u32[]{:S(2)}) collective-permute-start(bf16[112,5120]{1,0:T(8,128)(2,1)} %collective-permute-done.1.refs_8_), channel_id=1, source_target_pairs={{0,8},{1,33},{2,10},{3,35},{4,12},{5,37},{6,14},{7,39},{8,16},{9,4... | collective-permute-start | bytes 3440648 | tf_op jit(solution)/shard_map/r4/ppermute | solution.py:34
  43.2 27.5 %collective-permute-start.9 = (bf16[112,5120]{1,0:T(8,128)(2,1)}, bf16[112,5120]{1,0:T(8,128)(2,1)S(1)}, u32[]{:S(2)}, u32[]{:S(2)}) collective-permute-start(bf16[112,5120]{1,0:T(8,128)(2,1)} %collective-permute-done.refs_7_), channel_id=1, source_target_pairs={{0,8},{1,33},{2,10},{3,35},{4,12},{5,37},{6,14},{7,39},{8,16},{9,4... | collective-permute-start | bytes 3440648 | tf_op jit(solution)/shard_map/r5/ppermute | solution.py:34
  44.7 27.0 %collective-permute-start.10 = (bf16[112,5120]{1,0:T(8,128)(2,1)}, bf16[112,5120]{1,0:T(8,128)(2,1)S(1)}, u32[]{:S(2)}, u32[]{:S(2)}) collective-permute-start(bf16[112,5120]{1,0:T(8,128)(2,1)} %collective-permute-done.1.refs_8_), channel_id=1, source_target_pairs={{0,24},{1,25},{2,26},{3,27},{4,28},{5,29},{6,30},{7,31},{8,0},{9,1... | collective-permute-start | bytes 3440648 | tf_op jit(solution)/shard_map/r6/ppermute | solution.py:34
  58.0 3.7 %collective-permute-start.13 = (f32[256,192]{1,0:T(8,128)S(1)}, f32[256,192]{1,0:T(8,128)S(1)}, u32[]{:S(2)}, u32[]{:S(2)}) collective-permute-start(f32[256,192]{1,0:T(8,128)S(1)} %slice_select_fusion), channel_id=1, source_target_pairs={{0,1},{1,0},{2,3},{3,2},{4,5},{5,4},{6,7},{7,6},{8,9},{9,8},{10,11... | collective-permute-start | bytes 589832 | tf_op jit(solution)/shard_map/s_core/ppermute | solution.py:34
  60.5 11.2 %collective-permute-start.12 = (bf16[512,640]{1,0:T(8,128)(2,1)S(1)}, bf16[512,640]{1,0:T(8,128)(2,1)S(1)}, u32[]{:S(2)}, u32[]{:S(2)}) collective-permute-start(bf16[512,640]{1,0:T(8,128)(2,1)S(1)} %collective-permute-done.6.refs_1_), channel_id=1, source_target_pairs={{0,2},{1,7},{2,4},{3,1},{4,6},{5,3},{6,0},{7,5},{8,10},{9,15},{10,... | collective-permute-start | bytes 1966088 | tf_op jit(solution)/shard_map/a_far/ppermute | solution.py:34
  61.6 10.1 %collective-permute-start.15 = (bf16[512,640]{1,0:T(8,128)(2,1)S(1)}, bf16[512,640]{1,0:T(8,128)(2,1)S(1)}, u32[]{:S(2)}, u32[]{:S(2)}) collective-permute-start(bf16[512,640]{1,0:T(8,128)(2,1)S(1)} %collective-permute-done.11.refs_3_), channel_id=1, source_target_pairs={{0,1},{1,0},{2,3},{3,2},{4,5},{5,4},{6,7},{7,6},{8,9},{9,8},{10,11... | collective-permute-start | bytes 1966088 | tf_op jit(solution)/shard_map/b_swap/ppermute | solution.py:34
  76.6 16.5 %collective-permute-start.16 = (bf16[1536,640]{1,0:T(8,128)(2,1)S(1)}, bf16[1536,640]{1,0:T(8,128)(2,1)S(1)}, u32[]{:S(2)}, u32[]{:S(2)}) collective-permute-start(bf16[1536,640]{1,0:T(8,128)(2,1)S(1)} %pad_maximum_fusion.1), channel_id=1, source_target_pairs={{0,1},{1,0},{2,3},{3,2},{4,5},{5,4},{6,7},{7,6},{8,9},{9,8},{10,11... | collective-permute-start | bytes 5898248 | tf_op jit(solution)/shard_map/a_swap/ppermute | solution.py:34
  77.8 22.9 %collective-permute-start.19 = (bf16[112,5120]{1,0:T(8,128)(2,1)S(1)}, bf16[112,5120]{1,0:T(8,128)(2,1)S(1)}, u32[]{:S(2)}, u32[]{:S(2)}) collective-permute-start(bf16[112,5120]{1,0:T(8,128)(2,1)S(1)} %collective-permute-done.10.refs_8_.refs_12_), channel_id=1, source_target_pairs={{0,24},{1,33},{2,26},{3,35},{4,28},{5,37},{6,30},{7,39},{8,0},{9,4... | collective-permute-start | bytes 3440648 | tf_op jit(solution)/shard_map/r7/ppermute | solution.py:34
  77.9 14.0 %collective-permute-start.17 = (bf16[512,640]{1,0:T(8,128)(2,1)S(1)}, bf16[512,640]{1,0:T(8,128)(2,1)S(1)}, u32[]{:S(2)}, u32[]{:S(2)}) collective-permute-start(bf16[512,640]{1,0:T(8,128)(2,1)S(1)} %collective-permute-done.12.refs_3_), channel_id=1, source_target_pairs={{0,1},{1,0},{2,3},{3,2},{4,5},{5,4},{6,7},{7,6},{8,9},{9,8},{10,11... | collective-permute-start | bytes 1966088 | tf_op jit(solution)/shard_map/a_swap/ppermute | solution.py:34
  81.5 19.2 %collective-permute-start.18 = (bf16[512,512]{1,0:T(8,128)(2,1)S(1)}, bf16[512,512]{1,0:T(8,128)(2,1)S(1)}, u32[]{:S(2)}, u32[]{:S(2)}) collective-permute-start(bf16[512,512]{1,0:T(8,128)(2,1)S(1)} %product.5), channel_id=1, source_target_pairs={{0,96},{1,97},{2,98},{3,99},{4,100},{5,101},{6,102},{7,103},{8,104... | collective-permute-start | bytes 1572872 | tf_op jit(solution)/shard_map/mate_grad1/ppermute | solution.py:34
  82.6 7.6 %collective-permute-start.22 = (f32[256,192]{1,0:T(8,128)S(1)}, f32[256,192]{1,0:T(8,128)S(1)}, u32[]{:S(2)}, u32[]{:S(2)}) collective-permute-start(f32[256,192]{1,0:T(8,128)S(1)} %select_add_fusion), channel_id=1, source_target_pairs={{0,2},{1,3},{2,0},{3,1},{4,6},{5,7},{6,4},{7,5},{8,10},{9,11},{10,... | collective-permute-start | bytes 589832 | tf_op jit(solution)/shard_map/s_near/ppermute | solution.py:34
  90.3 19.0 %collective-permute-start.20 = (bf16[512,384]{1,0:T(8,128)(2,1)S(1)}, bf16[512,384]{1,0:T(8,128)(2,1)S(1)}, u32[]{:S(2)}, u32[]{:S(2)}) collective-permute-start(bf16[512,384]{1,0:T(8,128)(2,1)S(1)} %product.6), channel_id=1, source_target_pairs={{0,96},{1,97},{2,98},{3,99},{4,100},{5,101},{6,102},{7,103},{8,104... | collective-permute-start | bytes 1179656 | tf_op jit(solution)/shard_map/mate_grad2/ppermute | solution.py:34
  91.9 11.4 %collective-permute-start.23 = (f32[256,192]{1,0:T(8,128)S(1)}, f32[256,192]{1,0:T(8,128)S(1)}, u32[]{:S(2)}, u32[]{:S(2)}) collective-permute-start(f32[256,192]{1,0:T(8,128)S(1)} %add.231), channel_id=1, source_target_pairs={{0,4},{1,5},{2,6},{3,7},{4,0},{5,1},{6,2},{7,3},{8,12},{9,13},{10,... | collective-permute-start | bytes 589832 | tf_op jit(solution)/shard_map/s_far/ppermute | solution.py:34
  102.9 6.4 %collective-permute-start.21 = (bf16[512,128]{1,0:T(8,128)(2,1)S(1)}, bf16[512,128]{1,0:T(8,128)(2,1)S(1)}, u32[]{:S(2)}, u32[]{:S(2)}) collective-permute-start(bf16[512,128]{1,0:T(8,128)(2,1)S(1)} %product.8), channel_id=1, source_target_pairs={{0,96},{1,97},{2,98},{3,99},{4,100},{5,101},{6,102},{7,103},{8,104... | collective-permute-start | bytes 393224 | tf_op jit(solution)/shard_map/mate_grad3/ppermute | solution.py:34
  109.3 5.8 %collective-permute-start.24 = (f32[256,192]{1,0:T(8,128)S(1)}, f32[256,192]{1,0:T(8,128)S(1)}, u32[]{:S(2)}, u32[]{:S(2)}) collective-permute-start(f32[256,192]{1,0:T(8,128)S(1)} %add.232), channel_id=1, source_target_pairs={{0,1},{1,0},{2,3},{3,2},{4,5},{5,4},{6,7},{7,6},{8,9},{9,8},{10,11... | collective-permute-start | bytes 589832 | tf_op jit(solution)/shard_map/s_core/ppermute | solution.py:34
  116.6 1.3 %collective-permute-start.25 = (f32[128,128]{1,0:T(8,128)S(1)}, f32[128,128]{1,0:T(8,128)S(1)}, u32[]{:S(2)}, u32[]{:S(2)}) collective-permute-start(f32[128,128]{1,0:T(8,128)S(1)} %slice_select_fusion.1), channel_id=1, source_target_pairs={{0,1},{1,0},{2,3},{3,2},{4,5},{5,4},{6,7},{7,6},{8,9},{9,8},{10,11... | collective-permute-start | bytes 196616 | tf_op jit(solution)/shard_map/swap/ppermute | solution.py:34
  118.0 4.8 %collective-permute-start.27 = (f32[128,128]{1,0:T(8,128)S(1)}, f32[128,128]{1,0:T(8,128)S(1)}, u32[]{:S(2)}, u32[]{:S(2)}) collective-permute-start(f32[128,128]{1,0:T(8,128)S(1)} %select_add_fusion.1), channel_id=1, source_target_pairs={{0,2},{1,3},{2,4},{3,5},{4,6},{5,7},{6,0},{7,1},{8,10},{9,11},{10,... | collective-permute-start | bytes 196616 | tf_op jit(solution)/shard_map/up/ppermute | solution.py:34
  118.8 4.1 %collective-permute-start.28 = (f32[128,128]{1,0:T(8,128)S(1)}, f32[128,128]{1,0:T(8,128)S(1)}, u32[]{:S(2)}, u32[]{:S(2)}) collective-permute-start(f32[128,128]{1,0:T(8,128)S(1)} %select_add_fusion.1), channel_id=1, source_target_pairs={{0,6},{1,7},{2,0},{3,1},{4,2},{5,3},{6,4},{7,5},{8,14},{9,15},{10,... | collective-permute-start | bytes 196616 | tf_op jit(solution)/shard_map/down/ppermute | solution.py:34
  120.7 4.6 %collective-permute-start.26 = (f32[128,128]{1,0:T(8,128)S(1)}, f32[128,128]{1,0:T(8,128)S(1)}, u32[]{:S(2)}, u32[]{:S(2)}) collective-permute-start(f32[128,128]{1,0:T(8,128)S(1)} %select_add_fusion.1), channel_id=1, source_target_pairs={{0,4},{1,5},{2,6},{3,7},{4,0},{5,1},{6,2},{7,3},{8,12},{9,13},{10,... | collective-permute-start | bytes 196616 | tf_op jit(solution)/shard_map/send/ppermute | solution.py:34
  125.4 2.8 %collective-permute-start.29 = (f32[128,128]{1,0:T(8,128)S(1)}, f32[128,128]{1,0:T(8,128)S(1)}, u32[]{:S(2)}, u32[]{:S(2)}) collective-permute-start(f32[128,128]{1,0:T(8,128)S(1)} %add_add_fusion), channel_id=1, source_target_pairs={{0,1},{1,0},{2,3},{3,2},{4,5},{5,4},{6,7},{7,6},{8,9},{9,8},{10,11... | collective-permute-start | bytes 196616 | tf_op jit(solution)/shard_map/swap/ppermute | solution.py:34
  (6 other events, 47.7 us)
